TPU v7x, 256 devices: a whole 4x4x8 slice. The times are simulated.
256 devices in a mesh: gx: 32 (over y, z), gy: 8 (over x, core).
Axes of the slice: x: 4, y: 4, z: 8, core: 2. Of those that a mesh axis runs over, the one named last changes fastest.
Arguments:
- rhs: bfloat16 [512, 262144], P(None, ('gy', 'gx')), may hold values from -6 to 6
- leaf_inverse: bfloat16 [256, 1024, 1024], P(('gy', 'gx')), may hold values from -0.1875 to 0.1875
- up_basis: bfloat16 [8, 128, 262144], P(None, None, ('gy', 'gx')), may hold values from -0.25 to 0.25
- projection: bfloat16 [8, 256, 262144], P(None, None, ('gy', 'gx')), may hold values from -0.13258252 to 0.13258252, as said below
Outputs:
- solution: float32 [512, 262144], P(None, ('gy', 'gx'))
Inputs may be any that keep to these rules, and one draw needn't show every extreme that they name: `projection`: rows of level h (counted from 1) have entries of order (2^h * 1024)^(-1/2).
All inputs are finite; a program needn't handle non-finite values.
Results may differ from a plain program's by a relative error of at most 0.0095.
Values sent between devices are 32-bit elements; how exact they have to be, the bound alone decides.
No kernel may reach another device: no remote copies, remote signals or barrier semaphores. Data moves between devices by JAX's collectives and lax.ppermute only.
A program may use at most 64 MiB of HBM per device.

v0:
```python
import jax
import jax.numpy as jnp
from jax import lax
from jax.sharding import PartitionSpec as P

RANK = 128


def partner(value, axis, stride):
    mask = 2**stride
    pairs = [(source, source ^ mask) for source in range(lax.axis_size(axis))]
    return lax.ppermute(value, axis, pairs)


def own_half(partial_value, child_bit):
    return lax.dynamic_slice_in_dim(partial_value, child_bit * RANK, RANK, 1)


def node_sum(partial_value, height, bits_x, child_bit):
    mine = own_half(partial_value, child_bit)
    other = own_half(partial_value, 1 - child_bit)
    if height <= bits_x:
        total = mine + partner(other, "gx", height - 1)
        for bit_pos in range(height - 1):
            total = total + partner(total, "gx", bit_pos)
        return total
    total = mine + partner(other, "gy", height - 1 - bits_x)
    for bit_pos in range(bits_x):
        total = total + partner(total, "gx", bit_pos)
    for bit_pos in range(height - 1 - bits_x):
        total = total + partner(total, "gy", bit_pos)
    return total


def shards(rhs, leaf_inverse, up_basis, projection):
    size_x = lax.axis_size("gx")
    bits_x = size_x.bit_length() - 1
    bits_y = lax.axis_size("gy").bit_length() - 1
    leaf_pos = lax.axis_index("gy") * size_x + lax.axis_index("gx")
    state = jnp.dot(rhs, leaf_inverse[0], preferred_element_type=jnp.float32)
    for height in range(1, bits_x + bits_y + 1):
        rounded = state.astype(jnp.bfloat16)
        partial_value = lax.dot_general(
            rounded,
            projection[height - 1],
            (((1,), (1,)), ((), ())),
            preferred_element_type=jnp.float32,
        )
        child_bit = leaf_pos >> height - 1 & 1
        node_total = node_sum(partial_value, height, bits_x, child_bit)
        coefficient = node_total.astype(jnp.bfloat16)
        state = state - jnp.dot(
            coefficient, up_basis[height - 1], preferred_element_type=jnp.float32
        )
    return state


def solution(mesh):
    return jax.shard_map(
        shards,
        mesh=mesh,
        in_specs=(
            P(None, ("gy", "gx")),
            P(("gy", "gx"), None, None),
            P(None, None, ("gy", "gx")),
            P(None, None, ("gy", "gx")),
        ),
        out_specs=P(None, ("gy", "gx")),
        check_vma=False,
    )
```

profile of v0, /device:TPU:1, one launch (start us, length us, event | category | flops | bytes accessed | tf_op | source)
XLA Modules:
  0.0 408.7 jit_solution(12366668345906977567)
XLA Ops:
  23.5 11.3 %collective-permute-done.1 = f32[512,128]{1,0:T(8,128)S(1)} collective-permute-done((f32[512,128]{1,0:T(8,128)S(1)}, f32[512,128]{1,0:T(8,128)S(1)}, u32[]{:S(2)}, u32[]{:S(2)}) %collective-permute-start.1) | collective-permute-done | bytes 262176 | tf_op jit(solution)/shard_map/ppermute | solution.py:12
  36.5 5.2 %collective-permute-done.2 = f32[512,128]{1,0:T(8,128)S(1)} collective-permute-done((f32[512,128]{1,0:T(8,128)S(1)}, f32[512,128]{1,0:T(8,128)S(1)}, u32[]{:S(2)}, u32[]{:S(2)}) %collective-permute-start.2) | collective-permute-done | bytes 262176 | tf_op jit(solution)/shard_map/ppermute | solution.py:12
  46.6 6.6 %collective-permute-start.3 = (f32[512,128]{1,0:T(8,128)S(1)}, f32[512,128]{1,0:T(8,128)S(1)}, u32[]{:S(2)}, u32[]{:S(2)}) collective-permute-start(f32[512,128]{1,0:T(8,128)S(1)} %constant_dynamic-slice_fusion.5), channel_id=1, source_target_pairs={{0,32},{8,40},{16,48},{24,56},{32,0},{40,8},{48,16},{56,24},{64,96... | collective-permute-start | bytes 786440 | tf_op jit(solution)/shard_map/ppermute | solution.py:12
  61.1 10.2 %collective-permute-done.4 = f32[512,128]{1,0:T(8,128)S(1)} collective-permute-done((f32[512,128]{1,0:T(8,128)S(1)}, f32[512,128]{1,0:T(8,128)S(1)}, u32[]{:S(2)}, u32[]{:S(2)}) %collective-permute-start.4) | collective-permute-done | bytes 262176 | tf_op jit(solution)/shard_map/ppermute | solution.py:12
  74.8 12.3 %collective-permute-done.5 = f32[512,128]{1,0:T(8,128)S(1)} collective-permute-done((f32[512,128]{1,0:T(8,128)S(1)}, f32[512,128]{1,0:T(8,128)S(1)}, u32[]{:S(2)}, u32[]{:S(2)}) %collective-permute-start.5) | collective-permute-done | bytes 262176 | tf_op jit(solution)/shard_map/ppermute | solution.py:12
  93.4 6.0 %collective-permute-done.6 = f32[512,128]{1,0:T(8,128)S(1)} collective-permute-done((f32[512,128]{1,0:T(8,128)S(1)}, f32[512,128]{1,0:T(8,128)S(1)}, u32[]{:S(2)}, u32[]{:S(2)}) %collective-permute-start.6) | collective-permute-done | bytes 262176 | tf_op jit(solution)/shard_map/ppermute | solution.py:12
  99.6 6.3 %collective-permute-done.7 = f32[512,128]{1,0:T(8,128)S(1)} collective-permute-done((f32[512,128]{1,0:T(8,128)S(1)}, f32[512,128]{1,0:T(8,128)S(1)}, u32[]{:S(2)}, u32[]{:S(2)}) %collective-permute-start.7) | collective-permute-done | bytes 262176 | tf_op jit(solution)/shard_map/ppermute | solution.py:12
  106.0 14.7 %collective-permute-done.8 = f32[512,128]{1,0:T(8,128)S(1)} collective-permute-done((f32[512,128]{1,0:T(8,128)S(1)}, f32[512,128]{1,0:T(8,128)S(1)}, u32[]{:S(2)}, u32[]{:S(2)}) %collective-permute-start.8) | collective-permute-done | bytes 262176 | tf_op jit(solution)/shard_map/ppermute | solution.py:12
  120.9 14.0 %collective-permute-done.9 = f32[512,128]{1,0:T(8,128)S(1)} collective-permute-done((f32[512,128]{1,0:T(8,128)S(1)}, f32[512,128]{1,0:T(8,128)S(1)}, u32[]{:S(2)}, u32[]{:S(2)}) %collective-permute-start.9) | collective-permute-done | bytes 262176 | tf_op jit(solution)/shard_map/ppermute | solution.py:12
  147.9 5.2 %collective-permute-done.11 = f32[512,128]{1,0:T(8,128)S(1)} collective-permute-done((f32[512,128]{1,0:T(8,128)S(1)}, f32[512,128]{1,0:T(8,128)S(1)}, u32[]{:S(2)}, u32[]{:S(2)}) %collective-permute-start.11) | collective-permute-done | bytes 262176 | tf_op jit(solution)/shard_map/ppermute | solution.py:12
  153.4 13.8 %collective-permute-done.12 = f32[512,128]{1,0:T(8,128)S(1)} collective-permute-done((f32[512,128]{1,0:T(8,128)S(1)}, f32[512,128]{1,0:T(8,128)S(1)}, u32[]{:S(2)}, u32[]{:S(2)}) %collective-permute-start.12) | collective-permute-done | bytes 262176 | tf_op jit(solution)/shard_map/ppermute | solution.py:12
  169.4 14.7 %collective-permute-done.13 = f32[512,128]{1,0:T(8,128)S(1)} collective-permute-done((f32[512,128]{1,0:T(8,128)S(1)}, f32[512,128]{1,0:T(8,128)S(1)}, u32[]{:S(2)}, u32[]{:S(2)}) %collective-permute-start.13) | collective-permute-done | bytes 262176 | tf_op jit(solution)/shard_map/ppermute | solution.py:12
  184.7 6.9 %collective-permute-done.14 = f32[512,128]{1,0:T(8,128)S(1)} collective-permute-done((f32[512,128]{1,0:T(8,128)S(1)}, f32[512,128]{1,0:T(8,128)S(1)}, u32[]{:S(2)}, u32[]{:S(2)}) %collective-permute-start.14) | collective-permute-done | bytes 262176 | tf_op jit(solution)/shard_map/ppermute | solution.py:12
  199.3 7.5 %collective-permute-done.16 = f32[512,128]{1,0:T(8,128)S(1)} collective-permute-done((f32[512,128]{1,0:T(8,128)S(1)}, f32[512,128]{1,0:T(8,128)S(1)}, u32[]{:S(2)}, u32[]{:S(2)}) %collective-permute-start.16) | collective-permute-done | bytes 262176 | tf_op jit(solution)/shard_map/ppermute | solution.py:12
  207.0 14.7 %collective-permute-done.17 = f32[512,128]{1,0:T(8,128)S(1)} collective-permute-done((f32[512,128]{1,0:T(8,128)S(1)}, f32[512,128]{1,0:T(8,128)S(1)}, u32[]{:S(2)}, u32[]{:S(2)}) %collective-permute-start.17) | collective-permute-done | bytes 262176 | tf_op jit(solution)/shard_map/ppermute | solution.py:12
  224.7 14.7 %collective-permute-done.18 = f32[512,128]{1,0:T(8,128)S(1)} collective-permute-done((f32[512,128]{1,0:T(8,128)S(1)}, f32[512,128]{1,0:T(8,128)S(1)}, u32[]{:S(2)}, u32[]{:S(2)}) %collective-permute-start.18) | collective-permute-done | bytes 262176 | tf_op jit(solution)/shard_map/ppermute | solution.py:12
  239.8 7.1 %collective-permute-done.19 = f32[512,128]{1,0:T(8,128)S(1)} collective-permute-done((f32[512,128]{1,0:T(8,128)S(1)}, f32[512,128]{1,0:T(8,128)S(1)}, u32[]{:S(2)}, u32[]{:S(2)}) %collective-permute-start.19) | collective-permute-done | bytes 262176 | tf_op jit(solution)/shard_map/ppermute | solution.py:12
  247.0 7.9 %collective-permute-done.20 = f32[512,128]{1,0:T(8,128)S(1)} collective-permute-done((f32[512,128]{1,0:T(8,128)S(1)}, f32[512,128]{1,0:T(8,128)S(1)}, u32[]{:S(2)}, u32[]{:S(2)}) %collective-permute-start.20) | collective-permute-done | bytes 262176 | tf_op jit(solution)/shard_map/ppermute | solution.py:12
  265.7 5.2 %collective-permute-done.22 = f32[512,128]{1,0:T(8,128)S(1)} collective-permute-done((f32[512,128]{1,0:T(8,128)S(1)}, f32[512,128]{1,0:T(8,128)S(1)}, u32[]{:S(2)}, u32[]{:S(2)}) %collective-permute-start.22) | collective-permute-done | bytes 262176 | tf_op jit(solution)/shard_map/ppermute | solution.py:12
  271.1 12.2 %collective-permute-done.23 = f32[512,128]{1,0:T(8,128)S(1)} collective-permute-done((f32[512,128]{1,0:T(8,128)S(1)}, f32[512,128]{1,0:T(8,128)S(1)}, u32[]{:S(2)}, u32[]{:S(2)}) %collective-permute-start.23) | collective-permute-done | bytes 262176 | tf_op jit(solution)/shard_map/ppermute | solution.py:12
  285.8 13.9 %collective-permute-done.24 = f32[512,128]{1,0:T(8,128)S(1)} collective-permute-done((f32[512,128]{1,0:T(8,128)S(1)}, f32[512,128]{1,0:T(8,128)S(1)}, u32[]{:S(2)}, u32[]{:S(2)}) %collective-permute-start.24) | collective-permute-done | bytes 262176 | tf_op jit(solution)/shard_map/ppermute | solution.py:12
  299.9 5.2 %collective-permute-done.25 = f32[512,128]{1,0:T(8,128)S(1)} collective-permute-done((f32[512,128]{1,0:T(8,128)S(1)}, f32[512,128]{1,0:T(8,128)S(1)}, u32[]{:S(2)}, u32[]{:S(2)}) %collective-permute-start.25) | collective-permute-done | bytes 262176 | tf_op jit(solution)/shard_map/ppermute | solution.py:12
  305.1 6.1 %collective-permute-start.26 = (f32[512,128]{1,0:T(8,128)S(1)}, f32[512,128]{1,0:T(8,128)S(1)}, u32[]{:S(2)}, u32[]{:S(2)}) collective-permute-start(f32[512,128]{1,0:T(8,128)S(1)} %add.199), channel_id=1, source_target_pairs={{0,128},{8,136},{16,144},{24,152},{32,160},{40,168},{48,176},{56,1... | collective-permute-start | bytes 786440 | tf_op jit(solution)/shard_map/ppermute | solution.py:12
  315.9 5.1 %collective-permute-start.27 = (f32[512,128]{1,0:T(8,128)S(1)}, f32[512,128]{1,0:T(8,128)S(1)}, u32[]{:S(2)}, u32[]{:S(2)}) collective-permute-start(f32[512,128]{1,0:T(8,128)S(1)} %add.200), channel_id=1, source_target_pairs={{0,1},{1,0},{2,3},{3,2},{4,5},{5,4},{6,7},{7,6},{8,9},{9,8},{10,11... | collective-permute-start | bytes 786440 | tf_op jit(solution)/shard_map/ppermute | solution.py:12
  327.1 5.1 %collective-permute-start.28 = (f32[512,128]{1,0:T(8,128)S(1)}, f32[512,128]{1,0:T(8,128)S(1)}, u32[]{:S(2)}, u32[]{:S(2)}) collective-permute-start(f32[512,128]{1,0:T(8,128)S(1)} %constant_dynamic-slice_fusion), channel_id=1, source_target_pairs={{0,4},{1,5},{2,6},{3,7},{4,0},{5,1},{6,2},{7,3},{8,12},{9,13},{10,... | collective-permute-start | bytes 786440 | tf_op jit(solution)/shard_map/ppermute | solution.py:12
  332.2 6.4 %collective-permute-done.28 = f32[512,128]{1,0:T(8,128)S(1)} collective-permute-done((f32[512,128]{1,0:T(8,128)S(1)}, f32[512,128]{1,0:T(8,128)S(1)}, u32[]{:S(2)}, u32[]{:S(2)}) %collective-permute-start.28) | collective-permute-done | bytes 262176 | tf_op jit(solution)/shard_map/ppermute | solution.py:12
  338.9 6.9 %collective-permute-done.29 = f32[512,128]{1,0:T(8,128)S(1)} collective-permute-done((f32[512,128]{1,0:T(8,128)S(1)}, f32[512,128]{1,0:T(8,128)S(1)}, u32[]{:S(2)}, u32[]{:S(2)}) %collective-permute-start.29) | collective-permute-done | bytes 262176 | tf_op jit(solution)/shard_map/ppermute | solution.py:12
  346.0 14.7 %collective-permute-done.30 = f32[512,128]{1,0:T(8,128)S(1)} collective-permute-done((f32[512,128]{1,0:T(8,128)S(1)}, f32[512,128]{1,0:T(8,128)S(1)}, u32[]{:S(2)}, u32[]{:S(2)}) %collective-permute-start.30) | collective-permute-done | bytes 262176 | tf_op jit(solution)/shard_map/ppermute | solution.py:12
  364.1 14.3 %collective-permute-done.31 = f32[512,128]{1,0:T(8,128)S(1)} collective-permute-done((f32[512,128]{1,0:T(8,128)S(1)}, f32[512,128]{1,0:T(8,128)S(1)}, u32[]{:S(2)}, u32[]{:S(2)}) %collective-permute-start.31) | collective-permute-done | bytes 262176 | tf_op jit(solution)/shard_map/ppermute | solution.py:12
  380.7 6.0 %collective-permute-done.32 = f32[512,128]{1,0:T(8,128)S(1)} collective-permute-done((f32[512,128]{1,0:T(8,128)S(1)}, f32[512,128]{1,0:T(8,128)S(1)}, u32[]{:S(2)}, u32[]{:S(2)}) %collective-permute-start.32) | collective-permute-done | bytes 262176 | tf_op jit(solution)/shard_map/ppermute | solution.py:12
  387.2 7.7 %collective-permute-done.33 = f32[512,128]{1,0:T(8,128)S(1)} collective-permute-done((f32[512,128]{1,0:T(8,128)S(1)}, f32[512,128]{1,0:T(8,128)S(1)}, u32[]{:S(2)}, u32[]{:S(2)}) %collective-permute-start.33) | collective-permute-done | bytes 262176 | tf_op jit(solution)/shard_map/ppermute | solution.py:12
  398.5 7.5 %collective-permute-done.35 = f32[512,128]{1,0:T(8,128)S(1)} collective-permute-done((f32[512,128]{1,0:T(8,128)S(1)}, f32[512,128]{1,0:T(8,128)S(1)}, u32[]{:S(2)}, u32[]{:S(2)}) %collective-permute-start.35) | collective-permute-done | bytes 262176 | tf_op jit(solution)/shard_map/ppermute | solution.py:12
  (113 shorter events, 112.7 us)
Async XLA Ops:
  7.0 7.5 %collective-permute-start = (f32[512,128]{1,0:T(8,128)S(1)}, f32[512,128]{1,0:T(8,128)S(1)}, u32[]{:S(2)}, u32[]{:S(2)}) collective-permute-start(f32[512,128]{1,0:T(8,128)S(1)} %constant_dynamic-slice_fusion.7), channel_id=1, source_target_pairs={{0,8},{8,0},{16,24},{24,16},{32,40},{40,32},{48,56},{56,48},{64,72... | collective-permute-start | bytes 786440 | tf_op jit(solution)/shard_map/ppermute | solution.py:12
  19.5 15.4 %collective-permute-start.1 = (f32[512,128]{1,0:T(8,128)S(1)}, f32[512,128]{1,0:T(8,128)S(1)}, u32[]{:S(2)}, u32[]{:S(2)}) collective-permute-start(f32[512,128]{1,0:T(8,128)S(1)} %constant_dynamic-slice_fusion.6), channel_id=1, source_target_pairs={{0,16},{8,24},{16,0},{24,8},{32,48},{40,56},{48,32},{56,40},{64,80... | collective-permute-start | bytes 786440 | tf_op jit(solution)/shard_map/ppermute | solution.py:12
  34.9 6.8 %collective-permute-start.2 = (f32[512,128]{1,0:T(8,128)S(1)}, f32[512,128]{1,0:T(8,128)S(1)}, u32[]{:S(2)}, u32[]{:S(2)}) collective-permute-start(f32[512,128]{1,0:T(8,128)S(1)} %dynamic-slice_add_fusion.6), channel_id=1, source_target_pairs={{0,8},{8,0},{16,24},{24,16},{32,40},{40,32},{48,56},{56,48},{64,72... | collective-permute-start | bytes 786440 | tf_op jit(solution)/shard_map/ppermute | solution.py:12
  46.6 11.3 %collective-permute-start.3 = (f32[512,128]{1,0:T(8,128)S(1)}, f32[512,128]{1,0:T(8,128)S(1)}, u32[]{:S(2)}, u32[]{:S(2)}) collective-permute-start(f32[512,128]{1,0:T(8,128)S(1)} %constant_dynamic-slice_fusion.5), channel_id=1, source_target_pairs={{0,32},{8,40},{16,48},{24,56},{32,0},{40,8},{48,16},{56,24},{64,96... | collective-permute-start | bytes 786440 | tf_op jit(solution)/shard_map/ppermute | solution.py:12
  58.0 13.3 %collective-permute-start.4 = (f32[512,128]{1,0:T(8,128)S(1)}, f32[512,128]{1,0:T(8,128)S(1)}, u32[]{:S(2)}, u32[]{:S(2)}) collective-permute-start(f32[512,128]{1,0:T(8,128)S(1)} %dynamic-slice_add_fusion.5), channel_id=1, source_target_pairs={{0,8},{8,0},{16,24},{24,16},{32,40},{40,32},{48,56},{56,48},{64,72... | collective-permute-start | bytes 786440 | tf_op jit(solution)/shard_map/ppermute | solution.py:12
  71.3 15.8 %collective-permute-start.5 = (f32[512,128]{1,0:T(8,128)S(1)}, f32[512,128]{1,0:T(8,128)S(1)}, u32[]{:S(2)}, u32[]{:S(2)}) collective-permute-start(f32[512,128]{1,0:T(8,128)S(1)} %add.170), channel_id=1, source_target_pairs={{0,16},{8,24},{16,0},{24,8},{32,48},{40,56},{48,32},{56,40},{64,80... | collective-permute-start | bytes 786440 | tf_op jit(solution)/shard_map/ppermute | solution.py:12
  92.1 7.4 %collective-permute-start.6 = (f32[512,128]{1,0:T(8,128)S(1)}, f32[512,128]{1,0:T(8,128)S(1)}, u32[]{:S(2)}, u32[]{:S(2)}) collective-permute-start(f32[512,128]{1,0:T(8,128)S(1)} %constant_dynamic-slice_fusion.4), channel_id=1, source_target_pairs={{0,64},{8,72},{16,80},{24,88},{32,96},{40,104},{48,112},{56,120},{... | collective-permute-start | bytes 786440 | tf_op jit(solution)/shard_map/ppermute | solution.py:12
  99.5 6.4 %collective-permute-start.7 = (f32[512,128]{1,0:T(8,128)S(1)}, f32[512,128]{1,0:T(8,128)S(1)}, u32[]{:S(2)}, u32[]{:S(2)}) collective-permute-start(f32[512,128]{1,0:T(8,128)S(1)} %dynamic-slice_add_fusion.4), channel_id=1, source_target_pairs={{0,8},{8,0},{16,24},{24,16},{32,40},{40,32},{48,56},{56,48},{64,72... | collective-permute-start | bytes 786440 | tf_op jit(solution)/shard_map/ppermute | solution.py:12
  105.9 14.8 %collective-permute-start.8 = (f32[512,128]{1,0:T(8,128)S(1)}, f32[512,128]{1,0:T(8,128)S(1)}, u32[]{:S(2)}, u32[]{:S(2)}) collective-permute-start(f32[512,128]{1,0:T(8,128)S(1)} %add.175), channel_id=1, source_target_pairs={{0,16},{8,24},{16,0},{24,8},{32,48},{40,56},{48,32},{56,40},{64,80... | collective-permute-start | bytes 786440 | tf_op jit(solution)/shard_map/ppermute | solution.py:12
  120.8 14.1 %collective-permute-start.9 = (f32[512,128]{1,0:T(8,128)S(1)}, f32[512,128]{1,0:T(8,128)S(1)}, u32[]{:S(2)}, u32[]{:S(2)}) collective-permute-start(f32[512,128]{1,0:T(8,128)S(1)} %add.176), channel_id=1, source_target_pairs={{0,32},{8,40},{16,48},{24,56},{32,0},{40,8},{48,16},{56,24},{64,96... | collective-permute-start | bytes 786440 | tf_op jit(solution)/shard_map/ppermute | solution.py:12
  139.9 7.9 %collective-permute-start.10 = (f32[512,128]{1,0:T(8,128)S(1)}, f32[512,128]{1,0:T(8,128)S(1)}, u32[]{:S(2)}, u32[]{:S(2)}) collective-permute-start(f32[512,128]{1,0:T(8,128)S(1)} %constant_dynamic-slice_fusion.3), channel_id=1, source_target_pairs={{0,128},{8,136},{16,144},{24,152},{32,160},{40,168},{48,176},{56,1... | collective-permute-start | bytes 786440 | tf_op jit(solution)/shard_map/ppermute | solution.py:12
  147.8 5.3 %collective-permute-start.11 = (f32[512,128]{1,0:T(8,128)S(1)}, f32[512,128]{1,0:T(8,128)S(1)}, u32[]{:S(2)}, u32[]{:S(2)}) collective-permute-start(f32[512,128]{1,0:T(8,128)S(1)} %dynamic-slice_add_fusion.3), channel_id=1, source_target_pairs={{0,8},{8,0},{16,24},{24,16},{32,40},{40,32},{48,56},{56,48},{64,72... | collective-permute-start | bytes 786440 | tf_op jit(solution)/shard_map/ppermute | solution.py:12
  153.1 14.0 %collective-permute-start.12 = (f32[512,128]{1,0:T(8,128)S(1)}, f32[512,128]{1,0:T(8,128)S(1)}, u32[]{:S(2)}, u32[]{:S(2)}) collective-permute-start(f32[512,128]{1,0:T(8,128)S(1)} %add.181), channel_id=1, source_target_pairs={{0,16},{8,24},{16,0},{24,8},{32,48},{40,56},{48,32},{56,40},{64,80... | collective-permute-start | bytes 786440 | tf_op jit(solution)/shard_map/ppermute | solution.py:12
  167.2 16.9 %collective-permute-start.13 = (f32[512,128]{1,0:T(8,128)S(1)}, f32[512,128]{1,0:T(8,128)S(1)}, u32[]{:S(2)}, u32[]{:S(2)}) collective-permute-start(f32[512,128]{1,0:T(8,128)S(1)} %add.182), channel_id=1, source_target_pairs={{0,32},{8,40},{16,48},{24,56},{32,0},{40,8},{48,16},{56,24},{64,96... | collective-permute-start | bytes 786440 | tf_op jit(solution)/shard_map/ppermute | solution.py:12
  184.1 7.5 %collective-permute-start.14 = (f32[512,128]{1,0:T(8,128)S(1)}, f32[512,128]{1,0:T(8,128)S(1)}, u32[]{:S(2)}, u32[]{:S(2)}) collective-permute-start(f32[512,128]{1,0:T(8,128)S(1)} %add.183), channel_id=1, source_target_pairs={{0,64},{8,72},{16,80},{24,88},{32,96},{40,104},{48,112},{56,120},{... | collective-permute-start | bytes 786440 | tf_op jit(solution)/shard_map/ppermute | solution.py:12
  199.2 7.6 %collective-permute-start.16 = (f32[512,128]{1,0:T(8,128)S(1)}, f32[512,128]{1,0:T(8,128)S(1)}, u32[]{:S(2)}, u32[]{:S(2)}) collective-permute-start(f32[512,128]{1,0:T(8,128)S(1)} %dynamic-slice_add_fusion.2), channel_id=1, source_target_pairs={{0,8},{8,0},{16,24},{24,16},{32,40},{40,32},{48,56},{56,48},{64,72... | collective-permute-start | bytes 786440 | tf_op jit(solution)/shard_map/ppermute | solution.py:12
  206.9 14.8 %collective-permute-start.17 = (f32[512,128]{1,0:T(8,128)S(1)}, f32[512,128]{1,0:T(8,128)S(1)}, u32[]{:S(2)}, u32[]{:S(2)}) collective-permute-start(f32[512,128]{1,0:T(8,128)S(1)} %add.188), channel_id=1, source_target_pairs={{0,16},{8,24},{16,0},{24,8},{32,48},{40,56},{48,32},{56,40},{64,80... | collective-permute-start | bytes 786440 | tf_op jit(solution)/shard_map/ppermute | solution.py:12
  221.7 17.7 %collective-permute-start.18 = (f32[512,128]{1,0:T(8,128)S(1)}, f32[512,128]{1,0:T(8,128)S(1)}, u32[]{:S(2)}, u32[]{:S(2)}) collective-permute-start(f32[512,128]{1,0:T(8,128)S(1)} %add.189), channel_id=1, source_target_pairs={{0,32},{8,40},{16,48},{24,56},{32,0},{40,8},{48,16},{56,24},{64,96... | collective-permute-start | bytes 786440 | tf_op jit(solution)/shard_map/ppermute | solution.py:12
  239.4 7.5 %collective-permute-start.19 = (f32[512,128]{1,0:T(8,128)S(1)}, f32[512,128]{1,0:T(8,128)S(1)}, u32[]{:S(2)}, u32[]{:S(2)}) collective-permute-start(f32[512,128]{1,0:T(8,128)S(1)} %add.190), channel_id=1, source_target_pairs={{0,64},{8,72},{16,80},{24,88},{32,96},{40,104},{48,112},{56,120},{... | collective-permute-start | bytes 786440 | tf_op jit(solution)/shard_map/ppermute | solution.py:12
  246.9 8.1 %collective-permute-start.20 = (f32[512,128]{1,0:T(8,128)S(1)}, f32[512,128]{1,0:T(8,128)S(1)}, u32[]{:S(2)}, u32[]{:S(2)}) collective-permute-start(f32[512,128]{1,0:T(8,128)S(1)} %add.191), channel_id=1, source_target_pairs={{0,128},{8,136},{16,144},{24,152},{32,160},{40,168},{48,176},{56,1... | collective-permute-start | bytes 786440 | tf_op jit(solution)/shard_map/ppermute | solution.py:12
  260.0 5.6 %collective-permute-start.21 = (f32[512,128]{1,0:T(8,128)S(1)}, f32[512,128]{1,0:T(8,128)S(1)}, u32[]{:S(2)}, u32[]{:S(2)}) collective-permute-start(f32[512,128]{1,0:T(8,128)S(1)} %constant_dynamic-slice_fusion.1), channel_id=1, source_target_pairs={{0,2},{1,3},{2,0},{3,1},{4,6},{5,7},{6,4},{7,5},{8,10},{9,11},{10,... | collective-permute-start | bytes 786440 | tf_op jit(solution)/shard_map/ppermute | solution.py:12
  271.0 12.3 %collective-permute-start.23 = (f32[512,128]{1,0:T(8,128)S(1)}, f32[512,128]{1,0:T(8,128)S(1)}, u32[]{:S(2)}, u32[]{:S(2)}) collective-permute-start(f32[512,128]{1,0:T(8,128)S(1)} %add.196), channel_id=1, source_target_pairs={{0,16},{8,24},{16,0},{24,8},{32,48},{40,56},{48,32},{56,40},{64,80... | collective-permute-start | bytes 786440 | tf_op jit(solution)/shard_map/ppermute | solution.py:12
  283.3 16.4 %collective-permute-start.24 = (f32[512,128]{1,0:T(8,128)S(1)}, f32[512,128]{1,0:T(8,128)S(1)}, u32[]{:S(2)}, u32[]{:S(2)}) collective-permute-start(f32[512,128]{1,0:T(8,128)S(1)} %add.197), channel_id=1, source_target_pairs={{0,32},{8,40},{16,48},{24,56},{32,0},{40,8},{48,16},{56,24},{64,96... | collective-permute-start | bytes 786440 | tf_op jit(solution)/shard_map/ppermute | solution.py:12
  305.1 10.8 %collective-permute-start.26 = (f32[512,128]{1,0:T(8,128)S(1)}, f32[512,128]{1,0:T(8,128)S(1)}, u32[]{:S(2)}, u32[]{:S(2)}) collective-permute-start(f32[512,128]{1,0:T(8,128)S(1)} %add.199), channel_id=1, source_target_pairs={{0,128},{8,136},{16,144},{24,152},{32,160},{40,168},{48,176},{56,1... | collective-permute-start | bytes 786440 | tf_op jit(solution)/shard_map/ppermute | solution.py:12
  315.9 6.2 %collective-permute-start.27 = (f32[512,128]{1,0:T(8,128)S(1)}, f32[512,128]{1,0:T(8,128)S(1)}, u32[]{:S(2)}, u32[]{:S(2)}) collective-permute-start(f32[512,128]{1,0:T(8,128)S(1)} %add.200), channel_id=1, source_target_pairs={{0,1},{1,0},{2,3},{3,2},{4,5},{5,4},{6,7},{7,6},{8,9},{9,8},{10,11... | collective-permute-start | bytes 786440 | tf_op jit(solution)/shard_map/ppermute | solution.py:12
  327.1 11.4 %collective-permute-start.28 = (f32[512,128]{1,0:T(8,128)S(1)}, f32[512,128]{1,0:T(8,128)S(1)}, u32[]{:S(2)}, u32[]{:S(2)}) collective-permute-start(f32[512,128]{1,0:T(8,128)S(1)} %constant_dynamic-slice_fusion), channel_id=1, source_target_pairs={{0,4},{1,5},{2,6},{3,7},{4,0},{5,1},{6,2},{7,3},{8,12},{9,13},{10,... | collective-permute-start | bytes 786440 | tf_op jit(solution)/shard_map/ppermute | solution.py:12
  338.6 7.2 %collective-permute-start.29 = (f32[512,128]{1,0:T(8,128)S(1)}, f32[512,128]{1,0:T(8,128)S(1)}, u32[]{:S(2)}, u32[]{:S(2)}) collective-permute-start(f32[512,128]{1,0:T(8,128)S(1)} %dynamic-slice_add_fusion), channel_id=1, source_target_pairs={{0,8},{8,0},{16,24},{24,16},{32,40},{40,32},{48,56},{56,48},{64,72... | collective-permute-start | bytes 786440 | tf_op jit(solution)/shard_map/ppermute | solution.py:12
  345.9 14.8 %collective-permute-start.30 = (f32[512,128]{1,0:T(8,128)S(1)}, f32[512,128]{1,0:T(8,128)S(1)}, u32[]{:S(2)}, u32[]{:S(2)}) collective-permute-start(f32[512,128]{1,0:T(8,128)S(1)} %add.205), channel_id=1, source_target_pairs={{0,16},{8,24},{16,0},{24,8},{32,48},{40,56},{48,32},{56,40},{64,80... | collective-permute-start | bytes 786440 | tf_op jit(solution)/shard_map/ppermute | solution.py:12
  360.7 17.7 %collective-permute-start.31 = (f32[512,128]{1,0:T(8,128)S(1)}, f32[512,128]{1,0:T(8,128)S(1)}, u32[]{:S(2)}, u32[]{:S(2)}) collective-permute-start(f32[512,128]{1,0:T(8,128)S(1)} %add.206), channel_id=1, source_target_pairs={{0,32},{8,40},{16,48},{24,56},{32,0},{40,8},{48,16},{56,24},{64,96... | collective-permute-start | bytes 786440 | tf_op jit(solution)/shard_map/ppermute | solution.py:12
  378.4 8.3 %collective-permute-start.32 = (f32[512,128]{1,0:T(8,128)S(1)}, f32[512,128]{1,0:T(8,128)S(1)}, u32[]{:S(2)}, u32[]{:S(2)}) collective-permute-start(f32[512,128]{1,0:T(8,128)S(1)} %add.207), channel_id=1, source_target_pairs={{0,64},{8,72},{16,80},{24,88},{32,96},{40,104},{48,112},{56,120},{... | collective-permute-start | bytes 786440 | tf_op jit(solution)/shard_map/ppermute | solution.py:12
  386.7 8.1 %collective-permute-start.33 = (f32[512,128]{1,0:T(8,128)S(1)}, f32[512,128]{1,0:T(8,128)S(1)}, u32[]{:S(2)}, u32[]{:S(2)}) collective-permute-start(f32[512,128]{1,0:T(8,128)S(1)} %add.208), channel_id=1, source_target_pairs={{0,128},{8,136},{16,144},{24,152},{32,160},{40,168},{48,176},{56,1... | collective-permute-start | bytes 786440 | tf_op jit(solution)/shard_map/ppermute | solution.py:12
  398.4 7.6 %collective-permute-start.35 = (f32[512,128]{1,0:T(8,128)S(1)}, f32[512,128]{1,0:T(8,128)S(1)}, u32[]{:S(2)}, u32[]{:S(2)}) collective-permute-start(f32[512,128]{1,0:T(8,128)S(1)} %add.210), channel_id=1, source_target_pairs={{0,2},{1,3},{2,0},{3,1},{4,6},{5,7},{6,4},{7,5},{8,10},{9,11},{10,... | collective-permute-start | bytes 786440 | tf_op jit(solution)/shard_map/ppermute | solution.py:12
  (14 other events, 88.9 us)
where the time goes:
time: 409 us
  waiting for transfers between devices  299 us (73%)
  starting transfers between devices  63.6 us (16%)
  matrix products  32.1 us (8%)
  local copies, waits for them, and re-layouts  12.3 us (3%)
    ppermute x36, waiting for transfers between devices, partner(): return lax.ppermute(value, axis, pairs)  299 us
    ppermute x36, starting transfers between devices, partner(): return lax.ppermute(value, axis, pairs)  63.6 us
    dot_general x8, matrix products, shards(): jnp.dot(coefficient, up_basis[height - 1], preferred_element_type=jnp.flo...  17.4 us
    dot_general x8, matrix products, shards(): lax.dot_general(rounded, projection[height - 1], (((1,), (1,)), ((), ()))...  12.1 us
    unnamed x20, local copies, waits for them, and re-layouts  12.1 us
  transfers between devices with their start and end apart: 36, of which 36 were waited for; matrix products, arithmetic and copies ran while one was open for 0% of the time, Pallas kernels for 0%

commit v1 on v0

v1 whole, which is shorter than its diff:
```python
import functools

import jax
import jax.numpy as jnp
from jax import lax
from jax.experimental import pallas as pl
from jax.experimental.pallas import tpu as pltpu
from jax.sharding import PartitionSpec as P

AXES = ("gy", "gx")
STEPS = 4
VMEM_BYTES = 32 * 1024 * 1024


def dot(a, b):
    return jnp.dot(a, b, preferred_element_type=jnp.float32)


def dot_t(a, b):
    return lax.dot_general(a, b, (((1,), (1,)), ((), ())), preferred_element_type=jnp.float32)


def exact_dot(a, b):
    return jnp.dot(a, b, precision=lax.Precision.HIGHEST, preferred_element_type=jnp.float32)


def swap(value, axis, mask, size):
    return lax.ppermute(value, axis, [(source, source ^ mask) for source in range(size)])


def exchange(value, groups):
    return lax.all_to_all(value, AXES, 0, 0, tiled=True, axis_index_groups=groups)


def half(value, which, rank):
    return lax.dynamic_slice_in_dim(value, which * rank, rank, value.ndim - 1)


def whole(shape):
    return pl.BlockSpec(shape, lambda j, bits: (0,) * len(shape))


def columns(rows, width):
    return pl.BlockSpec((rows, width), lambda j, bits: (0, j))


def level(index, rows, width):
    return pl.BlockSpec((None, rows, width), lambda j, bits: (index, 0, j))


def run(body, bits, args, in_specs, out_shape, out_specs, scratch, flops, nbytes):
    return pl.pallas_call(
        body,
        out_shape=out_shape,
        grid_spec=pltpu.PrefetchScalarGridSpec(
            num_scalar_prefetch=1,
            grid=(STEPS,),
            in_specs=in_specs,
            out_specs=out_specs,
            scratch_shapes=scratch,
        ),
        compiler_params=pltpu.CompilerParams(
            dimension_semantics=("arbitrary",), vmem_limit_bytes=VMEM_BYTES
        ),
        cost_estimate=pl.CostEstimate(flops=flops, bytes_accessed=nbytes, transcendentals=0),
    )(bits, *args)


def f32(*shape):
    return jax.ShapeDtypeStruct(shape, jnp.float32)


def accumulate(ref, value):
    @pl.when(pl.program_id(0) == 0)
    def _():
        ref[...] = value

    @pl.when(pl.program_id(0) > 0)
    def _():
        ref[...] += value


def gram_body(pairs, bits, *refs):
    ups, projs, outs = refs[: len(pairs)], refs[len(pairs) : 2 * len(pairs)], refs[2 * len(pairs) :]
    for up, proj, out in zip(ups, projs, outs, strict=True):
        accumulate(out, dot_t(up[...], proj[...]))


def grams(pairs, bits, up_basis, projection):
    rank, leaf = up_basis.shape[1:]
    width = leaf // STEPS
    count = len(pairs)
    return run(
        functools.partial(gram_body, pairs),
        bits,
        [up_basis] * count + [projection] * count,
        [level(k - 1, rank, width) for k, _ in pairs]
        + [level(h - 1, 2 * rank, width) for _, h in pairs],
        [f32(rank, 2 * rank)] * count,
        [whole((rank, 2 * rank))] * count,
        [],
        4 * count * rank * rank * leaf,
        6 * count * rank * leaf,
    )


def leaf_body(bits, rhs, inverse, own_rows, other_rows, state, own, other):
    block = dot(rhs[...], inverse[...])
    state[...] = block
    rounded = block.astype(jnp.bfloat16)
    accumulate(own, dot_t(rounded, own_rows[...]))
    accumulate(other, dot_t(rounded, other_rows[...]))


def leaf_solve(bits, rhs, leaf_inverse, projection):
    rows, leaf = rhs.shape
    rank = projection.shape[1] // 2
    width = leaf // STEPS
    return run(
        leaf_body,
        bits,
        [rhs, leaf_inverse, projection, projection],
        [
            whole((rows, leaf)),
            pl.BlockSpec((None, leaf, width), lambda j, bits: (0, 0, j)),
            pl.BlockSpec((None, rank, width), lambda j, bits: (0, bits[0], j)),
            pl.BlockSpec((None, rank, width), lambda j, bits: (0, 1 - bits[0], j)),
        ],
        [f32(rows, leaf), f32(rows, rank), f32(rows, rank)],
        [columns(rows, width), whole((rows, rank)), whole((rows, rank))],
        [],
        2 * rows * leaf * (leaf + 2 * rank),
        leaf * (6 * rows + 2 * leaf),
    )


def step_body(n_coef, n_up, n_proj, fill, emit, bits, state, *refs):
    coefs, refs = refs[:n_coef], refs[n_coef:]
    ups, refs = refs[:n_up], refs[n_up:]
    projs, refs = refs[:n_proj], refs[n_proj:]
    extra, outs, coef = refs[0], refs[1:-2], refs[-2]
    new_state, sums = outs[0], refs[-1]

    @pl.when(pl.program_id(0) == 0)
    def _():
        fill(bits, coef, *coefs)

    basis = jnp.concatenate([up[...] for up in ups], axis=0)
    block = state[...] - dot(coef[...], basis)
    new_state[...] = block
    if n_proj:
        rows = jnp.concatenate([proj[...] for proj in projs], axis=0)
        accumulate(sums, dot_t(block.astype(jnp.bfloat16), rows))

        @pl.when(pl.program_id(0) == STEPS - 1)
        def _():
            emit(bits, sums, extra, *outs[1:])


def step(bits, state, coefs, up_levels, proj_levels, up_basis, projection, extra, fill, emit, out_shape):
    rows, leaf = state.shape
    rank = up_basis.shape[1]
    width = leaf // STEPS
    depth, wide = rank * len(up_levels), 2 * rank * len(proj_levels)
    return run(
        functools.partial(step_body, len(coefs), len(up_levels), len(proj_levels), fill, emit),
        bits,
        [state, *coefs] + [up_basis] * len(up_levels) + [projection] * len(proj_levels) + [extra],
        [columns(rows, width)]
        + [whole(c.shape) for c in coefs]
        + [level(k - 1, rank, width) for k in up_levels]
        + [level(h - 1, 2 * rank, width) for h in proj_levels]
        + [whole(extra.shape)],
        [f32(rows, leaf), *out_shape],
        [columns(rows, width)] + [whole(s.shape) for s in out_shape],
        [
            pltpu.VMEM((rows, depth), jnp.bfloat16),
            pltpu.VMEM((rows, wide) if wide else (8, 128), jnp.float32),
        ],
        2 * rows * leaf * (depth + wide),
        leaf * (8 * rows + 2 * depth + 2 * wide),
    )


def fill_sum(bits, coef, mine, received):
    coef[...] = (mine[...] + received[...]).astype(jnp.bfloat16)


def fill_pair(bits, coef, mine, received):
    count = mine.shape[0]
    coef[pl.ds(pl.multiple_of(bits[0] * count, count), count)] = mine[...].astype(jnp.bfloat16)
    coef[pl.ds(pl.multiple_of((1 - bits[0]) * count, count), count)] = received[...].astype(jnp.bfloat16)


def fill_row(count, bits, coef, packed):
    coef[...] = packed[:, :count, :].reshape(coef.shape).astype(jnp.bfloat16)


def fill_top(bits, coef, mine, received):
    count = mine.shape[0]
    rank = received.shape[1] // 3
    depth = coef.shape[1]
    coef[pl.ds(pl.multiple_of(bits[1] * count, count), count), :] = mine[:, :depth].astype(jnp.bfloat16)
    there = pl.ds(pl.multiple_of((1 - bits[1]) * count, count), count)
    coef[there, :rank] = received[:, 2 * rank :].astype(jnp.bfloat16)
    coef[there, rank:] = received[:, : 2 * rank].astype(jnp.bfloat16)


def emit_halves(which, bits, sums, extra, keep, send):
    count = keep.shape[0]
    keep[...] = sums[pl.ds(pl.multiple_of(bits[which] * count, count), count)]
    send[...] = sums[pl.ds(pl.multiple_of((1 - bits[which]) * count, count), count)]


def emit_rows(bits, sums, extra, packed):
    parts, _, wide = packed.shape
    count = sums.shape[0] // parts
    packed[:, :count, :] = sums[:, :wide].reshape(parts, count, wide)
    packed[:, count : 2 * count, :] = sums[:, wide:].reshape(parts, count, wide)
    pieces = extra.shape[1] // parts
    for i in range(extra.shape[0]):
        start = 2 * count + i * pieces
        packed[:, start : start + pieces, :] = extra[i].reshape(parts, pieces, wide)


def shards(groups_z, groups_zy, rhs, leaf_inverse, up_basis, projection):
    size_x, size_y = lax.axis_size("gx"), lax.axis_size("gy")
    rows, leaf = rhs.shape
    rank = up_basis.shape[1]
    wide = 2 * rank
    gx, gy = lax.axis_index("gx"), lax.axis_index("gy")
    z0, z1, z2, y0, y1 = (gx >> i & 1 for i in range(5))
    core, x0, x1 = (gy >> i & 1 for i in range(3))
    bits = jnp.stack([z0, core])
    over_x = functools.partial(swap, axis="gx", size=size_x)
    over_y = functools.partial(swap, axis="gy", size=size_y)
    nothing = jnp.zeros((8, 128), jnp.float32)

    low = jnp.concatenate(grams(((2, 3), (4, 5)), bits, up_basis, projection), axis=0)
    low = low + over_x(low, mask=1)
    gram_23 = low[:rank].astype(jnp.bfloat16)
    gram_45 = low[rank:]
    gram_45 = gram_45 + over_x(gram_45, mask=2)
    gram_45 = gram_45 + over_x(gram_45, mask=6)
    gram_45 = gram_45.astype(jnp.bfloat16)

    state, own, other = leaf_solve(bits, rhs, leaf_inverse, projection)
    received = over_x(other, mask=1)
    high = jnp.stack(grams(((6, 7), (6, 8), (7, 8)), bits, up_basis, projection))

    pair_rows = rows // 2
    state, keep, send = step(
        bits, state, [own, received], (1,), (2, 3), up_basis, projection, nothing,
        fill_sum, functools.partial(emit_halves, 0), [f32(pair_rows, 2 * wide)] * 2,
    )
    value = keep + over_x(send, mask=1)
    c2 = half(value[:, :wide], z1, rank) + over_x(half(value[:, :wide], 1 - z1, rank), mask=2)
    value = value[:, wide:] - dot(c2.astype(jnp.bfloat16), gram_23)
    c3 = half(value, z2, rank) + over_x(half(value, 1 - z2, rank), mask=6)
    c3 = c3 + over_x(c3, mask=2)
    mine = jnp.concatenate([c2, c3], axis=1)
    received = over_x(mine, mask=1)

    ring = len(groups_z[0])
    count, pieces = rows // ring, rank // ring
    state, packed = step(
        bits, state, [mine, received], (2, 3), (4, 5), up_basis, projection, high,
        fill_pair, emit_rows, [f32(ring, 2 * count + 3 * pieces, wide)],
    )
    value = exchange(packed, groups_z).sum(axis=0)
    high = value[2 * count :]
    high = high + over_x(high, mask=8)
    high = high + over_x(high, mask=24)
    c4 = half(value[:count], y0, rank) + over_x(half(value[:count], 1 - y0, rank), mask=8)
    value = value[count : 2 * count] - dot(c4.astype(jnp.bfloat16), gram_45)
    c5 = half(value, y1, rank) + over_x(half(value, 1 - y1, rank), mask=24)
    c5 = c5 + over_x(c5, mask=8)
    packed = jnp.concatenate([jnp.concatenate([c4, c5], axis=1), high], axis=0)
    packed = exchange(jnp.broadcast_to(packed, (ring, *packed.shape)), groups_z)
    high = packed[:, count:].reshape(ring, 3, pieces, wide).transpose(1, 0, 2, 3).reshape(3, rank, wide)
    high_there = over_y(high, mask=1)

    half_rows = rows // 2
    state, keep, send = step(
        bits, state, [packed], (4, 5), (6, 7, 8), up_basis, projection, nothing,
        functools.partial(fill_row, count), functools.partial(emit_halves, 1), [f32(half_rows, 3 * wide)] * 2,
    )
    value = keep + over_y(send, mask=1)
    share = half_rows // size_x
    value = exchange(value.reshape(size_x, share, 3 * wide), groups_zy).sum(axis=0)
    c6, c6_there = half(value[:, :wide], core, rank), half(value[:, :wide], 1 - core, rank)
    z7 = value[:, wide : 2 * wide] - exact_dot(c6, high[0]) - exact_dot(c6_there, high_there[0])
    z8 = value[:, 2 * wide :] - exact_dot(c6, high[1]) - exact_dot(c6_there, high_there[1])
    c7 = half(z7, x0, rank) + over_y(half(z7, 1 - x0, rank), mask=2)
    z8 = z8 - exact_dot(c7, high[2] + high_there[2])
    c8 = half(z8, x1, rank) + over_y(half(z8, 1 - x1, rank), mask=6)
    c8 = c8 + over_y(c8, mask=2)
    packed = jnp.concatenate([c6, c7, c8, c6_there], axis=1)
    packed = exchange(jnp.broadcast_to(packed, (size_x, *packed.shape)), groups_zy)
    packed = packed.reshape(half_rows, 4 * rank)
    received = over_y(packed[:, rank:], mask=1)
    return step(
        bits, state, [packed, received], (6, 7, 8), (), up_basis, projection, nothing,
        fill_top, None, [],
    )[0]


def solution(mesh):
    size_x, size_y = mesh.shape["gx"], mesh.shape["gy"]
    ring = 8
    groups_z = [
        [gy * size_x + start + i for i in range(ring)]
        for gy in range(size_y)
        for start in range(0, size_x, ring)
    ]
    groups_zy = [[gy * size_x + i for i in range(size_x)] for gy in range(size_y)]
    return jax.shard_map(
        functools.partial(shards, groups_z, groups_zy),
        mesh=mesh,
        in_specs=(
            P(None, ("gy", "gx")),
            P(("gy", "gx"), None, None),
            P(None, None, ("gy", "gx")),
            P(None, None, ("gy", "gx")),
        ),
        out_specs=P(None, ("gy", "gx")),
        check_vma=False,
    )
```

time: 409 us -> 234 us (0.57)
  waiting for transfers between devices: 299 us -> 89.7 us
  blocking collectives: 0 us -> 38.7 us
  matrix products: 32.1 us -> 1.1 us
  Pallas kernels: 0 us -> 26.4 us
  starting transfers between devices: 63.6 us -> 57.9 us
  other arithmetic: 0.81 us -> 6.14 us
    ppermute x36 -> x20, waiting for transfers between devices: 299 us -> 40.4 us  [swap(): lax.ppermute(value, axis, [(source, source ^ mask) for source in range(si...]
    all_to_all x0 -> x2, waiting for transfers between devices: none -> 49.3 us  [exchange(): lax.all_to_all(value, AXES, 0, 0, tiled=True, axis_index_groups=groups)]
    all_to_all x0 -> x2, blocking collectives: none -> 38.7 us  [exchange(): lax.all_to_all(value, AXES, 0, 0, tiled=True, axis_index_groups=groups)]
    dot_general x17 -> x7, matrix products: 32.1 us -> 1.1 us  [the longest x5 0.79 us: exact_dot(): jnp.dot(a, b, precision=lax.Precision.HIGHEST, preferred_element_type=jnp...]
    pallas_call x0 -> x7, Pallas kernels: none -> 26.4 us  [run(): pl.pallas_call(body, out_shape=out_shape, grid_spec=pltpu.PrefetchScalarG...]
    ppermute x36 -> x20, starting transfers between devices: 63.6 us -> 48.2 us  [swap(): lax.ppermute(value, axis, [(source, source ^ mask) for source in range(si...]
    all_to_all x0 -> x2, starting transfers between devices: none -> 9.64 us  [exchange(): lax.all_to_all(value, AXES, 0, 0, tiled=True, axis_index_groups=groups)]
    unnamed x20 -> x27, local copies, waits for them, and re-layouts: 12.1 us -> 12.1 us
  transfers between devices with their start and end apart: 36 -> 22, of which waited for: 36 -> 19; matrix products, arithmetic and copies ran while one was open for 0% -> 3% of each run, Pallas kernels for 0% -> 3%
where the time goes in v1:
time: 234 us; the launch traced here: 233 us
  waiting for transfers between devices  89.7 us (38%)
  starting transfers between devices  57.9 us (25%)
  blocking collectives  38.7 us (17%)
  Pallas kernels  26.4 us (11%)
  local copies, waits for them, and re-layouts  13.1 us (6%)
  other arithmetic  6.14 us (3%)
    all_to_all x2, waiting for transfers between devices, exchange(): lax.all_to_all(value, AXES, 0, 0, tiled=True, axis_index_groups=groups)  49.3 us
    ppermute x20, starting transfers between devices, swap(): lax.ppermute(value, axis, [(source, source ^ mask) for source in range(si...  48.2 us
    ppermute x20, waiting for transfers between devices, swap(): lax.ppermute(value, axis, [(source, source ^ mask) for source in range(si...  40.4 us
    all_to_all x2, blocking collectives, exchange(): lax.all_to_all(value, AXES, 0, 0, tiled=True, axis_index_groups=groups)  38.7 us
    pallas_call x7, Pallas kernels, run(): pl.pallas_call(body, out_shape=out_shape, grid_spec=pltpu.PrefetchScalarG...  26.4 us
    unnamed x27, local copies, waits for them, and re-layouts  12.1 us
    all_to_all x2, starting transfers between devices, exchange(): lax.all_to_all(value, AXES, 0, 0, tiled=True, axis_index_groups=groups)  9.64 us
  transfers between devices with their start and end apart: 22, of which 19 were waited for; matrix products, arithmetic and copies ran while one was open for 3% of the time, Pallas kernels for 3%

profile of v1, /device:TPU:1, one launch (start us, length us, event | category | flops | bytes accessed | tf_op | source)
XLA Modules:
  0.0 233.3 jit_solution(15688839545548502106)
XLA Ops:
  0.1 2.2 copy-done
  5.1 5.2 %shard_map.46 = (f32[512,1024]{1,0:T(8,128)S(1)}, f32[512,128]{1,0:T(8,128)S(1)}, f32[512,128]{1,0:T(8,128)S(1)}) custom-call(s32[2]{0:T(128)S(1)} %pad_add_fusion.bits, bf16[512,1024]{1,0:T(8,128)(2,1)S(1)} %copy-done.12, bf16[1,1024,1024]{2,1,0:T(8,128)(2,1)S(1)} %copy-done.9, bf16[8,256,1024]{2,1,0:T(8,128)(2,1)S(1)} %copy-done, ...), custom_call_target="tpu_custom_call" | custom-call | flops 1342177280 | bytes 5242880 | tf_op jit(solution)/shard_map/pallas_call | solution.py:52
  10.3 2.6 %collective-permute-start = (f32[512,128]{1,0:T(8,128)S(1)}, f32[512,128]{1,0:T(8,128)S(1)}, u32[]{:S(2)}, u32[]{:S(2)}) collective-permute-start(f32[512,128]{1,0:T(8,128)S(1)} %get-tuple-element.23), channel_id=1, source_target_pairs={{0,8},{8,0},{16,24},{24,16},{32,40},{40,32},{48,56},{56,48},{64,72... | collective-permute-start | bytes 786440 | tf_op jit(solution)/shard_map/ppermute | solution.py:28
  12.8 5.0 %collective-permute-done.refs_1_ = f32[512,128]{1,0:T(8,128)S(1)} collective-permute-done((f32[512,128]{1,0:T(8,128)S(1)}, f32[512,128]{1,0:T(8,128)S(1)}, u32[]{:S(2)}, u32[]{:S(2)}) %collective-permute-start) | collective-permute-done | bytes 262176 | tf_op jit(solution)/shard_map/ppermute | solution.py:28
  17.8 3.2 %shard_map.47 = (f32[512,1024]{1,0:T(8,128)S(1)}, f32[256,512]{1,0:T(8,128)S(1)}, f32[256,512]{1,0:T(8,128)S(1)}) custom-call(s32[2]{0:T(128)S(1)} %pad_add_fusion.bits, f32[512,1024]{1,0:T(8,128)S(1)} %get-tuple-element.21.state, f32[512,128]{1,0:T(8,128)S(1)} %get-tuple-element.22.refs_0_, f32[512,128]{1,0:T(8,128)S(1)} %collective-permute-done.refs_1_, ...), custom_call_target="tpu_custom_call" | custom-call | flops 671088640 | bytes 5505024 | tf_op jit(solution)/shard_map/pallas_call | solution.py:52
  21.0 2.3 collective-permute-start.1
  23.3 2.6 %shard_map.48 = (f32[128,256]{1,0:T(8,128)S(1)}, f32[128,256]{1,0:T(8,128)S(1)}) custom-call(s32[2]{0:T(128)S(1)} %pad_add_fusion.bits, bf16[8,128,1024]{2,1,0:T(8,128)(2,1)S(1)} %copy-done.4, bf16[8,128,1024]{2,1,0:T(8,128)(2,1)S(1)} %copy-done.4, bf16[8,256,1024]{2,1,0:T(8,128)(2,1)S(1)} %copy-done.1, bf16[8,256,1024]{2,1,0:T(8,128)(2,1)S(1)} %copy-done.1), custom_call_target="tpu_custom_call" | custom-call | flops 134217728 | bytes 1572864 | tf_op jit(solution)/shard_map/pallas_call | solution.py:52
  27.3 6.5 %collective-permute-done.1 = f32[256,512]{1,0:T(8,128)} collective-permute-done((f32[256,512]{1,0:T(8,128)S(1)}, f32[256,512]{1,0:T(8,128)}, u32[]{:S(2)}, u32[]{:S(2)}) %collective-permute-start.1) | collective-permute-done | bytes 524320 | tf_op jit(solution)/shard_map/ppermute | solution.py:28
  35.0 3.5 %collective-permute-start.2 = (f32[256,128]{1,0:T(8,128)S(1)}, f32[256,128]{1,0:T(8,128)S(1)}, u32[]{:S(2)}, u32[]{:S(2)}) collective-permute-start(f32[256,128]{1,0:T(8,128)S(1)} %constant_dynamic-slice_fusion.7), channel_id=1, source_target_pairs={{0,16},{8,24},{16,0},{24,8},{32,48},{40,56},{48,32},{56,40},{64,80... | collective-permute-start | bytes 393224 | tf_op jit(solution)/shard_map/ppermute | solution.py:28
  42.1 6.3 %collective-permute-start.4 = (f32[256,128]{1,0:T(8,128)S(1)}, f32[256,128]{1,0:T(8,128)S(1)}, u32[]{:S(2)}, u32[]{:S(2)}) collective-permute-start(f32[256,128]{1,0:T(8,128)S(1)} %constant_dynamic-slice_fusion.6), channel_id=1, source_target_pairs={{0,48},{8,56},{16,32},{24,40},{32,16},{40,24},{48,0},{56,8},{64,11... | collective-permute-start | bytes 393224 | tf_op jit(solution)/shard_map/ppermute | solution.py:28
  48.5 3.3 %collective-permute-done.4 = f32[256,128]{1,0:T(8,128)S(1)} collective-permute-done((f32[256,128]{1,0:T(8,128)S(1)}, f32[256,128]{1,0:T(8,128)S(1)}, u32[]{:S(2)}, u32[]{:S(2)}) %collective-permute-start.4) | collective-permute-done | bytes 131104 | tf_op jit(solution)/shard_map/ppermute | solution.py:28
  52.9 5.1 %collective-permute-done.5 = f32[256,128]{1,0:T(8,128)S(1)} collective-permute-done((f32[256,128]{1,0:T(8,128)S(1)}, f32[256,128]{1,0:T(8,128)S(1)}, u32[]{:S(2)}, u32[]{:S(2)}) %collective-permute-start.5) | collective-permute-done | bytes 131104 | tf_op jit(solution)/shard_map/ppermute | solution.py:28
  58.2 2.2 copy-done.2
  60.4 3.6 %shard_map.49 = (f32[128,256]{1,0:T(8,128)S(1)}, f32[128,256]{1,0:T(8,128)S(1)}, f32[128,256]{1,0:T(8,128)S(1)}) custom-call(s32[2]{0:T(128)S(1)} %pad_add_fusion.bits, bf16[8,128,1024]{2,1,0:T(8,128)(2,1)S(1)} %copy-done.4, bf16[8,128,1024]{2,1,0:T(8,128)(2,1)S(1)} %copy-done.4, bf16[8,128,1024]{2,1,0:T(8,128)(2,1)S(1)} %copy-done.4, ...), custom_call_target="tpu_custom_call" | custom-call | flops 201326592 | bytes 2359296 | tf_op jit(solution)/shard_map/pallas_call | solution.py:52
  64.5 4.5 %shard_map.50 = (f32[512,1024]{1,0:T(8,128)S(1)}, f32[8,176,256]{2,1,0:T(8,128)}) custom-call(s32[2]{0:T(128)S(1)} %pad_add_fusion.bits, f32[512,1024]{1,0:T(8,128)S(1)} %copy-done.8, f32[256,256]{1,0:T(8,128)S(1)} %pad_maximum_fusion.1.refs_0_, f32[256,256]{1,0:T(8,128)S(1)} %collective-permute-done.6.refs_1_, bf16[8,128,1024]{2,1,0:T(8,128)(2,1)S(1)} %copy-done.4, ...), custom_call_target="tpu_custom_call" | custom-call | flops 805306368 | bytes 5767168 | tf_op jit(solution)/shard_map/pallas_call | solution.py:52
  70.3 5.0 %all-to-all-start = ((f32[8,176,256]{2,1,0:T(8,128)}), f32[8,176,256]{2,1,0:T(8,128)}, u32[]{:S(2)}, u32[]{:S(2)}) async-start(f32[8,176,256]{2,1,0:T(8,128)} %get-tuple-element.33), calls=%async_computation | async-start | bytes 2883584 | tf_op jit(solution)/shard_map/all_to_all | solution.py:32
  75.3 2.4 %collective-permute-start.8 = (f32[128,256]{1,0:T(8,128)S(1)}, f32[128,256]{1,0:T(8,128)S(1)}, u32[]{:S(2)}, u32[]{:S(2)}) collective-permute-start(f32[128,256]{1,0:T(8,128)S(1)} %slice.84), channel_id=1, source_target_pairs={{0,16},{8,24},{16,0},{24,8},{32,48},{40,56},{48,32},{56,40},{64,80... | collective-permute-start | bytes 393224 | tf_op jit(solution)/shard_map/ppermute | solution.py:28
  77.7 29.9 %all-to-all-done = f32[8,176,256]{2,1,0:T(8,128)} async-done(((f32[8,176,256]{2,1,0:T(8,128)}), f32[8,176,256]{2,1,0:T(8,128)}, u32[]{:S(2)}, u32[]{:S(2)}) %all-to-all-start) | async-done | bytes 1441824 | tf_op jit(solution)/shard_map/all_to_all | solution.py:32
  112.4 5.6 %collective-permute-done.9 = f32[128,256]{1,0:T(8,128)S(1)} collective-permute-done((f32[128,256]{1,0:T(8,128)S(1)}, f32[128,256]{1,0:T(8,128)S(1)}, u32[]{:S(2)}, u32[]{:S(2)}) %collective-permute-start.9) | collective-permute-done | bytes 131104 | tf_op jit(solution)/shard_map/ppermute | solution.py:28
  118.6 2.3 collective-permute-start.13
  122.9 2.0 collective-permute-done.11
  125.0 19.5 %all_to_all.20.refs_0_ = f32[8,112,256]{2,1,0:T(8,128)S(1)} all-to-all(f32[8,112,256]{2,1,0:T(8,128)S(1)} %broadcast_in_dim.10), channel_id=1, replica_groups={{0,8,16,24,32,40,48,56},{64,72,80,88,96,104,112,120},{128,136,144,152,1..., dimensions={0} | all-to-all | bytes 1835008 | tf_op jit(solution)/shard_map/all_to_all | solution.py:32
  146.1 4.0 %shard_map.51 = (f32[512,1024]{1,0:T(8,128)S(1)}, f32[256,768]{1,0:T(8,128)S(1)}, f32[256,768]{1,0:T(8,128)S(1)}) custom-call(s32[2]{0:T(128)S(1)} %pad_add_fusion.bits, f32[512,1024]{1,0:T(8,128)S(1)} %copy-done.6, f32[8,112,256]{2,1,0:T(8,128)S(1)} %all_to_all.20.refs_0_, bf16[8,128,1024]{2,1,0:T(8,128)(2,1)S(1)} %copy-done.4, ...), custom_call_target="tpu_custom_call" | custom-call | flops 1073741824 | bytes 6291456 | tf_op jit(solution)/shard_map/pallas_call | solution.py:52
  151.4 12.7 %collective-permute-start.14 = (f32[256,768]{1,0:T(8,128)S(1)}, f32[256,768]{1,0:T(8,128)S(1)}, u32[]{:S(2)}, u32[]{:S(2)}) collective-permute-start(f32[256,768]{1,0:T(8,128)S(1)} %get-tuple-element.36), channel_id=1, source_target_pairs={{0,1},{1,0},{2,3},{3,2},{4,5},{5,4},{6,7},{7,6},{8,9},{9,8},{10,11... | collective-permute-start | bytes 2359304 | tf_op jit(solution)/shard_map/ppermute | solution.py:28
  164.1 1.9 collective-permute-done.14
  167.0 4.6 %all-to-all-start.2 = ((f32[32,8,768]{2,1,0:T(8,128)}), f32[32,8,768]{2,1,0:T(8,128)}, u32[]{:S(2)}, u32[]{:S(2)}) async-start(f32[32,8,768]{2,1,0:T(8,128)} %add_bitcast_fusion), calls=%async_computation.2 | async-start | bytes 1572864 | tf_op jit(solution)/shard_map/all_to_all | solution.py:32
  172.2 19.4 %all-to-all-done.2 = f32[32,8,768]{2,1,0:T(8,128)} async-done(((f32[32,8,768]{2,1,0:T(8,128)}), f32[32,8,768]{2,1,0:T(8,128)}, u32[]{:S(2)}, u32[]{:S(2)}) %all-to-all-start.2) | async-done | bytes 786464 | tf_op jit(solution)/shard_map/all_to_all | solution.py:32
  196.1 2.6 %collective-permute-start.17 = (f32[8,128]{1,0:T(8,128)S(1)}, f32[8,128]{1,0:T(8,128)S(1)}, u32[]{:S(2)}, u32[]{:S(2)}) collective-permute-start(f32[8,128]{1,0:T(8,128)S(1)} %constant_dynamic-slice_fusion), channel_id=1, source_target_pairs={{0,6},{1,7},{2,4},{3,5},{4,2},{5,3},{6,0},{7,1},{8,14},{9,15},{10,... | collective-permute-start | bytes 12296 | tf_op jit(solution)/shard_map/ppermute | solution.py:28
  199.9 2.4 %collective-permute-done.18 = f32[8,128]{1,0:T(8,128)S(1)} collective-permute-done((f32[8,128]{1,0:T(8,128)S(1)}, f32[8,128]{1,0:T(8,128)S(1)}, u32[]{:S(2)}, u32[]{:S(2)}) %collective-permute-start.18) | collective-permute-done | bytes 4128 | tf_op jit(solution)/shard_map/ppermute | solution.py:28
  202.4 19.2 %all_to_all.21 = f32[32,8,512]{2,1,0:T(8,128)S(1)} all-to-all(f32[32,8,512]{2,1,0:T(8,128)S(1)} %broadcast_in_dim.11), channel_id=1, replica_groups={{0,8,16,24,32,40,48,56,64,72,80,88,96,104,112,120,128,136,144,152,160,1..., dimensions={0} | all-to-all | bytes 1048576 | tf_op jit(solution)/shard_map/all_to_all | solution.py:32
  221.6 7.0 %collective-permute-start.19 = (f32[256,384]{1,0:T(8,128)S(1)}, f32[256,384]{1,0:T(8,128)S(1)}, u32[]{:S(2)}, u32[]{:S(2)}) collective-permute-start(f32[256,384]{1,0:T(8,128)S(1)} %slice.96), channel_id=1, source_target_pairs={{0,1},{1,0},{2,3},{3,2},{4,5},{5,4},{6,7},{7,6},{8,9},{9,8},{10,11... | collective-permute-start | bytes 1179656 | tf_op jit(solution)/shard_map/ppermute | solution.py:28
  229.9 3.3 %shard_map.52 = f32[512,1024]{1,0:T(8,128)} custom-call(s32[2]{0:T(128)S(1)} %pad_add_fusion.bits, f32[512,1024]{1,0:T(8,128)S(1)} %copy-done.11, f32[256,512]{1,0:T(8,128)S(1)} %bitcast.36, f32[256,384]{1,0:T(8,128)S(1)} %collective-permute-done.19.refs_1_, bf16[8,128,1024]{2,1,0:T(8,128)(2,1)S(1)} %copy-done.4, bf16[8,128,1024]{2,1,0:T(8,128)(2,1)S(1)} %copy-done.4, ...), custom_call_target="tpu_custom_call" | custom-call | flops 402653184 | bytes 4980736 | tf_op jit(solution)/shard_map/pallas_call | solution.py:52
  (97 shorter events, 31.1 us)
Async XLA Ops:
  0.1 2.2 copy-start
  2.3 1.6 copy-start.9
  5.1 12.7 %copy-start.1 = (bf16[8,256,1024]{2,1,0:T(8,128)(2,1)S(1)}, bf16[8,256,1024]{2,1,0:T(8,128)(2,1)}, u32[]{:S(2)}) copy-start(bf16[8,256,1024]{2,1,0:T(8,128)(2,1)} %refs_5_.5) | copy-start | bytes 12582916
  5.1 12.7 %copy-start.4 = (bf16[8,128,1024]{2,1,0:T(8,128)(2,1)S(1)}, bf16[8,128,1024]{2,1,0:T(8,128)(2,1)}, u32[]{:S(2)}) copy-start(bf16[8,128,1024]{2,1,0:T(8,128)(2,1)} %refs_4_.9) | copy-start | bytes 6291460
  10.3 7.5 %collective-permute-start = (f32[512,128]{1,0:T(8,128)S(1)}, f32[512,128]{1,0:T(8,128)S(1)}, u32[]{:S(2)}, u32[]{:S(2)}) collective-permute-start(f32[512,128]{1,0:T(8,128)S(1)} %get-tuple-element.23), channel_id=1, source_target_pairs={{0,8},{8,0},{16,24},{24,16},{32,40},{40,32},{48,56},{56,48},{64,72... | collective-permute-start | bytes 786440 | tf_op jit(solution)/shard_map/ppermute | solution.py:28
  21.0 4.9 %copy-start.7 = (f32[512,1024]{1,0:T(8,128)}, f32[512,1024]{1,0:T(8,128)S(1)}, u32[]{:S(2)}) copy-start(f32[512,1024]{1,0:T(8,128)S(1)} %get-tuple-element.24.state) | copy-start | bytes 6291460
  21.0 12.8 %collective-permute-start.1 = (f32[256,512]{1,0:T(8,128)S(1)}, f32[256,512]{1,0:T(8,128)}, u32[]{:S(2)}, u32[]{:S(2)}) collective-permute-start(f32[256,512]{1,0:T(8,128)S(1)} %get-tuple-element.26), channel_id=1, source_target_pairs={{0,8},{8,0},{16,24},{24,16},{32,40},{40,32},{48,56},{56,48},{64,72... | collective-permute-start | bytes 1572872 | tf_op jit(solution)/shard_map/ppermute | solution.py:28
  27.3 12.2 %collective-permute-start.3 = (f32[256,256]{1,0:T(8,128)}, f32[256,256]{1,0:T(8,128)}, u32[]{:S(2)}, u32[]{:S(2)}) collective-permute-start(f32[256,256]{1,0:T(8,128)} %constant_dynamic-update-slice_fusion), channel_id=1, source_target_pairs={{0,8},{8,0},{16,24},{24,16},{32,40},{40,32},{48,56},{56,48},{64,72... | collective-permute-start | bytes 786440 | tf_op jit(solution)/shard_map/ppermute | solution.py:28
  35.0 6.9 %collective-permute-start.2 = (f32[256,128]{1,0:T(8,128)S(1)}, f32[256,128]{1,0:T(8,128)S(1)}, u32[]{:S(2)}, u32[]{:S(2)}) collective-permute-start(f32[256,128]{1,0:T(8,128)S(1)} %constant_dynamic-slice_fusion.7), channel_id=1, source_target_pairs={{0,16},{8,24},{16,0},{24,8},{32,48},{40,56},{48,32},{56,40},{64,80... | collective-permute-start | bytes 393224 | tf_op jit(solution)/shard_map/ppermute | solution.py:28
  42.1 9.7 %collective-permute-start.4 = (f32[256,128]{1,0:T(8,128)S(1)}, f32[256,128]{1,0:T(8,128)S(1)}, u32[]{:S(2)}, u32[]{:S(2)}) collective-permute-start(f32[256,128]{1,0:T(8,128)S(1)} %constant_dynamic-slice_fusion.6), channel_id=1, source_target_pairs={{0,48},{8,56},{16,32},{24,40},{32,16},{40,24},{48,0},{56,8},{64,11... | collective-permute-start | bytes 393224 | tf_op jit(solution)/shard_map/ppermute | solution.py:28
  51.8 6.2 %collective-permute-start.5 = (f32[256,128]{1,0:T(8,128)S(1)}, f32[256,128]{1,0:T(8,128)S(1)}, u32[]{:S(2)}, u32[]{:S(2)}) collective-permute-start(f32[256,128]{1,0:T(8,128)S(1)} %dynamic-slice_add_fusion), channel_id=1, source_target_pairs={{0,16},{8,24},{16,0},{24,8},{32,48},{40,56},{48,32},{56,40},{64,80... | collective-permute-start | bytes 393224 | tf_op jit(solution)/shard_map/ppermute | solution.py:28
  58.1 6.4 %collective-permute-start.6 = (f32[256,256]{1,0:T(8,128)S(1)}, f32[256,256]{1,0:T(8,128)S(1)}, u32[]{:S(2)}, u32[]{:S(2)}) collective-permute-start(f32[256,256]{1,0:T(8,128)S(1)} %pad_maximum_fusion.1.refs_0_), channel_id=1, source_target_pairs={{0,8},{8,0},{16,24},{24,16},{32,40},{40,32},{48,56},{56,48},{64,72... | collective-permute-start | bytes 786440 | tf_op jit(solution)/shard_map/ppermute | solution.py:28
  58.2 2.2 copy-start.2
  60.4 4.1 %copy-start.8 = (f32[512,1024]{1,0:T(8,128)S(1)}, f32[512,1024]{1,0:T(8,128)}, u32[]{:S(2)}) copy-start(f32[512,1024]{1,0:T(8,128)} %copy-done.7) | copy-start | bytes 6291460
  70.3 37.3 %all-to-all-start = ((f32[8,176,256]{2,1,0:T(8,128)}), f32[8,176,256]{2,1,0:T(8,128)}, u32[]{:S(2)}, u32[]{:S(2)}) async-start(f32[8,176,256]{2,1,0:T(8,128)} %get-tuple-element.33), calls=%async_computation | async-start | bytes 2883584 | tf_op jit(solution)/shard_map/all_to_all | solution.py:32
  75.3 35.2 %collective-permute-start.8 = (f32[128,256]{1,0:T(8,128)S(1)}, f32[128,256]{1,0:T(8,128)S(1)}, u32[]{:S(2)}, u32[]{:S(2)}) collective-permute-start(f32[128,256]{1,0:T(8,128)S(1)} %slice.84), channel_id=1, source_target_pairs={{0,16},{8,24},{16,0},{24,8},{32,48},{40,56},{48,32},{56,40},{64,80... | collective-permute-start | bytes 393224 | tf_op jit(solution)/shard_map/ppermute | solution.py:28
  109.1 3.3 %collective-permute-start.7 = (f32[64,128]{1,0:T(8,128)S(1)}, f32[64,128]{1,0:T(8,128)S(1)}, u32[]{:S(2)}, u32[]{:S(2)}) collective-permute-start(f32[64,128]{1,0:T(8,128)S(1)} %constant_dynamic-slice_fusion.5), channel_id=1, source_target_pairs={{0,64},{8,72},{16,80},{24,88},{32,96},{40,104},{48,112},{56,120},{... | collective-permute-start | bytes 98312 | tf_op jit(solution)/shard_map/ppermute | solution.py:28
  110.5 7.4 %collective-permute-start.9 = (f32[128,256]{1,0:T(8,128)S(1)}, f32[128,256]{1,0:T(8,128)S(1)}, u32[]{:S(2)}, u32[]{:S(2)}) collective-permute-start(f32[128,256]{1,0:T(8,128)S(1)} %slice_add_fusion.1), channel_id=1, source_target_pairs={{0,48},{8,56},{16,32},{24,40},{32,16},{40,24},{48,0},{56,8},{64,11... | collective-permute-start | bytes 393224 | tf_op jit(solution)/shard_map/ppermute | solution.py:28
  111.9 32.5 %copy-start.3 = (bf16[8,256,1024]{2,1,0:T(8,128)(2,1)S(1)}, bf16[8,256,1024]{2,1,0:T(8,128)(2,1)}, u32[]{:S(2)}) copy-start(bf16[8,256,1024]{2,1,0:T(8,128)(2,1)} %refs_5_.5) | copy-start | bytes 12582916
  112.0 6.7 %collective-permute-start.12 = (f32[48,256]{1,0:T(8,128)S(1)}, f32[48,256]{1,0:T(8,128)S(1)}, u32[]{:S(2)}, u32[]{:S(2)}) collective-permute-start(f32[48,256]{1,0:T(8,128)S(1)} %slice.85), channel_id=1, source_target_pairs={{0,64},{8,72},{16,80},{24,88},{32,96},{40,104},{48,112},{56,120},{... | collective-permute-start | bytes 147464 | tf_op jit(solution)/shard_map/ppermute | solution.py:28
  118.1 4.1 %collective-permute-start.10 = (f32[64,128]{1,0:T(8,128)S(1)}, f32[64,128]{1,0:T(8,128)S(1)}, u32[]{:S(2)}, u32[]{:S(2)}) collective-permute-start(f32[64,128]{1,0:T(8,128)S(1)} %constant_dynamic-slice_fusion.4), channel_id=1, source_target_pairs={{0,192},{8,200},{16,208},{24,216},{32,224},{40,232},{48,240},{56,2... | collective-permute-start | bytes 98312 | tf_op jit(solution)/shard_map/ppermute | solution.py:28
  118.6 4.2 %collective-permute-start.13 = (f32[48,256]{1,0:T(8,128)S(1)}, f32[48,256]{1,0:T(8,128)S(1)}, u32[]{:S(2)}, u32[]{:S(2)}) collective-permute-start(f32[48,256]{1,0:T(8,128)S(1)} %slice_add_fusion), channel_id=1, source_target_pairs={{0,192},{8,200},{16,208},{24,216},{32,224},{40,232},{48,240},{56,2... | collective-permute-start | bytes 147464 | tf_op jit(solution)/shard_map/ppermute | solution.py:28
  122.1 2.8 %collective-permute-start.11 = (f32[64,128]{1,0:T(8,128)S(1)}, f32[64,128]{1,0:T(8,128)S(1)}, u32[]{:S(2)}, u32[]{:S(2)}) collective-permute-start(f32[64,128]{1,0:T(8,128)S(1)} %dynamic-slice_add_fusion.2), channel_id=1, source_target_pairs={{0,64},{8,72},{16,80},{24,88},{32,96},{40,104},{48,112},{56,120},{... | collective-permute-start | bytes 98312 | tf_op jit(solution)/shard_map/ppermute | solution.py:28
  144.5 1.6 copy-start.6
  151.4 14.6 %collective-permute-start.14 = (f32[256,768]{1,0:T(8,128)S(1)}, f32[256,768]{1,0:T(8,128)S(1)}, u32[]{:S(2)}, u32[]{:S(2)}) collective-permute-start(f32[256,768]{1,0:T(8,128)S(1)} %get-tuple-element.36), channel_id=1, source_target_pairs={{0,1},{1,0},{2,3},{3,2},{4,5},{5,4},{6,7},{7,6},{8,9},{9,8},{10,11... | collective-permute-start | bytes 2359304 | tf_op jit(solution)/shard_map/ppermute | solution.py:28
  167.0 24.6 %all-to-all-start.2 = ((f32[32,8,768]{2,1,0:T(8,128)}), f32[32,8,768]{2,1,0:T(8,128)}, u32[]{:S(2)}, u32[]{:S(2)}) async-start(f32[32,8,768]{2,1,0:T(8,128)} %add_bitcast_fusion), calls=%async_computation.2 | async-start | bytes 1572864 | tf_op jit(solution)/shard_map/all_to_all | solution.py:32
  171.7 21.3 %collective-permute-start.15 = (f32[3,128,256]{2,1,0:T(8,128)S(1)}, f32[3,128,256]{2,1,0:T(8,128)S(1)}, u32[]{:S(2)}, u32[]{:S(2)}) collective-permute-start(f32[3,128,256]{2,1,0:T(8,128)S(1)} %bitcast.40), channel_id=1, source_target_pairs={{0,1},{1,0},{2,3},{3,2},{4,5},{5,4},{6,7},{7,6},{8,9},{9,8},{10,11... | collective-permute-start | bytes 1179656 | tf_op jit(solution)/shard_map/ppermute | solution.py:28
  193.2 2.5 %collective-permute-start.16 = (f32[8,128]{1,0:T(8,128)S(1)}, f32[8,128]{1,0:T(8,128)S(1)}, u32[]{:S(2)}, u32[]{:S(2)}) collective-permute-start(f32[8,128]{1,0:T(8,128)S(1)} %constant_dynamic-slice_fusion.1), channel_id=1, source_target_pairs={{0,2},{1,3},{2,0},{3,1},{4,6},{5,7},{6,4},{7,5},{8,10},{9,11},{10,... | collective-permute-start | bytes 12296 | tf_op jit(solution)/shard_map/ppermute | solution.py:28
  196.1 3.8 %collective-permute-start.17 = (f32[8,128]{1,0:T(8,128)S(1)}, f32[8,128]{1,0:T(8,128)S(1)}, u32[]{:S(2)}, u32[]{:S(2)}) collective-permute-start(f32[8,128]{1,0:T(8,128)S(1)} %constant_dynamic-slice_fusion), channel_id=1, source_target_pairs={{0,6},{1,7},{2,4},{3,5},{4,2},{5,3},{6,0},{7,1},{8,14},{9,15},{10,... | collective-permute-start | bytes 12296 | tf_op jit(solution)/shard_map/ppermute | solution.py:28
  198.7 31.3 %copy-start.11 = (f32[512,1024]{1,0:T(8,128)S(1)}, f32[512,1024]{1,0:T(8,128)}, u32[]{:S(2)}) copy-start(f32[512,1024]{1,0:T(8,128)} %copy-done.10) | copy-start | bytes 6291460
  199.9 2.5 %collective-permute-start.18 = (f32[8,128]{1,0:T(8,128)S(1)}, f32[8,128]{1,0:T(8,128)S(1)}, u32[]{:S(2)}, u32[]{:S(2)}) collective-permute-start(f32[8,128]{1,0:T(8,128)S(1)} %dynamic-slice_add_fusion.4), channel_id=1, source_target_pairs={{0,2},{1,3},{2,0},{3,1},{4,6},{5,7},{6,4},{7,5},{8,10},{9,11},{10,... | collective-permute-start | bytes 12296 | tf_op jit(solution)/shard_map/ppermute | solution.py:28
  221.6 8.3 %collective-permute-start.19 = (f32[256,384]{1,0:T(8,128)S(1)}, f32[256,384]{1,0:T(8,128)S(1)}, u32[]{:S(2)}, u32[]{:S(2)}) collective-permute-start(f32[256,384]{1,0:T(8,128)S(1)} %slice.96), channel_id=1, source_target_pairs={{0,1},{1,0},{2,3},{3,2},{4,5},{5,4},{6,7},{7,6},{8,9},{9,8},{10,11... | collective-permute-start | bytes 1179656 | tf_op jit(solution)/shard_map/ppermute | solution.py:28
  (3 other events, 3.9 us)

commit v2 on v0

v2 whole, which is shorter than its diff:
```python
import functools

import jax
import jax.numpy as jnp
from jax import lax
from jax.experimental import pallas as pl
from jax.experimental.pallas import tpu as pltpu
from jax.sharding import PartitionSpec as P

AXES = ("gy", "gx")
STEPS = 4
VMEM_BYTES = 58 * 1024 * 1024


def dot(a, b):
    return jnp.dot(a, b, preferred_element_type=jnp.float32)


def dot_t(a, b):
    return lax.dot_general(a, b, (((1,), (1,)), ((), ())), preferred_element_type=jnp.float32)


def exact_dot(a, b):
    return jnp.dot(a, b, precision=lax.Precision.HIGHEST, preferred_element_type=jnp.float32)


def swap(value, axis, mask, size):
    return lax.ppermute(value, axis, [(source, source ^ mask) for source in range(size)])


def exchange(value, groups):
    return lax.all_to_all(value, AXES, 0, 0, tiled=True, axis_index_groups=groups)


def half(value, which, rank):
    return lax.dynamic_slice_in_dim(value, which * rank, rank, value.ndim - 1)


def split(value, bit):
    count = value.shape[0] // 2
    mine = lax.dynamic_slice_in_dim(value, bit * count, count, 0)
    return mine, lax.dynamic_slice_in_dim(value, (1 - bit) * count, count, 0)


def join(mine, other, bit):
    return jnp.where(bit == 0, jnp.concatenate([mine, other]), jnp.concatenate([other, mine]))


def hbm(value):
    return pltpu.with_memory_space_constraint(value, pltpu.HBM)


def whole(shape):
    return pl.BlockSpec(shape, lambda j, bits: (0,) * len(shape))


def block(shape, *index):
    return pl.BlockSpec(shape, lambda j, bits: index)


def columns(rows, width):
    return pl.BlockSpec((rows, width), lambda j, bits: (0, j))


def run(body, steps, bits, args, in_specs, out_shape, out_specs, scratch, flops, nbytes):
    return pl.pallas_call(
        body,
        out_shape=out_shape,
        grid_spec=pltpu.PrefetchScalarGridSpec(
            num_scalar_prefetch=1,
            grid=(steps,),
            in_specs=in_specs,
            out_specs=out_specs,
            scratch_shapes=scratch,
        ),
        compiler_params=pltpu.CompilerParams(
            dimension_semantics=("arbitrary",), vmem_limit_bytes=VMEM_BYTES
        ),
        cost_estimate=pl.CostEstimate(flops=flops, bytes_accessed=nbytes, transcendentals=0),
    )(bits, *args)


def f32(*shape):
    return jax.ShapeDtypeStruct(shape, jnp.float32)


def bf16(*shape):
    return jax.ShapeDtypeStruct(shape, jnp.bfloat16)


def leaf_body(bits, rhs, inverse, own_rows, other_rows, state, own, other, sums):
    rank = own.shape[1]
    rounded = dot(rhs[...], inverse[...]).astype(jnp.bfloat16)
    state[...] = rounded
    part = dot_t(rounded, jnp.concatenate([own_rows[...], other_rows[...]], axis=0))

    @pl.when(pl.program_id(0) == 0)
    def _():
        sums[...] = part

    @pl.when(pl.program_id(0) > 0)
    def _():
        sums[...] += part

    @pl.when(pl.program_id(0) == STEPS - 1)
    def _():
        own[...] = sums[:, :rank]
        other[...] = sums[:, rank:]


def leaf_solve(bits, rhs, leaf_inverse, projection):
    rows, leaf = rhs.shape
    rank = projection.shape[1] // 2
    width = leaf // STEPS
    return run(
        leaf_body,
        STEPS,
        bits,
        [hbm(rhs), hbm(leaf_inverse), hbm(projection), hbm(projection)],
        [
            whole((rows, leaf)),
            pl.BlockSpec((None, leaf, width), lambda j, bits: (0, 0, j)),
            pl.BlockSpec((None, rank, width), lambda j, bits: (0, bits[0], j)),
            pl.BlockSpec((None, rank, width), lambda j, bits: (0, 1 - bits[0], j)),
        ],
        [bf16(rows, leaf), f32(rows, rank), f32(rows, rank)],
        [columns(rows, width), whole((rows, rank)), whole((rows, rank))],
        [pltpu.VMEM((rows, 2 * rank), jnp.float32)],
        2 * rows * leaf * (leaf + 2 * rank),
        leaf * (4 * rows + 2 * leaf),
    )


PAIRS = ((2, 3), (4, 5), (6, 7), (6, 8), (7, 8))


def project_body(levels, bits, state, up, proj, value, gram, kept):
    rank = up.shape[1]
    value[...] = dot_t(state[...], proj[...])
    for h in range(2, levels + 1):

        @pl.when(pl.program_id(0) == h - 2)
        def _(h=h):
            depth = (h - 1) * rank
            full = dot_t(up[: h - 1].reshape(depth, up.shape[2]), proj[...])
            gram[:depth, :] = full.astype(jnp.bfloat16)
            for i, (k, of) in enumerate(PAIRS):
                if of == h:
                    kept[i] = full[(k - 1) * rank : k * rank]


def project(bits, state, up_basis, projection):
    rows, leaf = state.shape
    levels, rank = up_basis.shape[:2]
    wide, count = 2 * rank, levels - 1
    return run(
        functools.partial(project_body, levels),
        count,
        bits,
        [state, up_basis, projection],
        [
            whole((rows, leaf)),
            whole((count, rank, leaf)),
            pl.BlockSpec((None, wide, leaf), lambda j, bits: (j + 1, 0, 0)),
        ],
        [f32(count, rows, wide), bf16(count, count * rank, wide), f32(len(PAIRS), rank, wide)],
        [
            pl.BlockSpec((None, rows, wide), lambda j, bits: (j, 0, 0)),
            pl.BlockSpec((None, count * rank, wide), lambda j, bits: (j, 0, 0)),
            whole((len(PAIRS), rank, wide)),
        ],
        [],
        2 * leaf * wide * (count * rows + rank * count * (count + 1) // 2),
        2 * leaf * (rows + count * 3 * rank),
    )


def emit_halves(which, parts, keep, send):
    count, wide = keep.shape[0], parts[0].shape[1]
    for bit in range(2):

        @pl.when(which == bit)
        def _(bit=bit):
            for i, part in enumerate(parts):
                keep[:, i * wide : (i + 1) * wide] = part[bit * count : (bit + 1) * count]
                send[:, i * wide : (i + 1) * wide] = part[(1 - bit) * count : (2 - bit) * count]


def second_body(bits, mine, received, value, gram, keep, send, coef):
    c1 = (mine[...] + received[...]).astype(jnp.bfloat16)
    coef[...] = c1
    emit_halves(bits[0], [value[i] - dot(c1, gram[i]) for i in range(2)], keep, send)


def second(bits, mine, received, value, gram):
    rows, rank = mine.shape
    wide = 2 * rank
    return run(
        second_body,
        1,
        bits,
        [mine, received, value, gram],
        [whole(mine.shape)] * 2 + [block((2, rows, wide), 0, 0, 0), block((2, rank, wide), 0, 0, 0)],
        [f32(rows // 2, 2 * wide)] * 2 + [bf16(rows, rank)],
        [whole((rows // 2, 2 * wide))] * 2 + [whole((rows, rank))],
        [],
        4 * rows * rank * wide,
        16 * rows * wide,
    )


def fourth_body(bits, c1, mine, received, value, gram, low, high, packed, coef):
    count, rank = mine.shape[0], c1.shape[1]
    for bit in range(2):

        @pl.when(bits[0] == bit)
        def _(bit=bit):
            coef[bit * count : (bit + 1) * count] = mine[...].astype(jnp.bfloat16)
            coef[(1 - bit) * count : (2 - bit) * count] = received[...].astype(jnp.bfloat16)

    parts, total, _ = packed.shape
    share = value.shape[1] // parts
    lhs = jnp.concatenate([c1[...], coef[...]], axis=1)
    for i in range(2):
        left = value[i] - dot(lhs, gram[i])
        for j in range(2):
            start = (2 * i + j) * share
            packed[:, start : start + share, :] = left[:, j * rank : (j + 1) * rank].reshape(parts, share, rank)
    start = 4 * share
    for j in range(2):
        packed[:, start : start + low.shape[0], :] = jnp.broadcast_to(
            low[:, j * rank : (j + 1) * rank], (parts, low.shape[0], rank)
        )
        start += low.shape[0]
    packed[:, start:total, :] = high[...].reshape(parts, total - start, rank)


def fourth(bits, c1, mine, received, value, gram, low, high, parts):
    rows, rank = c1.shape
    wide = 2 * rank
    total = 4 * rows // parts + 2 * low.shape[0] + high.shape[0] // parts
    return run(
        fourth_body,
        1,
        bits,
        [c1, mine, received, value, gram, low, high],
        [whole(c1.shape), whole(mine.shape), whole(received.shape)]
        + [block((2, rows, wide), 1, 0, 0), block((2, 3 * rank, wide), 1, 0, 0)]
        + [whole(low.shape), whole(high.shape)],
        [f32(parts, total, rank), bf16(rows, wide)],
        [whole((parts, total, rank)), whole((rows, wide))],
        [],
        12 * rows * rank * wide,
        16 * rows * wide,
    )


def gather_body(places, bits, packed, own, other, fifth, gram, high):
    parts, total, rank = packed.shape
    share, piece = own.shape[0], gram.shape[0] // parts
    for ref, bit in ((own, 0), (other, 1)):
        for b in range(2):

            @pl.when(bits[2] == b)
            def _(ref=ref, start=(bit ^ b) * share):
                ref[...] = packed[:, start : start + share, :].sum(axis=0)

    for j in range(2):
        start = (2 + j) * share
        fifth[:, j * rank : (j + 1) * rank] = packed[:, start : start + share, :].sum(axis=0)
    for i, place in enumerate(places):
        for j in range(2):
            start = 4 * share + j * piece
            gram[place * piece : (place + 1) * piece, j * rank : (j + 1) * rank] = packed[i, start : start + piece, :]
    high[...] = packed[:, 4 * share + 2 * piece :, :].sum(axis=0)


def gather_rows(bits, packed, places, share):
    parts, total, rank = packed.shape
    rest = total - 4 * share - 2 * rank // parts
    shapes = [(share, rank), (share, rank), (share, 2 * rank), (rank, 2 * rank), (rest, rank)]
    return run(
        functools.partial(gather_body, places),
        1,
        bits,
        [packed],
        [whole(packed.shape)],
        [f32(*s) for s in shapes],
        [whole(s) for s in shapes],
        [],
        parts * total * rank,
        4 * parts * total * rank,
    )


def sixth_body(bits, c1, c23, packed, value, gram, keep, send, coef):
    rank = c1.shape[1]
    share = c1.shape[0] // packed.shape[0]
    for j in range(2):
        coef[:, j * rank : (j + 1) * rank] = (
            packed[:, j * share : (j + 1) * share, :].reshape(c1.shape).astype(jnp.bfloat16)
        )
    lhs = jnp.concatenate([c1[...], c23[...], coef[...]], axis=1)
    emit_halves(bits[1], [value[i] - dot(lhs, gram[i, : lhs.shape[1], :]) for i in range(3)], keep, send)


def sixth(bits, c1, c23, packed, value, gram):
    rows, rank = c1.shape
    wide = 2 * rank
    value, gram = value[4:], gram[4:]
    return run(
        sixth_body,
        1,
        bits,
        [c1, c23, packed, value, gram],
        [whole(c1.shape), whole(c23.shape), whole(packed.shape), whole(value.shape), whole(gram.shape)],
        [f32(rows // 2, 3 * wide)] * 2 + [bf16(rows, wide)],
        [whole((rows // 2, 3 * wide))] * 2 + [whole((rows, wide))],
        [],
        30 * rows * rank * wide,
        24 * rows * wide,
    )


def last_body(bits, state, c1, c23, c45, mine, received, up, out, coef):
    rank, count = c1.shape[1], mine.shape[0]

    @pl.when(pl.program_id(0) == 0)
    def _():
        coef[:, :rank] = c1[...]
        coef[:, rank : 3 * rank] = c23[...]
        coef[:, 3 * rank : 5 * rank] = c45[...]
        for bit in range(2):

            @pl.when(bits[1] == bit)
            def _(bit=bit):
                here = slice(bit * count, (bit + 1) * count)
                there = slice((1 - bit) * count, (2 - bit) * count)
                coef[here, 5 * rank :] = mine[:, : 3 * rank].astype(jnp.bfloat16)
                coef[there, 5 * rank : 6 * rank] = received[:, 2 * rank :].astype(jnp.bfloat16)
                coef[there, 6 * rank :] = received[:, : 2 * rank].astype(jnp.bfloat16)

    basis = up[...].reshape(coef.shape[1], up.shape[2])
    out[...] = state[...].astype(jnp.float32) - dot(coef[...], basis)


def last(bits, state, c1, c23, c45, mine, received, up_basis):
    rows, leaf = state.shape
    levels, rank = up_basis.shape[:2]
    width = leaf // STEPS
    coefs = [c1, c23, c45, mine, received]
    return run(
        last_body,
        STEPS,
        bits,
        [state, *coefs, up_basis],
        [columns(rows, width)]
        + [whole(c.shape) for c in coefs]
        + [pl.BlockSpec((levels, rank, width), lambda j, bits: (0, 0, j))],
        f32(rows, leaf),
        columns(rows, width),
        [pltpu.VMEM((rows, levels * rank), jnp.bfloat16)],
        2 * rows * leaf * levels * rank,
        6 * rows * leaf + 2 * leaf * levels * rank,
    )


def shards(groups_z, groups_zy, rhs, leaf_inverse, up_basis, projection):
    size_x, size_y = lax.axis_size("gx"), lax.axis_size("gy")
    rows = rhs.shape[0]
    rank = up_basis.shape[1]
    wide = 2 * rank
    gx, gy = lax.axis_index("gx"), lax.axis_index("gy")
    z0, z1, z2, y0, y1 = (gx >> i & 1 for i in range(5))
    core, x0, x1 = (gy >> i & 1 for i in range(3))
    bits = jnp.stack([z0, core, y0])
    over_x = functools.partial(swap, axis="gx", size=size_x)
    over_y = functools.partial(swap, axis="gy", size=size_y)
    ring = len(groups_z[0])
    share = rows // ring

    state, own, other = leaf_solve(bits, rhs, leaf_inverse, projection)
    received = over_x(other, mask=1)
    value, gram, kept = project(bits, state, up_basis, projection)

    keep, send, c1 = second(bits, own, received, value, gram)
    received = over_x(send, mask=1)
    low, low_send = split(kept[1], z0)
    both = over_x(jnp.concatenate([kept[0], low_send]), mask=1)
    gram_23 = (kept[0] + both[:rank]).astype(jnp.bfloat16)
    low, low_send = split(low + both[rank:], z1 ^ z2)
    low, low_send = split(low + over_x(low_send, mask=2), z2)
    low = low + over_x(low_send, mask=6)
    places = [(i & 1) * 4 + (i >> 1 & 1 ^ i >> 2) * 2 + (i >> 2) for i in range(ring)]
    high, high_send = split(kept[2:].reshape(3 * rank, wide), y0 ^ y1)
    high, high_send = split(high + over_x(high_send, mask=8), y1)
    high = high + over_x(high_send, mask=24)
    high = jnp.concatenate([high[:, :rank], high[:, rank:]])

    left = keep + received
    c2 = half(left[:, :wide], z1, rank) + over_x(half(left[:, :wide], 1 - z1, rank), mask=2)
    left = left[:, wide:] - dot(c2.astype(jnp.bfloat16), gram_23)
    c3 = half(left, z2, rank) + over_x(half(left, 1 - z2, rank), mask=6)
    c3 = c3 + over_x(c3, mask=2)
    mine = jnp.concatenate([c2, c3], axis=1)
    received = over_x(mine, mask=1)

    packed, c23 = fourth(bits, c1, mine, received, value, gram, low, high, ring)
    packed = exchange(packed, groups_z)
    own, other, left, gram_45, high = gather_rows(bits, packed, places, share)
    c4 = own + over_x(other, mask=8)
    left = left - dot(c4, gram_45)
    c5 = half(left, y1, rank) + over_x(half(left, 1 - y1, rank), mask=24)
    c5 = c5 + over_x(c5, mask=8)
    packed = jnp.concatenate([c4, c5, high], axis=0)
    packed = exchange(jnp.broadcast_to(packed, (ring, *packed.shape)), groups_z)

    keep, send, c45 = sixth(bits, c1, c23, packed, value, gram)
    left = keep + over_y(send, mask=1)
    high = packed[:, 2 * share :].reshape(2, 3 * wide // ring, rank)
    high = jnp.concatenate([high[0], high[1]], axis=1)
    high = join(high, over_x(high, mask=24), y1)
    high = join(high, over_x(high, mask=8), y0 ^ y1)
    high_there = over_y(high, mask=1)
    left, high, high_there = lax.optimization_barrier((left, high, high_there))
    half_rows = rows // 2
    count = half_rows // size_x
    left = exchange(left.reshape(size_x, count, 3 * wide), groups_zy).sum(axis=0)
    high, high_there = high.reshape(3, rank, wide), high_there.reshape(3, rank, wide)
    c6, c6_there = half(left[:, :wide], core, rank), half(left[:, :wide], 1 - core, rank)
    z7 = left[:, wide : 2 * wide] - exact_dot(c6, high[0]) - exact_dot(c6_there, high_there[0])
    z8 = left[:, 2 * wide :] - exact_dot(c6, high[1]) - exact_dot(c6_there, high_there[1])
    c7 = half(z7, x0, rank) + over_y(half(z7, 1 - x0, rank), mask=2)
    z8 = z8 - exact_dot(c7, high[2] + high_there[2])
    c8 = half(z8, x1, rank) + over_y(half(z8, 1 - x1, rank), mask=6)
    c8 = c8 + over_y(c8, mask=2)
    packed = jnp.concatenate([c6, c7, c8, c6_there], axis=1)
    packed = exchange(jnp.broadcast_to(packed, (size_x, *packed.shape)), groups_zy)
    packed = packed.reshape(half_rows, 4 * rank)
    received = over_y(packed[:, rank:], mask=1)
    return last(bits, state, c1, c23, c45, packed, received, up_basis)


def solution(mesh):
    size_x, size_y = mesh.shape["gx"], mesh.shape["gy"]
    ring = 8
    groups_z = [
        [gy * size_x + start + i for i in range(ring)]
        for gy in range(size_y)
        for start in range(0, size_x, ring)
    ]
    groups_zy = [[gy * size_x + i for i in range(size_x)] for gy in range(size_y)]
    return jax.shard_map(
        functools.partial(shards, groups_z, groups_zy),
        mesh=mesh,
        in_specs=(
            P(None, ("gy", "gx")),
            P(("gy", "gx"), None, None),
            P(None, None, ("gy", "gx")),
            P(None, None, ("gy", "gx")),
        ),
        out_specs=P(None, ("gy", "gx")),
        check_vma=False,
    )
```

time: 409 us -> 244 us (0.60)
  waiting for transfers between devices: 299 us -> 58.8 us
  blocking collectives: 0 us -> 66.2 us
  Pallas kernels: 0 us -> 39.3 us
  matrix products: 32.1 us -> 2.91 us
  other arithmetic: 0.81 us -> 7.73 us
  starting transfers between devices: 63.6 us -> 57.9 us
    ppermute x36 -> x22, waiting for transfers between devices: 299 us -> 37.2 us  [swap(): lax.ppermute(value, axis, [(source, source ^ mask) for source in range(si...]
    all_to_all x0 -> x3, blocking collectives: none -> 66.2 us  [exchange(): lax.all_to_all(value, AXES, 0, 0, tiled=True, axis_index_groups=groups)]
    pallas_call x0 -> x7, Pallas kernels: none -> 39.3 us  [run(): pl.pallas_call(body, out_shape=out_shape, grid_spec=pltpu.PrefetchScalarG...]
    dot_general x17 -> x7, matrix products: 32.1 us -> 2.91 us  [the longest x2 2.11 us: dot(): return jnp.dot(a, b, preferred_element_type=jnp.float32)]
    all_to_all x0 -> x1, waiting for transfers between devices: none -> 21.6 us  [exchange(): lax.all_to_all(value, AXES, 0, 0, tiled=True, axis_index_groups=groups)]
    unnamed x20 -> x12, local copies, waits for them, and re-layouts: 12.1 us -> 2.18 us
    ppermute x36 -> x22, starting transfers between devices: 63.6 us -> 54 us  [swap(): lax.ppermute(value, axis, [(source, source ^ mask) for source in range(si...]
    slice x0 -> x8, local copies, waits for them, and re-layouts: none -> 6.28 us  [the longest x2 5.19 us: sixth(): value, gram = (value[4:], gram[4:])]
  transfers between devices with their start and end apart: 36 -> 23, of which waited for: 36 -> 13; matrix products, arithmetic and copies ran while one was open for 0% -> 5% of each run, Pallas kernels for 0% -> 8%
where the time goes in v2:
time: 244 us; the launch traced here: 243 us
  blocking collectives  66.2 us (27%)
  waiting for transfers between devices  58.8 us (24%)
  starting transfers between devices  57.9 us (24%)
  Pallas kernels  39.3 us (16%)
  local copies, waits for them, and re-layouts  9.69 us (4%)
  other arithmetic  7.73 us (3%)
  matrix products  2.91 us (1%)
    all_to_all x3, blocking collectives, exchange(): lax.all_to_all(value, AXES, 0, 0, tiled=True, axis_index_groups=groups)  66.2 us
    ppermute x22, starting transfers between devices, swap(): lax.ppermute(value, axis, [(source, source ^ mask) for source in range(si...  54 us
    pallas_call x7, Pallas kernels, run(): pl.pallas_call(body, out_shape=out_shape, grid_spec=pltpu.PrefetchScalarG...  39.3 us
    ppermute x22, waiting for transfers between devices, swap(): lax.ppermute(value, axis, [(source, source ^ mask) for source in range(si...  37.2 us
    all_to_all x1, waiting for transfers between devices, exchange(): lax.all_to_all(value, AXES, 0, 0, tiled=True, axis_index_groups=groups)  21.6 us
    slice x2, local copies, waits for them, and re-layouts, sixth(): value, gram = (value[4:], gram[4:])  5.19 us
  transfers between devices with their start and end apart: 23, of which 13 were waited for; matrix products, arithmetic and copies ran while one was open for 5% of the time, Pallas kernels for 8%

profile of v2, /device:TPU:1, one launch (start us, length us, event | category | flops | bytes accessed | tf_op | source)
XLA Modules:
  0.0 242.9 jit_solution(15305177547775047356)
XLA Ops:
  0.7 6.4 %shard_map.46 = (bf16[512,1024]{1,0:T(8,128)(2,1)}, f32[512,128]{1,0:T(8,128)}, f32[512,128]{1,0:T(8,128)}) custom-call(s32[3]{0:T(128)} %pad_add_fusion.bits, bf16[512,1024]{1,0:T(8,128)(2,1)} %rhs.1, bf16[1,1024,1024]{2,1,0:T(8,128)(2,1)} %inverse.1, bf16[8,256,1024]{2,1,0:T(8,128)(2,1)} %proj.1, bf16[8,256,1024]{2,1,0:T(8,128)(2,1)} %proj.1), custom_call_target="tpu_custom_call" | custom-call | flops 1342177280 | bytes 4194304 | tf_op jit(solution)/shard_map/pallas_call | solution.py:66
  7.1 2.5 %collective-permute-start = (f32[512,128]{1,0:T(8,128)}, f32[512,128]{1,0:T(8,128)S(1)}, u32[]{:S(2)}, u32[]{:S(2)}) collective-permute-start(f32[512,128]{1,0:T(8,128)} %get-tuple-element.29), channel_id=1, source_target_pairs={{0,8},{8,0},{16,24},{24,16},{32,40},{40,32},{48,56},{56,48},{64,72... | collective-permute-start | bytes 786440 | tf_op jit(solution)/shard_map/ppermute | solution.py:28
  9.6 12.0 %shard_map.47 = (f32[7,512,256]{2,1,0:T(8,128)}, bf16[7,896,256]{2,1,0:T(8,128)(2,1)}, f32[5,128,256]{2,1,0:T(8,128)}) custom-call(s32[3]{0:T(128)} %pad_add_fusion.bits, bf16[512,1024]{1,0:T(8,128)(2,1)} %get-tuple-element.27.state, bf16[8,128,1024]{2,1,0:T(8,128)(2,1)} %up.3, bf16[8,256,1024]{2,1,0:T(8,128)(2,1)} %proj.1), custom_call_target="tpu_custom_call" | custom-call | flops 3758096384 | bytes 6553600 | tf_op jit(solution)/shard_map/pallas_call | solution.py:66
  25.9 3.5 %shard_map.48 = (f32[256,512]{1,0:T(8,128)}, f32[256,512]{1,0:T(8,128)}, bf16[512,128]{1,0:T(8,128)(2,1)}) custom-call(s32[3]{0:T(128)} %pad_add_fusion.bits, f32[512,128]{1,0:T(8,128)} %get-tuple-element.28.mine, f32[512,128]{1,0:T(8,128)} %copy-done.5, f32[7,512,256]{2,1,0:T(8,128)} %get-tuple-element.30.value, bf16[7,896,256]{2,1,0:T(8,128)(2,1)} %get-tuple-element.31.gram), custom_call_target="tpu_custom_call" | custom-call | flops 67108864 | bytes 2097152 | tf_op jit(solution)/shard_map/pallas_call | solution.py:66
  30.8 3.1 %collective-permute-start.7 = (f32[32,256]{1,0:T(8,128)S(1)}, f32[32,256]{1,0:T(8,128)S(1)}, u32[]{:S(2)}, u32[]{:S(2)}) collective-permute-start(f32[32,256]{1,0:T(8,128)S(1)} %constant_dynamic-slice_fusion.10), channel_id=1, source_target_pairs={{0,16},{8,24},{16,0},{24,8},{32,48},{40,56},{48,32},{56,40},{64,80... | collective-permute-start | bytes 98312 | tf_op jit(solution)/shard_map/ppermute | solution.py:28
  35.9 6.2 %collective-permute-done.1 = f32[256,512]{1,0:T(8,128)S(1)} collective-permute-done((f32[256,512]{1,0:T(8,128)}, f32[256,512]{1,0:T(8,128)S(1)}, u32[]{:S(2)}, u32[]{:S(2)}) %collective-permute-start.1) | collective-permute-done | bytes 524320 | tf_op jit(solution)/shard_map/ppermute | solution.py:28
  43.3 2.8 %collective-permute-start.2 = (f32[256,128]{1,0:T(8,128)S(1)}, f32[256,128]{1,0:T(8,128)S(1)}, u32[]{:S(2)}, u32[]{:S(2)}) collective-permute-start(f32[256,128]{1,0:T(8,128)S(1)} %constant_dynamic-slice_fusion.12), channel_id=1, source_target_pairs={{0,16},{8,24},{16,0},{24,8},{32,48},{40,56},{48,32},{56,40},{64,80... | collective-permute-start | bytes 393224 | tf_op jit(solution)/shard_map/ppermute | solution.py:28
  46.2 4.7 %collective-permute-start.8 = (f32[16,256]{1,0:T(8,128)S(1)}, f32[16,256]{1,0:T(8,128)S(1)}, u32[]{:S(2)}, u32[]{:S(2)}) collective-permute-start(f32[16,256]{1,0:T(8,128)S(1)} %constant_dynamic-slice_fusion.9), channel_id=1, source_target_pairs={{0,48},{8,56},{16,32},{24,40},{32,16},{40,24},{48,0},{56,8},{64,11... | collective-permute-start | bytes 49160 | tf_op jit(solution)/shard_map/ppermute | solution.py:28
  52.0 2.7 %collective-permute-start.4 = (f32[256,128]{1,0:T(8,128)S(1)}, f32[256,128]{1,0:T(8,128)S(1)}, u32[]{:S(2)}, u32[]{:S(2)}) collective-permute-start(f32[256,128]{1,0:T(8,128)S(1)} %constant_dynamic-slice_fusion.11), channel_id=1, source_target_pairs={{0,48},{8,56},{16,32},{24,40},{32,16},{40,24},{48,0},{56,8},{64,11... | collective-permute-start | bytes 393224 | tf_op jit(solution)/shard_map/ppermute | solution.py:28
  55.3 3.8 %collective-permute-done.4 = f32[256,128]{1,0:T(8,128)S(1)} collective-permute-done((f32[256,128]{1,0:T(8,128)S(1)}, f32[256,128]{1,0:T(8,128)S(1)}, u32[]{:S(2)}, u32[]{:S(2)}) %collective-permute-start.4) | collective-permute-done | bytes 131104 | tf_op jit(solution)/shard_map/ppermute | solution.py:28
  59.1 2.3 collective-permute-start.5
  61.4 2.6 %collective-permute-done.5 = f32[256,128]{1,0:T(8,128)S(1)} collective-permute-done((f32[256,128]{1,0:T(8,128)S(1)}, f32[256,128]{1,0:T(8,128)S(1)}, u32[]{:S(2)}, u32[]{:S(2)}) %collective-permute-start.5) | collective-permute-done | bytes 131104 | tf_op jit(solution)/shard_map/ppermute | solution.py:28
  64.1 2.7 %collective-permute-start.6 = (f32[256,256]{1,0:T(8,128)S(1)}, f32[256,256]{1,0:T(8,128)S(1)}, u32[]{:S(2)}, u32[]{:S(2)}) collective-permute-start(f32[256,256]{1,0:T(8,128)S(1)} %pad_maximum_fusion.mine), channel_id=1, source_target_pairs={{0,8},{8,0},{16,24},{24,16},{32,40},{40,32},{48,56},{56,48},{64,72... | collective-permute-start | bytes 786440 | tf_op jit(solution)/shard_map/ppermute | solution.py:28
  67.4 4.2 %collective-permute-done.6.received = f32[256,256]{1,0:T(8,128)S(1)} collective-permute-done((f32[256,256]{1,0:T(8,128)S(1)}, f32[256,256]{1,0:T(8,128)S(1)}, u32[]{:S(2)}, u32[]{:S(2)}) %collective-permute-start.6) | collective-permute-done | bytes 262176 | tf_op jit(solution)/shard_map/ppermute | solution.py:28
  72.3 3.7 %shard_map.49 = (f32[8,312,128]{2,1,0:T(8,128)}, bf16[512,256]{1,0:T(8,128)(2,1)}) custom-call(s32[3]{0:T(128)} %pad_add_fusion.bits, bf16[512,128]{1,0:T(8,128)(2,1)} %get-tuple-element.32.c1, f32[256,256]{1,0:T(8,128)} %copy-done.2, f32[256,256]{1,0:T(8,128)} %copy-done.4, f32[7,512,256]{2,1,0:T(8,128)} %get-tuple-element.30.value, ...), custom_call_target="tpu_custom_call" | custom-call | flops 201326592 | bytes 2097152 | tf_op jit(solution)/shard_map/pallas_call | solution.py:66
  76.0 31.6 %all_to_all.20.packed = f32[8,312,128]{2,1,0:T(8,128)} all-to-all(f32[8,312,128]{2,1,0:T(8,128)} %get-tuple-element.37), channel_id=1, replica_groups={{0,8,16,24,32,40,48,56},{64,72,80,88,96,104,112,120},{128,136,144,152,1..., dimensions={0} | all-to-all | bytes 2555904 | tf_op jit(solution)/shard_map/all_to_all | solution.py:32
  107.7 2.7 %shard_map.50 = (f32[64,128]{1,0:T(8,128)}, f32[64,128]{1,0:T(8,128)}, f32[64,256]{1,0:T(8,128)}, f32[128,256]{1,0:T(8,128)}, f32[24,128]{1,0:T(8,128)}) custom-call(s32[3]{0:T(128)} %pad_add_fusion.bits, f32[8,312,128]{2,1,0:T(8,128)} %all_to_all.20.packed), custom_call_target="tpu_custom_call" | custom-call | flops 319488 | bytes 1277952 | tf_op jit(solution)/shard_map/pallas_call | solution.py:66
  110.6 2.7 %collective-permute-done.11 = f32[64,128]{1,0:T(8,128)S(1)} collective-permute-done((f32[64,128]{1,0:T(8,128)}, f32[64,128]{1,0:T(8,128)S(1)}, u32[]{:S(2)}, u32[]{:S(2)}) %collective-permute-start.11) | collective-permute-done | bytes 32800 | tf_op jit(solution)/shard_map/ppermute | solution.py:28
  120.1 3.0 %collective-permute-done.13 = f32[64,128]{1,0:T(8,128)S(1)} collective-permute-done((f32[64,128]{1,0:T(8,128)S(1)}, f32[64,128]{1,0:T(8,128)S(1)}, u32[]{:S(2)}, u32[]{:S(2)}) %collective-permute-start.13) | collective-permute-done | bytes 32800 | tf_op jit(solution)/shard_map/ppermute | solution.py:28
  123.9 16.8 %all_to_all.21.packed = f32[8,152,128]{2,1,0:T(8,128)S(1)} all-to-all(f32[8,152,128]{2,1,0:T(8,128)S(1)} %broadcast_in_dim.6), channel_id=1, replica_groups={{0,8,16,24,32,40,48,56},{64,72,80,88,96,104,112,120},{128,136,144,152,1..., dimensions={0} | all-to-all | bytes 1245184 | tf_op jit(solution)/shard_map/all_to_all | solution.py:32
  142.8 2.7 %slice.92.value = f32[3,512,256]{2,1,0:T(8,128)} slice(f32[7,512,256]{2,1,0:T(8,128)} %get-tuple-element.30.value), slice={[4:7], [0:512], [0:256]} | slice | bytes 3145728 | tf_op jit(solution)/shard_map/slice | solution.py:310
  145.4 2.5 %slice.93.gram = bf16[3,896,256]{2,1,0:T(8,128)(2,1)} slice(bf16[7,896,256]{2,1,0:T(8,128)(2,1)} %get-tuple-element.31.gram), slice={[4:7], [0:896], [0:256]} | slice | bytes 2752512 | tf_op jit(solution)/shard_map/slice | solution.py:310
  148.0 4.9 %shard_map.51 = (f32[256,768]{1,0:T(8,128)}, f32[256,768]{1,0:T(8,128)}, bf16[512,256]{1,0:T(8,128)(2,1)}) custom-call(s32[3]{0:T(128)} %pad_add_fusion.bits, bf16[512,128]{1,0:T(8,128)(2,1)} %get-tuple-element.32.c1, bf16[512,256]{1,0:T(8,128)(2,1)} %get-tuple-element.36.c23, f32[8,152,128]{2,1,0:T(8,128)} %copy-done.1, f32[3,512,256]{2,1,0:T(8,128)} %slice.92.value, ...), custom_call_target="tpu_custom_call" | custom-call | flops 503316480 | bytes 3145728 | tf_op jit(solution)/shard_map/pallas_call | solution.py:66
  152.8 12.4 %collective-permute-start.14 = (f32[256,768]{1,0:T(8,128)}, f32[256,768]{1,0:T(8,128)S(1)}, u32[]{:S(2)}, u32[]{:S(2)}) collective-permute-start(f32[256,768]{1,0:T(8,128)} %get-tuple-element.45), channel_id=1, source_target_pairs={{0,1},{1,0},{2,3},{3,2},{4,5},{5,4},{6,7},{7,6},{8,9},{9,8},{10,11... | collective-permute-start | bytes 2359304 | tf_op jit(solution)/shard_map/ppermute | solution.py:28
  165.3 6.5 %collective-permute-done.16 = f32[192,256]{1,0:T(8,128)S(1)} collective-permute-done((f32[192,256]{1,0:T(8,128)S(1)}, f32[192,256]{1,0:T(8,128)S(1)}, u32[]{:S(2)}, u32[]{:S(2)}) %collective-permute-start.16) | collective-permute-done | bytes 196640 | tf_op jit(solution)/shard_map/ppermute | solution.py:28
  174.9 3.9 %all-to-all-start.2 = ((f32[32,8,768]{2,1,0:T(8,128)}), f32[32,8,768]{2,1,0:T(8,128)S(1)}, u32[]{:S(2)}, u32[]{:S(2)}) async-start(f32[32,8,768]{2,1,0:T(8,128)} %bitcast.9), calls=%async_computation.2 | async-start | bytes 1572864 | tf_op jit(solution)/shard_map/all_to_all | solution.py:32
  178.8 21.6 %all-to-all-done.2 = f32[32,8,768]{2,1,0:T(8,128)S(1)} async-done(((f32[32,8,768]{2,1,0:T(8,128)}), f32[32,8,768]{2,1,0:T(8,128)S(1)}, u32[]{:S(2)}, u32[]{:S(2)}) %all-to-all-start.2) | async-done | bytes 786464 | tf_op jit(solution)/shard_map/all_to_all | solution.py:32
  203.7 2.5 %collective-permute-start.19 = (f32[8,128]{1,0:T(8,128)S(1)}, f32[8,128]{1,0:T(8,128)S(1)}, u32[]{:S(2)}, u32[]{:S(2)}) collective-permute-start(f32[8,128]{1,0:T(8,128)S(1)} %constant_dynamic-slice_fusion), channel_id=1, source_target_pairs={{0,6},{1,7},{2,4},{3,5},{4,2},{5,3},{6,0},{7,1},{8,14},{9,15},{10,... | collective-permute-start | bytes 12296 | tf_op jit(solution)/shard_map/ppermute | solution.py:28
  207.5 2.5 %collective-permute-done.20 = f32[8,128]{1,0:T(8,128)S(1)} collective-permute-done((f32[8,128]{1,0:T(8,128)S(1)}, f32[8,128]{1,0:T(8,128)S(1)}, u32[]{:S(2)}, u32[]{:S(2)}) %collective-permute-start.20) | collective-permute-done | bytes 4128 | tf_op jit(solution)/shard_map/ppermute | solution.py:28
  210.0 17.8 %all_to_all.22 = f32[32,8,512]{2,1,0:T(8,128)S(1)} all-to-all(f32[32,8,512]{2,1,0:T(8,128)S(1)} %broadcast_in_dim.7), channel_id=1, replica_groups={{0,8,16,24,32,40,48,56,64,72,80,88,96,104,112,120,128,136,144,152,160,1..., dimensions={0} | all-to-all | bytes 1048576 | tf_op jit(solution)/shard_map/all_to_all | solution.py:32
  227.8 6.8 %collective-permute-start.21 = (f32[256,384]{1,0:T(8,128)S(1)}, f32[256,384]{1,0:T(8,128)S(1)}, u32[]{:S(2)}, u32[]{:S(2)}) collective-permute-start(f32[256,384]{1,0:T(8,128)S(1)} %slice.117), channel_id=1, source_target_pairs={{0,1},{1,0},{2,3},{3,2},{4,5},{5,4},{6,7},{7,6},{8,9},{9,8},{10,11... | collective-permute-start | bytes 1179656 | tf_op jit(solution)/shard_map/ppermute | solution.py:28
  236.8 6.1 %shard_map.52 = f32[512,1024]{1,0:T(8,128)} custom-call(s32[3]{0:T(128)} %pad_add_fusion.bits, bf16[512,1024]{1,0:T(8,128)(2,1)} %get-tuple-element.27.state, bf16[512,128]{1,0:T(8,128)(2,1)} %get-tuple-element.32.c1, bf16[512,256]{1,0:T(8,128)(2,1)} %get-tuple-element.36.c23, bf16[512,256]{1,0:T(8,128)(2,1)} %get-tuple-element.43.c45, f32[256,512]{1,0:T(8,128)} %bitcast.25, ...), custom_call_target="tpu_custom_call" | custom-call | flops 1073741824 | bytes 5242880 | tf_op jit(solution)/shard_map/pallas_call | solution.py:66
  (92 shorter events, 32.4 us)
Async XLA Ops:
  7.1 18.0 %collective-permute-start = (f32[512,128]{1,0:T(8,128)}, f32[512,128]{1,0:T(8,128)S(1)}, u32[]{:S(2)}, u32[]{:S(2)}) collective-permute-start(f32[512,128]{1,0:T(8,128)} %get-tuple-element.29), channel_id=1, source_target_pairs={{0,8},{8,0},{16,24},{24,16},{32,40},{40,32},{48,56},{56,48},{64,72... | collective-permute-start | bytes 786440 | tf_op jit(solution)/shard_map/ppermute | solution.py:28
  22.6 8.2 %collective-permute-start.3 = (f32[192,256]{1,0:T(8,128)S(1)}, f32[192,256]{1,0:T(8,128)S(1)}, u32[]{:S(2)}, u32[]{:S(2)}) collective-permute-start(f32[192,256]{1,0:T(8,128)S(1)} %pad_maximum_fusion.1), channel_id=1, source_target_pairs={{0,8},{8,0},{16,24},{24,16},{32,40},{40,32},{48,56},{56,48},{64,72... | collective-permute-start | bytes 589832 | tf_op jit(solution)/shard_map/ppermute | solution.py:28
  23.8 10.2 %collective-permute-start.9 = (f32[192,256]{1,0:T(8,128)S(1)}, f32[192,256]{1,0:T(8,128)S(1)}, u32[]{:S(2)}, u32[]{:S(2)}) collective-permute-start(f32[192,256]{1,0:T(8,128)S(1)} %constant_dynamic-slice_fusion.8), channel_id=1, source_target_pairs={{0,64},{8,72},{16,80},{24,88},{32,96},{40,104},{48,112},{56,120},{... | collective-permute-start | bytes 589832 | tf_op jit(solution)/shard_map/ppermute | solution.py:28
  25.1 0.7 copy-start.5
  29.3 12.8 %collective-permute-start.1 = (f32[256,512]{1,0:T(8,128)}, f32[256,512]{1,0:T(8,128)S(1)}, u32[]{:S(2)}, u32[]{:S(2)}) collective-permute-start(f32[256,512]{1,0:T(8,128)} %get-tuple-element.34), channel_id=1, source_target_pairs={{0,8},{8,0},{16,24},{24,16},{32,40},{40,32},{48,56},{56,48},{64,72... | collective-permute-start | bytes 1572872 | tf_op jit(solution)/shard_map/ppermute | solution.py:28
  30.8 15.3 %collective-permute-start.7 = (f32[32,256]{1,0:T(8,128)S(1)}, f32[32,256]{1,0:T(8,128)S(1)}, u32[]{:S(2)}, u32[]{:S(2)}) collective-permute-start(f32[32,256]{1,0:T(8,128)S(1)} %constant_dynamic-slice_fusion.10), channel_id=1, source_target_pairs={{0,16},{8,24},{16,0},{24,8},{32,48},{40,56},{48,32},{56,40},{64,80... | collective-permute-start | bytes 98312 | tf_op jit(solution)/shard_map/ppermute | solution.py:28
  34.0 27.4 %collective-permute-start.10 = (f32[96,256]{1,0:T(8,128)S(1)}, f32[96,256]{1,0:T(8,128)S(1)}, u32[]{:S(2)}, u32[]{:S(2)}) collective-permute-start(f32[96,256]{1,0:T(8,128)S(1)} %constant_dynamic-slice_fusion.7), channel_id=1, source_target_pairs={{0,192},{8,200},{16,208},{24,216},{32,224},{40,232},{48,240},{56,2... | collective-permute-start | bytes 294920 | tf_op jit(solution)/shard_map/ppermute | solution.py:28
  43.3 7.5 %collective-permute-start.2 = (f32[256,128]{1,0:T(8,128)S(1)}, f32[256,128]{1,0:T(8,128)S(1)}, u32[]{:S(2)}, u32[]{:S(2)}) collective-permute-start(f32[256,128]{1,0:T(8,128)S(1)} %constant_dynamic-slice_fusion.12), channel_id=1, source_target_pairs={{0,16},{8,24},{16,0},{24,8},{32,48},{40,56},{48,32},{56,40},{64,80... | collective-permute-start | bytes 393224 | tf_op jit(solution)/shard_map/ppermute | solution.py:28
  46.2 8.5 %collective-permute-start.8 = (f32[16,256]{1,0:T(8,128)S(1)}, f32[16,256]{1,0:T(8,128)S(1)}, u32[]{:S(2)}, u32[]{:S(2)}) collective-permute-start(f32[16,256]{1,0:T(8,128)S(1)} %constant_dynamic-slice_fusion.9), channel_id=1, source_target_pairs={{0,48},{8,56},{16,32},{24,40},{32,16},{40,24},{48,0},{56,8},{64,11... | collective-permute-start | bytes 49160 | tf_op jit(solution)/shard_map/ppermute | solution.py:28
  52.0 7.1 %collective-permute-start.4 = (f32[256,128]{1,0:T(8,128)S(1)}, f32[256,128]{1,0:T(8,128)S(1)}, u32[]{:S(2)}, u32[]{:S(2)}) collective-permute-start(f32[256,128]{1,0:T(8,128)S(1)} %constant_dynamic-slice_fusion.11), channel_id=1, source_target_pairs={{0,48},{8,56},{16,32},{24,40},{32,16},{40,24},{48,0},{56,8},{64,11... | collective-permute-start | bytes 393224 | tf_op jit(solution)/shard_map/ppermute | solution.py:28
  59.1 4.9 %collective-permute-start.5 = (f32[256,128]{1,0:T(8,128)S(1)}, f32[256,128]{1,0:T(8,128)S(1)}, u32[]{:S(2)}, u32[]{:S(2)}) collective-permute-start(f32[256,128]{1,0:T(8,128)S(1)} %dynamic-slice_add_fusion.1), channel_id=1, source_target_pairs={{0,16},{8,24},{16,0},{24,8},{32,48},{40,56},{48,32},{56,40},{64,80... | collective-permute-start | bytes 393224 | tf_op jit(solution)/shard_map/ppermute | solution.py:28
  64.0 7.5 %copy-start.2 = (f32[256,256]{1,0:T(8,128)}, f32[256,256]{1,0:T(8,128)S(1)}, u32[]{:S(2)}) copy-start(f32[256,256]{1,0:T(8,128)S(1)} %pad_maximum_fusion.mine) | copy-start | bytes 786436
  64.1 7.5 %collective-permute-start.6 = (f32[256,256]{1,0:T(8,128)S(1)}, f32[256,256]{1,0:T(8,128)S(1)}, u32[]{:S(2)}, u32[]{:S(2)}) collective-permute-start(f32[256,256]{1,0:T(8,128)S(1)} %pad_maximum_fusion.mine), channel_id=1, source_target_pairs={{0,8},{8,0},{16,24},{24,16},{32,40},{40,32},{48,56},{56,48},{64,72... | collective-permute-start | bytes 786440 | tf_op jit(solution)/shard_map/ppermute | solution.py:28
  71.6 0.7 copy-start.4
  110.4 3.0 %collective-permute-start.11 = (f32[64,128]{1,0:T(8,128)}, f32[64,128]{1,0:T(8,128)S(1)}, u32[]{:S(2)}, u32[]{:S(2)}) collective-permute-start(f32[64,128]{1,0:T(8,128)} %get-tuple-element.39), channel_id=1, source_target_pairs={{0,64},{8,72},{16,80},{24,88},{32,96},{40,104},{48,112},{56,120},{... | collective-permute-start | bytes 98312 | tf_op jit(solution)/shard_map/ppermute | solution.py:28
  116.0 4.1 %collective-permute-start.12 = (f32[64,128]{1,0:T(8,128)S(1)}, f32[64,128]{1,0:T(8,128)S(1)}, u32[]{:S(2)}, u32[]{:S(2)}) collective-permute-start(f32[64,128]{1,0:T(8,128)S(1)} %constant_dynamic-slice_fusion.6), channel_id=1, source_target_pairs={{0,192},{8,200},{16,208},{24,216},{32,224},{40,232},{48,240},{56,2... | collective-permute-start | bytes 98312 | tf_op jit(solution)/shard_map/ppermute | solution.py:28
  120.1 3.1 %collective-permute-start.13 = (f32[64,128]{1,0:T(8,128)S(1)}, f32[64,128]{1,0:T(8,128)S(1)}, u32[]{:S(2)}, u32[]{:S(2)}) collective-permute-start(f32[64,128]{1,0:T(8,128)S(1)} %dynamic-slice_add_fusion.4), channel_id=1, source_target_pairs={{0,64},{8,72},{16,80},{24,88},{32,96},{40,104},{48,112},{56,120},{... | collective-permute-start | bytes 98312 | tf_op jit(solution)/shard_map/ppermute | solution.py:28
  140.7 7.2 %copy-start.1 = (f32[8,152,128]{2,1,0:T(8,128)}, f32[8,152,128]{2,1,0:T(8,128)S(1)}, u32[]{:S(2)}) copy-start(f32[8,152,128]{2,1,0:T(8,128)S(1)} %all_to_all.21.packed) | copy-start | bytes 1867780
  140.7 24.5 %collective-permute-start.15 = (f32[96,256]{1,0:T(8,128)S(1)}, f32[96,256]{1,0:T(8,128)S(1)}, u32[]{:S(2)}, u32[]{:S(2)}) collective-permute-start(f32[96,256]{1,0:T(8,128)S(1)} %pad_maximum_fusion.3), channel_id=1, source_target_pairs={{0,192},{8,200},{16,208},{24,216},{32,224},{40,232},{48,240},{56,2... | collective-permute-start | bytes 294920 | tf_op jit(solution)/shard_map/ppermute | solution.py:28
  152.8 19.9 %collective-permute-start.14 = (f32[256,768]{1,0:T(8,128)}, f32[256,768]{1,0:T(8,128)S(1)}, u32[]{:S(2)}, u32[]{:S(2)}) collective-permute-start(f32[256,768]{1,0:T(8,128)} %get-tuple-element.45), channel_id=1, source_target_pairs={{0,1},{1,0},{2,3},{3,2},{4,5},{5,4},{6,7},{7,6},{8,9},{9,8},{10,11... | collective-permute-start | bytes 2359304 | tf_op jit(solution)/shard_map/ppermute | solution.py:28
  165.2 6.6 %collective-permute-start.16 = (f32[192,256]{1,0:T(8,128)S(1)}, f32[192,256]{1,0:T(8,128)S(1)}, u32[]{:S(2)}, u32[]{:S(2)}) collective-permute-start(f32[192,256]{1,0:T(8,128)S(1)} %maximum_select_fusion.1), channel_id=1, source_target_pairs={{0,64},{8,72},{16,80},{24,88},{32,96},{40,104},{48,112},{56,120},{... | collective-permute-start | bytes 589832 | tf_op jit(solution)/shard_map/ppermute | solution.py:28
  171.9 3.0 %collective-permute-start.17 = (f32[384,256]{1,0:T(8,128)S(1)}, f32[384,256]{1,0:T(8,128)S(1)}, u32[]{:S(2)}, u32[]{:S(2)}) collective-permute-start(f32[384,256]{1,0:T(8,128)S(1)} %maximum_select_fusion), channel_id=1, source_target_pairs={{0,1},{1,0},{2,3},{3,2},{4,5},{5,4},{6,7},{7,6},{8,9},{9,8},{10,11... | collective-permute-start | bytes 1179656 | tf_op jit(solution)/shard_map/ppermute | solution.py:28
  174.9 25.6 %all-to-all-start.2 = ((f32[32,8,768]{2,1,0:T(8,128)}), f32[32,8,768]{2,1,0:T(8,128)S(1)}, u32[]{:S(2)}, u32[]{:S(2)}) async-start(f32[32,8,768]{2,1,0:T(8,128)} %bitcast.9), calls=%async_computation.2 | async-start | bytes 1572864 | tf_op jit(solution)/shard_map/all_to_all | solution.py:32
  201.0 2.5 %collective-permute-start.18 = (f32[8,128]{1,0:T(8,128)S(1)}, f32[8,128]{1,0:T(8,128)S(1)}, u32[]{:S(2)}, u32[]{:S(2)}) collective-permute-start(f32[8,128]{1,0:T(8,128)S(1)} %constant_dynamic-slice_fusion.2), channel_id=1, source_target_pairs={{0,2},{1,3},{2,0},{3,1},{4,6},{5,7},{6,4},{7,5},{8,10},{9,11},{10,... | collective-permute-start | bytes 12296 | tf_op jit(solution)/shard_map/ppermute | solution.py:28
  203.7 3.7 %collective-permute-start.19 = (f32[8,128]{1,0:T(8,128)S(1)}, f32[8,128]{1,0:T(8,128)S(1)}, u32[]{:S(2)}, u32[]{:S(2)}) collective-permute-start(f32[8,128]{1,0:T(8,128)S(1)} %constant_dynamic-slice_fusion), channel_id=1, source_target_pairs={{0,6},{1,7},{2,4},{3,5},{4,2},{5,3},{6,0},{7,1},{8,14},{9,15},{10,... | collective-permute-start | bytes 12296 | tf_op jit(solution)/shard_map/ppermute | solution.py:28
  207.5 2.5 %collective-permute-start.20 = (f32[8,128]{1,0:T(8,128)S(1)}, f32[8,128]{1,0:T(8,128)S(1)}, u32[]{:S(2)}, u32[]{:S(2)}) collective-permute-start(f32[8,128]{1,0:T(8,128)S(1)} %fusion.14), channel_id=1, source_target_pairs={{0,2},{1,3},{2,0},{3,1},{4,6},{5,7},{6,4},{7,5},{8,10},{9,11},{10,... | collective-permute-start | bytes 12296 | tf_op jit(solution)/shard_map/ppermute | solution.py:28
  227.8 8.2 %copy-start = (f32[32,8,512]{2,1,0:T(8,128)}, f32[32,8,512]{2,1,0:T(8,128)S(1)}, u32[]{:S(2)}) copy-start(f32[32,8,512]{2,1,0:T(8,128)S(1)} %all_to_all.22) | copy-start | bytes 1572868
  227.8 8.2 %collective-permute-start.21 = (f32[256,384]{1,0:T(8,128)S(1)}, f32[256,384]{1,0:T(8,128)S(1)}, u32[]{:S(2)}, u32[]{:S(2)}) collective-permute-start(f32[256,384]{1,0:T(8,128)S(1)} %slice.117), channel_id=1, source_target_pairs={{0,1},{1,0},{2,3},{3,2},{4,5},{5,4},{6,7},{7,6},{8,9},{9,8},{10,11... | collective-permute-start | bytes 1179656 | tf_op jit(solution)/shard_map/ppermute | solution.py:28
  236.0 0.7 copy-start.3

commit v3 on v2

--- a/solution.py
+++ b/solution.py
@@ -9,7 +9,7 @@
 
 AXES = ("gy", "gx")
 STEPS = 4
-VMEM_BYTES = 58 * 1024 * 1024
+VMEM_BYTES = 16 * 1024 * 1024
 
 
 def dot(a, b):
@@ -32,18 +32,21 @@
     return lax.all_to_all(value, AXES, 0, 0, tiled=True, axis_index_groups=groups)
 
 
-def half(value, which, rank):
-    return lax.dynamic_slice_in_dim(value, which * rank, rank, value.ndim - 1)
-
-
-def split(value, bit):
+def half(value, start):
+    return lax.dynamic_slice_in_dim(value, start, value.shape[-1] // 2, value.ndim - 1)
+
+
+def split(value, starts):
     count = value.shape[0] // 2
-    mine = lax.dynamic_slice_in_dim(value, bit * count, count, 0)
-    return mine, lax.dynamic_slice_in_dim(value, (1 - bit) * count, count, 0)
-
-
-def join(mine, other, bit):
-    return jnp.where(bit == 0, jnp.concatenate([mine, other]), jnp.concatenate([other, mine]))
+    return tuple(lax.dynamic_slice_in_dim(value, start, count, 0) for start in starts)
+
+
+def join(mine, other, first):
+    return jnp.where(first, jnp.concatenate([mine, other]), jnp.concatenate([other, mine]))
+
+
+def starts(bit, count):
+    return (bit * count).astype(jnp.uint32), ((1 - bit) * count).astype(jnp.uint32)
 
 
 def hbm(value):
@@ -88,6 +91,23 @@
     return jax.ShapeDtypeStruct(shape, jnp.bfloat16)
 
 
+def vmem(*shape, dtype=jnp.float32):
+    return pltpu.VMEM(shape, dtype)
+
+
+def local(body, bits, args, outs, flops, nbytes):
+    args = [pltpu.with_memory_space_constraint(a, pltpu.VMEM) for a in args]
+    return pl.pallas_call(
+        body,
+        out_shape=outs,
+        in_specs=[pl.BlockSpec(memory_space=pltpu.SMEM)]
+        + [pl.BlockSpec(memory_space=pltpu.VMEM)] * len(args),
+        out_specs=[pl.BlockSpec(memory_space=pltpu.VMEM)] * len(outs),
+        compiler_params=pltpu.CompilerParams(vmem_limit_bytes=VMEM_BYTES),
+        cost_estimate=pl.CostEstimate(flops=flops, bytes_accessed=nbytes, transcendentals=0),
+    )(bits, *args)
+
+
 def leaf_body(bits, rhs, inverse, own_rows, other_rows, state, own, other, sums):
     rank = own.shape[1]
     rounded = dot(rhs[...], inverse[...]).astype(jnp.bfloat16)
@@ -123,7 +143,7 @@
             pl.BlockSpec((None, rank, width), lambda j, bits: (0, bits[0], j)),
             pl.BlockSpec((None, rank, width), lambda j, bits: (0, 1 - bits[0], j)),
         ],
-        [bf16(rows, leaf), f32(rows, rank), f32(rows, rank)],
+        [vmem(rows, leaf, dtype=jnp.bfloat16), vmem(rows, rank), vmem(rows, rank)],
         [columns(rows, width), whole((rows, rank)), whole((rows, rank))],
         [pltpu.VMEM((rows, 2 * rank), jnp.float32)],
         2 * rows * leaf * (leaf + 2 * rank),
@@ -131,46 +151,28 @@
     )
 
 
-PAIRS = ((2, 3), (4, 5), (6, 7), (6, 8), (7, 8))
-
-
-def project_body(levels, bits, state, up, proj, value, gram, kept):
+def project_body(heights, depth, pairs, bits, state, up, proj, value, gram, *kept):
     rank = up.shape[1]
-    value[...] = dot_t(state[...], proj[...])
-    for h in range(2, levels + 1):
-
-        @pl.when(pl.program_id(0) == h - 2)
-        def _(h=h):
-            depth = (h - 1) * rank
-            full = dot_t(up[: h - 1].reshape(depth, up.shape[2]), proj[...])
-            gram[:depth, :] = full.astype(jnp.bfloat16)
-            for i, (k, of) in enumerate(PAIRS):
-                if of == h:
-                    kept[i] = full[(k - 1) * rank : k * rank]
-
-
-def project(bits, state, up_basis, projection):
+    for i, h in enumerate(heights):
+        rows = proj[h - 1]
+        value[i] = dot_t(state[...], rows)
+        gram[i] = dot_t(up[:depth].reshape(depth * rank, up.shape[2]), rows).astype(jnp.bfloat16)
+        for j, (k, of) in enumerate(pairs):
+            if of == h:
+                kept[0][j] = dot_t(up[k - 1], rows)
+
+
+def project(heights, pairs, bits, state, up_basis, projection):
     rows, leaf = state.shape
-    levels, rank = up_basis.shape[:2]
-    wide, count = 2 * rank, levels - 1
-    return run(
-        functools.partial(project_body, levels),
-        count,
+    rank = up_basis.shape[1]
+    wide, count, depth = 2 * rank, len(heights), heights[0] - 1
+    return local(
+        functools.partial(project_body, heights, depth, pairs),
         bits,
         [state, up_basis, projection],
-        [
-            whole((rows, leaf)),
-            whole((count, rank, leaf)),
-            pl.BlockSpec((None, wide, leaf), lambda j, bits: (j + 1, 0, 0)),
-        ],
-        [f32(count, rows, wide), bf16(count, count * rank, wide), f32(len(PAIRS), rank, wide)],
-        [
-            pl.BlockSpec((None, rows, wide), lambda j, bits: (j, 0, 0)),
-            pl.BlockSpec((None, count * rank, wide), lambda j, bits: (j, 0, 0)),
-            whole((len(PAIRS), rank, wide)),
-        ],
-        [],
-        2 * leaf * wide * (count * rows + rank * count * (count + 1) // 2),
+        [vmem(count, rows, wide), vmem(count, depth * rank, wide, dtype=jnp.bfloat16)]
+        + ([vmem(len(pairs), rank, wide)] if pairs else []),
+        2 * leaf * wide * (count * (rows + rank * depth) + rank * len(pairs)),
         2 * leaf * (rows + count * 3 * rank),
     )
 
@@ -195,15 +197,11 @@
 def second(bits, mine, received, value, gram):
     rows, rank = mine.shape
     wide = 2 * rank
-    return run(
+    return local(
         second_body,
-        1,
         bits,
         [mine, received, value, gram],
-        [whole(mine.shape)] * 2 + [block((2, rows, wide), 0, 0, 0), block((2, rank, wide), 0, 0, 0)],
-        [f32(rows // 2, 2 * wide)] * 2 + [bf16(rows, rank)],
-        [whole((rows // 2, 2 * wide))] * 2 + [whole((rows, rank))],
-        [],
+        [vmem(rows // 2, 2 * wide)] * 2 + [vmem(rows, rank, dtype=jnp.bfloat16)],
         4 * rows * rank * wide,
         16 * rows * wide,
     )
@@ -239,17 +237,11 @@
     rows, rank = c1.shape
     wide = 2 * rank
     total = 4 * rows // parts + 2 * low.shape[0] + high.shape[0] // parts
-    return run(
+    return local(
         fourth_body,
-        1,
         bits,
         [c1, mine, received, value, gram, low, high],
-        [whole(c1.shape), whole(mine.shape), whole(received.shape)]
-        + [block((2, rows, wide), 1, 0, 0), block((2, 3 * rank, wide), 1, 0, 0)]
-        + [whole(low.shape), whole(high.shape)],
-        [f32(parts, total, rank), bf16(rows, wide)],
-        [whole((parts, total, rank)), whole((rows, wide))],
-        [],
+        [vmem(parts, total, rank), vmem(rows, wide, dtype=jnp.bfloat16)],
         12 * rows * rank * wide,
         16 * rows * wide,
     )
@@ -279,15 +271,11 @@
     parts, total, rank = packed.shape
     rest = total - 4 * share - 2 * rank // parts
     shapes = [(share, rank), (share, rank), (share, 2 * rank), (rank, 2 * rank), (rest, rank)]
-    return run(
+    return local(
         functools.partial(gather_body, places),
-        1,
         bits,
         [packed],
-        [whole(packed.shape)],
-        [f32(*s) for s in shapes],
-        [whole(s) for s in shapes],
-        [],
+        [vmem(*s) for s in shapes],
         parts * total * rank,
         4 * parts * total * rank,
     )
@@ -301,67 +289,95 @@
             packed[:, j * share : (j + 1) * share, :].reshape(c1.shape).astype(jnp.bfloat16)
         )
     lhs = jnp.concatenate([c1[...], c23[...], coef[...]], axis=1)
-    emit_halves(bits[1], [value[i] - dot(lhs, gram[i, : lhs.shape[1], :]) for i in range(3)], keep, send)
+    emit_halves(bits[1], [value[i] - dot(lhs, gram[i]) for i in range(3)], keep, send)
 
 
 def sixth(bits, c1, c23, packed, value, gram):
     rows, rank = c1.shape
     wide = 2 * rank
-    value, gram = value[4:], gram[4:]
-    return run(
+    return local(
         sixth_body,
-        1,
         bits,
         [c1, c23, packed, value, gram],
-        [whole(c1.shape), whole(c23.shape), whole(packed.shape), whole(value.shape), whole(gram.shape)],
-        [f32(rows // 2, 3 * wide)] * 2 + [bf16(rows, wide)],
-        [whole((rows // 2, 3 * wide))] * 2 + [whole((rows, wide))],
-        [],
+        [vmem(rows // 2, 3 * wide)] * 2 + [vmem(rows, wide, dtype=jnp.bfloat16)],
         30 * rows * rank * wide,
         24 * rows * wide,
     )
 
 
-def last_body(bits, state, c1, c23, c45, mine, received, up, out, coef):
-    rank, count = c1.shape[1], mine.shape[0]
+def add_body(bits, left, right, out):
+    out[...] = left[...] + right[...]
+
+
+def add(bits, left, right):
+    return local(add_body, bits, [left, right], [vmem(*left.shape)], left.size, 12 * left.size)[0]
+
+
+def total_body(bits, parts, out):
+    out[...] = parts[...].sum(axis=0)
+
+
+def total(bits, parts):
+    return local(total_body, bits, [parts], [vmem(*parts.shape[1:])], parts.size, 4 * parts.size)[0]
+
+
+def lower_body(bits, state, c1, c23, c45, up, out):
+    coef = jnp.concatenate([c1[...], c23[...], c45[...]], axis=1)
+    depth, leaf = coef.shape[1], state.shape[1]
+    width = leaf // STEPS
+    for i in range(STEPS):
+        here = slice(i * width, (i + 1) * width)
+        basis = up[: depth // c1.shape[1], :, here].reshape(depth, width)
+        out[:, here] = state[:, here].astype(jnp.float32) - dot(coef, basis)
+
+
+def lower(bits, state, c1, c23, c45, up_basis):
+    rows, leaf = state.shape
+    return local(
+        lower_body,
+        bits,
+        [state, c1, c23, c45, up_basis],
+        [vmem(rows, leaf)],
+        10 * rows * leaf * c1.shape[1],
+        6 * rows * leaf,
+    )[0]
+
+
+def last_body(bits, state, mine, received, up6, up7, up8, out, coef):
+    rank, count = up6.shape[0], mine.shape[0]
 
     @pl.when(pl.program_id(0) == 0)
     def _():
-        coef[:, :rank] = c1[...]
-        coef[:, rank : 3 * rank] = c23[...]
-        coef[:, 3 * rank : 5 * rank] = c45[...]
         for bit in range(2):
 
             @pl.when(bits[1] == bit)
             def _(bit=bit):
                 here = slice(bit * count, (bit + 1) * count)
                 there = slice((1 - bit) * count, (2 - bit) * count)
-                coef[here, 5 * rank :] = mine[:, : 3 * rank].astype(jnp.bfloat16)
-                coef[there, 5 * rank : 6 * rank] = received[:, 2 * rank :].astype(jnp.bfloat16)
-                coef[there, 6 * rank :] = received[:, : 2 * rank].astype(jnp.bfloat16)
-
-    basis = up[...].reshape(coef.shape[1], up.shape[2])
-    out[...] = state[...].astype(jnp.float32) - dot(coef[...], basis)
-
-
-def last(bits, state, c1, c23, c45, mine, received, up_basis):
+                coef[here, :] = mine[:, : 3 * rank].astype(jnp.bfloat16)
+                coef[there, :rank] = received[:, 2 * rank :].astype(jnp.bfloat16)
+                coef[there, rank:] = received[:, : 2 * rank].astype(jnp.bfloat16)
+
+    basis = jnp.concatenate([up6[...], up7[...], up8[...]], axis=0)
+    out[...] = state[...] - dot(coef[...], basis)
+
+
+def last(bits, state, mine, received, up_basis):
     rows, leaf = state.shape
     levels, rank = up_basis.shape[:2]
     width = leaf // STEPS
-    coefs = [c1, c23, c45, mine, received]
     return run(
         last_body,
         STEPS,
         bits,
-        [state, *coefs, up_basis],
-        [columns(rows, width)]
-        + [whole(c.shape) for c in coefs]
-        + [pl.BlockSpec((levels, rank, width), lambda j, bits: (0, 0, j))],
+        [state, mine, received] + [hbm(up_basis)] * 3,
+        [columns(rows, width), whole(mine.shape), whole(received.shape)]
+        + [pl.BlockSpec((None, rank, width), lambda j, bits, k=k: (k - 1, 0, j)) for k in (6, 7, 8)],
         f32(rows, leaf),
         columns(rows, width),
-        [pltpu.VMEM((rows, levels * rank), jnp.bfloat16)],
-        2 * rows * leaf * levels * rank,
-        6 * rows * leaf + 2 * leaf * levels * rank,
+        [pltpu.VMEM((rows, 3 * rank), jnp.bfloat16)],
+        6 * rows * leaf * rank,
+        6 * rows * leaf,
     )
 
 
@@ -378,67 +394,86 @@
     over_y = functools.partial(swap, axis="gy", size=size_y)
     ring = len(groups_z[0])
     share = rows // ring
+    by_z0, by_z12, by_z2 = starts(z0, rank // 2), starts(z1 ^ z2, rank // 4), starts(z2, rank // 8)
+    by_y01, by_y1 = starts(y0 ^ y1, 3 * rank // 2), starts(y1, 3 * rank // 4)
+    half_z1, half_z2, half_y1 = starts(z1, rank), starts(z2, rank), starts(y1, rank)
+    half_core, half_x0, half_x1 = starts(core, rank), starts(x0, rank), starts(x1, rank)
+    indices = (
+        bits, by_z0, by_z12, by_z2, by_y01, by_y1, half_z1, half_z2, half_y1,
+        half_core, half_x0, half_x1, y1 == 0, (y0 ^ y1) == 0,
+    )
+    indices, rhs = lax.optimization_barrier((indices, rhs))
+    (
+        bits, by_z0, by_z12, by_z2, by_y01, by_y1, half_z1, half_z2, half_y1,
+        half_core, half_x0, half_x1, first_y1, first_y01,
+    ) = indices
 
     state, own, other = leaf_solve(bits, rhs, leaf_inverse, projection)
     received = over_x(other, mask=1)
-    value, gram, kept = project(bits, state, up_basis, projection)
+    value, gram, kept = project((2, 3), ((2, 3),), bits, state, up_basis, projection)
+    value_45, gram_45, kept_45 = project((4, 5), ((4, 5),), bits, state, up_basis, projection)
 
     keep, send, c1 = second(bits, own, received, value, gram)
+    send, later = lax.optimization_barrier((send, state))
     received = over_x(send, mask=1)
-    low, low_send = split(kept[1], z0)
+    value_678, gram_678, kept_678 = project((6, 7, 8), ((6, 7), (6, 8), (7, 8)), bits, later, up_basis, projection)
+    low, low_send = split(kept_45[0], by_z0)
     both = over_x(jnp.concatenate([kept[0], low_send]), mask=1)
     gram_23 = (kept[0] + both[:rank]).astype(jnp.bfloat16)
-    low, low_send = split(low + both[rank:], z1 ^ z2)
-    low, low_send = split(low + over_x(low_send, mask=2), z2)
+    low, low_send = split(low + both[rank:], by_z12)
+    low, low_send = split(low + over_x(low_send, mask=2), by_z2)
     low = low + over_x(low_send, mask=6)
     places = [(i & 1) * 4 + (i >> 1 & 1 ^ i >> 2) * 2 + (i >> 2) for i in range(ring)]
-    high, high_send = split(kept[2:].reshape(3 * rank, wide), y0 ^ y1)
-    high, high_send = split(high + over_x(high_send, mask=8), y1)
+    high, high_send = split(kept_678.reshape(3 * rank, wide), by_y01)
+    high, high_send = split(high + over_x(high_send, mask=8), by_y1)
     high = high + over_x(high_send, mask=24)
     high = jnp.concatenate([high[:, :rank], high[:, rank:]])
 
     left = keep + received
-    c2 = half(left[:, :wide], z1, rank) + over_x(half(left[:, :wide], 1 - z1, rank), mask=2)
+    c2 = half(left[:, :wide], half_z1[0]) + over_x(half(left[:, :wide], half_z1[1]), mask=2)
     left = left[:, wide:] - dot(c2.astype(jnp.bfloat16), gram_23)
-    c3 = half(left, z2, rank) + over_x(half(left, 1 - z2, rank), mask=6)
+    c3 = half(left, half_z2[0]) + over_x(half(left, half_z2[1]), mask=6)
     c3 = c3 + over_x(c3, mask=2)
     mine = jnp.concatenate([c2, c3], axis=1)
     received = over_x(mine, mask=1)
 
-    packed, c23 = fourth(bits, c1, mine, received, value, gram, low, high, ring)
+    packed, c23 = fourth(bits, c1, mine, received, value_45, gram_45, low, high, ring)
     packed = exchange(packed, groups_z)
     own, other, left, gram_45, high = gather_rows(bits, packed, places, share)
     c4 = own + over_x(other, mask=8)
     left = left - dot(c4, gram_45)
-    c5 = half(left, y1, rank) + over_x(half(left, 1 - y1, rank), mask=24)
+    c5 = half(left, half_y1[0]) + over_x(half(left, half_y1[1]), mask=24)
     c5 = c5 + over_x(c5, mask=8)
     packed = jnp.concatenate([c4, c5, high], axis=0)
     packed = exchange(jnp.broadcast_to(packed, (ring, *packed.shape)), groups_z)
 
-    keep, send, c45 = sixth(bits, c1, c23, packed, value, gram)
-    left = keep + over_y(send, mask=1)
+    keep, send, c45 = sixth(bits, c1, c23, packed, value_678, gram_678)
+    left = add(bits, keep, over_y(send, mask=1))
     high = packed[:, 2 * share :].reshape(2, 3 * wide // ring, rank)
     high = jnp.concatenate([high[0], high[1]], axis=1)
-    high = join(high, over_x(high, mask=24), y1)
-    high = join(high, over_x(high, mask=8), y0 ^ y1)
+    high = join(high, over_x(high, mask=24), first_y1)
+    high = join(high, over_x(high, mask=8), first_y01)
     high_there = over_y(high, mask=1)
     left, high, high_there = lax.optimization_barrier((left, high, high_there))
     half_rows = rows // 2
     count = half_rows // size_x
-    left = exchange(left.reshape(size_x, count, 3 * wide), groups_zy).sum(axis=0)
+    left = total(bits, exchange(left.reshape(size_x, count, 3 * wide), groups_zy))
+    left, c45 = lax.optimization_barrier((left, c45))
     high, high_there = high.reshape(3, rank, wide), high_there.reshape(3, rank, wide)
-    c6, c6_there = half(left[:, :wide], core, rank), half(left[:, :wide], 1 - core, rank)
+    c6, c6_there = half(left[:, :wide], half_core[0]), half(left[:, :wide], half_core[1])
     z7 = left[:, wide : 2 * wide] - exact_dot(c6, high[0]) - exact_dot(c6_there, high_there[0])
     z8 = left[:, 2 * wide :] - exact_dot(c6, high[1]) - exact_dot(c6_there, high_there[1])
-    c7 = half(z7, x0, rank) + over_y(half(z7, 1 - x0, rank), mask=2)
+    c7 = half(z7, half_x0[0]) + over_y(half(z7, half_x0[1]), mask=2)
     z8 = z8 - exact_dot(c7, high[2] + high_there[2])
-    c8 = half(z8, x1, rank) + over_y(half(z8, 1 - x1, rank), mask=6)
+    c8 = half(z8, half_x1[0]) + over_y(half(z8, half_x1[1]), mask=6)
     c8 = c8 + over_y(c8, mask=2)
+    state = lower(bits, state, c1, c23, c45, up_basis)
     packed = jnp.concatenate([c6, c7, c8, c6_there], axis=1)
+    packed, state = lax.optimization_barrier((packed, state))
     packed = exchange(jnp.broadcast_to(packed, (size_x, *packed.shape)), groups_zy)
     packed = packed.reshape(half_rows, 4 * rank)
     received = over_y(packed[:, rank:], mask=1)
-    return last(bits, state, c1, c23, c45, packed, received, up_basis)
+    return last(bits, state, packed, received, up_basis)
 
 
 def solution(mesh):

time: 244 us -> 217 us (0.89)
  blocking collectives: 66.2 us -> 89.1 us
  waiting for transfers between devices: 58.8 us -> 42.2 us
  Pallas kernels: 39.3 us -> 23.6 us
  local copies, waits for them, and re-layouts: 9.69 us -> 0.8 us
  other arithmetic: 7.73 us -> 0.82 us
    pallas_call x7 -> x2, Pallas kernels: 39.3 us -> 10.3 us  [run(): pl.pallas_call(body, out_shape=out_shape, grid_spec=pltpu.PrefetchScalarG...]
    all_to_all x3 -> x4, blocking collectives: 66.2 us -> 89.1 us  [exchange(): lax.all_to_all(value, AXES, 0, 0, tiled=True, axis_index_groups=groups)]
    all_to_all x1 -> x0, waiting for transfers between devices: 21.6 us -> none  [exchange(): lax.all_to_all(value, AXES, 0, 0, tiled=True, axis_index_groups=groups)]
    pallas_call x0 -> x10, Pallas kernels: none -> 13.3 us  [local(): pl.pallas_call(body, out_shape=outs, in_specs=[pl.BlockSpec(memory_space=...]
    slice x3 -> x0, local copies, waits for them, and re-layouts: 6.21 us -> none  [the longest x2 5.19 us: sixth(): value, gram = (value[4:], gram[4:])]
    ppermute x22, waiting for transfers between devices: 37.2 us -> 42.2 us  [swap(): lax.ppermute(value, axis, [(source, source ^ mask) for source in range(si...]
    ppermute x22, starting transfers between devices: 54 us -> 58.1 us  [swap(): lax.ppermute(value, axis, [(source, source ^ mask) for source in range(si...]
    all_to_all x1 -> x0, starting transfers between devices: 3.91 us -> none  [exchange(): lax.all_to_all(value, AXES, 0, 0, tiled=True, axis_index_groups=groups)]
  transfers between devices with their start and end apart: 23 -> 22, of which waited for: 13 -> 17; matrix products, arithmetic and copies ran while one was open for 5% -> 0% of each run, Pallas kernels for 8% -> 3%
where the time goes in v3:
time: 217 us; the launch traced here: 216 us
  blocking collectives  89.1 us (41%)
  starting transfers between devices  58.1 us (27%)
  waiting for transfers between devices  42.2 us (19%)
  Pallas kernels  23.6 us (11%)
    all_to_all x4, blocking collectives, exchange(): lax.all_to_all(value, AXES, 0, 0, tiled=True, axis_index_groups=groups)  89.1 us
    ppermute x22, starting transfers between devices, swap(): lax.ppermute(value, axis, [(source, source ^ mask) for source in range(si...  58.1 us
    ppermute x22, waiting for transfers between devices, swap(): lax.ppermute(value, axis, [(source, source ^ mask) for source in range(si...  42.2 us
    pallas_call x10, Pallas kernels, local(): pl.pallas_call(body, out_shape=outs, in_specs=[pl.BlockSpec(memory_space=...  13.3 us
    pallas_call x2, Pallas kernels, run(): pl.pallas_call(body, out_shape=out_shape, grid_spec=pltpu.PrefetchScalarG...  10.3 us
  transfers between devices with their start and end apart: 22, of which 17 were waited for; matrix products, arithmetic and copies ran while one was open for 0% of the time, Pallas kernels for 3%

profile of v3, /device:TPU:1, one launch (start us, length us, event | category | flops | bytes accessed | tf_op | source)
XLA Modules:
  0.0 216.1 jit_solution(12798553708892238332)
XLA Ops:
  0.1 5.6 %shard_map.46 = (bf16[512,1024]{1,0:T(8,128)(2,1)S(1)}, f32[512,128]{1,0:T(8,128)S(1)}, f32[512,128]{1,0:T(8,128)S(1)}) custom-call(s32[3]{0:T(128)S(1)} %pad_add_fusion.bits, bf16[512,1024]{1,0:T(8,128)(2,1)} %rhs, bf16[1,1024,1024]{2,1,0:T(8,128)(2,1)} %inverse.1, bf16[8,256,1024]{2,1,0:T(8,128)(2,1)} %proj.5, bf16[8,256,1024]{2,1,0:T(8,128)(2,1)} %proj.5), custom_call_target="tpu_custom_call" | custom-call | flops 1342177280 | bytes 4194304 | tf_op jit(solution)/shard_map/pallas_call | solution.py:69
  5.7 1.7 shard_map.47
  7.5 1.9 shard_map.49
  9.4 2.6 %collective-permute-start.3 = (f32[192,256]{1,0:T(8,128)S(1)}, f32[192,256]{1,0:T(8,128)S(1)}, u32[]{:S(2)}, u32[]{:S(2)}) collective-permute-start(f32[192,256]{1,0:T(8,128)S(1)} %pad_maximum_fusion.1), channel_id=1, source_target_pairs={{0,8},{8,0},{16,24},{24,16},{32,40},{40,32},{48,56},{56,48},{64,72... | collective-permute-start | bytes 589832 | tf_op jit(solution)/shard_map/ppermute | solution.py:28
  12.0 3.5 %collective-permute-done.3 = f32[192,256]{1,0:T(8,128)S(1)} collective-permute-done((f32[192,256]{1,0:T(8,128)S(1)}, f32[192,256]{1,0:T(8,128)S(1)}, u32[]{:S(2)}, u32[]{:S(2)}) %collective-permute-start.3) | collective-permute-done | bytes 196640 | tf_op jit(solution)/shard_map/ppermute | solution.py:28
  15.5 4.0 %collective-permute-start.7 = (f32[32,256]{1,0:T(8,128)S(1)}, f32[32,256]{1,0:T(8,128)S(1)}, u32[]{:S(2)}, u32[]{:S(2)}) collective-permute-start(f32[32,256]{1,0:T(8,128)S(1)} %constant_dynamic-slice_fusion.10), channel_id=1, source_target_pairs={{0,16},{8,24},{16,0},{24,8},{32,48},{40,56},{48,32},{56,40},{64,80... | collective-permute-start | bytes 98312 | tf_op jit(solution)/shard_map/ppermute | solution.py:28
  19.6 1.6 collective-permute-done.received
  22.0 2.3 %collective-permute-start.1 = (f32[256,512]{1,0:T(8,128)S(1)}, f32[256,512]{1,0:T(8,128)S(1)}, u32[]{:S(2)}, u32[]{:S(2)}) collective-permute-start(f32[256,512]{1,0:T(8,128)S(1)} %get-tuple-element.75), channel_id=1, source_target_pairs={{0,8},{8,0},{16,24},{24,16},{32,40},{40,32},{48,56},{56,48},{64,72... | collective-permute-start | bytes 1572872 | tf_op jit(solution)/shard_map/ppermute | solution.py:28
  24.3 5.6 %collective-permute-start.8 = (f32[16,256]{1,0:T(8,128)S(1)}, f32[16,256]{1,0:T(8,128)S(1)}, u32[]{:S(2)}, u32[]{:S(2)}) collective-permute-start(f32[16,256]{1,0:T(8,128)S(1)} %constant_dynamic-slice_fusion.9), channel_id=1, source_target_pairs={{0,48},{8,56},{16,32},{24,40},{32,16},{40,24},{48,0},{56,8},{64,11... | collective-permute-start | bytes 49160 | tf_op jit(solution)/shard_map/ppermute | solution.py:28
  29.9 10.2 %collective-permute-done.8 = f32[16,256]{1,0:T(8,128)S(1)} collective-permute-done((f32[16,256]{1,0:T(8,128)S(1)}, f32[16,256]{1,0:T(8,128)S(1)}, u32[]{:S(2)}, u32[]{:S(2)}) %collective-permute-start.8) | collective-permute-done | bytes 16416 | tf_op jit(solution)/shard_map/ppermute | solution.py:28
  40.4 3.0 %shard_map.50 = (f32[3,512,256]{2,1,0:T(8,128)S(1)}, bf16[3,640,256]{2,1,0:T(8,128)(2,1)S(1)}, f32[3,128,256]{2,1,0:T(8,128)S(1)}) custom-call(s32[3]{0:T(128)S(1)} %pad_add_fusion.bits, bf16[512,1024]{1,0:T(8,128)(2,1)S(1)} %get-tuple-element.90.state, bf16[8,128,1024]{2,1,0:T(8,128)(2,1)S(1)} %copy-done, bf16[8,256,1024]{2,1,0:T(8,128)(2,1)S(1)} %copy-done.1), custom_call_target="tpu_custom_call" | custom-call | flops 2013265920 | bytes 3407872 | tf_op jit(solution)/shard_map/pallas_call | solution.py:100
  48.4 2.8 %collective-permute-start.10 = (f32[96,256]{1,0:T(8,128)S(1)}, f32[96,256]{1,0:T(8,128)S(1)}, u32[]{:S(2)}, u32[]{:S(2)}) collective-permute-start(f32[96,256]{1,0:T(8,128)S(1)} %constant_dynamic-slice_fusion.7), channel_id=1, source_target_pairs={{0,192},{8,200},{16,208},{24,216},{32,224},{40,232},{48,240},{56,2... | collective-permute-start | bytes 294920 | tf_op jit(solution)/shard_map/ppermute | solution.py:28
  52.4 2.8 %collective-permute-start.5 = (f32[256,128]{1,0:T(8,128)S(1)}, f32[256,128]{1,0:T(8,128)S(1)}, u32[]{:S(2)}, u32[]{:S(2)}) collective-permute-start(f32[256,128]{1,0:T(8,128)S(1)} %dynamic-slice_add_fusion.1), channel_id=1, source_target_pairs={{0,16},{8,24},{16,0},{24,8},{32,48},{40,56},{48,32},{56,40},{64,80... | collective-permute-start | bytes 393224 | tf_op jit(solution)/shard_map/ppermute | solution.py:28
  55.2 2.6 %collective-permute-done.5 = f32[256,128]{1,0:T(8,128)S(1)} collective-permute-done((f32[256,128]{1,0:T(8,128)S(1)}, f32[256,128]{1,0:T(8,128)S(1)}, u32[]{:S(2)}, u32[]{:S(2)}) %collective-permute-start.5) | collective-permute-done | bytes 131104 | tf_op jit(solution)/shard_map/ppermute | solution.py:28
  57.9 2.4 %collective-permute-start.6 = (f32[256,256]{1,0:T(8,128)S(1)}, f32[256,256]{1,0:T(8,128)S(1)}, u32[]{:S(2)}, u32[]{:S(2)}) collective-permute-start(f32[256,256]{1,0:T(8,128)S(1)} %pad_maximum_fusion.mine), channel_id=1, source_target_pairs={{0,8},{8,0},{16,24},{24,16},{32,40},{40,32},{48,56},{56,48},{64,72... | collective-permute-start | bytes 786440 | tf_op jit(solution)/shard_map/ppermute | solution.py:28
  60.3 5.1 %collective-permute-done.6.received = f32[256,256]{1,0:T(8,128)S(1)} collective-permute-done((f32[256,256]{1,0:T(8,128)S(1)}, f32[256,256]{1,0:T(8,128)S(1)}, u32[]{:S(2)}, u32[]{:S(2)}) %collective-permute-start.6) | collective-permute-done | bytes 262176 | tf_op jit(solution)/shard_map/ppermute | solution.py:28
  66.4 30.0 %all_to_all.20.packed = f32[8,312,128]{2,1,0:T(8,128)S(1)} all-to-all(f32[8,312,128]{2,1,0:T(8,128)S(1)} %get-tuple-element.97), channel_id=1, replica_groups={{0,8,16,24,32,40,48,56},{64,72,80,88,96,104,112,120},{128,136,144,152,1..., dimensions={0} | all-to-all | bytes 2555904 | tf_op jit(solution)/shard_map/all_to_all | solution.py:32
  97.1 1.9 collective-permute-start.11
  99.0 1.6 collective-permute-done.11
  100.8 2.9 %collective-permute-start.12 = (f32[64,128]{1,0:T(8,128)S(1)}, f32[64,128]{1,0:T(8,128)S(1)}, u32[]{:S(2)}, u32[]{:S(2)}) collective-permute-start(f32[64,128]{1,0:T(8,128)S(1)} %constant_dynamic-slice_fusion.6), channel_id=1, source_target_pairs={{0,192},{8,200},{16,208},{24,216},{32,224},{40,232},{48,240},{56,2... | collective-permute-start | bytes 98312 | tf_op jit(solution)/shard_map/ppermute | solution.py:28
  105.2 2.7 %collective-permute-done.13 = f32[64,128]{1,0:T(8,128)S(1)} collective-permute-done((f32[64,128]{1,0:T(8,128)S(1)}, f32[64,128]{1,0:T(8,128)S(1)}, u32[]{:S(2)}, u32[]{:S(2)}) %collective-permute-start.13) | collective-permute-done | bytes 32800 | tf_op jit(solution)/shard_map/ppermute | solution.py:28
  108.0 16.5 %all_to_all.21.packed = f32[8,152,128]{2,1,0:T(8,128)S(1)} all-to-all(f32[8,152,128]{2,1,0:T(8,128)S(1)} %broadcast_in_dim.6), channel_id=1, replica_groups={{0,8,16,24,32,40,48,56},{64,72,80,88,96,104,112,120},{128,136,144,152,1..., dimensions={0} | all-to-all | bytes 1245184 | tf_op jit(solution)/shard_map/all_to_all | solution.py:32
  124.5 2.8 %collective-permute-start.15 = (f32[96,256]{1,0:T(8,128)S(1)}, f32[96,256]{1,0:T(8,128)S(1)}, u32[]{:S(2)}, u32[]{:S(2)}) collective-permute-start(f32[96,256]{1,0:T(8,128)S(1)} %pad_maximum_fusion.3), channel_id=1, source_target_pairs={{0,192},{8,200},{16,208},{24,216},{32,224},{40,232},{48,240},{56,2... | collective-permute-start | bytes 294920 | tf_op jit(solution)/shard_map/ppermute | solution.py:28
  128.7 11.2 %collective-permute-start.14 = (f32[256,768]{1,0:T(8,128)S(1)}, f32[256,768]{1,0:T(8,128)S(1)}, u32[]{:S(2)}, u32[]{:S(2)}) collective-permute-start(f32[256,768]{1,0:T(8,128)S(1)} %get-tuple-element.108), channel_id=1, source_target_pairs={{0,1},{1,0},{2,3},{3,2},{4,5},{5,4},{6,7},{7,6},{8,9},{9,8},{10,11... | collective-permute-start | bytes 2359304 | tf_op jit(solution)/shard_map/ppermute | solution.py:28
  140.0 4.9 %collective-permute-done.16 = f32[192,256]{1,0:T(8,128)S(1)} collective-permute-done((f32[192,256]{1,0:T(8,128)S(1)}, f32[192,256]{1,0:T(8,128)S(1)}, u32[]{:S(2)}, u32[]{:S(2)}) %collective-permute-start.16) | collective-permute-done | bytes 196640 | tf_op jit(solution)/shard_map/ppermute | solution.py:28
  144.9 2.5 %collective-permute-start.17 = (f32[384,256]{1,0:T(8,128)S(1)}, f32[384,256]{1,0:T(8,128)S(1)}, u32[]{:S(2)}, u32[]{:S(2)}) collective-permute-start(f32[384,256]{1,0:T(8,128)S(1)} %maximum_select_fusion), channel_id=1, source_target_pairs={{0,1},{1,0},{2,3},{3,2},{4,5},{5,4},{6,7},{7,6},{8,9},{9,8},{10,11... | collective-permute-start | bytes 1179656 | tf_op jit(solution)/shard_map/ppermute | solution.py:28
  148.8 22.7 %all_to_all.22.parts = f32[32,8,768]{2,1,0:T(8,128)S(1)} all-to-all(f32[32,8,768]{2,1,0:T(8,128)S(1)} %bitcast.26), channel_id=1, replica_groups={{0,8,16,24,32,40,48,56,64,72,80,88,96,104,112,120,128,136,144,152,160,1..., dimensions={0} | all-to-all | bytes 1572864 | tf_op jit(solution)/shard_map/all_to_all | solution.py:32
  175.8 2.5 %collective-permute-start.19 = (f32[8,128]{1,0:T(8,128)S(1)}, f32[8,128]{1,0:T(8,128)S(1)}, u32[]{:S(2)}, u32[]{:S(2)}) collective-permute-start(f32[8,128]{1,0:T(8,128)S(1)} %constant_dynamic-slice_fusion), channel_id=1, source_target_pairs={{0,6},{1,7},{2,4},{3,5},{4,2},{5,3},{6,0},{7,1},{8,14},{9,15},{10,... | collective-permute-start | bytes 12296 | tf_op jit(solution)/shard_map/ppermute | solution.py:28
  179.6 1.5 shard_map.56.state
  182.1 19.9 %all_to_all.23 = f32[32,8,512]{2,1,0:T(8,128)S(1)} all-to-all(f32[32,8,512]{2,1,0:T(8,128)S(1)} %broadcast_in_dim.7), channel_id=1, replica_groups={{0,8,16,24,32,40,48,56,64,72,80,88,96,104,112,120,128,136,144,152,160,1..., dimensions={0} | all-to-all | bytes 1048576 | tf_op jit(solution)/shard_map/all_to_all | solution.py:32
  202.1 8.0 %collective-permute-start.21 = (f32[256,384]{1,0:T(8,128)S(1)}, f32[256,384]{1,0:T(8,128)S(1)}, u32[]{:S(2)}, u32[]{:S(2)}) collective-permute-start(f32[256,384]{1,0:T(8,128)S(1)} %slice.93), channel_id=1, source_target_pairs={{0,1},{1,0},{2,3},{3,2},{4,5},{5,4},{6,7},{7,6},{8,9},{9,8},{10,11... | collective-permute-start | bytes 1179656 | tf_op jit(solution)/shard_map/ppermute | solution.py:28
  211.5 4.7 %shard_map.57 = f32[512,1024]{1,0:T(8,128)} custom-call(s32[3]{0:T(128)S(1)} %pad_add_fusion.bits, f32[512,1024]{1,0:T(8,128)S(1)} %shard_map.56.state, f32[256,512]{1,0:T(8,128)S(1)} %bitcast.25, f32[256,384]{1,0:T(8,128)S(1)} %collective-permute-done.21.received, bf16[8,128,1024]{2,1,0:T(8,128)(2,1)} %up8.1, bf16[8,128,1024]{2,1,0:T(8,128)(2,1)} %up8.1, ...), custom_call_target="tpu_custom_call" | custom-call | flops 402653184 | bytes 3145728 | tf_op jit(solution)/shard_map/pallas_call | solution.py:69
  (82 shorter events, 22.1 us)
Async XLA Ops:
  0.1 5.6 %copy-start = (bf16[8,128,1024]{2,1,0:T(8,128)(2,1)S(1)}, bf16[8,128,1024]{2,1,0:T(8,128)(2,1)}, u32[]{:S(2)}) copy-start(bf16[8,128,1024]{2,1,0:T(8,128)(2,1)} %up8.1) | copy-start | bytes 6291460
  0.1 5.6 %copy-start.1 = (bf16[8,256,1024]{2,1,0:T(8,128)(2,1)S(1)}, bf16[8,256,1024]{2,1,0:T(8,128)(2,1)}, u32[]{:S(2)}) copy-start(bf16[8,256,1024]{2,1,0:T(8,128)(2,1)} %proj.5) | copy-start | bytes 12582916
  9.4 6.1 %collective-permute-start.3 = (f32[192,256]{1,0:T(8,128)S(1)}, f32[192,256]{1,0:T(8,128)S(1)}, u32[]{:S(2)}, u32[]{:S(2)}) collective-permute-start(f32[192,256]{1,0:T(8,128)S(1)} %pad_maximum_fusion.1), channel_id=1, source_target_pairs={{0,8},{8,0},{16,24},{24,16},{32,40},{40,32},{48,56},{56,48},{64,72... | collective-permute-start | bytes 589832 | tf_op jit(solution)/shard_map/ppermute | solution.py:28
  11.9 9.2 %collective-permute-start = (f32[512,128]{1,0:T(8,128)S(1)}, f32[512,128]{1,0:T(8,128)S(1)}, u32[]{:S(2)}, u32[]{:S(2)}) collective-permute-start(f32[512,128]{1,0:T(8,128)S(1)} %get-tuple-element.68), channel_id=1, source_target_pairs={{0,8},{8,0},{16,24},{24,16},{32,40},{40,32},{48,56},{56,48},{64,72... | collective-permute-start | bytes 786440 | tf_op jit(solution)/shard_map/ppermute | solution.py:28
  15.5 8.8 %collective-permute-start.7 = (f32[32,256]{1,0:T(8,128)S(1)}, f32[32,256]{1,0:T(8,128)S(1)}, u32[]{:S(2)}, u32[]{:S(2)}) collective-permute-start(f32[32,256]{1,0:T(8,128)S(1)} %constant_dynamic-slice_fusion.10), channel_id=1, source_target_pairs={{0,16},{8,24},{16,0},{24,8},{32,48},{40,56},{48,32},{56,40},{64,80... | collective-permute-start | bytes 98312 | tf_op jit(solution)/shard_map/ppermute | solution.py:28
  22.0 18.1 %collective-permute-start.1 = (f32[256,512]{1,0:T(8,128)S(1)}, f32[256,512]{1,0:T(8,128)S(1)}, u32[]{:S(2)}, u32[]{:S(2)}) collective-permute-start(f32[256,512]{1,0:T(8,128)S(1)} %get-tuple-element.75), channel_id=1, source_target_pairs={{0,8},{8,0},{16,24},{24,16},{32,40},{40,32},{48,56},{56,48},{64,72... | collective-permute-start | bytes 1572872 | tf_op jit(solution)/shard_map/ppermute | solution.py:28
  24.3 15.7 %collective-permute-start.8 = (f32[16,256]{1,0:T(8,128)S(1)}, f32[16,256]{1,0:T(8,128)S(1)}, u32[]{:S(2)}, u32[]{:S(2)}) collective-permute-start(f32[16,256]{1,0:T(8,128)S(1)} %constant_dynamic-slice_fusion.9), channel_id=1, source_target_pairs={{0,48},{8,56},{16,32},{24,40},{32,16},{40,24},{48,0},{56,8},{64,11... | collective-permute-start | bytes 49160 | tf_op jit(solution)/shard_map/ppermute | solution.py:28
  40.3 5.4 %collective-permute-start.2 = (f32[256,128]{1,0:T(8,128)S(1)}, f32[256,128]{1,0:T(8,128)S(1)}, u32[]{:S(2)}, u32[]{:S(2)}) collective-permute-start(f32[256,128]{1,0:T(8,128)S(1)} %constant_dynamic-slice_fusion.12), channel_id=1, source_target_pairs={{0,16},{8,24},{16,0},{24,8},{32,48},{40,56},{48,32},{56,40},{64,80... | collective-permute-start | bytes 393224 | tf_op jit(solution)/shard_map/ppermute | solution.py:28
  43.4 4.9 %collective-permute-start.9 = (f32[192,256]{1,0:T(8,128)S(1)}, f32[192,256]{1,0:T(8,128)S(1)}, u32[]{:S(2)}, u32[]{:S(2)}) collective-permute-start(f32[192,256]{1,0:T(8,128)S(1)} %constant_dynamic-slice_fusion.8), channel_id=1, source_target_pairs={{0,64},{8,72},{16,80},{24,88},{32,96},{40,104},{48,112},{56,120},{... | collective-permute-start | bytes 589832 | tf_op jit(solution)/shard_map/ppermute | solution.py:28
  46.1 6.1 %collective-permute-start.4 = (f32[256,128]{1,0:T(8,128)S(1)}, f32[256,128]{1,0:T(8,128)S(1)}, u32[]{:S(2)}, u32[]{:S(2)}) collective-permute-start(f32[256,128]{1,0:T(8,128)S(1)} %constant_dynamic-slice_fusion.11), channel_id=1, source_target_pairs={{0,48},{8,56},{16,32},{24,40},{32,16},{40,24},{48,0},{56,8},{64,11... | collective-permute-start | bytes 393224 | tf_op jit(solution)/shard_map/ppermute | solution.py:28
  48.4 6.8 %collective-permute-start.10 = (f32[96,256]{1,0:T(8,128)S(1)}, f32[96,256]{1,0:T(8,128)S(1)}, u32[]{:S(2)}, u32[]{:S(2)}) collective-permute-start(f32[96,256]{1,0:T(8,128)S(1)} %constant_dynamic-slice_fusion.7), channel_id=1, source_target_pairs={{0,192},{8,200},{16,208},{24,216},{32,224},{40,232},{48,240},{56,2... | collective-permute-start | bytes 294920 | tf_op jit(solution)/shard_map/ppermute | solution.py:28
  52.4 5.5 %collective-permute-start.5 = (f32[256,128]{1,0:T(8,128)S(1)}, f32[256,128]{1,0:T(8,128)S(1)}, u32[]{:S(2)}, u32[]{:S(2)}) collective-permute-start(f32[256,128]{1,0:T(8,128)S(1)} %dynamic-slice_add_fusion.1), channel_id=1, source_target_pairs={{0,16},{8,24},{16,0},{24,8},{32,48},{40,56},{48,32},{56,40},{64,80... | collective-permute-start | bytes 393224 | tf_op jit(solution)/shard_map/ppermute | solution.py:28
  57.9 7.5 %collective-permute-start.6 = (f32[256,256]{1,0:T(8,128)S(1)}, f32[256,256]{1,0:T(8,128)S(1)}, u32[]{:S(2)}, u32[]{:S(2)}) collective-permute-start(f32[256,256]{1,0:T(8,128)S(1)} %pad_maximum_fusion.mine), channel_id=1, source_target_pairs={{0,8},{8,0},{16,24},{24,16},{32,40},{40,32},{48,56},{56,48},{64,72... | collective-permute-start | bytes 786440 | tf_op jit(solution)/shard_map/ppermute | solution.py:28
  97.1 3.5 %collective-permute-start.11 = (f32[64,128]{1,0:T(8,128)S(1)}, f32[64,128]{1,0:T(8,128)S(1)}, u32[]{:S(2)}, u32[]{:S(2)}) collective-permute-start(f32[64,128]{1,0:T(8,128)S(1)} %get-tuple-element.99), channel_id=1, source_target_pairs={{0,64},{8,72},{16,80},{24,88},{32,96},{40,104},{48,112},{56,120},{... | collective-permute-start | bytes 98312 | tf_op jit(solution)/shard_map/ppermute | solution.py:28
  100.8 4.2 %collective-permute-start.12 = (f32[64,128]{1,0:T(8,128)S(1)}, f32[64,128]{1,0:T(8,128)S(1)}, u32[]{:S(2)}, u32[]{:S(2)}) collective-permute-start(f32[64,128]{1,0:T(8,128)S(1)} %constant_dynamic-slice_fusion.6), channel_id=1, source_target_pairs={{0,192},{8,200},{16,208},{24,216},{32,224},{40,232},{48,240},{56,2... | collective-permute-start | bytes 98312 | tf_op jit(solution)/shard_map/ppermute | solution.py:28
  105.1 2.8 %collective-permute-start.13 = (f32[64,128]{1,0:T(8,128)S(1)}, f32[64,128]{1,0:T(8,128)S(1)}, u32[]{:S(2)}, u32[]{:S(2)}) collective-permute-start(f32[64,128]{1,0:T(8,128)S(1)} %dynamic-slice_add_fusion.4), channel_id=1, source_target_pairs={{0,64},{8,72},{16,80},{24,88},{32,96},{40,104},{48,112},{56,120},{... | collective-permute-start | bytes 98312 | tf_op jit(solution)/shard_map/ppermute | solution.py:28
  124.5 15.4 %collective-permute-start.15 = (f32[96,256]{1,0:T(8,128)S(1)}, f32[96,256]{1,0:T(8,128)S(1)}, u32[]{:S(2)}, u32[]{:S(2)}) collective-permute-start(f32[96,256]{1,0:T(8,128)S(1)} %pad_maximum_fusion.3), channel_id=1, source_target_pairs={{0,192},{8,200},{16,208},{24,216},{32,224},{40,232},{48,240},{56,2... | collective-permute-start | bytes 294920 | tf_op jit(solution)/shard_map/ppermute | solution.py:28
  128.7 18.8 %collective-permute-start.14 = (f32[256,768]{1,0:T(8,128)S(1)}, f32[256,768]{1,0:T(8,128)S(1)}, u32[]{:S(2)}, u32[]{:S(2)}) collective-permute-start(f32[256,768]{1,0:T(8,128)S(1)} %get-tuple-element.108), channel_id=1, source_target_pairs={{0,1},{1,0},{2,3},{3,2},{4,5},{5,4},{6,7},{7,6},{8,9},{9,8},{10,11... | collective-permute-start | bytes 2359304 | tf_op jit(solution)/shard_map/ppermute | solution.py:28
  139.9 5.0 %collective-permute-start.16 = (f32[192,256]{1,0:T(8,128)S(1)}, f32[192,256]{1,0:T(8,128)S(1)}, u32[]{:S(2)}, u32[]{:S(2)}) collective-permute-start(f32[192,256]{1,0:T(8,128)S(1)} %maximum_select_fusion.1), channel_id=1, source_target_pairs={{0,64},{8,72},{16,80},{24,88},{32,96},{40,104},{48,112},{56,120},{... | collective-permute-start | bytes 589832 | tf_op jit(solution)/shard_map/ppermute | solution.py:28
  144.9 3.9 %collective-permute-start.17 = (f32[384,256]{1,0:T(8,128)S(1)}, f32[384,256]{1,0:T(8,128)S(1)}, u32[]{:S(2)}, u32[]{:S(2)}) collective-permute-start(f32[384,256]{1,0:T(8,128)S(1)} %maximum_select_fusion), channel_id=1, source_target_pairs={{0,1},{1,0},{2,3},{3,2},{4,5},{5,4},{6,7},{7,6},{8,9},{9,8},{10,11... | collective-permute-start | bytes 1179656 | tf_op jit(solution)/shard_map/ppermute | solution.py:28
  172.7 2.8 %collective-permute-start.18 = (f32[8,128]{1,0:T(8,128)S(1)}, f32[8,128]{1,0:T(8,128)S(1)}, u32[]{:S(2)}, u32[]{:S(2)}) collective-permute-start(f32[8,128]{1,0:T(8,128)S(1)} %constant_dynamic-slice_fusion.2), channel_id=1, source_target_pairs={{0,2},{1,3},{2,0},{3,1},{4,6},{5,7},{6,4},{7,5},{8,10},{9,11},{10,... | collective-permute-start | bytes 12296 | tf_op jit(solution)/shard_map/ppermute | solution.py:28
  175.8 3.7 %collective-permute-start.19 = (f32[8,128]{1,0:T(8,128)S(1)}, f32[8,128]{1,0:T(8,128)S(1)}, u32[]{:S(2)}, u32[]{:S(2)}) collective-permute-start(f32[8,128]{1,0:T(8,128)S(1)} %constant_dynamic-slice_fusion), channel_id=1, source_target_pairs={{0,6},{1,7},{2,4},{3,5},{4,2},{5,3},{6,0},{7,1},{8,14},{9,15},{10,... | collective-permute-start | bytes 12296 | tf_op jit(solution)/shard_map/ppermute | solution.py:28
  179.6 2.5 %collective-permute-start.20 = (f32[8,128]{1,0:T(8,128)S(1)}, f32[8,128]{1,0:T(8,128)S(1)}, u32[]{:S(2)}, u32[]{:S(2)}) collective-permute-start(f32[8,128]{1,0:T(8,128)S(1)} %fusion.14), channel_id=1, source_target_pairs={{0,2},{1,3},{2,0},{3,1},{4,6},{5,7},{6,4},{7,5},{8,10},{9,11},{10,... | collective-permute-start | bytes 12296 | tf_op jit(solution)/shard_map/ppermute | solution.py:28
  202.1 9.3 %collective-permute-start.21 = (f32[256,384]{1,0:T(8,128)S(1)}, f32[256,384]{1,0:T(8,128)S(1)}, u32[]{:S(2)}, u32[]{:S(2)}) collective-permute-start(f32[256,384]{1,0:T(8,128)S(1)} %slice.93), channel_id=1, source_target_pairs={{0,1},{1,0},{2,3},{3,2},{4,5},{5,4},{6,7},{7,6},{8,9},{9,8},{10,11... | collective-permute-start | bytes 1179656 | tf_op jit(solution)/shard_map/ppermute | solution.py:28

commit v4 on v3

--- a/solution.py
+++ b/solution.py
@@ -178,32 +178,109 @@
 
 
 def emit_halves(which, parts, keep, send):
-    count, wide = keep.shape[0], parts[0].shape[1]
+    count, wide = parts[0].shape[0] // 2, parts[0].shape[1]
     for bit in range(2):
 
         @pl.when(which == bit)
         def _(bit=bit):
             for i, part in enumerate(parts):
-                keep[:, i * wide : (i + 1) * wide] = part[bit * count : (bit + 1) * count]
-                send[:, i * wide : (i + 1) * wide] = part[(1 - bit) * count : (2 - bit) * count]
-
-
-def second_body(bits, mine, received, value, gram, keep, send, coef):
+                keep[:count, i * wide : (i + 1) * wide] = part[bit * count : (bit + 1) * count]
+                send[:count, i * wide : (i + 1) * wide] = part[(1 - bit) * count : (2 - bit) * count]
+
+
+def second_body(bits, mine, received, value, gram, pair, ring, keep, send, coef):
     c1 = (mine[...] + received[...]).astype(jnp.bfloat16)
     coef[...] = c1
+    rows, rank = keep.shape[0] - 3 * pair.shape[1] // 4, mine.shape[1]
+    count, wide = pair.shape[1] // 2, 2 * rank
     emit_halves(bits[0], [value[i] - dot(c1, gram[i]) for i in range(2)], keep, send)
-
-
-def second(bits, mine, received, value, gram):
+    for ref in (keep, send):
+        for j in range(2):
+            ref[rows : rows + count, j * wide : (j + 1) * wide] = pair[0, j * count : (j + 1) * count]
+    for bit in range(2):
+
+        @pl.when(bits[0] == bit)
+        def _(bit=bit):
+            for ref, first in ((keep, bit * count), (send, (1 - bit) * count)):
+                for j in range(2):
+                    start = first + j * count // 2
+                    ref[rows + count :, j * wide : (j + 1) * wide] = ring[0, start : start + count // 2]
+
+
+def second(bits, mine, received, value, gram, pair, ring):
     rows, rank = mine.shape
     wide = 2 * rank
     return local(
         second_body,
         bits,
-        [mine, received, value, gram],
-        [vmem(rows // 2, 2 * wide)] * 2 + [vmem(rows, rank, dtype=jnp.bfloat16)],
+        [mine, received, value, gram, pair, ring],
+        [vmem(rows // 2 + 3 * rank // 4, 2 * wide)] * 2 + [vmem(rows, rank, dtype=jnp.bfloat16)],
         4 * rows * rank * wide,
         16 * rows * wide,
+    )
+
+
+def choose(bit, left, right, keep, send):
+    for b in range(2):
+
+        @pl.when(bit == b)
+        def _(b=b):
+            keep[...] = (left, right)[b]
+            send[...] = (left, right)[1 - b]
+
+
+def stack(value, rank):
+    return jnp.concatenate([value[:, :rank], value[:, rank:]], axis=0)
+
+
+def third_body(bits, keep, received, own, send, low, left, gram):
+    total = keep[...] + received[...]
+    rows, rank = own.shape
+    wide, count = 2 * rank, gram.shape[0] // 2
+    choose(bits[3], total[:rows, :rank], total[:rows, rank:wide], own, send.at[:rows])
+    tail = total[rows + count :]
+    choose(bits[4], stack(tail[:, :wide], rank), stack(tail[:, wide:], rank), low, send.at[rows:])
+    left[...] = total[:rows, wide:]
+    for j in range(2):
+        gram[j * count : (j + 1) * count] = total[rows : rows + count, j * wide : (j + 1) * wide].astype(jnp.bfloat16)
+
+
+def third(bits, keep, received, rank):
+    rows = keep.shape[0] - 3 * rank // 4
+    return local(
+        third_body,
+        bits,
+        [keep, received],
+        [
+            vmem(rows, rank), vmem(rows + rank // 2, rank), vmem(rank // 2, rank),
+            vmem(rows, 2 * rank), vmem(rank, 2 * rank, dtype=jnp.bfloat16),
+        ],
+        keep.size,
+        12 * keep.size,
+    )
+
+
+def correct_body(bits, own, received, low, left, gram, coef, mine, send, kept):
+    rows, rank = own.shape
+    count = low.shape[0] // 4
+    c2 = own[...] + received[:rows]
+    coef[...] = c2
+    rest = left[...] - dot(c2.astype(jnp.bfloat16), gram[...])
+    choose(bits[5], rest[:, :rank], rest[:, rank:], mine, send.at[:rows])
+    total = low[...] + received[rows:]
+    parts = [jnp.concatenate([total[i * count : (i + 1) * count], total[(i + 2) * count : (i + 3) * count]]) for i in range(2)]
+    choose(bits[5], parts[0], parts[1], kept, send.at[rows:])
+
+
+def correct(bits, own, received, low, left, gram):
+    rows, rank = own.shape
+    return local(
+        correct_body,
+        bits,
+        [own, received, low, left, gram],
+        [vmem(rows, rank), vmem(rows, rank), vmem(rows + rank // 4, rank), vmem(rank // 4, rank)],
+        4 * rows * rank * rank,
+        20 * rows * rank,
     )
 
 
@@ -225,18 +302,15 @@
             start = (2 * i + j) * share
             packed[:, start : start + share, :] = left[:, j * rank : (j + 1) * rank].reshape(parts, share, rank)
     start = 4 * share
-    for j in range(2):
-        packed[:, start : start + low.shape[0], :] = jnp.broadcast_to(
-            low[:, j * rank : (j + 1) * rank], (parts, low.shape[0], rank)
-        )
-        start += low.shape[0]
+    packed[:, start : start + low.shape[0], :] = jnp.broadcast_to(low[...], (parts, *low.shape))
+    start += low.shape[0]
     packed[:, start:total, :] = high[...].reshape(parts, total - start, rank)
 
 
 def fourth(bits, c1, mine, received, value, gram, low, high, parts):
     rows, rank = c1.shape
     wide = 2 * rank
-    total = 4 * rows // parts + 2 * low.shape[0] + high.shape[0] // parts
+    total = 4 * rows // parts + low.shape[0] + high.shape[0] // parts
     return local(
         fourth_body,
         bits,
@@ -343,42 +417,49 @@
     )[0]
 
 
-def last_body(bits, state, mine, received, up6, up7, up8, out, coef):
-    rank, count = up6.shape[0], mine.shape[0]
-
-    @pl.when(pl.program_id(0) == 0)
-    def _():
-        for bit in range(2):
-
-            @pl.when(bits[1] == bit)
-            def _(bit=bit):
-                here = slice(bit * count, (bit + 1) * count)
-                there = slice((1 - bit) * count, (2 - bit) * count)
-                coef[here, :] = mine[:, : 3 * rank].astype(jnp.bfloat16)
-                coef[there, :rank] = received[:, 2 * rank :].astype(jnp.bfloat16)
-                coef[there, rank:] = received[:, : 2 * rank].astype(jnp.bfloat16)
-
-    basis = jnp.concatenate([up6[...], up7[...], up8[...]], axis=0)
-    out[...] = state[...] - dot(coef[...], basis)
+def last_body(bits, state, mine, received, up, out, coef, block, done):
+    rank, count = up.shape[1], mine.shape[0]
+    for bit in range(2):
+
+        @pl.when(bits[1] == bit)
+        def _(bit=bit):
+            here = slice(bit * count, (bit + 1) * count)
+            there = slice((1 - bit) * count, (2 - bit) * count)
+            coef[here, :] = mine[:, : 3 * rank].astype(jnp.bfloat16)
+            coef[there, :rank] = received[:, 2 * rank :].astype(jnp.bfloat16)
+            coef[there, rank:] = received[:, : 2 * rank].astype(jnp.bfloat16)
+
+    basis = up[5:8].reshape(3 * rank, up.shape[2])
+    share = state.shape[0] // STEPS
+    copies = []
+    for i in range(STEPS):
+        here = pl.ds(i * share, share)
+        block[here] = state[here] - dot(coef[here], basis)
+        copies.append(pltpu.make_async_copy(block.at[here], out.at[here], done.at[i]))
+        copies[-1].start()
+    for copy in copies:
+        copy.wait()
 
 
 def last(bits, state, mine, received, up_basis):
     rows, leaf = state.shape
-    levels, rank = up_basis.shape[:2]
-    width = leaf // STEPS
-    return run(
+    rank = up_basis.shape[1]
+    args = [pltpu.with_memory_space_constraint(a, pltpu.VMEM) for a in (state, mine, received, up_basis)]
+    return pl.pallas_call(
         last_body,
-        STEPS,
-        bits,
-        [state, mine, received] + [hbm(up_basis)] * 3,
-        [columns(rows, width), whole(mine.shape), whole(received.shape)]
-        + [pl.BlockSpec((None, rank, width), lambda j, bits, k=k: (k - 1, 0, j)) for k in (6, 7, 8)],
-        f32(rows, leaf),
-        columns(rows, width),
-        [pltpu.VMEM((rows, 3 * rank), jnp.bfloat16)],
-        6 * rows * leaf * rank,
-        6 * rows * leaf,
-    )
+        out_shape=f32(rows, leaf),
+        in_specs=[pl.BlockSpec(memory_space=pltpu.SMEM)] + [pl.BlockSpec(memory_space=pltpu.VMEM)] * 4,
+        out_specs=pl.BlockSpec(memory_space=pltpu.HBM),
+        scratch_shapes=[
+            pltpu.VMEM((rows, 3 * rank), jnp.bfloat16),
+            pltpu.VMEM((rows, leaf), jnp.float32),
+            pltpu.SemaphoreType.DMA((STEPS,)),
+        ],
+        compiler_params=pltpu.CompilerParams(vmem_limit_bytes=VMEM_BYTES),
+        cost_estimate=pl.CostEstimate(
+            flops=6 * rows * leaf * rank, bytes_accessed=6 * rows * leaf, transcendentals=0
+        ),
+    )(bits, *args)
 
 
 def shards(groups_z, groups_zy, rhs, leaf_inverse, up_basis, projection):
@@ -389,22 +470,21 @@
     gx, gy = lax.axis_index("gx"), lax.axis_index("gy")
     z0, z1, z2, y0, y1 = (gx >> i & 1 for i in range(5))
     core, x0, x1 = (gy >> i & 1 for i in range(3))
-    bits = jnp.stack([z0, core, y0])
+    bits = jnp.stack([z0, core, y0, z1, z1 ^ z2, z2])
     over_x = functools.partial(swap, axis="gx", size=size_x)
     over_y = functools.partial(swap, axis="gy", size=size_y)
     ring = len(groups_z[0])
     share = rows // ring
-    by_z0, by_z12, by_z2 = starts(z0, rank // 2), starts(z1 ^ z2, rank // 4), starts(z2, rank // 8)
     by_y01, by_y1 = starts(y0 ^ y1, 3 * rank // 2), starts(y1, 3 * rank // 4)
-    half_z1, half_z2, half_y1 = starts(z1, rank), starts(z2, rank), starts(y1, rank)
+    half_y1 = starts(y1, rank)
     half_core, half_x0, half_x1 = starts(core, rank), starts(x0, rank), starts(x1, rank)
     indices = (
-        bits, by_z0, by_z12, by_z2, by_y01, by_y1, half_z1, half_z2, half_y1,
+        bits, by_y01, by_y1, half_y1,
         half_core, half_x0, half_x1, y1 == 0, (y0 ^ y1) == 0,
     )
     indices, rhs = lax.optimization_barrier((indices, rhs))
     (
-        bits, by_z0, by_z12, by_z2, by_y01, by_y1, half_z1, half_z2, half_y1,
+        bits, by_y01, by_y1, half_y1,
         half_core, half_x0, half_x1, first_y1, first_y01,
     ) = indices
 
@@ -413,26 +493,22 @@
     value, gram, kept = project((2, 3), ((2, 3),), bits, state, up_basis, projection)
     value_45, gram_45, kept_45 = project((4, 5), ((4, 5),), bits, state, up_basis, projection)
 
-    keep, send, c1 = second(bits, own, received, value, gram)
-    send, later = lax.optimization_barrier((send, state))
+    value_678, gram_678, kept_678 = project((6, 7, 8), ((6, 7), (6, 8), (7, 8)), bits, state, up_basis, projection)
+    received, kept, kept_45, kept_678 = lax.optimization_barrier((received, kept, kept_45, kept_678))
+
+    keep, send, c1 = second(bits, own, received, value, gram, kept, kept_45)
     received = over_x(send, mask=1)
-    value_678, gram_678, kept_678 = project((6, 7, 8), ((6, 7), (6, 8), (7, 8)), bits, later, up_basis, projection)
-    low, low_send = split(kept_45[0], by_z0)
-    both = over_x(jnp.concatenate([kept[0], low_send]), mask=1)
-    gram_23 = (kept[0] + both[:rank]).astype(jnp.bfloat16)
-    low, low_send = split(low + both[rank:], by_z12)
-    low, low_send = split(low + over_x(low_send, mask=2), by_z2)
-    low = low + over_x(low_send, mask=6)
     places = [(i & 1) * 4 + (i >> 1 & 1 ^ i >> 2) * 2 + (i >> 2) for i in range(ring)]
     high, high_send = split(kept_678.reshape(3 * rank, wide), by_y01)
     high, high_send = split(high + over_x(high_send, mask=8), by_y1)
     high = high + over_x(high_send, mask=24)
     high = jnp.concatenate([high[:, :rank], high[:, rank:]])
 
-    left = keep + received
-    c2 = half(left[:, :wide], half_z1[0]) + over_x(half(left[:, :wide], half_z1[1]), mask=2)
-    left = left[:, wide:] - dot(c2.astype(jnp.bfloat16), gram_23)
-    c3 = half(left, half_z2[0]) + over_x(half(left, half_z2[1]), mask=6)
+    received, high = lax.optimization_barrier((received, high))
+    own, send, low, left, gram_23 = third(bits, keep, received, rank)
+    c2, own, send, low = correct(bits, own, over_x(send, mask=2), low, left, gram_23)
+    received = over_x(send, mask=6)
+    c3, low = own + received[: rows // 2], low + received[rows // 2 :]
     c3 = c3 + over_x(c3, mask=2)
     mine = jnp.concatenate([c2, c3], axis=1)
     received = over_x(mine, mask=1)
@@ -442,17 +518,19 @@
     own, other, left, gram_45, high = gather_rows(bits, packed, places, share)
     c4 = own + over_x(other, mask=8)
     left = left - dot(c4, gram_45)
-    c5 = half(left, half_y1[0]) + over_x(half(left, half_y1[1]), mask=24)
-    c5 = c5 + over_x(c5, mask=8)
+    received = over_x(jnp.concatenate([half(left, half_y1[1]), high]), mask=24)
+    c5 = half(left, half_y1[0]) + received[:share]
+    high = join(high, received[share:], first_y1)
+    received = over_x(jnp.concatenate([c5, high]), mask=8)
+    c5 = c5 + received[:share]
+    high = join(high, received[share:], first_y01)
     packed = jnp.concatenate([c4, c5, high], axis=0)
     packed = exchange(jnp.broadcast_to(packed, (ring, *packed.shape)), groups_z)
 
     keep, send, c45 = sixth(bits, c1, c23, packed, value_678, gram_678)
     left = add(bits, keep, over_y(send, mask=1))
-    high = packed[:, 2 * share :].reshape(2, 3 * wide // ring, rank)
-    high = jnp.concatenate([high[0], high[1]], axis=1)
-    high = join(high, over_x(high, mask=24), first_y1)
-    high = join(high, over_x(high, mask=8), first_y01)
+    high = packed[:, 2 * share :].reshape(2, ring // 2, 4, 3 * rank // (2 * ring), rank)
+    high = jnp.concatenate(list(high.transpose(0, 2, 1, 3, 4).reshape(2, 3 * rank, rank)), axis=1)
     high_there = over_y(high, mask=1)
     left, high, high_there = lax.optimization_barrier((left, high, high_there))
     half_rows = rows // 2

time: 217 us -> 213 us (0.982)
  starting transfers between devices: 58.1 us -> 43.2 us
  blocking collectives: 89.1 us -> 96.2 us
  waiting for transfers between devices: 42.2 us -> 48.2 us
    ppermute x22 -> x17, starting transfers between devices: 58.1 us -> 43.2 us  [swap(): lax.ppermute(value, axis, [(source, source ^ mask) for source in range(si...]
    all_to_all x4, blocking collectives: 89.1 us -> 96.2 us  [exchange(): lax.all_to_all(value, AXES, 0, 0, tiled=True, axis_index_groups=groups)]
    ppermute x22 -> x17, waiting for transfers between devices: 42.2 us -> 48.2 us  [swap(): lax.ppermute(value, axis, [(source, source ^ mask) for source in range(si...]
    pallas_call x2 -> x1, Pallas kernels: 10.3 us -> 5.62 us  [run(): pl.pallas_call(body, out_shape=out_shape, grid_spec=pltpu.PrefetchScalarG...]
    pallas_call x0 -> x1, Pallas kernels: none -> 2.26 us  [last(): pl.pallas_call(last_body, out_shape=f32(rows, leaf), in_specs=[pl.BlockSp...]
    pallas_call x10 -> x12, Pallas kernels: 13.3 us -> 14.7 us  [local(): pl.pallas_call(body, out_shape=outs, in_specs=[pl.BlockSpec(memory_space=...]
  transfers between devices with their start and end apart: 22 -> 17, of which waited for: 17 -> 15; matrix products, arithmetic and copies ran while one was open for 0% -> 0% of each run, Pallas kernels for 3% -> 5%
where the time goes in v4:
time: 213 us
  blocking collectives  96.2 us (45%)
  waiting for transfers between devices  48.2 us (23%)
  starting transfers between devices  43.2 us (20%)
  Pallas kernels  22.6 us (11%)
    all_to_all x4, blocking collectives, exchange(): lax.all_to_all(value, AXES, 0, 0, tiled=True, axis_index_groups=groups)  96.2 us
    ppermute x17, waiting for transfers between devices, swap(): lax.ppermute(value, axis, [(source, source ^ mask) for source in range(si...  48.2 us
    ppermute x17, starting transfers between devices, swap(): lax.ppermute(value, axis, [(source, source ^ mask) for source in range(si...  43.2 us
    pallas_call x12, Pallas kernels, local(): pl.pallas_call(body, out_shape=outs, in_specs=[pl.BlockSpec(memory_space=...  14.7 us
    pallas_call x1, Pallas kernels, run(): pl.pallas_call(body, out_shape=out_shape, grid_spec=pltpu.PrefetchScalarG...  5.62 us
  transfers between devices with their start and end apart: 17, of which 15 were waited for; matrix products, arithmetic and copies ran while one was open for 0% of the time, Pallas kernels for 5%

profile of v4, /device:TPU:1, one launch (start us, length us, event | category | flops | bytes accessed | tf_op | source)
XLA Modules:
  0.0 212.8 jit_solution(126872899912602354)
XLA Ops:
  0.1 5.6 %shard_map.46 = (bf16[512,1024]{1,0:T(8,128)(2,1)S(1)}, f32[512,128]{1,0:T(8,128)S(1)}, f32[512,128]{1,0:T(8,128)S(1)}) custom-call(s32[6]{0:T(128)S(1)} %stack.27.bits, bf16[512,1024]{1,0:T(8,128)(2,1)} %rhs, bf16[1,1024,1024]{2,1,0:T(8,128)(2,1)} %inverse.1, bf16[8,256,1024]{2,1,0:T(8,128)(2,1)} %proj.5, bf16[8,256,1024]{2,1,0:T(8,128)(2,1)} %proj.5), custom_call_target="tpu_custom_call" | custom-call | flops 1342177280 | bytes 4194304 | tf_op jit(solution)/shard_map/pallas_call | solution.py:69
  5.7 2.6 %collective-permute-start = (f32[512,128]{1,0:T(8,128)S(1)}, f32[512,128]{1,0:T(8,128)S(1)}, u32[]{:S(2)}, u32[]{:S(2)}) collective-permute-start(f32[512,128]{1,0:T(8,128)S(1)} %get-tuple-element.71), channel_id=1, source_target_pairs={{0,8},{8,0},{16,24},{24,16},{32,40},{40,32},{48,56},{56,48},{64,72... | collective-permute-start | bytes 786440 | tf_op jit(solution)/shard_map/ppermute | solution.py:28
  8.3 1.9 shard_map.48
  10.1 1.7 shard_map.47
  11.9 3.0 %shard_map.49 = (f32[3,512,256]{2,1,0:T(8,128)S(1)}, bf16[3,640,256]{2,1,0:T(8,128)(2,1)S(1)}, f32[3,128,256]{2,1,0:T(8,128)S(1)}) custom-call(s32[6]{0:T(128)S(1)} %stack.27.bits, bf16[512,1024]{1,0:T(8,128)(2,1)S(1)} %get-tuple-element.72.state, bf16[8,128,1024]{2,1,0:T(8,128)(2,1)S(1)} %copy-done.1, bf16[8,256,1024]{2,1,0:T(8,128)(2,1)S(1)} %copy-done), custom_call_target="tpu_custom_call" | custom-call | flops 2013265920 | bytes 3407872 | tf_op jit(solution)/shard_map/pallas_call | solution.py:100
  17.9 2.6 %collective-permute-done.2 = f32[192,256]{1,0:T(8,128)S(1)} collective-permute-done((f32[192,256]{1,0:T(8,128)S(1)}, f32[192,256]{1,0:T(8,128)S(1)}, u32[]{:S(2)}, u32[]{:S(2)}) %collective-permute-start.2) | collective-permute-done | bytes 196640 | tf_op jit(solution)/shard_map/ppermute | solution.py:28
  20.5 2.8 %collective-permute-start.3 = (f32[96,256]{1,0:T(8,128)S(1)}, f32[96,256]{1,0:T(8,128)S(1)}, u32[]{:S(2)}, u32[]{:S(2)}) collective-permute-start(f32[96,256]{1,0:T(8,128)S(1)} %constant_dynamic-slice_fusion.5), channel_id=1, source_target_pairs={{0,192},{8,200},{16,208},{24,216},{32,224},{40,232},{48,240},{56,2... | collective-permute-start | bytes 294920 | tf_op jit(solution)/shard_map/ppermute | solution.py:28
  23.3 2.0 collective-permute-done.3
  25.4 8.3 %collective-permute-done.1.received = f32[352,512]{1,0:T(8,128)S(1)} collective-permute-done((f32[352,512]{1,0:T(8,128)S(1)}, f32[352,512]{1,0:T(8,128)S(1)}, u32[]{:S(2)}, u32[]{:S(2)}) %collective-permute-start.1) | collective-permute-done | bytes 720928 | tf_op jit(solution)/shard_map/ppermute | solution.py:28
  34.4 3.1 %collective-permute-start.4 = (f32[320,128]{1,0:T(8,128)S(1)}, f32[320,128]{1,0:T(8,128)S(1)}, u32[]{:S(2)}, u32[]{:S(2)}) collective-permute-start(f32[320,128]{1,0:T(8,128)S(1)} %get-tuple-element.91), channel_id=1, source_target_pairs={{0,16},{8,24},{16,0},{24,8},{32,48},{40,56},{48,32},{56,40},{64,80... | collective-permute-start | bytes 491528 | tf_op jit(solution)/shard_map/ppermute | solution.py:28
  37.5 6.9 %collective-permute-done.4.received = f32[320,128]{1,0:T(8,128)S(1)} collective-permute-done((f32[320,128]{1,0:T(8,128)S(1)}, f32[320,128]{1,0:T(8,128)S(1)}, u32[]{:S(2)}, u32[]{:S(2)}) %collective-permute-start.4) | collective-permute-done | bytes 163872 | tf_op jit(solution)/shard_map/ppermute | solution.py:28
  45.5 6.0 %collective-permute-done.5 = f32[288,128]{1,0:T(8,128)S(1)} collective-permute-done((f32[288,128]{1,0:T(8,128)S(1)}, f32[288,128]{1,0:T(8,128)S(1)}, u32[]{:S(2)}, u32[]{:S(2)}) %collective-permute-start.5) | collective-permute-done | bytes 147488 | tf_op jit(solution)/shard_map/ppermute | solution.py:28
  51.5 2.6 %collective-permute-start.6 = (f32[256,128]{1,0:T(8,128)S(1)}, f32[256,128]{1,0:T(8,128)S(1)}, u32[]{:S(2)}, u32[]{:S(2)}) collective-permute-start(f32[256,128]{1,0:T(8,128)S(1)} %slice_add_fusion), channel_id=1, source_target_pairs={{0,16},{8,24},{16,0},{24,8},{32,48},{40,56},{48,32},{56,40},{64,80... | collective-permute-start | bytes 393224 | tf_op jit(solution)/shard_map/ppermute | solution.py:28
  54.1 2.7 %collective-permute-done.6 = f32[256,128]{1,0:T(8,128)S(1)} collective-permute-done((f32[256,128]{1,0:T(8,128)S(1)}, f32[256,128]{1,0:T(8,128)S(1)}, u32[]{:S(2)}, u32[]{:S(2)}) %collective-permute-start.6) | collective-permute-done | bytes 131104 | tf_op jit(solution)/shard_map/ppermute | solution.py:28
  56.8 6.0 %collective-permute-start.7 = (f32[256,256]{1,0:T(8,128)S(1)}, f32[256,256]{1,0:T(8,128)S(1)}, u32[]{:S(2)}, u32[]{:S(2)}) collective-permute-start(f32[256,256]{1,0:T(8,128)S(1)} %pad_maximum_fusion.1.mine), channel_id=1, source_target_pairs={{0,8},{8,0},{16,24},{24,16},{32,40},{40,32},{48,56},{56,48},{64,72... | collective-permute-start | bytes 786440 | tf_op jit(solution)/shard_map/ppermute | solution.py:28
  62.8 5.0 %collective-permute-done.7.received = f32[256,256]{1,0:T(8,128)S(1)} collective-permute-done((f32[256,256]{1,0:T(8,128)S(1)}, f32[256,256]{1,0:T(8,128)S(1)}, u32[]{:S(2)}, u32[]{:S(2)}) %collective-permute-start.7) | collective-permute-done | bytes 262176 | tf_op jit(solution)/shard_map/ppermute | solution.py:28
  68.8 33.3 %all_to_all.20.packed = f32[8,312,128]{2,1,0:T(8,128)S(1)} all-to-all(f32[8,312,128]{2,1,0:T(8,128)S(1)} %get-tuple-element.103), channel_id=1, replica_groups={{0,8,16,24,32,40,48,56},{64,72,80,88,96,104,112,120},{128,136,144,152,1..., dimensions={0} | all-to-all | bytes 2555904 | tf_op jit(solution)/shard_map/all_to_all | solution.py:32
  103.0 2.9 %collective-permute-done.8 = f32[64,128]{1,0:T(8,128)S(1)} collective-permute-done((f32[64,128]{1,0:T(8,128)S(1)}, f32[64,128]{1,0:T(8,128)S(1)}, u32[]{:S(2)}, u32[]{:S(2)}) %collective-permute-start.8) | collective-permute-done | bytes 32800 | tf_op jit(solution)/shard_map/ppermute | solution.py:28
  106.1 2.0 collective-permute-start.9
  108.1 2.2 %collective-permute-done.9 = f32[88,128]{1,0:T(8,128)S(1)} collective-permute-done((f32[88,128]{1,0:T(8,128)S(1)}, f32[88,128]{1,0:T(8,128)S(1)}, u32[]{:S(2)}, u32[]{:S(2)}) %collective-permute-start.9) | collective-permute-done | bytes 45088 | tf_op jit(solution)/shard_map/ppermute | solution.py:28
  110.7 3.0 %collective-permute-done.10 = f32[112,128]{1,0:T(8,128)S(1)} collective-permute-done((f32[112,128]{1,0:T(8,128)S(1)}, f32[112,128]{1,0:T(8,128)S(1)}, u32[]{:S(2)}, u32[]{:S(2)}) %collective-permute-start.10) | collective-permute-done | bytes 57376 | tf_op jit(solution)/shard_map/ppermute | solution.py:28
  113.8 20.8 %all_to_all.21.packed = f32[8,224,128]{2,1,0:T(8,128)S(1)} all-to-all(f32[8,224,128]{2,1,0:T(8,128)S(1)} %broadcast_in_dim.6), channel_id=1, replica_groups={{0,8,16,24,32,40,48,56},{64,72,80,88,96,104,112,120},{128,136,144,152,1..., dimensions={0} | all-to-all | bytes 1835008 | tf_op jit(solution)/shard_map/all_to_all | solution.py:32
  134.6 1.4 shard_map.55
  136.0 9.5 %collective-permute-start.11 = (f32[256,768]{1,0:T(8,128)S(1)}, f32[256,768]{1,0:T(8,128)S(1)}, u32[]{:S(2)}, u32[]{:S(2)}) collective-permute-start(f32[256,768]{1,0:T(8,128)S(1)} %get-tuple-element.116), channel_id=1, source_target_pairs={{0,1},{1,0},{2,3},{3,2},{4,5},{5,4},{6,7},{7,6},{8,9},{9,8},{10,11... | collective-permute-start | bytes 2359304 | tf_op jit(solution)/shard_map/ppermute | solution.py:28
  145.8 1.7 collective-permute-done.11.right
  148.1 22.2 %all_to_all.22.parts = f32[32,8,768]{2,1,0:T(8,128)S(1)} all-to-all(f32[32,8,768]{2,1,0:T(8,128)S(1)} %bitcast.24), channel_id=1, replica_groups={{0,8,16,24,32,40,48,56,64,72,80,88,96,104,112,120,128,136,144,152,160,1..., dimensions={0} | all-to-all | bytes 1572864 | tf_op jit(solution)/shard_map/all_to_all | solution.py:32
  172.9 1.4 collective-permute-done.13
  174.7 2.4 %collective-permute-start.14 = (f32[8,128]{1,0:T(8,128)S(1)}, f32[8,128]{1,0:T(8,128)S(1)}, u32[]{:S(2)}, u32[]{:S(2)}) collective-permute-start(f32[8,128]{1,0:T(8,128)S(1)} %constant_dynamic-slice_fusion), channel_id=1, source_target_pairs={{0,6},{1,7},{2,4},{3,5},{4,2},{5,3},{6,0},{7,1},{8,14},{9,15},{10,... | collective-permute-start | bytes 12296 | tf_op jit(solution)/shard_map/ppermute | solution.py:28
  178.5 1.5 shard_map.58.state
  181.0 19.9 %all_to_all.23 = f32[32,8,512]{2,1,0:T(8,128)S(1)} all-to-all(f32[32,8,512]{2,1,0:T(8,128)S(1)} %broadcast_in_dim.7), channel_id=1, replica_groups={{0,8,16,24,32,40,48,56,64,72,80,88,96,104,112,120,128,136,144,152,160,1..., dimensions={0} | all-to-all | bytes 1048576 | tf_op jit(solution)/shard_map/all_to_all | solution.py:32
  201.0 8.0 %collective-permute-start.16 = (f32[256,384]{1,0:T(8,128)S(1)}, f32[256,384]{1,0:T(8,128)S(1)}, u32[]{:S(2)}, u32[]{:S(2)}) collective-permute-start(f32[256,384]{1,0:T(8,128)S(1)} %slice.94), channel_id=1, source_target_pairs={{0,1},{1,0},{2,3},{3,2},{4,5},{5,4},{6,7},{7,6},{8,9},{9,8},{10,11... | collective-permute-start | bytes 1179656 | tf_op jit(solution)/shard_map/ppermute | solution.py:28
  210.3 2.3 %shard_map.59 = f32[512,1024]{1,0:T(8,128)} custom-call(s32[6]{0:T(128)S(1)} %stack.27.bits, f32[512,1024]{1,0:T(8,128)S(1)} %shard_map.58.state, f32[256,512]{1,0:T(8,128)S(1)} %bitcast.23, f32[256,384]{1,0:T(8,128)S(1)} %collective-permute-done.16.received, bf16[8,128,1024]{2,1,0:T(8,128)(2,1)S(1)} %copy-done.1), custom_call_target="tpu_custom_call" | custom-call | flops 402653184 | bytes 3145728 | tf_op jit(solution)/shard_map/pallas_call | solution.py:448
  (68 shorter events, 15.0 us)
Async XLA Ops:
  0.1 8.2 %copy-start = (bf16[8,256,1024]{2,1,0:T(8,128)(2,1)S(1)}, bf16[8,256,1024]{2,1,0:T(8,128)(2,1)}, u32[]{:S(2)}) copy-start(bf16[8,256,1024]{2,1,0:T(8,128)(2,1)} %proj.5) | copy-start | bytes 12582916
  0.1 8.2 %copy-start.1 = (bf16[8,128,1024]{2,1,0:T(8,128)(2,1)S(1)}, bf16[8,128,1024]{2,1,0:T(8,128)(2,1)}, u32[]{:S(2)}) copy-start(bf16[8,128,1024]{2,1,0:T(8,128)(2,1)} %up.9) | copy-start | bytes 6291460
  5.7 9.2 %collective-permute-start = (f32[512,128]{1,0:T(8,128)S(1)}, f32[512,128]{1,0:T(8,128)S(1)}, u32[]{:S(2)}, u32[]{:S(2)}) collective-permute-start(f32[512,128]{1,0:T(8,128)S(1)} %get-tuple-element.71), channel_id=1, source_target_pairs={{0,8},{8,0},{16,24},{24,16},{32,40},{40,32},{48,56},{56,48},{64,72... | collective-permute-start | bytes 786440 | tf_op jit(solution)/shard_map/ppermute | solution.py:28
  14.9 5.5 %collective-permute-start.2 = (f32[192,256]{1,0:T(8,128)S(1)}, f32[192,256]{1,0:T(8,128)S(1)}, u32[]{:S(2)}, u32[]{:S(2)}) collective-permute-start(f32[192,256]{1,0:T(8,128)S(1)} %constant_dynamic-slice_fusion.6), channel_id=1, source_target_pairs={{0,64},{8,72},{16,80},{24,88},{32,96},{40,104},{48,112},{56,120},{... | collective-permute-start | bytes 589832 | tf_op jit(solution)/shard_map/ppermute | solution.py:28
  17.2 16.5 %collective-permute-start.1 = (f32[352,512]{1,0:T(8,128)S(1)}, f32[352,512]{1,0:T(8,128)S(1)}, u32[]{:S(2)}, u32[]{:S(2)}) collective-permute-start(f32[352,512]{1,0:T(8,128)S(1)} %get-tuple-element.83), channel_id=1, source_target_pairs={{0,8},{8,0},{16,24},{24,16},{32,40},{40,32},{48,56},{56,48},{64,72... | collective-permute-start | bytes 2162696 | tf_op jit(solution)/shard_map/ppermute | solution.py:28
  20.5 4.8 %collective-permute-start.3 = (f32[96,256]{1,0:T(8,128)S(1)}, f32[96,256]{1,0:T(8,128)S(1)}, u32[]{:S(2)}, u32[]{:S(2)}) collective-permute-start(f32[96,256]{1,0:T(8,128)S(1)} %constant_dynamic-slice_fusion.5), channel_id=1, source_target_pairs={{0,192},{8,200},{16,208},{24,216},{32,224},{40,232},{48,240},{56,2... | collective-permute-start | bytes 294920 | tf_op jit(solution)/shard_map/ppermute | solution.py:28
  34.4 10.0 %collective-permute-start.4 = (f32[320,128]{1,0:T(8,128)S(1)}, f32[320,128]{1,0:T(8,128)S(1)}, u32[]{:S(2)}, u32[]{:S(2)}) collective-permute-start(f32[320,128]{1,0:T(8,128)S(1)} %get-tuple-element.91), channel_id=1, source_target_pairs={{0,16},{8,24},{16,0},{24,8},{32,48},{40,56},{48,32},{56,40},{64,80... | collective-permute-start | bytes 491528 | tf_op jit(solution)/shard_map/ppermute | solution.py:28
  45.2 6.3 %collective-permute-start.5 = (f32[288,128]{1,0:T(8,128)S(1)}, f32[288,128]{1,0:T(8,128)S(1)}, u32[]{:S(2)}, u32[]{:S(2)}) collective-permute-start(f32[288,128]{1,0:T(8,128)S(1)} %get-tuple-element.97), channel_id=1, source_target_pairs={{0,48},{8,56},{16,32},{24,40},{32,16},{40,24},{48,0},{56,8},{64,11... | collective-permute-start | bytes 442376 | tf_op jit(solution)/shard_map/ppermute | solution.py:28
  51.5 5.3 %collective-permute-start.6 = (f32[256,128]{1,0:T(8,128)S(1)}, f32[256,128]{1,0:T(8,128)S(1)}, u32[]{:S(2)}, u32[]{:S(2)}) collective-permute-start(f32[256,128]{1,0:T(8,128)S(1)} %slice_add_fusion), channel_id=1, source_target_pairs={{0,16},{8,24},{16,0},{24,8},{32,48},{40,56},{48,32},{56,40},{64,80... | collective-permute-start | bytes 393224 | tf_op jit(solution)/shard_map/ppermute | solution.py:28
  56.8 11.0 %collective-permute-start.7 = (f32[256,256]{1,0:T(8,128)S(1)}, f32[256,256]{1,0:T(8,128)S(1)}, u32[]{:S(2)}, u32[]{:S(2)}) collective-permute-start(f32[256,256]{1,0:T(8,128)S(1)} %pad_maximum_fusion.1.mine), channel_id=1, source_target_pairs={{0,8},{8,0},{16,24},{24,16},{32,40},{40,32},{48,56},{56,48},{64,72... | collective-permute-start | bytes 786440 | tf_op jit(solution)/shard_map/ppermute | solution.py:28
  102.7 3.1 %collective-permute-start.8 = (f32[64,128]{1,0:T(8,128)S(1)}, f32[64,128]{1,0:T(8,128)S(1)}, u32[]{:S(2)}, u32[]{:S(2)}) collective-permute-start(f32[64,128]{1,0:T(8,128)S(1)} %get-tuple-element.105), channel_id=1, source_target_pairs={{0,64},{8,72},{16,80},{24,88},{32,96},{40,104},{48,112},{56,120},{... | collective-permute-start | bytes 98312 | tf_op jit(solution)/shard_map/ppermute | solution.py:28
  106.1 4.2 %collective-permute-start.9 = (f32[88,128]{1,0:T(8,128)S(1)}, f32[88,128]{1,0:T(8,128)S(1)}, u32[]{:S(2)}, u32[]{:S(2)}) collective-permute-start(f32[88,128]{1,0:T(8,128)S(1)} %pad_maximum_fusion.5), channel_id=1, source_target_pairs={{0,192},{8,200},{16,208},{24,216},{32,224},{40,232},{48,240},{56,2... | collective-permute-start | bytes 135176 | tf_op jit(solution)/shard_map/ppermute | solution.py:28
  110.4 3.3 %collective-permute-start.10 = (f32[112,128]{1,0:T(8,128)S(1)}, f32[112,128]{1,0:T(8,128)S(1)}, u32[]{:S(2)}, u32[]{:S(2)}) collective-permute-start(f32[112,128]{1,0:T(8,128)S(1)} %pad_maximum_fusion.4), channel_id=1, source_target_pairs={{0,64},{8,72},{16,80},{24,88},{32,96},{40,104},{48,112},{56,120},{... | collective-permute-start | bytes 172040 | tf_op jit(solution)/shard_map/ppermute | solution.py:28
  136.0 11.4 %collective-permute-start.11 = (f32[256,768]{1,0:T(8,128)S(1)}, f32[256,768]{1,0:T(8,128)S(1)}, u32[]{:S(2)}, u32[]{:S(2)}) collective-permute-start(f32[256,768]{1,0:T(8,128)S(1)} %get-tuple-element.116), channel_id=1, source_target_pairs={{0,1},{1,0},{2,3},{3,2},{4,5},{5,4},{6,7},{7,6},{8,9},{9,8},{10,11... | collective-permute-start | bytes 2359304 | tf_op jit(solution)/shard_map/ppermute | solution.py:28
  145.7 2.4 %collective-permute-start.12 = (f32[384,256]{1,0:T(8,128)S(1)}, f32[384,256]{1,0:T(8,128)S(1)}, u32[]{:S(2)}, u32[]{:S(2)}) collective-permute-start(f32[384,256]{1,0:T(8,128)S(1)} %pad_maximum_fusion), channel_id=1, source_target_pairs={{0,1},{1,0},{2,3},{3,2},{4,5},{5,4},{6,7},{7,6},{8,9},{9,8},{10,11... | collective-permute-start | bytes 1179656 | tf_op jit(solution)/shard_map/ppermute | solution.py:28
  171.6 2.8 %collective-permute-start.13 = (f32[8,128]{1,0:T(8,128)S(1)}, f32[8,128]{1,0:T(8,128)S(1)}, u32[]{:S(2)}, u32[]{:S(2)}) collective-permute-start(f32[8,128]{1,0:T(8,128)S(1)} %constant_dynamic-slice_fusion.1), channel_id=1, source_target_pairs={{0,2},{1,3},{2,0},{3,1},{4,6},{5,7},{6,4},{7,5},{8,10},{9,11},{10,... | collective-permute-start | bytes 12296 | tf_op jit(solution)/shard_map/ppermute | solution.py:28
  174.7 3.7 %collective-permute-start.14 = (f32[8,128]{1,0:T(8,128)S(1)}, f32[8,128]{1,0:T(8,128)S(1)}, u32[]{:S(2)}, u32[]{:S(2)}) collective-permute-start(f32[8,128]{1,0:T(8,128)S(1)} %constant_dynamic-slice_fusion), channel_id=1, source_target_pairs={{0,6},{1,7},{2,4},{3,5},{4,2},{5,3},{6,0},{7,1},{8,14},{9,15},{10,... | collective-permute-start | bytes 12296 | tf_op jit(solution)/shard_map/ppermute | solution.py:28
  178.5 2.5 %collective-permute-start.15 = (f32[8,128]{1,0:T(8,128)S(1)}, f32[8,128]{1,0:T(8,128)S(1)}, u32[]{:S(2)}, u32[]{:S(2)}) collective-permute-start(f32[8,128]{1,0:T(8,128)S(1)} %dynamic-slice_add_fusion.2), channel_id=1, source_target_pairs={{0,2},{1,3},{2,0},{3,1},{4,6},{5,7},{6,4},{7,5},{8,10},{9,11},{10,... | collective-permute-start | bytes 12296 | tf_op jit(solution)/shard_map/ppermute | solution.py:28
  201.0 9.3 %collective-permute-start.16 = (f32[256,384]{1,0:T(8,128)S(1)}, f32[256,384]{1,0:T(8,128)S(1)}, u32[]{:S(2)}, u32[]{:S(2)}) collective-permute-start(f32[256,384]{1,0:T(8,128)S(1)} %slice.94), channel_id=1, source_target_pairs={{0,1},{1,0},{2,3},{3,2},{4,5},{5,4},{6,7},{7,6},{8,9},{9,8},{10,11... | collective-permute-start | bytes 1179656 | tf_op jit(solution)/shard_map/ppermute | solution.py:28

commit v5 on v4

--- a/solution.py
+++ b/solution.py
@@ -9,6 +9,7 @@
 
 AXES = ("gy", "gx")
 STEPS = 4
+RING = 8
 VMEM_BYTES = 16 * 1024 * 1024
 
 
@@ -95,7 +96,7 @@
     return pltpu.VMEM(shape, dtype)
 
 
-def local(body, bits, args, outs, flops, nbytes):
+def local(body, bits, args, outs, flops, nbytes, scratch=()):
     args = [pltpu.with_memory_space_constraint(a, pltpu.VMEM) for a in args]
     return pl.pallas_call(
         body,
@@ -103,6 +104,7 @@
         in_specs=[pl.BlockSpec(memory_space=pltpu.SMEM)]
         + [pl.BlockSpec(memory_space=pltpu.VMEM)] * len(args),
         out_specs=[pl.BlockSpec(memory_space=pltpu.VMEM)] * len(outs),
+        scratch_shapes=scratch,
         compiler_params=pltpu.CompilerParams(vmem_limit_bytes=VMEM_BYTES),
         cost_estimate=pl.CostEstimate(flops=flops, bytes_accessed=nbytes, transcendentals=0),
     )(bits, *args)
@@ -284,7 +286,7 @@
     )
 
 
-def fourth_body(bits, c1, mine, received, value, gram, low, high, packed, coef):
+def fourth_body(bits, c1, mine, received, value, gram, low, high, keep_a, send_a, keep_b, send_b, coef, sums):
     count, rank = mine.shape[0], c1.shape[1]
     for bit in range(2):
 
@@ -293,65 +295,121 @@
             coef[bit * count : (bit + 1) * count] = mine[...].astype(jnp.bfloat16)
             coef[(1 - bit) * count : (2 - bit) * count] = received[...].astype(jnp.bfloat16)
 
-    parts, total, _ = packed.shape
-    share = value.shape[1] // parts
+    rows, wide = value.shape[1:]
+    share = rows // RING
+    piece = high.shape[0] // RING
     lhs = jnp.concatenate([c1[...], coef[...]], axis=1)
     for i in range(2):
-        left = value[i] - dot(lhs, gram[i])
-        for j in range(2):
-            start = (2 * i + j) * share
-            packed[:, start : start + share, :] = left[:, j * rank : (j + 1) * rank].reshape(parts, share, rank)
-    start = 4 * share
-    packed[:, start : start + low.shape[0], :] = jnp.broadcast_to(low[...], (parts, *low.shape))
-    start += low.shape[0]
-    packed[:, start:total, :] = high[...].reshape(parts, total - start, rank)
-
-
-def fourth(bits, c1, mine, received, value, gram, low, high, parts):
+        sums[i] = value[i] - dot(lhs, gram[i])
+    for keep, send, level in ((keep_a, send_a, 0), (keep_b, send_b, 1)):
+        for ref, parity in ((keep, bits[0]), (send, 1 - bits[0])):
+            for i in range(RING // 2):
+                place = 2 * i + parity
+                for j in range(2):
+                    start = (2 * i + j) * share
+                    ref[start : start + share] = sums[
+                        level, pl.ds(pl.multiple_of(place * share, share), share), j * rank : (j + 1) * rank
+                    ]
+                if level == 0:
+                    start = rows + i * piece
+                    ref[start : start + piece] = high[pl.ds(pl.multiple_of(place * piece, piece), piece)]
+    send_a[rows + RING // 2 * piece :] = low[...]
+
+
+def fourth(bits, c1, mine, received, value, gram, low, high):
     rows, rank = c1.shape
     wide = 2 * rank
-    total = 4 * rows // parts + low.shape[0] + high.shape[0] // parts
+    extra = high.shape[0] // 2
     return local(
         fourth_body,
         bits,
         [c1, mine, received, value, gram, low, high],
-        [vmem(parts, total, rank), vmem(rows, wide, dtype=jnp.bfloat16)],
+        [
+            vmem(rows + extra, rank), vmem(rows + extra + low.shape[0], rank),
+            vmem(rows, rank), vmem(rows, rank), vmem(rows, wide, dtype=jnp.bfloat16),
+        ],
         12 * rows * rank * wide,
         16 * rows * wide,
-    )
-
-
-def gather_body(places, bits, packed, own, other, fifth, gram, high):
-    parts, total, rank = packed.shape
-    share, piece = own.shape[0], gram.shape[0] // parts
-    for ref, bit in ((own, 0), (other, 1)):
-        for b in range(2):
-
-            @pl.when(bits[2] == b)
-            def _(ref=ref, start=(bit ^ b) * share):
-                ref[...] = packed[:, start : start + share, :].sum(axis=0)
-
+        [pltpu.VMEM((2, rows, wide), jnp.float32)],
+    )
+
+
+def halve_body(steps, bits, *refs):
+    (keep_a, got_a, keep_b, got_b, low), (next_a, send_a, next_b, send_b, lows) = refs[:5], refs[5:]
+    count = keep_b.shape[0] // (2 * steps)
+    piece = (keep_a.shape[0] - keep_b.shape[0]) // (2 * steps)
+    rows = keep_b.shape[0]
+    for out, to, got, keep, far, near in (
+        (next_a, send_a, got_a, keep_a, 1, 3),
+        (next_b, send_b, got_b, keep_b, 3, 1),
+    ):
+        if steps == 2:
+            mine = [bits[6], bits[6] ^ near]
+            theirs = [bits[6] ^ far, bits[6] ^ far ^ near]
+        else:
+            mine, theirs = [0], [1]
+        for ref, slots in ((out, mine), (to, theirs)):
+            for i, slot in enumerate(slots):
+                here = pl.ds(slot * count, count)
+                ref[i * count : (i + 1) * count] = keep[here] + got[here]
+                if keep.shape[0] > rows:
+                    there = pl.ds(rows + slot * piece, piece)
+                    start = len(slots) * count + i * piece
+                    ref[start : start + piece] = keep[there] + got[there]
+    done = low.shape[0]
+    lows[:done] = low[...]
+    lows[done:] = got_a[keep_a.shape[0] :]
+    send_a[next_a.shape[0] :] = lows[...]
+
+
+def halve(bits, steps, keep_a, got_a, keep_b, got_b, low):
+    rank = low.shape[1]
+    size_a, size_b, lows = keep_a.shape[0] // 2, keep_b.shape[0] // 2, 2 * low.shape[0]
+    return local(
+        functools.partial(halve_body, steps),
+        bits,
+        [keep_a, got_a, keep_b, got_b, low],
+        [vmem(size_a, rank), vmem(size_a + lows, rank), vmem(size_b, rank), vmem(size_b, rank), vmem(lows, rank)],
+        2 * keep_a.size,
+        20 * keep_a.size,
+    )
+
+
+def gather_body(bits, keep_a, got_a, keep_b, got_b, low, own, other, fifth, gram, high):
+    share, rank = own.shape
+    rows = 2 * share
+    total = keep_a[...] + got_a[: keep_a.shape[0]]
+    choose(bits[2], total[:share], total[share:rows], own, other)
+    high[...] = total[rows:]
     for j in range(2):
-        start = (2 + j) * share
-        fifth[:, j * rank : (j + 1) * rank] = packed[:, start : start + share, :].sum(axis=0)
-    for i, place in enumerate(places):
+        here = slice(j * share, (j + 1) * share)
+        fifth[:, j * rank : (j + 1) * rank] = keep_b[here] + got_b[here]
+    count = gram.shape[0] // RING
+    half_list = low.shape[0]
+    z0, z1, z2 = bits[0], bits[3], bits[5]
+    for i, mask in enumerate((0, 1, 2, 3, 6, 7, 4, 5)):
+        p0, p1, p2 = z0 ^ (mask & 1), z1 ^ (mask >> 1 & 1), z2 ^ (mask >> 2)
+        place = pl.multiple_of((p0 * 4 + (p1 ^ p2) * 2 + p2) * count, count)
         for j in range(2):
-            start = 4 * share + j * piece
-            gram[place * piece : (place + 1) * piece, j * rank : (j + 1) * rank] = packed[i, start : start + piece, :]
-    high[...] = packed[:, 4 * share + 2 * piece :, :].sum(axis=0)
-
-
-def gather_rows(bits, packed, places, share):
-    parts, total, rank = packed.shape
-    rest = total - 4 * share - 2 * rank // parts
-    shapes = [(share, rank), (share, rank), (share, 2 * rank), (rank, 2 * rank), (rest, rank)]
-    return local(
-        functools.partial(gather_body, places),
-        bits,
-        [packed],
+            start = 2 * i * count + j * count
+            if start < half_list:
+                part = low[start : start + count]
+            else:
+                start += keep_a.shape[0] - half_list
+                part = got_a[start : start + count]
+            gram[pl.ds(place, count), j * rank : (j + 1) * rank] = part
+
+
+def gather_rows(bits, keep_a, got_a, keep_b, got_b, low):
+    share, rank = keep_b.shape[0] // 2, keep_b.shape[1]
+    shapes = [(share, rank), (share, rank), (share, 2 * rank), (rank, 2 * rank), (keep_a.shape[0] - 2 * share, rank)]
+    return local(
+        gather_body,
+        bits,
+        [keep_a, got_a, keep_b, got_b, low],
         [vmem(*s) for s in shapes],
-        parts * total * rank,
-        4 * parts * total * rank,
+        2 * keep_a.size,
+        20 * keep_a.size,
     )
 
 
@@ -470,10 +528,10 @@
     gx, gy = lax.axis_index("gx"), lax.axis_index("gy")
     z0, z1, z2, y0, y1 = (gx >> i & 1 for i in range(5))
     core, x0, x1 = (gy >> i & 1 for i in range(3))
-    bits = jnp.stack([z0, core, y0, z1, z1 ^ z2, z2])
+    bits = jnp.stack([z0, core, y0, z1, z1 ^ z2, z2, z1 + 2 * z2])
     over_x = functools.partial(swap, axis="gx", size=size_x)
     over_y = functools.partial(swap, axis="gy", size=size_y)
-    ring = len(groups_z[0])
+    ring = RING
     share = rows // ring
     by_y01, by_y1 = starts(y0 ^ y1, 3 * rank // 2), starts(y1, 3 * rank // 4)
     half_y1 = starts(y1, rank)
@@ -498,7 +556,6 @@
 
     keep, send, c1 = second(bits, own, received, value, gram, kept, kept_45)
     received = over_x(send, mask=1)
-    places = [(i & 1) * 4 + (i >> 1 & 1 ^ i >> 2) * 2 + (i >> 2) for i in range(ring)]
     high, high_send = split(kept_678.reshape(3 * rank, wide), by_y01)
     high, high_send = split(high + over_x(high_send, mask=8), by_y1)
     high = high + over_x(high_send, mask=24)
@@ -513,9 +570,14 @@
     mine = jnp.concatenate([c2, c3], axis=1)
     received = over_x(mine, mask=1)
 
-    packed, c23 = fourth(bits, c1, mine, received, value_45, gram_45, low, high, ring)
-    packed = exchange(packed, groups_z)
-    own, other, left, gram_45, high = gather_rows(bits, packed, places, share)
+    keep_a, send_a, keep_b, send_b, c23 = fourth(bits, c1, mine, received, value_45, gram_45, low, high)
+    turned = [(i & -RING) + ((i + 1 if i & 1 else i - 1) % RING) for i in range(size_x)]
+    got_a, got_b = over_x(send_a, mask=1), lax.ppermute(send_b, "gx", list(enumerate(turned)))
+    keep_a, send_a, keep_b, send_b, low = halve(bits, 2, keep_a, got_a, keep_b, got_b, low)
+    got_a, got_b = over_x(send_a, mask=2), over_x(send_b, mask=6)
+    keep_a, send_a, keep_b, send_b, low = halve(bits, 1, keep_a, got_a, keep_b, got_b, low)
+    got_a, got_b = over_x(send_a, mask=6), over_x(send_b, mask=2)
+    own, other, left, gram_45, high = gather_rows(bits, keep_a, got_a, keep_b, got_b, low)
     c4 = own + over_x(other, mask=8)
     left = left - dot(c4, gram_45)
     received = over_x(jnp.concatenate([half(left, half_y1[1]), high]), mask=24)
@@ -556,7 +618,7 @@
 
 def solution(mesh):
     size_x, size_y = mesh.shape["gx"], mesh.shape["gy"]
-    ring = 8
+    ring = RING
     groups_z = [
         [gy * size_x + start + i for i in range(ring)]
         for gy in range(size_y)

time: 213 us -> 211 us (level)
  blocking collectives: 96.2 us -> 61.2 us
  waiting for transfers between devices: 48.2 us -> 67.9 us
  starting transfers between devices: 43.2 us -> 55.8 us
    all_to_all x4 -> x3, blocking collectives: 96.2 us -> 61.2 us  [exchange(): lax.all_to_all(value, AXES, 0, 0, tiled=True, axis_index_groups=groups)]
    ppermute x17 -> x22, waiting for transfers between devices: 48.2 us -> 61.5 us  [swap(): lax.ppermute(value, axis, [(source, source ^ mask) for source in range(si...]
    ppermute x17 -> x22, starting transfers between devices: 43.2 us -> 55.8 us  [swap(): lax.ppermute(value, axis, [(source, source ^ mask) for source in range(si...]
    ppermute x0 -> x1, waiting for transfers between devices: none -> 6.43 us  [shards(): lax.ppermute(send_b, 'gx', list(enumerate(turned)))]
    pallas_call x12 -> x14, Pallas kernels: 14.7 us -> 15.9 us  [local(): pl.pallas_call(body, out_shape=outs, in_specs=[pl.BlockSpec(memory_space=...]
  transfers between devices with their start and end apart: 17 -> 23, of which waited for: 15 -> 19; matrix products, arithmetic and copies ran while one was open for 0% -> 0% of each run, Pallas kernels for 5% -> 5%
where the time goes in v5:
time: 211 us
  waiting for transfers between devices  67.9 us (32%)
  blocking collectives  61.2 us (29%)
  starting transfers between devices  55.8 us (26%)
  Pallas kernels  23.8 us (11%)
    ppermute x22, waiting for transfers between devices, swap(): lax.ppermute(value, axis, [(source, source ^ mask) for source in range(si...  61.5 us
    all_to_all x3, blocking collectives, exchange(): lax.all_to_all(value, AXES, 0, 0, tiled=True, axis_index_groups=groups)  61.2 us
    ppermute x22, starting transfers between devices, swap(): lax.ppermute(value, axis, [(source, source ^ mask) for source in range(si...  55.8 us
    pallas_call x14, Pallas kernels, local(): pl.pallas_call(body, out_shape=outs, in_specs=[pl.BlockSpec(memory_space=...  15.9 us
    ppermute x1, waiting for transfers between devices, shards(): lax.ppermute(send_b, 'gx', list(enumerate(turned)))  6.43 us
    pallas_call x1, Pallas kernels, run(): pl.pallas_call(body, out_shape=out_shape, grid_spec=pltpu.PrefetchScalarG...  5.63 us
  transfers between devices with their start and end apart: 23, of which 19 were waited for; matrix products, arithmetic and copies ran while one was open for 0% of the time, Pallas kernels for 5%

profile of v5, /device:TPU:1, one launch (start us, length us, event | category | flops | bytes accessed | tf_op | source)
XLA Modules:
  0.0 211.2 jit_solution(3883092387473297285)
XLA Ops:
  0.1 5.6 %shard_map.46 = (bf16[512,1024]{1,0:T(8,128)(2,1)S(1)}, f32[512,128]{1,0:T(8,128)S(1)}, f32[512,128]{1,0:T(8,128)S(1)}) custom-call(s32[7]{0:T(128)S(1)} %stack.31.bits, bf16[512,1024]{1,0:T(8,128)(2,1)} %rhs, bf16[1,1024,1024]{2,1,0:T(8,128)(2,1)} %inverse.1, bf16[8,256,1024]{2,1,0:T(8,128)(2,1)} %proj.5, bf16[8,256,1024]{2,1,0:T(8,128)(2,1)} %proj.5), custom_call_target="tpu_custom_call" | custom-call | flops 1342177280 | bytes 4194304 | tf_op jit(solution)/shard_map/pallas_call | solution.py:70
  5.7 2.6 %collective-permute-start = (f32[512,128]{1,0:T(8,128)S(1)}, f32[512,128]{1,0:T(8,128)S(1)}, u32[]{:S(2)}, u32[]{:S(2)}) collective-permute-start(f32[512,128]{1,0:T(8,128)S(1)} %get-tuple-element.84), channel_id=1, source_target_pairs={{0,8},{8,0},{16,24},{24,16},{32,40},{40,32},{48,56},{56,48},{64,72... | collective-permute-start | bytes 786440 | tf_op jit(solution)/shard_map/ppermute | solution.py:29
  8.3 1.9 shard_map.48
  11.9 3.0 %shard_map.49 = (f32[3,512,256]{2,1,0:T(8,128)S(1)}, bf16[3,640,256]{2,1,0:T(8,128)(2,1)S(1)}, f32[3,128,256]{2,1,0:T(8,128)S(1)}) custom-call(s32[7]{0:T(128)S(1)} %stack.31.bits, bf16[512,1024]{1,0:T(8,128)(2,1)S(1)} %get-tuple-element.85.state, bf16[8,128,1024]{2,1,0:T(8,128)(2,1)S(1)} %copy-done.1, bf16[8,256,1024]{2,1,0:T(8,128)(2,1)S(1)} %copy-done), custom_call_target="tpu_custom_call" | custom-call | flops 2013265920 | bytes 3407872 | tf_op jit(solution)/shard_map/pallas_call | solution.py:101
  17.9 2.6 %collective-permute-done.2 = f32[192,256]{1,0:T(8,128)S(1)} collective-permute-done((f32[192,256]{1,0:T(8,128)S(1)}, f32[192,256]{1,0:T(8,128)S(1)}, u32[]{:S(2)}, u32[]{:S(2)}) %collective-permute-start.2) | collective-permute-done | bytes 196640 | tf_op jit(solution)/shard_map/ppermute | solution.py:29
  20.5 2.8 %collective-permute-start.3 = (f32[96,256]{1,0:T(8,128)S(1)}, f32[96,256]{1,0:T(8,128)S(1)}, u32[]{:S(2)}, u32[]{:S(2)}) collective-permute-start(f32[96,256]{1,0:T(8,128)S(1)} %constant_dynamic-slice_fusion.5), channel_id=1, source_target_pairs={{0,192},{8,200},{16,208},{24,216},{32,224},{40,232},{48,240},{56,2... | collective-permute-start | bytes 294920 | tf_op jit(solution)/shard_map/ppermute | solution.py:29
  23.4 2.0 collective-permute-done.3
  25.4 8.3 %collective-permute-done.1.received = f32[352,512]{1,0:T(8,128)S(1)} collective-permute-done((f32[352,512]{1,0:T(8,128)S(1)}, f32[352,512]{1,0:T(8,128)S(1)}, u32[]{:S(2)}, u32[]{:S(2)}) %collective-permute-start.1) | collective-permute-done | bytes 720928 | tf_op jit(solution)/shard_map/ppermute | solution.py:29
  34.4 3.1 %collective-permute-start.4 = (f32[320,128]{1,0:T(8,128)S(1)}, f32[320,128]{1,0:T(8,128)S(1)}, u32[]{:S(2)}, u32[]{:S(2)}) collective-permute-start(f32[320,128]{1,0:T(8,128)S(1)} %get-tuple-element.104), channel_id=1, source_target_pairs={{0,16},{8,24},{16,0},{24,8},{32,48},{40,56},{48,32},{56,40},{64,80... | collective-permute-start | bytes 491528 | tf_op jit(solution)/shard_map/ppermute | solution.py:29
  37.5 7.0 %collective-permute-done.4.received = f32[320,128]{1,0:T(8,128)S(1)} collective-permute-done((f32[320,128]{1,0:T(8,128)S(1)}, f32[320,128]{1,0:T(8,128)S(1)}, u32[]{:S(2)}, u32[]{:S(2)}) %collective-permute-start.4) | collective-permute-done | bytes 163872 | tf_op jit(solution)/shard_map/ppermute | solution.py:29
  45.2 2.1 collective-permute-start.5
  47.2 4.2 %collective-permute-done.5 = f32[288,128]{1,0:T(8,128)S(1)} collective-permute-done((f32[288,128]{1,0:T(8,128)S(1)}, f32[288,128]{1,0:T(8,128)S(1)}, u32[]{:S(2)}, u32[]{:S(2)}) %collective-permute-start.5) | collective-permute-done | bytes 147488 | tf_op jit(solution)/shard_map/ppermute | solution.py:29
  51.5 2.6 %collective-permute-start.6 = (f32[256,128]{1,0:T(8,128)S(1)}, f32[256,128]{1,0:T(8,128)S(1)}, u32[]{:S(2)}, u32[]{:S(2)}) collective-permute-start(f32[256,128]{1,0:T(8,128)S(1)} %slice_add_fusion), channel_id=1, source_target_pairs={{0,16},{8,24},{16,0},{24,8},{32,48},{40,56},{48,32},{56,40},{64,80... | collective-permute-start | bytes 393224 | tf_op jit(solution)/shard_map/ppermute | solution.py:29
  54.1 2.7 %collective-permute-done.6 = f32[256,128]{1,0:T(8,128)S(1)} collective-permute-done((f32[256,128]{1,0:T(8,128)S(1)}, f32[256,128]{1,0:T(8,128)S(1)}, u32[]{:S(2)}, u32[]{:S(2)}) %collective-permute-start.6) | collective-permute-done | bytes 131104 | tf_op jit(solution)/shard_map/ppermute | solution.py:29
  56.8 6.0 %collective-permute-start.7 = (f32[256,256]{1,0:T(8,128)S(1)}, f32[256,256]{1,0:T(8,128)S(1)}, u32[]{:S(2)}, u32[]{:S(2)}) collective-permute-start(f32[256,256]{1,0:T(8,128)S(1)} %pad_maximum_fusion.1.mine), channel_id=1, source_target_pairs={{0,8},{8,0},{16,24},{24,16},{32,40},{40,32},{48,56},{56,48},{64,72... | collective-permute-start | bytes 786440 | tf_op jit(solution)/shard_map/ppermute | solution.py:29
  62.8 5.0 %collective-permute-done.7.received = f32[256,256]{1,0:T(8,128)S(1)} collective-permute-done((f32[256,256]{1,0:T(8,128)S(1)}, f32[256,256]{1,0:T(8,128)S(1)}, u32[]{:S(2)}, u32[]{:S(2)}) %collective-permute-start.7) | collective-permute-done | bytes 262176 | tf_op jit(solution)/shard_map/ppermute | solution.py:29
  70.1 6.4 %collective-permute-done.9.refs_3_ = f32[512,128]{1,0:T(8,128)S(1)} collective-permute-done((f32[512,128]{1,0:T(8,128)S(1)}, f32[512,128]{1,0:T(8,128)S(1)}, u32[]{:S(2)}, u32[]{:S(2)}) %collective-permute-start.9) | collective-permute-done | bytes 262176 | tf_op jit(solution)/shard_map/ppermute | solution.py:575
  77.1 1.9 collective-permute-start.10
  79.4 6.8 %collective-permute-done.11.refs_3_ = f32[256,128]{1,0:T(8,128)S(1)} collective-permute-done((f32[256,128]{1,0:T(8,128)S(1)}, f32[256,128]{1,0:T(8,128)S(1)}, u32[]{:S(2)}, u32[]{:S(2)}) %collective-permute-start.11) | collective-permute-done | bytes 131104 | tf_op jit(solution)/shard_map/ppermute | solution.py:29
  89.1 4.4 %collective-permute-done.13.got_b = f32[128,128]{1,0:T(8,128)S(1)} collective-permute-done((f32[128,128]{1,0:T(8,128)S(1)}, f32[128,128]{1,0:T(8,128)S(1)}, u32[]{:S(2)}, u32[]{:S(2)}) %collective-permute-start.13) | collective-permute-done | bytes 65568 | tf_op jit(solution)/shard_map/ppermute | solution.py:29
  93.5 3.7 %collective-permute-done.12.got_a = f32[280,128]{1,0:T(8,128)S(1)} collective-permute-done((f32[280,128]{1,0:T(8,128)S(1)}, f32[280,128]{1,0:T(8,128)S(1)}, u32[]{:S(2)}, u32[]{:S(2)}) %collective-permute-start.12) | collective-permute-done | bytes 143392 | tf_op jit(solution)/shard_map/ppermute | solution.py:29
  98.1 2.6 %collective-permute-done.14 = f32[64,128]{1,0:T(8,128)S(1)} collective-permute-done((f32[64,128]{1,0:T(8,128)S(1)}, f32[64,128]{1,0:T(8,128)S(1)}, u32[]{:S(2)}, u32[]{:S(2)}) %collective-permute-start.14) | collective-permute-done | bytes 32800 | tf_op jit(solution)/shard_map/ppermute | solution.py:29
  100.9 2.0 collective-permute-start.15
  102.9 2.5 %collective-permute-done.15 = f32[88,128]{1,0:T(8,128)S(1)} collective-permute-done((f32[88,128]{1,0:T(8,128)S(1)}, f32[88,128]{1,0:T(8,128)S(1)}, u32[]{:S(2)}, u32[]{:S(2)}) %collective-permute-start.15) | collective-permute-done | bytes 45088 | tf_op jit(solution)/shard_map/ppermute | solution.py:29
  105.6 3.0 %collective-permute-done.16 = f32[112,128]{1,0:T(8,128)S(1)} collective-permute-done((f32[112,128]{1,0:T(8,128)S(1)}, f32[112,128]{1,0:T(8,128)S(1)}, u32[]{:S(2)}, u32[]{:S(2)}) %collective-permute-start.16) | collective-permute-done | bytes 57376 | tf_op jit(solution)/shard_map/ppermute | solution.py:29
  108.7 18.9 %all_to_all.15.packed = f32[8,224,128]{2,1,0:T(8,128)S(1)} all-to-all(f32[8,224,128]{2,1,0:T(8,128)S(1)} %broadcast_in_dim.6), channel_id=1, replica_groups={{0,8,16,24,32,40,48,56},{64,72,80,88,96,104,112,120},{128,136,144,152,1..., dimensions={0} | all-to-all | bytes 1835008 | tf_op jit(solution)/shard_map/all_to_all | solution.py:33
  129.0 14.8 %collective-permute-start.17 = (f32[256,768]{1,0:T(8,128)S(1)}, f32[256,768]{1,0:T(8,128)S(1)}, u32[]{:S(2)}, u32[]{:S(2)}) collective-permute-start(f32[256,768]{1,0:T(8,128)S(1)} %get-tuple-element.142), channel_id=1, source_target_pairs={{0,1},{1,0},{2,3},{3,2},{4,5},{5,4},{6,7},{7,6},{8,9},{9,8},{10,11... | collective-permute-start | bytes 2359304 | tf_op jit(solution)/shard_map/ppermute | solution.py:29
  146.4 22.4 %all_to_all.16.parts = f32[32,8,768]{2,1,0:T(8,128)S(1)} all-to-all(f32[32,8,768]{2,1,0:T(8,128)S(1)} %bitcast.25), channel_id=1, replica_groups={{0,8,16,24,32,40,48,56,64,72,80,88,96,104,112,120,128,136,144,152,160,1..., dimensions={0} | all-to-all | bytes 1572864 | tf_op jit(solution)/shard_map/all_to_all | solution.py:33
  173.1 2.3 %collective-permute-start.20 = (f32[8,128]{1,0:T(8,128)S(1)}, f32[8,128]{1,0:T(8,128)S(1)}, u32[]{:S(2)}, u32[]{:S(2)}) collective-permute-start(f32[8,128]{1,0:T(8,128)S(1)} %constant_dynamic-slice_fusion), channel_id=1, source_target_pairs={{0,6},{1,7},{2,4},{3,5},{4,2},{5,3},{6,0},{7,1},{8,14},{9,15},{10,... | collective-permute-start | bytes 12296 | tf_op jit(solution)/shard_map/ppermute | solution.py:29
  179.5 19.9 %all_to_all.17 = f32[32,8,512]{2,1,0:T(8,128)S(1)} all-to-all(f32[32,8,512]{2,1,0:T(8,128)S(1)} %broadcast_in_dim.7), channel_id=1, replica_groups={{0,8,16,24,32,40,48,56,64,72,80,88,96,104,112,120,128,136,144,152,160,1..., dimensions={0} | all-to-all | bytes 1048576 | tf_op jit(solution)/shard_map/all_to_all | solution.py:33
  199.4 8.0 %collective-permute-start.22 = (f32[256,384]{1,0:T(8,128)S(1)}, f32[256,384]{1,0:T(8,128)S(1)}, u32[]{:S(2)}, u32[]{:S(2)}) collective-permute-start(f32[256,384]{1,0:T(8,128)S(1)} %slice.94), channel_id=1, source_target_pairs={{0,1},{1,0},{2,3},{3,2},{4,5},{5,4},{6,7},{7,6},{8,9},{9,8},{10,11... | collective-permute-start | bytes 1179656 | tf_op jit(solution)/shard_map/ppermute | solution.py:29
  208.8 2.3 %shard_map.61 = f32[512,1024]{1,0:T(8,128)} custom-call(s32[7]{0:T(128)S(1)} %stack.31.bits, f32[512,1024]{1,0:T(8,128)S(1)} %shard_map.60.state, f32[256,512]{1,0:T(8,128)S(1)} %bitcast.24, f32[256,384]{1,0:T(8,128)S(1)} %collective-permute-done.22.received, bf16[8,128,1024]{2,1,0:T(8,128)(2,1)S(1)} %copy-done.1), custom_call_target="tpu_custom_call" | custom-call | flops 402653184 | bytes 3145728 | tf_op jit(solution)/shard_map/pallas_call | solution.py:506
  (81 shorter events, 27.5 us)
Async XLA Ops:
  0.1 8.2 %copy-start = (bf16[8,256,1024]{2,1,0:T(8,128)(2,1)S(1)}, bf16[8,256,1024]{2,1,0:T(8,128)(2,1)}, u32[]{:S(2)}) copy-start(bf16[8,256,1024]{2,1,0:T(8,128)(2,1)} %proj.5) | copy-start | bytes 12582916
  0.1 8.2 %copy-start.1 = (bf16[8,128,1024]{2,1,0:T(8,128)(2,1)S(1)}, bf16[8,128,1024]{2,1,0:T(8,128)(2,1)}, u32[]{:S(2)}) copy-start(bf16[8,128,1024]{2,1,0:T(8,128)(2,1)} %up.9) | copy-start | bytes 6291460
  5.7 9.2 %collective-permute-start = (f32[512,128]{1,0:T(8,128)S(1)}, f32[512,128]{1,0:T(8,128)S(1)}, u32[]{:S(2)}, u32[]{:S(2)}) collective-permute-start(f32[512,128]{1,0:T(8,128)S(1)} %get-tuple-element.84), channel_id=1, source_target_pairs={{0,8},{8,0},{16,24},{24,16},{32,40},{40,32},{48,56},{56,48},{64,72... | collective-permute-start | bytes 786440 | tf_op jit(solution)/shard_map/ppermute | solution.py:29
  14.9 5.5 %collective-permute-start.2 = (f32[192,256]{1,0:T(8,128)S(1)}, f32[192,256]{1,0:T(8,128)S(1)}, u32[]{:S(2)}, u32[]{:S(2)}) collective-permute-start(f32[192,256]{1,0:T(8,128)S(1)} %constant_dynamic-slice_fusion.6), channel_id=1, source_target_pairs={{0,64},{8,72},{16,80},{24,88},{32,96},{40,104},{48,112},{56,120},{... | collective-permute-start | bytes 589832 | tf_op jit(solution)/shard_map/ppermute | solution.py:29
  17.2 16.5 %collective-permute-start.1 = (f32[352,512]{1,0:T(8,128)S(1)}, f32[352,512]{1,0:T(8,128)S(1)}, u32[]{:S(2)}, u32[]{:S(2)}) collective-permute-start(f32[352,512]{1,0:T(8,128)S(1)} %get-tuple-element.96), channel_id=1, source_target_pairs={{0,8},{8,0},{16,24},{24,16},{32,40},{40,32},{48,56},{56,48},{64,72... | collective-permute-start | bytes 2162696 | tf_op jit(solution)/shard_map/ppermute | solution.py:29
  20.5 4.8 %collective-permute-start.3 = (f32[96,256]{1,0:T(8,128)S(1)}, f32[96,256]{1,0:T(8,128)S(1)}, u32[]{:S(2)}, u32[]{:S(2)}) collective-permute-start(f32[96,256]{1,0:T(8,128)S(1)} %constant_dynamic-slice_fusion.5), channel_id=1, source_target_pairs={{0,192},{8,200},{16,208},{24,216},{32,224},{40,232},{48,240},{56,2... | collective-permute-start | bytes 294920 | tf_op jit(solution)/shard_map/ppermute | solution.py:29
  34.4 10.1 %collective-permute-start.4 = (f32[320,128]{1,0:T(8,128)S(1)}, f32[320,128]{1,0:T(8,128)S(1)}, u32[]{:S(2)}, u32[]{:S(2)}) collective-permute-start(f32[320,128]{1,0:T(8,128)S(1)} %get-tuple-element.104), channel_id=1, source_target_pairs={{0,16},{8,24},{16,0},{24,8},{32,48},{40,56},{48,32},{56,40},{64,80... | collective-permute-start | bytes 491528 | tf_op jit(solution)/shard_map/ppermute | solution.py:29
  45.2 6.3 %collective-permute-start.5 = (f32[288,128]{1,0:T(8,128)S(1)}, f32[288,128]{1,0:T(8,128)S(1)}, u32[]{:S(2)}, u32[]{:S(2)}) collective-permute-start(f32[288,128]{1,0:T(8,128)S(1)} %get-tuple-element.110), channel_id=1, source_target_pairs={{0,48},{8,56},{16,32},{24,40},{32,16},{40,24},{48,0},{56,8},{64,11... | collective-permute-start | bytes 442376 | tf_op jit(solution)/shard_map/ppermute | solution.py:29
  51.5 5.3 %collective-permute-start.6 = (f32[256,128]{1,0:T(8,128)S(1)}, f32[256,128]{1,0:T(8,128)S(1)}, u32[]{:S(2)}, u32[]{:S(2)}) collective-permute-start(f32[256,128]{1,0:T(8,128)S(1)} %slice_add_fusion), channel_id=1, source_target_pairs={{0,16},{8,24},{16,0},{24,8},{32,48},{40,56},{48,32},{56,40},{64,80... | collective-permute-start | bytes 393224 | tf_op jit(solution)/shard_map/ppermute | solution.py:29
  56.8 10.9 %collective-permute-start.7 = (f32[256,256]{1,0:T(8,128)S(1)}, f32[256,256]{1,0:T(8,128)S(1)}, u32[]{:S(2)}, u32[]{:S(2)}) collective-permute-start(f32[256,256]{1,0:T(8,128)S(1)} %pad_maximum_fusion.1.mine), channel_id=1, source_target_pairs={{0,8},{8,0},{16,24},{24,16},{32,40},{40,32},{48,56},{56,48},{64,72... | collective-permute-start | bytes 786440 | tf_op jit(solution)/shard_map/ppermute | solution.py:29
  68.8 7.7 %collective-permute-start.8 = (f32[640,128]{1,0:T(8,128)S(1)}, f32[640,128]{1,0:T(8,128)S(1)}, u32[]{:S(2)}, u32[]{:S(2)}) collective-permute-start(f32[640,128]{1,0:T(8,128)S(1)} %get-tuple-element.117), channel_id=1, source_target_pairs={{0,8},{8,0},{16,24},{24,16},{32,40},{40,32},{48,56},{56,48},{64,72... | collective-permute-start | bytes 983048 | tf_op jit(solution)/shard_map/ppermute | solution.py:29
  70.1 6.4 %collective-permute-start.9 = (f32[512,128]{1,0:T(8,128)S(1)}, f32[512,128]{1,0:T(8,128)S(1)}, u32[]{:S(2)}, u32[]{:S(2)}) collective-permute-start(f32[512,128]{1,0:T(8,128)S(1)} %get-tuple-element.119), channel_id=1, source_target_pairs={{0,56},{8,16},{16,8},{24,32},{32,24},{40,48},{48,40},{56,0},{64,12... | collective-permute-start | bytes 786440 | tf_op jit(solution)/shard_map/ppermute | solution.py:575
  77.1 9.0 %collective-permute-start.10 = (f32[368,128]{1,0:T(8,128)S(1)}, f32[368,128]{1,0:T(8,128)S(1)}, u32[]{:S(2)}, u32[]{:S(2)}) collective-permute-start(f32[368,128]{1,0:T(8,128)S(1)} %get-tuple-element.121), channel_id=1, source_target_pairs={{0,16},{8,24},{16,0},{24,8},{32,48},{40,56},{48,32},{56,40},{64,80... | collective-permute-start | bytes 565256 | tf_op jit(solution)/shard_map/ppermute | solution.py:29
  79.0 7.1 %collective-permute-start.11 = (f32[256,128]{1,0:T(8,128)S(1)}, f32[256,128]{1,0:T(8,128)S(1)}, u32[]{:S(2)}, u32[]{:S(2)}) collective-permute-start(f32[256,128]{1,0:T(8,128)S(1)} %get-tuple-element.123), channel_id=1, source_target_pairs={{0,48},{8,56},{16,32},{24,40},{32,16},{40,24},{48,0},{56,8},{64,11... | collective-permute-start | bytes 393224 | tf_op jit(solution)/shard_map/ppermute | solution.py:29
  86.8 10.5 %collective-permute-start.12 = (f32[280,128]{1,0:T(8,128)S(1)}, f32[280,128]{1,0:T(8,128)S(1)}, u32[]{:S(2)}, u32[]{:S(2)}) collective-permute-start(f32[280,128]{1,0:T(8,128)S(1)} %get-tuple-element.126), channel_id=1, source_target_pairs={{0,48},{8,56},{16,32},{24,40},{32,16},{40,24},{48,0},{56,8},{64,11... | collective-permute-start | bytes 430088 | tf_op jit(solution)/shard_map/ppermute | solution.py:29
  88.3 5.2 %collective-permute-start.13 = (f32[128,128]{1,0:T(8,128)S(1)}, f32[128,128]{1,0:T(8,128)S(1)}, u32[]{:S(2)}, u32[]{:S(2)}) collective-permute-start(f32[128,128]{1,0:T(8,128)S(1)} %get-tuple-element.128), channel_id=1, source_target_pairs={{0,16},{8,24},{16,0},{24,8},{32,48},{40,56},{48,32},{56,40},{64,80... | collective-permute-start | bytes 196616 | tf_op jit(solution)/shard_map/ppermute | solution.py:29
  97.8 2.9 %collective-permute-start.14 = (f32[64,128]{1,0:T(8,128)S(1)}, f32[64,128]{1,0:T(8,128)S(1)}, u32[]{:S(2)}, u32[]{:S(2)}) collective-permute-start(f32[64,128]{1,0:T(8,128)S(1)} %get-tuple-element.131), channel_id=1, source_target_pairs={{0,64},{8,72},{16,80},{24,88},{32,96},{40,104},{48,112},{56,120},{... | collective-permute-start | bytes 98312 | tf_op jit(solution)/shard_map/ppermute | solution.py:29
  100.9 4.5 %collective-permute-start.15 = (f32[88,128]{1,0:T(8,128)S(1)}, f32[88,128]{1,0:T(8,128)S(1)}, u32[]{:S(2)}, u32[]{:S(2)}) collective-permute-start(f32[88,128]{1,0:T(8,128)S(1)} %pad_maximum_fusion.5), channel_id=1, source_target_pairs={{0,192},{8,200},{16,208},{24,216},{32,224},{40,232},{48,240},{56,2... | collective-permute-start | bytes 135176 | tf_op jit(solution)/shard_map/ppermute | solution.py:29
  105.5 3.1 %collective-permute-start.16 = (f32[112,128]{1,0:T(8,128)S(1)}, f32[112,128]{1,0:T(8,128)S(1)}, u32[]{:S(2)}, u32[]{:S(2)}) collective-permute-start(f32[112,128]{1,0:T(8,128)S(1)} %pad_maximum_fusion.4), channel_id=1, source_target_pairs={{0,64},{8,72},{16,80},{24,88},{32,96},{40,104},{48,112},{56,120},{... | collective-permute-start | bytes 172040 | tf_op jit(solution)/shard_map/ppermute | solution.py:29
  129.0 16.7 %collective-permute-start.17 = (f32[256,768]{1,0:T(8,128)S(1)}, f32[256,768]{1,0:T(8,128)S(1)}, u32[]{:S(2)}, u32[]{:S(2)}) collective-permute-start(f32[256,768]{1,0:T(8,128)S(1)} %get-tuple-element.142), channel_id=1, source_target_pairs={{0,1},{1,0},{2,3},{3,2},{4,5},{5,4},{6,7},{7,6},{8,9},{9,8},{10,11... | collective-permute-start | bytes 2359304 | tf_op jit(solution)/shard_map/ppermute | solution.py:29
  144.0 2.4 %collective-permute-start.18 = (f32[384,256]{1,0:T(8,128)S(1)}, f32[384,256]{1,0:T(8,128)S(1)}, u32[]{:S(2)}, u32[]{:S(2)}) collective-permute-start(f32[384,256]{1,0:T(8,128)S(1)} %pad_maximum_fusion), channel_id=1, source_target_pairs={{0,1},{1,0},{2,3},{3,2},{4,5},{5,4},{6,7},{7,6},{8,9},{9,8},{10,11... | collective-permute-start | bytes 1179656 | tf_op jit(solution)/shard_map/ppermute | solution.py:29
  170.0 2.8 %collective-permute-start.19 = (f32[8,128]{1,0:T(8,128)S(1)}, f32[8,128]{1,0:T(8,128)S(1)}, u32[]{:S(2)}, u32[]{:S(2)}) collective-permute-start(f32[8,128]{1,0:T(8,128)S(1)} %constant_dynamic-slice_fusion.1), channel_id=1, source_target_pairs={{0,2},{1,3},{2,0},{3,1},{4,6},{5,7},{6,4},{7,5},{8,10},{9,11},{10,... | collective-permute-start | bytes 12296 | tf_op jit(solution)/shard_map/ppermute | solution.py:29
  173.1 3.7 %collective-permute-start.20 = (f32[8,128]{1,0:T(8,128)S(1)}, f32[8,128]{1,0:T(8,128)S(1)}, u32[]{:S(2)}, u32[]{:S(2)}) collective-permute-start(f32[8,128]{1,0:T(8,128)S(1)} %constant_dynamic-slice_fusion), channel_id=1, source_target_pairs={{0,6},{1,7},{2,4},{3,5},{4,2},{5,3},{6,0},{7,1},{8,14},{9,15},{10,... | collective-permute-start | bytes 12296 | tf_op jit(solution)/shard_map/ppermute | solution.py:29
  176.9 2.5 %collective-permute-start.21 = (f32[8,128]{1,0:T(8,128)S(1)}, f32[8,128]{1,0:T(8,128)S(1)}, u32[]{:S(2)}, u32[]{:S(2)}) collective-permute-start(f32[8,128]{1,0:T(8,128)S(1)} %dynamic-slice_add_fusion.2), channel_id=1, source_target_pairs={{0,2},{1,3},{2,0},{3,1},{4,6},{5,7},{6,4},{7,5},{8,10},{9,11},{10,... | collective-permute-start | bytes 12296 | tf_op jit(solution)/shard_map/ppermute | solution.py:29
  199.4 9.3 %collective-permute-start.22 = (f32[256,384]{1,0:T(8,128)S(1)}, f32[256,384]{1,0:T(8,128)S(1)}, u32[]{:S(2)}, u32[]{:S(2)}) collective-permute-start(f32[256,384]{1,0:T(8,128)S(1)} %slice.94), channel_id=1, source_target_pairs={{0,1},{1,0},{2,3},{3,2},{4,5},{5,4},{6,7},{7,6},{8,9},{9,8},{10,11... | collective-permute-start | bytes 1179656 | tf_op jit(solution)/shard_map/ppermute | solution.py:29

commit v6 on v5

--- a/solution.py
+++ b/solution.py
@@ -286,14 +286,16 @@
     )
 
 
-def fourth_body(bits, c1, mine, received, value, gram, low, high, keep_a, send_a, keep_b, send_b, coef, sums):
-    count, rank = mine.shape[0], c1.shape[1]
+def fourth_body(bits, c1, c2, c3, c2_there, c3_there, value, gram, low, high, keep_a, send_a, keep_b, send_b, coef, sums):
+    count, rank = c2.shape
     for bit in range(2):
 
         @pl.when(bits[0] == bit)
         def _(bit=bit):
-            coef[bit * count : (bit + 1) * count] = mine[...].astype(jnp.bfloat16)
-            coef[(1 - bit) * count : (2 - bit) * count] = received[...].astype(jnp.bfloat16)
+            for j, (mine, received) in enumerate(((c2, c2_there), (c3, c3_there))):
+                here = slice(j * rank, (j + 1) * rank)
+                coef[bit * count : (bit + 1) * count, here] = mine[...].astype(jnp.bfloat16)
+                coef[(1 - bit) * count : (2 - bit) * count, here] = received[...].astype(jnp.bfloat16)
 
     rows, wide = value.shape[1:]
     share = rows // RING
@@ -316,14 +318,14 @@
     send_a[rows + RING // 2 * piece :] = low[...]
 
 
-def fourth(bits, c1, mine, received, value, gram, low, high):
+def fourth(bits, c1, c2, c3, c2_there, c3_there, value, gram, low, high):
     rows, rank = c1.shape
     wide = 2 * rank
     extra = high.shape[0] // 2
     return local(
         fourth_body,
         bits,
-        [c1, mine, received, value, gram, low, high],
+        [c1, c2, c3, c2_there, c3_there, value, gram, low, high],
         [
             vmem(rows + extra, rank), vmem(rows + extra + low.shape[0], rank),
             vmem(rows, rank), vmem(rows, rank), vmem(rows, wide, dtype=jnp.bfloat16),
@@ -334,56 +336,50 @@
     )
 
 
-def halve_body(steps, bits, *refs):
-    (keep_a, got_a, keep_b, got_b, low), (next_a, send_a, next_b, send_b, lows) = refs[:5], refs[5:]
-    count = keep_b.shape[0] // (2 * steps)
-    piece = (keep_a.shape[0] - keep_b.shape[0]) // (2 * steps)
-    rows = keep_b.shape[0]
-    for out, to, got, keep, far, near in (
-        (next_a, send_a, got_a, keep_a, 1, 3),
-        (next_b, send_b, got_b, keep_b, 3, 1),
-    ):
-        if steps == 2:
-            mine = [bits[6], bits[6] ^ near]
-            theirs = [bits[6] ^ far, bits[6] ^ far ^ near]
-        else:
-            mine, theirs = [0], [1]
-        for ref, slots in ((out, mine), (to, theirs)):
-            for i, slot in enumerate(slots):
-                here = pl.ds(slot * count, count)
-                ref[i * count : (i + 1) * count] = keep[here] + got[here]
-                if keep.shape[0] > rows:
-                    there = pl.ds(rows + slot * piece, piece)
-                    start = len(slots) * count + i * piece
-                    ref[start : start + piece] = keep[there] + got[there]
-    done = low.shape[0]
-    lows[:done] = low[...]
-    lows[done:] = got_a[keep_a.shape[0] :]
-    send_a[next_a.shape[0] :] = lows[...]
-
-
-def halve(bits, steps, keep_a, got_a, keep_b, got_b, low):
-    rank = low.shape[1]
-    size_a, size_b, lows = keep_a.shape[0] // 2, keep_b.shape[0] // 2, 2 * low.shape[0]
-    return local(
-        functools.partial(halve_body, steps),
-        bits,
-        [keep_a, got_a, keep_b, got_b, low],
-        [vmem(size_a, rank), vmem(size_a + lows, rank), vmem(size_b, rank), vmem(size_b, rank), vmem(lows, rank)],
-        2 * keep_a.size,
-        20 * keep_a.size,
-    )
-
-
-def gather_body(bits, keep_a, got_a, keep_b, got_b, low, own, other, fifth, gram, high):
+def halve_body(steps, far, near, bits, keep, got, *refs):
+    low, (out, send, *lows) = refs[: len(refs) // 3], refs[len(refs) // 3 :]
+    rank = keep.shape[1]
+    extra = 3 * rank // 8 * steps if low else 0
+    rows = keep.shape[0] - extra
+    count, piece = rows // (2 * steps), extra // (2 * steps)
+    if steps == 2:
+        mine, theirs = [bits[6], bits[6] ^ near], [bits[6] ^ far, bits[6] ^ far ^ near]
+    else:
+        mine, theirs = [0], [1]
+    for ref, slots in ((out, mine), (send, theirs)):
+        for i, slot in enumerate(slots):
+            here = pl.ds(slot * count, count)
+            ref[i * count : (i + 1) * count] = keep[here] + got[here]
+            if low:
+                there = pl.ds(rows + slot * piece, piece)
+                start = len(slots) * count + i * piece
+                ref[start : start + piece] = keep[there] + got[there]
+    if low:
+        done = low[0].shape[0]
+        lows[0][:done] = low[0][...]
+        lows[0][done:] = got[keep.shape[0] :]
+        send[out.shape[0] :] = lows[0][...]
+
+
+def halve(bits, steps, far, near, keep, got, *low):
+    rank, size = keep.shape[1], keep.shape[0] // 2
+    lows = [2 * v.shape[0] for v in low]
+    return local(
+        functools.partial(halve_body, steps, far, near),
+        bits,
+        [keep, got, *low],
+        [vmem(size, rank), vmem(size + sum(lows), rank)] + [vmem(v, rank) for v in lows],
+        2 * keep.size,
+        20 * keep.size,
+    )
+
+
+def fourth_rows_body(bits, keep, got, low, own, other, gram, high):
     share, rank = own.shape
     rows = 2 * share
-    total = keep_a[...] + got_a[: keep_a.shape[0]]
+    total = keep[...] + got[: keep.shape[0]]
     choose(bits[2], total[:share], total[share:rows], own, other)
     high[...] = total[rows:]
-    for j in range(2):
-        here = slice(j * share, (j + 1) * share)
-        fifth[:, j * rank : (j + 1) * rank] = keep_b[here] + got_b[here]
     count = gram.shape[0] // RING
     half_list = low.shape[0]
     z0, z1, z2 = bits[0], bits[3], bits[5]
@@ -395,22 +391,28 @@
             if start < half_list:
                 part = low[start : start + count]
             else:
-                start += keep_a.shape[0] - half_list
-                part = got_a[start : start + count]
+                start += keep.shape[0] - half_list
+                part = got[start : start + count]
             gram[pl.ds(place, count), j * rank : (j + 1) * rank] = part
 
 
-def gather_rows(bits, keep_a, got_a, keep_b, got_b, low):
-    share, rank = keep_b.shape[0] // 2, keep_b.shape[1]
-    shapes = [(share, rank), (share, rank), (share, 2 * rank), (rank, 2 * rank), (keep_a.shape[0] - 2 * share, rank)]
-    return local(
-        gather_body,
-        bits,
-        [keep_a, got_a, keep_b, got_b, low],
-        [vmem(*s) for s in shapes],
-        2 * keep_a.size,
-        20 * keep_a.size,
-    )
+def fourth_rows(bits, keep, got, low, share):
+    rank = keep.shape[1]
+    return local(
+        fourth_rows_body,
+        bits,
+        [keep, got, low],
+        [vmem(share, rank), vmem(share, rank), vmem(rank, 2 * rank), vmem(keep.shape[0] - 2 * share, rank)],
+        2 * keep.size,
+        20 * keep.size,
+    )
+
+
+def fifth_rows_body(bits, keep, got, fifth):
+    share, rank = fifth.shape[0], keep.shape[1]
+    for j in range(2):
+        here = slice(j * share, (j + 1) * share)
+        fifth[:, j * rank : (j + 1) * rank] = keep[here] + got[here]
 
 
 def sixth_body(bits, c1, c23, packed, value, gram, keep, send, coef):
@@ -567,18 +569,23 @@
     received = over_x(send, mask=6)
     c3, low = own + received[: rows // 2], low + received[rows // 2 :]
     c3 = c3 + over_x(c3, mask=2)
-    mine = jnp.concatenate([c2, c3], axis=1)
-    received = over_x(mine, mask=1)
-
-    keep_a, send_a, keep_b, send_b, c23 = fourth(bits, c1, mine, received, value_45, gram_45, low, high)
+    c2_there = over_x(c2, mask=1)
+    c3_there = over_x(c3, mask=1)
+
+    keep_a, send_a, keep_b, send_b, c23 = fourth(bits, c1, c2, c3, c2_there, c3_there, value_45, gram_45, low, high)
     turned = [(i & -RING) + ((i + 1 if i & 1 else i - 1) % RING) for i in range(size_x)]
     got_a, got_b = over_x(send_a, mask=1), lax.ppermute(send_b, "gx", list(enumerate(turned)))
-    keep_a, send_a, keep_b, send_b, low = halve(bits, 2, keep_a, got_a, keep_b, got_b, low)
-    got_a, got_b = over_x(send_a, mask=2), over_x(send_b, mask=6)
-    keep_a, send_a, keep_b, send_b, low = halve(bits, 1, keep_a, got_a, keep_b, got_b, low)
-    got_a, got_b = over_x(send_a, mask=6), over_x(send_b, mask=2)
-    own, other, left, gram_45, high = gather_rows(bits, keep_a, got_a, keep_b, got_b, low)
+    keep_a, send_a, low = halve(bits, 2, 1, 3, keep_a, got_a, low)
+    got_a = over_x(send_a, mask=2)
+    keep_b, send_b = halve(bits, 2, 3, 1, keep_b, got_b)
+    got_b = over_x(send_b, mask=6)
+    keep_a, send_a, low = halve(bits, 1, 0, 0, keep_a, got_a, low)
+    got_a = over_x(send_a, mask=6)
+    keep_b, send_b = halve(bits, 1, 0, 0, keep_b, got_b)
+    got_b = over_x(send_b, mask=2)
+    own, other, gram_45, high = fourth_rows(bits, keep_a, got_a, low, share)
     c4 = own + over_x(other, mask=8)
+    left = local(fifth_rows_body, bits, [keep_b, got_b], [vmem(share, wide)], keep_b.size, 12 * keep_b.size)[0]
     left = left - dot(c4, gram_45)
     received = over_x(jnp.concatenate([half(left, half_y1[1]), high]), mask=24)
     c5 = half(left, half_y1[0]) + received[:share]

time: 211 us -> 206 us (0.976)
  waiting for transfers between devices: 67.9 us -> 54.7 us
  starting transfers between devices: 55.8 us -> 62.1 us
    ppermute x22 -> x23, waiting for transfers between devices: 61.5 us -> 54.7 us  [swap(): lax.ppermute(value, axis, [(source, source ^ mask) for source in range(si...]
    ppermute x1, waiting for transfers between devices: 6.43 us -> 0.01 us  [shards(): lax.ppermute(send_b, 'gx', list(enumerate(turned)))]
    ppermute x22 -> x23, starting transfers between devices: 55.8 us -> 62.1 us  [swap(): lax.ppermute(value, axis, [(source, source ^ mask) for source in range(si...]
    pallas_call x14 -> x17, Pallas kernels: 15.9 us -> 17.5 us  [local(): pl.pallas_call(body, out_shape=outs, in_specs=[pl.BlockSpec(memory_space=...]
  transfers between devices with their start and end apart: 23 -> 24, of which waited for: 19 -> 17; matrix products, arithmetic and copies ran while one was open for 0% -> 0% of each run, Pallas kernels for 5% -> 6%
where the time goes in v6:
time: 206 us; the launch traced here: 205 us
  starting transfers between devices  62.1 us (30%)
  blocking collectives  60.4 us (29%)
  waiting for transfers between devices  54.7 us (27%)
  Pallas kernels  25.4 us (12%)
    ppermute x23, starting transfers between devices, swap(): lax.ppermute(value, axis, [(source, source ^ mask) for source in range(si...  62.1 us
    all_to_all x3, blocking collectives, exchange(): lax.all_to_all(value, AXES, 0, 0, tiled=True, axis_index_groups=groups)  60.4 us
    ppermute x23, waiting for transfers between devices, swap(): lax.ppermute(value, axis, [(source, source ^ mask) for source in range(si...  54.7 us
    pallas_call x17, Pallas kernels, local(): pl.pallas_call(body, out_shape=outs, in_specs=[pl.BlockSpec(memory_space=...  17.5 us
    pallas_call x1, Pallas kernels, run(): pl.pallas_call(body, out_shape=out_shape, grid_spec=pltpu.PrefetchScalarG...  5.63 us
  transfers between devices with their start and end apart: 24, of which 17 were waited for; matrix products, arithmetic and copies ran while one was open for 0% of the time, Pallas kernels for 6%

profile of v6, /device:TPU:1, one launch (start us, length us, event | category | flops | bytes accessed | tf_op | source)
XLA Modules:
  0.0 205.2 jit_solution(11646239264895801428)
XLA Ops:
  0.1 5.6 %shard_map.46 = (bf16[512,1024]{1,0:T(8,128)(2,1)S(1)}, f32[512,128]{1,0:T(8,128)S(1)}, f32[512,128]{1,0:T(8,128)S(1)}) custom-call(s32[7]{0:T(128)S(1)} %stack.31.bits, bf16[512,1024]{1,0:T(8,128)(2,1)} %rhs, bf16[1,1024,1024]{2,1,0:T(8,128)(2,1)} %inverse.1, bf16[8,256,1024]{2,1,0:T(8,128)(2,1)} %proj.5, bf16[8,256,1024]{2,1,0:T(8,128)(2,1)} %proj.5), custom_call_target="tpu_custom_call" | custom-call | flops 1342177280 | bytes 4194304 | tf_op jit(solution)/shard_map/pallas_call | solution.py:70
  5.7 2.6 %collective-permute-start = (f32[512,128]{1,0:T(8,128)S(1)}, f32[512,128]{1,0:T(8,128)S(1)}, u32[]{:S(2)}, u32[]{:S(2)}) collective-permute-start(f32[512,128]{1,0:T(8,128)S(1)} %get-tuple-element.83), channel_id=1, source_target_pairs={{0,8},{8,0},{16,24},{24,16},{32,40},{40,32},{48,56},{56,48},{64,72... | collective-permute-start | bytes 786440 | tf_op jit(solution)/shard_map/ppermute | solution.py:29
  8.3 1.9 shard_map.48
  11.9 3.0 %shard_map.49 = (f32[3,512,256]{2,1,0:T(8,128)S(1)}, bf16[3,640,256]{2,1,0:T(8,128)(2,1)S(1)}, f32[3,128,256]{2,1,0:T(8,128)S(1)}) custom-call(s32[7]{0:T(128)S(1)} %stack.31.bits, bf16[512,1024]{1,0:T(8,128)(2,1)S(1)} %get-tuple-element.84.state, bf16[8,128,1024]{2,1,0:T(8,128)(2,1)S(1)} %copy-done.1, bf16[8,256,1024]{2,1,0:T(8,128)(2,1)S(1)} %copy-done), custom_call_target="tpu_custom_call" | custom-call | flops 2013265920 | bytes 3407872 | tf_op jit(solution)/shard_map/pallas_call | solution.py:101
  17.9 2.6 %collective-permute-done.2 = f32[192,256]{1,0:T(8,128)S(1)} collective-permute-done((f32[192,256]{1,0:T(8,128)S(1)}, f32[192,256]{1,0:T(8,128)S(1)}, u32[]{:S(2)}, u32[]{:S(2)}) %collective-permute-start.2) | collective-permute-done | bytes 196640 | tf_op jit(solution)/shard_map/ppermute | solution.py:29
  20.5 2.8 %collective-permute-start.3 = (f32[96,256]{1,0:T(8,128)S(1)}, f32[96,256]{1,0:T(8,128)S(1)}, u32[]{:S(2)}, u32[]{:S(2)}) collective-permute-start(f32[96,256]{1,0:T(8,128)S(1)} %constant_dynamic-slice_fusion.5), channel_id=1, source_target_pairs={{0,192},{8,200},{16,208},{24,216},{32,224},{40,232},{48,240},{56,2... | collective-permute-start | bytes 294920 | tf_op jit(solution)/shard_map/ppermute | solution.py:29
  23.4 2.0 collective-permute-done.3
  25.4 8.3 %collective-permute-done.1.received = f32[352,512]{1,0:T(8,128)S(1)} collective-permute-done((f32[352,512]{1,0:T(8,128)S(1)}, f32[352,512]{1,0:T(8,128)S(1)}, u32[]{:S(2)}, u32[]{:S(2)}) %collective-permute-start.1) | collective-permute-done | bytes 720928 | tf_op jit(solution)/shard_map/ppermute | solution.py:29
  34.4 3.1 %collective-permute-start.4 = (f32[320,128]{1,0:T(8,128)S(1)}, f32[320,128]{1,0:T(8,128)S(1)}, u32[]{:S(2)}, u32[]{:S(2)}) collective-permute-start(f32[320,128]{1,0:T(8,128)S(1)} %get-tuple-element.103), channel_id=1, source_target_pairs={{0,16},{8,24},{16,0},{24,8},{32,48},{40,56},{48,32},{56,40},{64,80... | collective-permute-start | bytes 491528 | tf_op jit(solution)/shard_map/ppermute | solution.py:29
  37.5 7.0 %collective-permute-done.4.received = f32[320,128]{1,0:T(8,128)S(1)} collective-permute-done((f32[320,128]{1,0:T(8,128)S(1)}, f32[320,128]{1,0:T(8,128)S(1)}, u32[]{:S(2)}, u32[]{:S(2)}) %collective-permute-start.4) | collective-permute-done | bytes 163872 | tf_op jit(solution)/shard_map/ppermute | solution.py:29
  45.2 2.1 %collective-permute-start.5 = (f32[288,128]{1,0:T(8,128)S(1)}, f32[288,128]{1,0:T(8,128)S(1)}, u32[]{:S(2)}, u32[]{:S(2)}) collective-permute-start(f32[288,128]{1,0:T(8,128)S(1)} %get-tuple-element.109), channel_id=1, source_target_pairs={{0,48},{8,56},{16,32},{24,40},{32,16},{40,24},{48,0},{56,8},{64,11... | collective-permute-start | bytes 442376 | tf_op jit(solution)/shard_map/ppermute | solution.py:29
  47.2 4.2 %collective-permute-done.5 = f32[288,128]{1,0:T(8,128)S(1)} collective-permute-done((f32[288,128]{1,0:T(8,128)S(1)}, f32[288,128]{1,0:T(8,128)S(1)}, u32[]{:S(2)}, u32[]{:S(2)}) %collective-permute-start.5) | collective-permute-done | bytes 147488 | tf_op jit(solution)/shard_map/ppermute | solution.py:29
  51.5 2.6 %collective-permute-start.6 = (f32[256,128]{1,0:T(8,128)S(1)}, f32[256,128]{1,0:T(8,128)S(1)}, u32[]{:S(2)}, u32[]{:S(2)}) collective-permute-start(f32[256,128]{1,0:T(8,128)S(1)} %slice_add_fusion), channel_id=1, source_target_pairs={{0,16},{8,24},{16,0},{24,8},{32,48},{40,56},{48,32},{56,40},{64,80... | collective-permute-start | bytes 393224 | tf_op jit(solution)/shard_map/ppermute | solution.py:29
  54.1 3.5 %collective-permute-start.7 = (f32[256,128]{1,0:T(8,128)S(1)}, f32[256,128]{1,0:T(8,128)S(1)}, u32[]{:S(2)}, u32[]{:S(2)}) collective-permute-start(f32[256,128]{1,0:T(8,128)S(1)} %get-tuple-element.107.c2), channel_id=1, source_target_pairs={{0,8},{8,0},{16,24},{24,16},{32,40},{40,32},{48,56},{56,48},{64,72... | collective-permute-start | bytes 393224 | tf_op jit(solution)/shard_map/ppermute | solution.py:29
  57.6 5.3 %collective-permute-start.8 = (f32[256,128]{1,0:T(8,128)S(1)}, f32[256,128]{1,0:T(8,128)S(1)}, u32[]{:S(2)}, u32[]{:S(2)}) collective-permute-start(f32[256,128]{1,0:T(8,128)S(1)} %add.43.c3), channel_id=1, source_target_pairs={{0,8},{8,0},{16,24},{24,16},{32,40},{40,32},{48,56},{56,48},{64,72... | collective-permute-start | bytes 393224 | tf_op jit(solution)/shard_map/ppermute | solution.py:29
  62.8 2.4 %collective-permute-done.8.c3_there = f32[256,128]{1,0:T(8,128)S(1)} collective-permute-done((f32[256,128]{1,0:T(8,128)S(1)}, f32[256,128]{1,0:T(8,128)S(1)}, u32[]{:S(2)}, u32[]{:S(2)}) %collective-permute-start.8) | collective-permute-done | bytes 131104 | tf_op jit(solution)/shard_map/ppermute | solution.py:29
  67.8 4.5 %collective-permute-done.9.got = f32[640,128]{1,0:T(8,128)S(1)} collective-permute-done((f32[640,128]{1,0:T(8,128)S(1)}, f32[640,128]{1,0:T(8,128)S(1)}, u32[]{:S(2)}, u32[]{:S(2)}) %collective-permute-start.9) | collective-permute-done | bytes 327712 | tf_op jit(solution)/shard_map/ppermute | solution.py:29
  72.9 5.1 %collective-permute-start.10 = (f32[368,128]{1,0:T(8,128)S(1)}, f32[368,128]{1,0:T(8,128)S(1)}, u32[]{:S(2)}, u32[]{:S(2)}) collective-permute-start(f32[368,128]{1,0:T(8,128)S(1)} %get-tuple-element.118), channel_id=1, source_target_pairs={{0,16},{8,24},{16,0},{24,8},{32,48},{40,56},{48,32},{56,40},{64,80... | collective-permute-start | bytes 565256 | tf_op jit(solution)/shard_map/ppermute | solution.py:29
  78.7 4.3 %collective-permute-done.10.got = f32[368,128]{1,0:T(8,128)S(1)} collective-permute-done((f32[368,128]{1,0:T(8,128)S(1)}, f32[368,128]{1,0:T(8,128)S(1)}, u32[]{:S(2)}, u32[]{:S(2)}) %collective-permute-start.10) | collective-permute-done | bytes 188448 | tf_op jit(solution)/shard_map/ppermute | solution.py:29
  85.3 1.9 collective-permute-start.15
  87.1 6.1 %collective-permute-done.11.got = f32[280,128]{1,0:T(8,128)S(1)} collective-permute-done((f32[280,128]{1,0:T(8,128)S(1)}, f32[280,128]{1,0:T(8,128)S(1)}, u32[]{:S(2)}, u32[]{:S(2)}) %collective-permute-start.11) | collective-permute-done | bytes 143392 | tf_op jit(solution)/shard_map/ppermute | solution.py:29
  94.7 2.1 %collective-permute-done.12 = f32[64,128]{1,0:T(8,128)S(1)} collective-permute-done((f32[64,128]{1,0:T(8,128)S(1)}, f32[64,128]{1,0:T(8,128)S(1)}, u32[]{:S(2)}, u32[]{:S(2)}) %collective-permute-start.12) | collective-permute-done | bytes 32800 | tf_op jit(solution)/shard_map/ppermute | solution.py:29
  97.1 2.2 %collective-permute-start.16 = (f32[88,128]{1,0:T(8,128)S(1)}, f32[88,128]{1,0:T(8,128)S(1)}, u32[]{:S(2)}, u32[]{:S(2)}) collective-permute-start(f32[88,128]{1,0:T(8,128)S(1)} %pad_maximum_fusion.4), channel_id=1, source_target_pairs={{0,192},{8,200},{16,208},{24,216},{32,224},{40,232},{48,240},{56,2... | collective-permute-start | bytes 135176 | tf_op jit(solution)/shard_map/ppermute | solution.py:29
  99.3 2.0 collective-permute-done.16
  101.5 3.0 %collective-permute-done.17 = f32[112,128]{1,0:T(8,128)S(1)} collective-permute-done((f32[112,128]{1,0:T(8,128)S(1)}, f32[112,128]{1,0:T(8,128)S(1)}, u32[]{:S(2)}, u32[]{:S(2)}) %collective-permute-start.17) | collective-permute-done | bytes 57376 | tf_op jit(solution)/shard_map/ppermute | solution.py:29
  104.6 18.8 %all_to_all.15.packed = f32[8,224,128]{2,1,0:T(8,128)S(1)} all-to-all(f32[8,224,128]{2,1,0:T(8,128)S(1)} %broadcast_in_dim.6), channel_id=1, replica_groups={{0,8,16,24,32,40,48,56},{64,72,80,88,96,104,112,120},{128,136,144,152,1..., dimensions={0} | all-to-all | bytes 1835008 | tf_op jit(solution)/shard_map/all_to_all | solution.py:33
  124.8 14.4 %collective-permute-start.18 = (f32[256,768]{1,0:T(8,128)S(1)}, f32[256,768]{1,0:T(8,128)S(1)}, u32[]{:S(2)}, u32[]{:S(2)}) collective-permute-start(f32[256,768]{1,0:T(8,128)S(1)} %get-tuple-element.140), channel_id=1, source_target_pairs={{0,1},{1,0},{2,3},{3,2},{4,5},{5,4},{6,7},{7,6},{8,9},{9,8},{10,11... | collective-permute-start | bytes 2359304 | tf_op jit(solution)/shard_map/ppermute | solution.py:29
  141.7 21.8 %all_to_all.16.parts = f32[32,8,768]{2,1,0:T(8,128)S(1)} all-to-all(f32[32,8,768]{2,1,0:T(8,128)S(1)} %bitcast.25), channel_id=1, replica_groups={{0,8,16,24,32,40,48,56,64,72,80,88,96,104,112,120,128,136,144,152,160,1..., dimensions={0} | all-to-all | bytes 1572864 | tf_op jit(solution)/shard_map/all_to_all | solution.py:33
  167.9 3.1 %collective-permute-start.21 = (f32[8,128]{1,0:T(8,128)S(1)}, f32[8,128]{1,0:T(8,128)S(1)}, u32[]{:S(2)}, u32[]{:S(2)}) collective-permute-start(f32[8,128]{1,0:T(8,128)S(1)} %constant_dynamic-slice_fusion), channel_id=1, source_target_pairs={{0,6},{1,7},{2,4},{3,5},{4,2},{5,3},{6,0},{7,1},{8,14},{9,15},{10,... | collective-permute-start | bytes 12296 | tf_op jit(solution)/shard_map/ppermute | solution.py:29
  174.6 19.9 %all_to_all.17 = f32[32,8,512]{2,1,0:T(8,128)S(1)} all-to-all(f32[32,8,512]{2,1,0:T(8,128)S(1)} %broadcast_in_dim.7), channel_id=1, replica_groups={{0,8,16,24,32,40,48,56,64,72,80,88,96,104,112,120,128,136,144,152,160,1..., dimensions={0} | all-to-all | bytes 1048576 | tf_op jit(solution)/shard_map/all_to_all | solution.py:33
  194.5 6.9 %collective-permute-start.23 = (f32[256,384]{1,0:T(8,128)S(1)}, f32[256,384]{1,0:T(8,128)S(1)}, u32[]{:S(2)}, u32[]{:S(2)}) collective-permute-start(f32[256,384]{1,0:T(8,128)S(1)} %slice.94), channel_id=1, source_target_pairs={{0,1},{1,0},{2,3},{3,2},{4,5},{5,4},{6,7},{7,6},{8,9},{9,8},{10,11... | collective-permute-start | bytes 1179656 | tf_op jit(solution)/shard_map/ppermute | solution.py:29
  202.8 2.3 %shard_map.64 = f32[512,1024]{1,0:T(8,128)} custom-call(s32[7]{0:T(128)S(1)} %stack.31.bits, f32[512,1024]{1,0:T(8,128)S(1)} %shard_map.63.state, f32[256,512]{1,0:T(8,128)S(1)} %bitcast.24, f32[256,384]{1,0:T(8,128)S(1)} %collective-permute-done.23.received, bf16[8,128,1024]{2,1,0:T(8,128)(2,1)S(1)} %copy-done.1), custom_call_target="tpu_custom_call" | custom-call | flops 402653184 | bytes 3145728 | tf_op jit(solution)/shard_map/pallas_call | solution.py:508
  (85 shorter events, 27.7 us)
Async XLA Ops:
  0.1 8.2 %copy-start = (bf16[8,256,1024]{2,1,0:T(8,128)(2,1)S(1)}, bf16[8,256,1024]{2,1,0:T(8,128)(2,1)}, u32[]{:S(2)}) copy-start(bf16[8,256,1024]{2,1,0:T(8,128)(2,1)} %proj.5) | copy-start | bytes 12582916
  0.1 8.2 %copy-start.1 = (bf16[8,128,1024]{2,1,0:T(8,128)(2,1)S(1)}, bf16[8,128,1024]{2,1,0:T(8,128)(2,1)}, u32[]{:S(2)}) copy-start(bf16[8,128,1024]{2,1,0:T(8,128)(2,1)} %up.9) | copy-start | bytes 6291460
  5.7 9.2 %collective-permute-start = (f32[512,128]{1,0:T(8,128)S(1)}, f32[512,128]{1,0:T(8,128)S(1)}, u32[]{:S(2)}, u32[]{:S(2)}) collective-permute-start(f32[512,128]{1,0:T(8,128)S(1)} %get-tuple-element.83), channel_id=1, source_target_pairs={{0,8},{8,0},{16,24},{24,16},{32,40},{40,32},{48,56},{56,48},{64,72... | collective-permute-start | bytes 786440 | tf_op jit(solution)/shard_map/ppermute | solution.py:29
  14.9 5.5 %collective-permute-start.2 = (f32[192,256]{1,0:T(8,128)S(1)}, f32[192,256]{1,0:T(8,128)S(1)}, u32[]{:S(2)}, u32[]{:S(2)}) collective-permute-start(f32[192,256]{1,0:T(8,128)S(1)} %constant_dynamic-slice_fusion.6), channel_id=1, source_target_pairs={{0,64},{8,72},{16,80},{24,88},{32,96},{40,104},{48,112},{56,120},{... | collective-permute-start | bytes 589832 | tf_op jit(solution)/shard_map/ppermute | solution.py:29
  17.2 16.5 %collective-permute-start.1 = (f32[352,512]{1,0:T(8,128)S(1)}, f32[352,512]{1,0:T(8,128)S(1)}, u32[]{:S(2)}, u32[]{:S(2)}) collective-permute-start(f32[352,512]{1,0:T(8,128)S(1)} %get-tuple-element.95), channel_id=1, source_target_pairs={{0,8},{8,0},{16,24},{24,16},{32,40},{40,32},{48,56},{56,48},{64,72... | collective-permute-start | bytes 2162696 | tf_op jit(solution)/shard_map/ppermute | solution.py:29
  20.5 4.8 %collective-permute-start.3 = (f32[96,256]{1,0:T(8,128)S(1)}, f32[96,256]{1,0:T(8,128)S(1)}, u32[]{:S(2)}, u32[]{:S(2)}) collective-permute-start(f32[96,256]{1,0:T(8,128)S(1)} %constant_dynamic-slice_fusion.5), channel_id=1, source_target_pairs={{0,192},{8,200},{16,208},{24,216},{32,224},{40,232},{48,240},{56,2... | collective-permute-start | bytes 294920 | tf_op jit(solution)/shard_map/ppermute | solution.py:29
  34.4 10.1 %collective-permute-start.4 = (f32[320,128]{1,0:T(8,128)S(1)}, f32[320,128]{1,0:T(8,128)S(1)}, u32[]{:S(2)}, u32[]{:S(2)}) collective-permute-start(f32[320,128]{1,0:T(8,128)S(1)} %get-tuple-element.103), channel_id=1, source_target_pairs={{0,16},{8,24},{16,0},{24,8},{32,48},{40,56},{48,32},{56,40},{64,80... | collective-permute-start | bytes 491528 | tf_op jit(solution)/shard_map/ppermute | solution.py:29
  45.2 6.3 %collective-permute-start.5 = (f32[288,128]{1,0:T(8,128)S(1)}, f32[288,128]{1,0:T(8,128)S(1)}, u32[]{:S(2)}, u32[]{:S(2)}) collective-permute-start(f32[288,128]{1,0:T(8,128)S(1)} %get-tuple-element.109), channel_id=1, source_target_pairs={{0,48},{8,56},{16,32},{24,40},{32,16},{40,24},{48,0},{56,8},{64,11... | collective-permute-start | bytes 442376 | tf_op jit(solution)/shard_map/ppermute | solution.py:29
  51.5 6.1 %collective-permute-start.6 = (f32[256,128]{1,0:T(8,128)S(1)}, f32[256,128]{1,0:T(8,128)S(1)}, u32[]{:S(2)}, u32[]{:S(2)}) collective-permute-start(f32[256,128]{1,0:T(8,128)S(1)} %slice_add_fusion), channel_id=1, source_target_pairs={{0,16},{8,24},{16,0},{24,8},{32,48},{40,56},{48,32},{56,40},{64,80... | collective-permute-start | bytes 393224 | tf_op jit(solution)/shard_map/ppermute | solution.py:29
  54.1 8.8 %collective-permute-start.7 = (f32[256,128]{1,0:T(8,128)S(1)}, f32[256,128]{1,0:T(8,128)S(1)}, u32[]{:S(2)}, u32[]{:S(2)}) collective-permute-start(f32[256,128]{1,0:T(8,128)S(1)} %get-tuple-element.107.c2), channel_id=1, source_target_pairs={{0,8},{8,0},{16,24},{24,16},{32,40},{40,32},{48,56},{56,48},{64,72... | collective-permute-start | bytes 393224 | tf_op jit(solution)/shard_map/ppermute | solution.py:29
  57.6 7.6 %collective-permute-start.8 = (f32[256,128]{1,0:T(8,128)S(1)}, f32[256,128]{1,0:T(8,128)S(1)}, u32[]{:S(2)}, u32[]{:S(2)}) collective-permute-start(f32[256,128]{1,0:T(8,128)S(1)} %add.43.c3), channel_id=1, source_target_pairs={{0,8},{8,0},{16,24},{24,16},{32,40},{40,32},{48,56},{56,48},{64,72... | collective-permute-start | bytes 393224 | tf_op jit(solution)/shard_map/ppermute | solution.py:29
  66.3 6.0 %collective-permute-start.9 = (f32[640,128]{1,0:T(8,128)S(1)}, f32[640,128]{1,0:T(8,128)S(1)}, u32[]{:S(2)}, u32[]{:S(2)}) collective-permute-start(f32[640,128]{1,0:T(8,128)S(1)} %get-tuple-element.116), channel_id=1, source_target_pairs={{0,8},{8,0},{16,24},{24,16},{32,40},{40,32},{48,56},{56,48},{64,72... | collective-permute-start | bytes 983048 | tf_op jit(solution)/shard_map/ppermute | solution.py:29
  67.8 10.2 %collective-permute-start.13 = (f32[512,128]{1,0:T(8,128)S(1)}, f32[512,128]{1,0:T(8,128)S(1)}, u32[]{:S(2)}, u32[]{:S(2)}) collective-permute-start(f32[512,128]{1,0:T(8,128)S(1)} %get-tuple-element.126), channel_id=1, source_target_pairs={{0,56},{8,16},{16,8},{24,32},{32,24},{40,48},{48,40},{56,0},{64,12... | collective-permute-start | bytes 786440 | tf_op jit(solution)/shard_map/ppermute | solution.py:577
  72.9 10.1 %collective-permute-start.10 = (f32[368,128]{1,0:T(8,128)S(1)}, f32[368,128]{1,0:T(8,128)S(1)}, u32[]{:S(2)}, u32[]{:S(2)}) collective-permute-start(f32[368,128]{1,0:T(8,128)S(1)} %get-tuple-element.118), channel_id=1, source_target_pairs={{0,16},{8,24},{16,0},{24,8},{32,48},{40,56},{48,32},{56,40},{64,80... | collective-permute-start | bytes 565256 | tf_op jit(solution)/shard_map/ppermute | solution.py:29
  78.6 6.1 %collective-permute-start.14 = (f32[256,128]{1,0:T(8,128)S(1)}, f32[256,128]{1,0:T(8,128)S(1)}, u32[]{:S(2)}, u32[]{:S(2)}) collective-permute-start(f32[256,128]{1,0:T(8,128)S(1)} %get-tuple-element.128), channel_id=1, source_target_pairs={{0,48},{8,56},{16,32},{24,40},{32,16},{40,24},{48,0},{56,8},{64,11... | collective-permute-start | bytes 393224 | tf_op jit(solution)/shard_map/ppermute | solution.py:29
  83.5 9.7 %collective-permute-start.11 = (f32[280,128]{1,0:T(8,128)S(1)}, f32[280,128]{1,0:T(8,128)S(1)}, u32[]{:S(2)}, u32[]{:S(2)}) collective-permute-start(f32[280,128]{1,0:T(8,128)S(1)} %get-tuple-element.121), channel_id=1, source_target_pairs={{0,48},{8,56},{16,32},{24,40},{32,16},{40,24},{48,0},{56,8},{64,11... | collective-permute-start | bytes 430088 | tf_op jit(solution)/shard_map/ppermute | solution.py:29
  85.3 8.9 %collective-permute-start.15 = (f32[128,128]{1,0:T(8,128)S(1)}, f32[128,128]{1,0:T(8,128)S(1)}, u32[]{:S(2)}, u32[]{:S(2)}) collective-permute-start(f32[128,128]{1,0:T(8,128)S(1)} %get-tuple-element.130), channel_id=1, source_target_pairs={{0,16},{8,24},{16,0},{24,8},{32,48},{40,56},{48,32},{56,40},{64,80... | collective-permute-start | bytes 196616 | tf_op jit(solution)/shard_map/ppermute | solution.py:29
  93.8 3.0 %collective-permute-start.12 = (f32[64,128]{1,0:T(8,128)S(1)}, f32[64,128]{1,0:T(8,128)S(1)}, u32[]{:S(2)}, u32[]{:S(2)}) collective-permute-start(f32[64,128]{1,0:T(8,128)S(1)} %get-tuple-element.124), channel_id=1, source_target_pairs={{0,64},{8,72},{16,80},{24,88},{32,96},{40,104},{48,112},{56,120},{... | collective-permute-start | bytes 98312 | tf_op jit(solution)/shard_map/ppermute | solution.py:29
  97.1 4.2 %collective-permute-start.16 = (f32[88,128]{1,0:T(8,128)S(1)}, f32[88,128]{1,0:T(8,128)S(1)}, u32[]{:S(2)}, u32[]{:S(2)}) collective-permute-start(f32[88,128]{1,0:T(8,128)S(1)} %pad_maximum_fusion.4), channel_id=1, source_target_pairs={{0,192},{8,200},{16,208},{24,216},{32,224},{40,232},{48,240},{56,2... | collective-permute-start | bytes 135176 | tf_op jit(solution)/shard_map/ppermute | solution.py:29
  101.4 3.1 %collective-permute-start.17 = (f32[112,128]{1,0:T(8,128)S(1)}, f32[112,128]{1,0:T(8,128)S(1)}, u32[]{:S(2)}, u32[]{:S(2)}) collective-permute-start(f32[112,128]{1,0:T(8,128)S(1)} %pad_maximum_fusion.3), channel_id=1, source_target_pairs={{0,64},{8,72},{16,80},{24,88},{32,96},{40,104},{48,112},{56,120},{... | collective-permute-start | bytes 172040 | tf_op jit(solution)/shard_map/ppermute | solution.py:29
  124.8 16.3 %collective-permute-start.18 = (f32[256,768]{1,0:T(8,128)S(1)}, f32[256,768]{1,0:T(8,128)S(1)}, u32[]{:S(2)}, u32[]{:S(2)}) collective-permute-start(f32[256,768]{1,0:T(8,128)S(1)} %get-tuple-element.140), channel_id=1, source_target_pairs={{0,1},{1,0},{2,3},{3,2},{4,5},{5,4},{6,7},{7,6},{8,9},{9,8},{10,11... | collective-permute-start | bytes 2359304 | tf_op jit(solution)/shard_map/ppermute | solution.py:29
  139.3 2.4 %collective-permute-start.19 = (f32[384,256]{1,0:T(8,128)S(1)}, f32[384,256]{1,0:T(8,128)S(1)}, u32[]{:S(2)}, u32[]{:S(2)}) collective-permute-start(f32[384,256]{1,0:T(8,128)S(1)} %pad_maximum_fusion), channel_id=1, source_target_pairs={{0,1},{1,0},{2,3},{3,2},{4,5},{5,4},{6,7},{7,6},{8,9},{9,8},{10,11... | collective-permute-start | bytes 1179656 | tf_op jit(solution)/shard_map/ppermute | solution.py:29
  164.8 2.8 %collective-permute-start.20 = (f32[8,128]{1,0:T(8,128)S(1)}, f32[8,128]{1,0:T(8,128)S(1)}, u32[]{:S(2)}, u32[]{:S(2)}) collective-permute-start(f32[8,128]{1,0:T(8,128)S(1)} %constant_dynamic-slice_fusion.1), channel_id=1, source_target_pairs={{0,2},{1,3},{2,0},{3,1},{4,6},{5,7},{6,4},{7,5},{8,10},{9,11},{10,... | collective-permute-start | bytes 12296 | tf_op jit(solution)/shard_map/ppermute | solution.py:29
  167.9 4.1 %collective-permute-start.21 = (f32[8,128]{1,0:T(8,128)S(1)}, f32[8,128]{1,0:T(8,128)S(1)}, u32[]{:S(2)}, u32[]{:S(2)}) collective-permute-start(f32[8,128]{1,0:T(8,128)S(1)} %constant_dynamic-slice_fusion), channel_id=1, source_target_pairs={{0,6},{1,7},{2,4},{3,5},{4,2},{5,3},{6,0},{7,1},{8,14},{9,15},{10,... | collective-permute-start | bytes 12296 | tf_op jit(solution)/shard_map/ppermute | solution.py:29
  172.1 2.5 %collective-permute-start.22 = (f32[8,128]{1,0:T(8,128)S(1)}, f32[8,128]{1,0:T(8,128)S(1)}, u32[]{:S(2)}, u32[]{:S(2)}) collective-permute-start(f32[8,128]{1,0:T(8,128)S(1)} %dynamic-slice_add_fusion.2), channel_id=1, source_target_pairs={{0,2},{1,3},{2,0},{3,1},{4,6},{5,7},{6,4},{7,5},{8,10},{9,11},{10,... | collective-permute-start | bytes 12296 | tf_op jit(solution)/shard_map/ppermute | solution.py:29
  194.5 8.2 %collective-permute-start.23 = (f32[256,384]{1,0:T(8,128)S(1)}, f32[256,384]{1,0:T(8,128)S(1)}, u32[]{:S(2)}, u32[]{:S(2)}) collective-permute-start(f32[256,384]{1,0:T(8,128)S(1)} %slice.94), channel_id=1, source_target_pairs={{0,1},{1,0},{2,3},{3,2},{4,5},{5,4},{6,7},{7,6},{8,9},{9,8},{10,11... | collective-permute-start | bytes 1179656 | tf_op jit(solution)/shard_map/ppermute | solution.py:29

commit v7 on v6

--- a/solution.py
+++ b/solution.py
@@ -190,23 +190,16 @@
                 send[:count, i * wide : (i + 1) * wide] = part[(1 - bit) * count : (2 - bit) * count]
 
 
-def second_body(bits, mine, received, value, gram, pair, ring, keep, send, coef):
+def second_body(bits, mine, received, value, gram, pair, ring, keep_2, send_2, keep_3, send_3, coef):
     c1 = (mine[...] + received[...]).astype(jnp.bfloat16)
     coef[...] = c1
-    rows, rank = keep.shape[0] - 3 * pair.shape[1] // 4, mine.shape[1]
-    count, wide = pair.shape[1] // 2, 2 * rank
-    emit_halves(bits[0], [value[i] - dot(c1, gram[i]) for i in range(2)], keep, send)
-    for ref in (keep, send):
-        for j in range(2):
-            ref[rows : rows + count, j * wide : (j + 1) * wide] = pair[0, j * count : (j + 1) * count]
-    for bit in range(2):
-
-        @pl.when(bits[0] == bit)
-        def _(bit=bit):
-            for ref, first in ((keep, bit * count), (send, (1 - bit) * count)):
-                for j in range(2):
-                    start = first + j * count // 2
-                    ref[rows + count :, j * wide : (j + 1) * wide] = ring[0, start : start + count // 2]
+    rows, count = keep_2.shape[0] - pair.shape[1] // 2, pair.shape[1] // 2
+    emit_halves(bits[0], [value[0] - dot(c1, gram[0])], keep_2, send_2)
+    emit_halves(bits[0], [value[1] - dot(c1, gram[1])], keep_3, send_3)
+    for ref in (keep_3, send_3):
+        ref[rows:] = pair[0]
+    for ref, which in ((keep_2, bits[0]), (send_2, 1 - bits[0])):
+        ref[rows:] = ring[0, pl.ds(pl.multiple_of(which * count, count), count)]
 
 
 def second(bits, mine, received, value, gram, pair, ring):
@@ -216,7 +209,7 @@
         second_body,
         bits,
         [mine, received, value, gram, pair, ring],
-        [vmem(rows // 2 + 3 * rank // 4, 2 * wide)] * 2 + [vmem(rows, rank, dtype=jnp.bfloat16)],
+        [vmem((rows + rank) // 2, wide)] * 2 + [vmem(rows // 2 + rank, wide)] * 2 + [vmem(rows, rank, dtype=jnp.bfloat16)],
         4 * rows * rank * wide,
         16 * rows * wide,
     )
@@ -235,51 +228,46 @@
     return jnp.concatenate([value[:, :rank], value[:, rank:]], axis=0)
 
 
-def third_body(bits, keep, received, own, send, low, left, gram):
+def third_body(bits, keep, received, own, send, low):
     total = keep[...] + received[...]
     rows, rank = own.shape
-    wide, count = 2 * rank, gram.shape[0] // 2
-    choose(bits[3], total[:rows, :rank], total[:rows, rank:wide], own, send.at[:rows])
-    tail = total[rows + count :]
-    choose(bits[4], stack(tail[:, :wide], rank), stack(tail[:, wide:], rank), low, send.at[rows:])
-    left[...] = total[:rows, wide:]
-    for j in range(2):
-        gram[j * count : (j + 1) * count] = total[rows : rows + count, j * wide : (j + 1) * wide].astype(jnp.bfloat16)
-
-
-def third(bits, keep, received, rank):
-    rows = keep.shape[0] - 3 * rank // 4
+    count = low.shape[0] // 2
+    choose(bits[3], total[:rows, :rank], total[:rows, rank:], own, send.at[:rows])
+    choose(bits[4], stack(total[rows : rows + count], rank), stack(total[rows + count :], rank), low, send.at[rows:])
+
+
+def third(bits, keep, received):
+    rank = keep.shape[1] // 2
+    rows = keep.shape[0] - rank // 2
     return local(
         third_body,
         bits,
         [keep, received],
-        [
-            vmem(rows, rank), vmem(rows + rank // 2, rank), vmem(rank // 2, rank),
-            vmem(rows, 2 * rank), vmem(rank, 2 * rank, dtype=jnp.bfloat16),
-        ],
+        [vmem(rows, rank), vmem(rows + rank // 2, rank), vmem(rank // 2, rank)],
         keep.size,
         12 * keep.size,
     )
 
 
-def correct_body(bits, own, received, low, left, gram, coef, mine, send, kept):
+def correct_body(bits, own, received, low, keep, left, coef, mine, send, kept):
     rows, rank = own.shape
     count = low.shape[0] // 4
     c2 = own[...] + received[:rows]
     coef[...] = c2
-    rest = left[...] - dot(c2.astype(jnp.bfloat16), gram[...])
+    total = keep[...] + left[...]
+    rest = total[:rows] - dot(c2.astype(jnp.bfloat16), total[rows:].astype(jnp.bfloat16))
     choose(bits[5], rest[:, :rank], rest[:, rank:], mine, send.at[:rows])
     total = low[...] + received[rows:]
     parts = [jnp.concatenate([total[i * count : (i + 1) * count], total[(i + 2) * count : (i + 3) * count]]) for i in range(2)]
     choose(bits[5], parts[0], parts[1], kept, send.at[rows:])
 
 
-def correct(bits, own, received, low, left, gram):
+def correct(bits, own, received, low, keep, left):
     rows, rank = own.shape
     return local(
         correct_body,
         bits,
-        [own, received, low, left, gram],
+        [own, received, low, keep, left],
         [vmem(rows, rank), vmem(rows, rank), vmem(rows + rank // 4, rank), vmem(rank // 4, rank)],
         4 * rows * rank * rank,
         20 * rows * rank,
@@ -556,16 +544,17 @@
     value_678, gram_678, kept_678 = project((6, 7, 8), ((6, 7), (6, 8), (7, 8)), bits, state, up_basis, projection)
     received, kept, kept_45, kept_678 = lax.optimization_barrier((received, kept, kept_45, kept_678))
 
-    keep, send, c1 = second(bits, own, received, value, gram, kept, kept_45)
+    keep, send, keep_3, send_3, c1 = second(bits, own, received, value, gram, kept, kept_45)
     received = over_x(send, mask=1)
+    left = over_x(send_3, mask=1)
     high, high_send = split(kept_678.reshape(3 * rank, wide), by_y01)
     high, high_send = split(high + over_x(high_send, mask=8), by_y1)
     high = high + over_x(high_send, mask=24)
     high = jnp.concatenate([high[:, :rank], high[:, rank:]])
 
-    received, high = lax.optimization_barrier((received, high))
-    own, send, low, left, gram_23 = third(bits, keep, received, rank)
-    c2, own, send, low = correct(bits, own, over_x(send, mask=2), low, left, gram_23)
+    own, send, low = third(bits, keep, received)
+    left, high = lax.optimization_barrier((left, high))
+    c2, own, send, low = correct(bits, own, over_x(send, mask=2), low, keep_3, left)
     received = over_x(send, mask=6)
     c3, low = own + received[: rows // 2], low + received[rows // 2 :]
     c3 = c3 + over_x(c3, mask=2)

time: 206 us -> 202 us (0.981)
  blocking collectives: 60.4 us -> 66.2 us
  starting transfers between devices: 62.1 us -> 56.6 us
  waiting for transfers between devices: 54.7 us -> 50.4 us
    ppermute x23 -> x24, starting transfers between devices: 62.1 us -> 52.8 us  [swap(): lax.ppermute(value, axis, [(source, source ^ mask) for source in range(si...]
    all_to_all x3, blocking collectives: 60.4 us -> 66.2 us  [exchange(): lax.all_to_all(value, AXES, 0, 0, tiled=True, axis_index_groups=groups)]
    ppermute x23 -> x24, waiting for transfers between devices: 54.7 us -> 50.4 us  [swap(): lax.ppermute(value, axis, [(source, source ^ mask) for source in range(si...]
    ppermute x1, starting transfers between devices: 0.01 us -> 3.78 us  [shards(): lax.ppermute(send_b, 'gx', list(enumerate(turned)))]
  transfers between devices with their start and end apart: 24 -> 25, of which waited for: 17 -> 19; matrix products, arithmetic and copies ran while one was open for 0% -> 0% of each run, Pallas kernels for 6% -> 7%
where the time goes in v7:
time: 202 us; the launch traced here: 201 us
  blocking collectives  66.2 us (33%)
  starting transfers between devices  56.6 us (28%)
  waiting for transfers between devices  50.4 us (25%)
  Pallas kernels  25.6 us (13%)
    all_to_all x3, blocking collectives, exchange(): lax.all_to_all(value, AXES, 0, 0, tiled=True, axis_index_groups=groups)  66.2 us
    ppermute x24, starting transfers between devices, swap(): lax.ppermute(value, axis, [(source, source ^ mask) for source in range(si...  52.8 us
    ppermute x24, waiting for transfers between devices, swap(): lax.ppermute(value, axis, [(source, source ^ mask) for source in range(si...  50.4 us
    pallas_call x17, Pallas kernels, local(): pl.pallas_call(body, out_shape=outs, in_specs=[pl.BlockSpec(memory_space=...  17.7 us
    pallas_call x1, Pallas kernels, run(): pl.pallas_call(body, out_shape=out_shape, grid_spec=pltpu.PrefetchScalarG...  5.63 us
  transfers between devices with their start and end apart: 25, of which 19 were waited for; matrix products, arithmetic and copies ran while one was open for 0% of the time, Pallas kernels for 7%

profile of v7, /device:TPU:1, one launch (start us, length us, event | category | flops | bytes accessed | tf_op | source)
XLA Modules:
  0.0 201.4 jit_solution(6222264106423884008)
XLA Ops:
  0.1 5.6 %shard_map.46 = (bf16[512,1024]{1,0:T(8,128)(2,1)S(1)}, f32[512,128]{1,0:T(8,128)S(1)}, f32[512,128]{1,0:T(8,128)S(1)}) custom-call(s32[7]{0:T(128)S(1)} %stack.31.bits, bf16[512,1024]{1,0:T(8,128)(2,1)} %rhs, bf16[1,1024,1024]{2,1,0:T(8,128)(2,1)} %inverse.1, bf16[8,256,1024]{2,1,0:T(8,128)(2,1)} %proj.5, bf16[8,256,1024]{2,1,0:T(8,128)(2,1)} %proj.5), custom_call_target="tpu_custom_call" | custom-call | flops 1342177280 | bytes 4194304 | tf_op jit(solution)/shard_map/pallas_call | solution.py:70
  5.7 2.6 %collective-permute-start = (f32[512,128]{1,0:T(8,128)S(1)}, f32[512,128]{1,0:T(8,128)S(1)}, u32[]{:S(2)}, u32[]{:S(2)}) collective-permute-start(f32[512,128]{1,0:T(8,128)S(1)} %get-tuple-element.83), channel_id=1, source_target_pairs={{0,8},{8,0},{16,24},{24,16},{32,40},{40,32},{48,56},{56,48},{64,72... | collective-permute-start | bytes 786440 | tf_op jit(solution)/shard_map/ppermute | solution.py:29
  8.3 1.9 shard_map.48
  10.2 1.7 shard_map.47
  11.9 3.0 %shard_map.49 = (f32[3,512,256]{2,1,0:T(8,128)S(1)}, bf16[3,640,256]{2,1,0:T(8,128)(2,1)S(1)}, f32[3,128,256]{2,1,0:T(8,128)S(1)}) custom-call(s32[7]{0:T(128)S(1)} %stack.31.bits, bf16[512,1024]{1,0:T(8,128)(2,1)S(1)} %get-tuple-element.84.state, bf16[8,128,1024]{2,1,0:T(8,128)(2,1)S(1)} %copy-done.1, bf16[8,256,1024]{2,1,0:T(8,128)(2,1)S(1)} %copy-done), custom_call_target="tpu_custom_call" | custom-call | flops 2013265920 | bytes 3407872 | tf_op jit(solution)/shard_map/pallas_call | solution.py:101
  18.1 2.4 %collective-permute-done.4 = f32[192,256]{1,0:T(8,128)S(1)} collective-permute-done((f32[192,256]{1,0:T(8,128)S(1)}, f32[192,256]{1,0:T(8,128)S(1)}, u32[]{:S(2)}, u32[]{:S(2)}) %collective-permute-start.4) | collective-permute-done | bytes 196640 | tf_op jit(solution)/shard_map/ppermute | solution.py:29
  20.5 2.8 %collective-permute-start.5 = (f32[96,256]{1,0:T(8,128)S(1)}, f32[96,256]{1,0:T(8,128)S(1)}, u32[]{:S(2)}, u32[]{:S(2)}) collective-permute-start(f32[96,256]{1,0:T(8,128)S(1)} %constant_dynamic-slice_fusion.5), channel_id=1, source_target_pairs={{0,192},{8,200},{16,208},{24,216},{32,224},{40,232},{48,240},{56,2... | collective-permute-start | bytes 294920 | tf_op jit(solution)/shard_map/ppermute | solution.py:29
  23.4 2.0 collective-permute-done.5
  26.1 3.1 %collective-permute-start.2 = (f32[320,128]{1,0:T(8,128)S(1)}, f32[320,128]{1,0:T(8,128)S(1)}, u32[]{:S(2)}, u32[]{:S(2)}) collective-permute-start(f32[320,128]{1,0:T(8,128)S(1)} %get-tuple-element.97), channel_id=1, source_target_pairs={{0,16},{8,24},{16,0},{24,8},{32,48},{40,56},{48,32},{56,40},{64,80... | collective-permute-start | bytes 491528 | tf_op jit(solution)/shard_map/ppermute | solution.py:29
  29.2 8.5 %collective-permute-done.3.left = f32[384,256]{1,0:T(8,128)S(1)} collective-permute-done((f32[384,256]{1,0:T(8,128)S(1)}, f32[384,256]{1,0:T(8,128)S(1)}, u32[]{:S(2)}, u32[]{:S(2)}) %collective-permute-start.3) | collective-permute-done | bytes 393248 | tf_op jit(solution)/shard_map/ppermute | solution.py:29
  38.5 5.5 %collective-permute-start.6 = (f32[288,128]{1,0:T(8,128)S(1)}, f32[288,128]{1,0:T(8,128)S(1)}, u32[]{:S(2)}, u32[]{:S(2)}) collective-permute-start(f32[288,128]{1,0:T(8,128)S(1)} %get-tuple-element.109), channel_id=1, source_target_pairs={{0,48},{8,56},{16,32},{24,40},{32,16},{40,24},{48,0},{56,8},{64,11... | collective-permute-start | bytes 442376 | tf_op jit(solution)/shard_map/ppermute | solution.py:29
  44.0 5.7 %collective-permute-done.6 = f32[288,128]{1,0:T(8,128)S(1)} collective-permute-done((f32[288,128]{1,0:T(8,128)S(1)}, f32[288,128]{1,0:T(8,128)S(1)}, u32[]{:S(2)}, u32[]{:S(2)}) %collective-permute-start.6) | collective-permute-done | bytes 147488 | tf_op jit(solution)/shard_map/ppermute | solution.py:29
  52.2 2.5 %collective-permute-done.7 = f32[256,128]{1,0:T(8,128)S(1)} collective-permute-done((f32[256,128]{1,0:T(8,128)S(1)}, f32[256,128]{1,0:T(8,128)S(1)}, u32[]{:S(2)}, u32[]{:S(2)}) %collective-permute-start.7) | collective-permute-done | bytes 131104 | tf_op jit(solution)/shard_map/ppermute | solution.py:29
  54.7 2.3 %collective-permute-start.9 = (f32[256,128]{1,0:T(8,128)S(1)}, f32[256,128]{1,0:T(8,128)S(1)}, u32[]{:S(2)}, u32[]{:S(2)}) collective-permute-start(f32[256,128]{1,0:T(8,128)S(1)} %add.43.c3), channel_id=1, source_target_pairs={{0,8},{8,0},{16,24},{24,16},{32,40},{40,32},{48,56},{56,48},{64,72... | collective-permute-start | bytes 393224 | tf_op jit(solution)/shard_map/ppermute | solution.py:29
  57.0 3.2 %collective-permute-done.9.c3_there = f32[256,128]{1,0:T(8,128)S(1)} collective-permute-done((f32[256,128]{1,0:T(8,128)S(1)}, f32[256,128]{1,0:T(8,128)S(1)}, u32[]{:S(2)}, u32[]{:S(2)}) %collective-permute-start.9) | collective-permute-done | bytes 131104 | tf_op jit(solution)/shard_map/ppermute | solution.py:29
  62.0 3.8 %collective-permute-start.14 = (f32[512,128]{1,0:T(8,128)S(1)}, f32[512,128]{1,0:T(8,128)S(1)}, u32[]{:S(2)}, u32[]{:S(2)}) collective-permute-start(f32[512,128]{1,0:T(8,128)S(1)} %get-tuple-element.126), channel_id=1, source_target_pairs={{0,56},{8,16},{16,8},{24,32},{32,24},{40,48},{48,40},{56,0},{64,12... | collective-permute-start | bytes 786440 | tf_op jit(solution)/shard_map/ppermute | solution.py:566
  65.8 1.9 collective-permute-done.10.got
  68.3 4.6 %collective-permute-start.11 = (f32[368,128]{1,0:T(8,128)S(1)}, f32[368,128]{1,0:T(8,128)S(1)}, u32[]{:S(2)}, u32[]{:S(2)}) collective-permute-start(f32[368,128]{1,0:T(8,128)S(1)} %get-tuple-element.118), channel_id=1, source_target_pairs={{0,16},{8,24},{16,0},{24,8},{32,48},{40,56},{48,32},{56,40},{64,80... | collective-permute-start | bytes 565256 | tf_op jit(solution)/shard_map/ppermute | solution.py:29
  73.6 4.4 %collective-permute-done.11.got = f32[368,128]{1,0:T(8,128)S(1)} collective-permute-done((f32[368,128]{1,0:T(8,128)S(1)}, f32[368,128]{1,0:T(8,128)S(1)}, u32[]{:S(2)}, u32[]{:S(2)}) %collective-permute-start.11) | collective-permute-done | bytes 188448 | tf_op jit(solution)/shard_map/ppermute | solution.py:29
  78.8 2.6 %collective-permute-done.15.got = f32[256,128]{1,0:T(8,128)S(1)} collective-permute-done((f32[256,128]{1,0:T(8,128)S(1)}, f32[256,128]{1,0:T(8,128)S(1)}, u32[]{:S(2)}, u32[]{:S(2)}) %collective-permute-start.15) | collective-permute-done | bytes 131104 | tf_op jit(solution)/shard_map/ppermute | solution.py:29
  82.3 3.2 %collective-permute-done.12.got = f32[280,128]{1,0:T(8,128)S(1)} collective-permute-done((f32[280,128]{1,0:T(8,128)S(1)}, f32[280,128]{1,0:T(8,128)S(1)}, u32[]{:S(2)}, u32[]{:S(2)}) %collective-permute-start.12) | collective-permute-done | bytes 143392 | tf_op jit(solution)/shard_map/ppermute | solution.py:29
  86.8 2.5 %collective-permute-done.13 = f32[64,128]{1,0:T(8,128)S(1)} collective-permute-done((f32[64,128]{1,0:T(8,128)S(1)}, f32[64,128]{1,0:T(8,128)S(1)}, u32[]{:S(2)}, u32[]{:S(2)}) %collective-permute-start.13) | collective-permute-done | bytes 32800 | tf_op jit(solution)/shard_map/ppermute | solution.py:29
  89.5 2.2 %collective-permute-start.17 = (f32[88,128]{1,0:T(8,128)S(1)}, f32[88,128]{1,0:T(8,128)S(1)}, u32[]{:S(2)}, u32[]{:S(2)}) collective-permute-start(f32[88,128]{1,0:T(8,128)S(1)} %pad_maximum_fusion.4), channel_id=1, source_target_pairs={{0,192},{8,200},{16,208},{24,216},{32,224},{40,232},{48,240},{56,2... | collective-permute-start | bytes 135176 | tf_op jit(solution)/shard_map/ppermute | solution.py:29
  91.7 2.0 collective-permute-done.17
  93.9 3.0 %collective-permute-done.18 = f32[112,128]{1,0:T(8,128)S(1)} collective-permute-done((f32[112,128]{1,0:T(8,128)S(1)}, f32[112,128]{1,0:T(8,128)S(1)}, u32[]{:S(2)}, u32[]{:S(2)}) %collective-permute-start.18) | collective-permute-done | bytes 57376 | tf_op jit(solution)/shard_map/ppermute | solution.py:29
  97.0 23.0 %all_to_all.15.packed = f32[8,224,128]{2,1,0:T(8,128)S(1)} all-to-all(f32[8,224,128]{2,1,0:T(8,128)S(1)} %broadcast_in_dim.6), channel_id=1, replica_groups={{0,8,16,24,32,40,48,56},{64,72,80,88,96,104,112,120},{128,136,144,152,1..., dimensions={0} | all-to-all | bytes 1835008 | tf_op jit(solution)/shard_map/all_to_all | solution.py:33
  121.5 11.6 %collective-permute-start.19 = (f32[256,768]{1,0:T(8,128)S(1)}, f32[256,768]{1,0:T(8,128)S(1)}, u32[]{:S(2)}, u32[]{:S(2)}) collective-permute-start(f32[256,768]{1,0:T(8,128)S(1)} %get-tuple-element.140), channel_id=1, source_target_pairs={{0,1},{1,0},{2,3},{3,2},{4,5},{5,4},{6,7},{7,6},{8,9},{9,8},{10,11... | collective-permute-start | bytes 2359304 | tf_op jit(solution)/shard_map/ppermute | solution.py:29
  135.7 23.3 %all_to_all.16.parts = f32[32,8,768]{2,1,0:T(8,128)S(1)} all-to-all(f32[32,8,768]{2,1,0:T(8,128)S(1)} %bitcast.25), channel_id=1, replica_groups={{0,8,16,24,32,40,48,56,64,72,80,88,96,104,112,120,128,136,144,152,160,1..., dimensions={0} | all-to-all | bytes 1572864 | tf_op jit(solution)/shard_map/all_to_all | solution.py:33
  163.3 2.6 %collective-permute-start.22 = (f32[8,128]{1,0:T(8,128)S(1)}, f32[8,128]{1,0:T(8,128)S(1)}, u32[]{:S(2)}, u32[]{:S(2)}) collective-permute-start(f32[8,128]{1,0:T(8,128)S(1)} %constant_dynamic-slice_fusion), channel_id=1, source_target_pairs={{0,6},{1,7},{2,4},{3,5},{4,2},{5,3},{6,0},{7,1},{8,14},{9,15},{10,... | collective-permute-start | bytes 12296 | tf_op jit(solution)/shard_map/ppermute | solution.py:29
  169.6 19.9 %all_to_all.17 = f32[32,8,512]{2,1,0:T(8,128)S(1)} all-to-all(f32[32,8,512]{2,1,0:T(8,128)S(1)} %broadcast_in_dim.7), channel_id=1, replica_groups={{0,8,16,24,32,40,48,56,64,72,80,88,96,104,112,120,128,136,144,152,160,1..., dimensions={0} | all-to-all | bytes 1048576 | tf_op jit(solution)/shard_map/all_to_all | solution.py:33
  189.6 8.0 %collective-permute-start.24 = (f32[256,384]{1,0:T(8,128)S(1)}, f32[256,384]{1,0:T(8,128)S(1)}, u32[]{:S(2)}, u32[]{:S(2)}) collective-permute-start(f32[256,384]{1,0:T(8,128)S(1)} %slice.94), channel_id=1, source_target_pairs={{0,1},{1,0},{2,3},{3,2},{4,5},{5,4},{6,7},{7,6},{8,9},{9,8},{10,11... | collective-permute-start | bytes 1179656 | tf_op jit(solution)/shard_map/ppermute | solution.py:29
  198.9 2.3 %shard_map.64 = f32[512,1024]{1,0:T(8,128)} custom-call(s32[7]{0:T(128)S(1)} %stack.31.bits, f32[512,1024]{1,0:T(8,128)S(1)} %shard_map.63.state, f32[256,512]{1,0:T(8,128)S(1)} %bitcast.24, f32[256,384]{1,0:T(8,128)S(1)} %collective-permute-done.24.received, bf16[8,128,1024]{2,1,0:T(8,128)(2,1)S(1)} %copy-done.1), custom_call_target="tpu_custom_call" | custom-call | flops 402653184 | bytes 3145728 | tf_op jit(solution)/shard_map/pallas_call | solution.py:496
  (87 shorter events, 27.3 us)
Async XLA Ops:
  0.1 8.2 %copy-start = (bf16[8,256,1024]{2,1,0:T(8,128)(2,1)S(1)}, bf16[8,256,1024]{2,1,0:T(8,128)(2,1)}, u32[]{:S(2)}) copy-start(bf16[8,256,1024]{2,1,0:T(8,128)(2,1)} %proj.5) | copy-start | bytes 12582916
  0.1 8.2 %copy-start.1 = (bf16[8,128,1024]{2,1,0:T(8,128)(2,1)S(1)}, bf16[8,128,1024]{2,1,0:T(8,128)(2,1)}, u32[]{:S(2)}) copy-start(bf16[8,128,1024]{2,1,0:T(8,128)(2,1)} %up.9) | copy-start | bytes 6291460
  5.7 9.2 %collective-permute-start = (f32[512,128]{1,0:T(8,128)S(1)}, f32[512,128]{1,0:T(8,128)S(1)}, u32[]{:S(2)}, u32[]{:S(2)}) collective-permute-start(f32[512,128]{1,0:T(8,128)S(1)} %get-tuple-element.83), channel_id=1, source_target_pairs={{0,8},{8,0},{16,24},{24,16},{32,40},{40,32},{48,56},{56,48},{64,72... | collective-permute-start | bytes 786440 | tf_op jit(solution)/shard_map/ppermute | solution.py:29
  14.9 5.5 %collective-permute-start.4 = (f32[192,256]{1,0:T(8,128)S(1)}, f32[192,256]{1,0:T(8,128)S(1)}, u32[]{:S(2)}, u32[]{:S(2)}) collective-permute-start(f32[192,256]{1,0:T(8,128)S(1)} %constant_dynamic-slice_fusion.6), channel_id=1, source_target_pairs={{0,64},{8,72},{16,80},{24,88},{32,96},{40,104},{48,112},{56,120},{... | collective-permute-start | bytes 589832 | tf_op jit(solution)/shard_map/ppermute | solution.py:29
  17.5 8.1 %collective-permute-start.1 = (f32[320,256]{1,0:T(8,128)S(1)}, f32[320,256]{1,0:T(8,128)S(1)}, u32[]{:S(2)}, u32[]{:S(2)}) collective-permute-start(f32[320,256]{1,0:T(8,128)S(1)} %get-tuple-element.95), channel_id=1, source_target_pairs={{0,8},{8,0},{16,24},{24,16},{32,40},{40,32},{48,56},{56,48},{64,72... | collective-permute-start | bytes 983048 | tf_op jit(solution)/shard_map/ppermute | solution.py:29
  20.5 4.8 %collective-permute-start.5 = (f32[96,256]{1,0:T(8,128)S(1)}, f32[96,256]{1,0:T(8,128)S(1)}, u32[]{:S(2)}, u32[]{:S(2)}) collective-permute-start(f32[96,256]{1,0:T(8,128)S(1)} %constant_dynamic-slice_fusion.5), channel_id=1, source_target_pairs={{0,192},{8,200},{16,208},{24,216},{32,224},{40,232},{48,240},{56,2... | collective-permute-start | bytes 294920 | tf_op jit(solution)/shard_map/ppermute | solution.py:29
  23.4 14.4 %collective-permute-start.3 = (f32[384,256]{1,0:T(8,128)S(1)}, f32[384,256]{1,0:T(8,128)S(1)}, u32[]{:S(2)}, u32[]{:S(2)}) collective-permute-start(f32[384,256]{1,0:T(8,128)S(1)} %get-tuple-element.100), channel_id=1, source_target_pairs={{0,8},{8,0},{16,24},{24,16},{32,40},{40,32},{48,56},{56,48},{64,72... | collective-permute-start | bytes 1179656 | tf_op jit(solution)/shard_map/ppermute | solution.py:29
  26.1 11.6 %collective-permute-start.2 = (f32[320,128]{1,0:T(8,128)S(1)}, f32[320,128]{1,0:T(8,128)S(1)}, u32[]{:S(2)}, u32[]{:S(2)}) collective-permute-start(f32[320,128]{1,0:T(8,128)S(1)} %get-tuple-element.97), channel_id=1, source_target_pairs={{0,16},{8,24},{16,0},{24,8},{32,48},{40,56},{48,32},{56,40},{64,80... | collective-permute-start | bytes 491528 | tf_op jit(solution)/shard_map/ppermute | solution.py:29
  38.5 11.3 %collective-permute-start.6 = (f32[288,128]{1,0:T(8,128)S(1)}, f32[288,128]{1,0:T(8,128)S(1)}, u32[]{:S(2)}, u32[]{:S(2)}) collective-permute-start(f32[288,128]{1,0:T(8,128)S(1)} %get-tuple-element.109), channel_id=1, source_target_pairs={{0,48},{8,56},{16,32},{24,40},{32,16},{40,24},{48,0},{56,8},{64,11... | collective-permute-start | bytes 442376 | tf_op jit(solution)/shard_map/ppermute | solution.py:29
  49.8 4.9 %collective-permute-start.7 = (f32[256,128]{1,0:T(8,128)S(1)}, f32[256,128]{1,0:T(8,128)S(1)}, u32[]{:S(2)}, u32[]{:S(2)}) collective-permute-start(f32[256,128]{1,0:T(8,128)S(1)} %slice_add_fusion), channel_id=1, source_target_pairs={{0,16},{8,24},{16,0},{24,8},{32,48},{40,56},{48,32},{56,40},{64,80... | collective-permute-start | bytes 393224 | tf_op jit(solution)/shard_map/ppermute | solution.py:29
  51.4 5.7 %collective-permute-start.8 = (f32[256,128]{1,0:T(8,128)S(1)}, f32[256,128]{1,0:T(8,128)S(1)}, u32[]{:S(2)}, u32[]{:S(2)}) collective-permute-start(f32[256,128]{1,0:T(8,128)S(1)} %get-tuple-element.107.c2), channel_id=1, source_target_pairs={{0,8},{8,0},{16,24},{24,16},{32,40},{40,32},{48,56},{56,48},{64,72... | collective-permute-start | bytes 393224 | tf_op jit(solution)/shard_map/ppermute | solution.py:29
  54.7 5.5 %collective-permute-start.9 = (f32[256,128]{1,0:T(8,128)S(1)}, f32[256,128]{1,0:T(8,128)S(1)}, u32[]{:S(2)}, u32[]{:S(2)}) collective-permute-start(f32[256,128]{1,0:T(8,128)S(1)} %add.43.c3), channel_id=1, source_target_pairs={{0,8},{8,0},{16,24},{24,16},{32,40},{40,32},{48,56},{56,48},{64,72... | collective-permute-start | bytes 393224 | tf_op jit(solution)/shard_map/ppermute | solution.py:29
  61.3 6.4 %collective-permute-start.10 = (f32[640,128]{1,0:T(8,128)S(1)}, f32[640,128]{1,0:T(8,128)S(1)}, u32[]{:S(2)}, u32[]{:S(2)}) collective-permute-start(f32[640,128]{1,0:T(8,128)S(1)} %get-tuple-element.116), channel_id=1, source_target_pairs={{0,8},{8,0},{16,24},{24,16},{32,40},{40,32},{48,56},{56,48},{64,72... | collective-permute-start | bytes 983048 | tf_op jit(solution)/shard_map/ppermute | solution.py:29
  62.0 10.8 %collective-permute-start.14 = (f32[512,128]{1,0:T(8,128)S(1)}, f32[512,128]{1,0:T(8,128)S(1)}, u32[]{:S(2)}, u32[]{:S(2)}) collective-permute-start(f32[512,128]{1,0:T(8,128)S(1)} %get-tuple-element.126), channel_id=1, source_target_pairs={{0,56},{8,16},{16,8},{24,32},{32,24},{40,48},{48,40},{56,0},{64,12... | collective-permute-start | bytes 786440 | tf_op jit(solution)/shard_map/ppermute | solution.py:566
  68.3 9.7 %collective-permute-start.11 = (f32[368,128]{1,0:T(8,128)S(1)}, f32[368,128]{1,0:T(8,128)S(1)}, u32[]{:S(2)}, u32[]{:S(2)}) collective-permute-start(f32[368,128]{1,0:T(8,128)S(1)} %get-tuple-element.118), channel_id=1, source_target_pairs={{0,16},{8,24},{16,0},{24,8},{32,48},{40,56},{48,32},{56,40},{64,80... | collective-permute-start | bytes 565256 | tf_op jit(solution)/shard_map/ppermute | solution.py:29
  73.5 7.9 %collective-permute-start.15 = (f32[256,128]{1,0:T(8,128)S(1)}, f32[256,128]{1,0:T(8,128)S(1)}, u32[]{:S(2)}, u32[]{:S(2)}) collective-permute-start(f32[256,128]{1,0:T(8,128)S(1)} %get-tuple-element.128), channel_id=1, source_target_pairs={{0,48},{8,56},{16,32},{24,40},{32,16},{40,24},{48,0},{56,8},{64,11... | collective-permute-start | bytes 393224 | tf_op jit(solution)/shard_map/ppermute | solution.py:29
  78.5 7.0 %collective-permute-start.12 = (f32[280,128]{1,0:T(8,128)S(1)}, f32[280,128]{1,0:T(8,128)S(1)}, u32[]{:S(2)}, u32[]{:S(2)}) collective-permute-start(f32[280,128]{1,0:T(8,128)S(1)} %get-tuple-element.121), channel_id=1, source_target_pairs={{0,48},{8,56},{16,32},{24,40},{32,16},{40,24},{48,0},{56,8},{64,11... | collective-permute-start | bytes 430088 | tf_op jit(solution)/shard_map/ppermute | solution.py:29
  81.9 4.3 %collective-permute-start.16 = (f32[128,128]{1,0:T(8,128)S(1)}, f32[128,128]{1,0:T(8,128)S(1)}, u32[]{:S(2)}, u32[]{:S(2)}) collective-permute-start(f32[128,128]{1,0:T(8,128)S(1)} %get-tuple-element.130), channel_id=1, source_target_pairs={{0,16},{8,24},{16,0},{24,8},{32,48},{40,56},{48,32},{56,40},{64,80... | collective-permute-start | bytes 196616 | tf_op jit(solution)/shard_map/ppermute | solution.py:29
  86.1 3.1 %collective-permute-start.13 = (f32[64,128]{1,0:T(8,128)S(1)}, f32[64,128]{1,0:T(8,128)S(1)}, u32[]{:S(2)}, u32[]{:S(2)}) collective-permute-start(f32[64,128]{1,0:T(8,128)S(1)} %get-tuple-element.124), channel_id=1, source_target_pairs={{0,64},{8,72},{16,80},{24,88},{32,96},{40,104},{48,112},{56,120},{... | collective-permute-start | bytes 98312 | tf_op jit(solution)/shard_map/ppermute | solution.py:29
  89.5 4.2 %collective-permute-start.17 = (f32[88,128]{1,0:T(8,128)S(1)}, f32[88,128]{1,0:T(8,128)S(1)}, u32[]{:S(2)}, u32[]{:S(2)}) collective-permute-start(f32[88,128]{1,0:T(8,128)S(1)} %pad_maximum_fusion.4), channel_id=1, source_target_pairs={{0,192},{8,200},{16,208},{24,216},{32,224},{40,232},{48,240},{56,2... | collective-permute-start | bytes 135176 | tf_op jit(solution)/shard_map/ppermute | solution.py:29
  93.8 3.1 %collective-permute-start.18 = (f32[112,128]{1,0:T(8,128)S(1)}, f32[112,128]{1,0:T(8,128)S(1)}, u32[]{:S(2)}, u32[]{:S(2)}) collective-permute-start(f32[112,128]{1,0:T(8,128)S(1)} %pad_maximum_fusion.3), channel_id=1, source_target_pairs={{0,64},{8,72},{16,80},{24,88},{32,96},{40,104},{48,112},{56,120},{... | collective-permute-start | bytes 172040 | tf_op jit(solution)/shard_map/ppermute | solution.py:29
  121.5 13.5 %collective-permute-start.19 = (f32[256,768]{1,0:T(8,128)S(1)}, f32[256,768]{1,0:T(8,128)S(1)}, u32[]{:S(2)}, u32[]{:S(2)}) collective-permute-start(f32[256,768]{1,0:T(8,128)S(1)} %get-tuple-element.140), channel_id=1, source_target_pairs={{0,1},{1,0},{2,3},{3,2},{4,5},{5,4},{6,7},{7,6},{8,9},{9,8},{10,11... | collective-permute-start | bytes 2359304 | tf_op jit(solution)/shard_map/ppermute | solution.py:29
  133.2 2.4 %collective-permute-start.20 = (f32[384,256]{1,0:T(8,128)S(1)}, f32[384,256]{1,0:T(8,128)S(1)}, u32[]{:S(2)}, u32[]{:S(2)}) collective-permute-start(f32[384,256]{1,0:T(8,128)S(1)} %pad_maximum_fusion), channel_id=1, source_target_pairs={{0,1},{1,0},{2,3},{3,2},{4,5},{5,4},{6,7},{7,6},{8,9},{9,8},{10,11... | collective-permute-start | bytes 1179656 | tf_op jit(solution)/shard_map/ppermute | solution.py:29
  160.2 2.8 %collective-permute-start.21 = (f32[8,128]{1,0:T(8,128)S(1)}, f32[8,128]{1,0:T(8,128)S(1)}, u32[]{:S(2)}, u32[]{:S(2)}) collective-permute-start(f32[8,128]{1,0:T(8,128)S(1)} %constant_dynamic-slice_fusion.1), channel_id=1, source_target_pairs={{0,2},{1,3},{2,0},{3,1},{4,6},{5,7},{6,4},{7,5},{8,10},{9,11},{10,... | collective-permute-start | bytes 12296 | tf_op jit(solution)/shard_map/ppermute | solution.py:29
  163.3 3.7 %collective-permute-start.22 = (f32[8,128]{1,0:T(8,128)S(1)}, f32[8,128]{1,0:T(8,128)S(1)}, u32[]{:S(2)}, u32[]{:S(2)}) collective-permute-start(f32[8,128]{1,0:T(8,128)S(1)} %constant_dynamic-slice_fusion), channel_id=1, source_target_pairs={{0,6},{1,7},{2,4},{3,5},{4,2},{5,3},{6,0},{7,1},{8,14},{9,15},{10,... | collective-permute-start | bytes 12296 | tf_op jit(solution)/shard_map/ppermute | solution.py:29
  167.1 2.5 %collective-permute-start.23 = (f32[8,128]{1,0:T(8,128)S(1)}, f32[8,128]{1,0:T(8,128)S(1)}, u32[]{:S(2)}, u32[]{:S(2)}) collective-permute-start(f32[8,128]{1,0:T(8,128)S(1)} %dynamic-slice_add_fusion.2), channel_id=1, source_target_pairs={{0,2},{1,3},{2,0},{3,1},{4,6},{5,7},{6,4},{7,5},{8,10},{9,11},{10,... | collective-permute-start | bytes 12296 | tf_op jit(solution)/shard_map/ppermute | solution.py:29
  189.6 9.3 %collective-permute-start.24 = (f32[256,384]{1,0:T(8,128)S(1)}, f32[256,384]{1,0:T(8,128)S(1)}, u32[]{:S(2)}, u32[]{:S(2)}) collective-permute-start(f32[256,384]{1,0:T(8,128)S(1)} %slice.94), channel_id=1, source_target_pairs={{0,1},{1,0},{2,3},{3,2},{4,5},{5,4},{6,7},{7,6},{8,9},{9,8},{10,11... | collective-permute-start | bytes 1179656 | tf_op jit(solution)/shard_map/ppermute | solution.py:29

commit v8 on v7

--- a/solution.py
+++ b/solution.py
@@ -274,7 +274,7 @@
     )
 
 
-def fourth_body(bits, c1, c2, c3, c2_there, c3_there, value, gram, low, high, keep_a, send_a, keep_b, send_b, coef, sums):
+def fourth_body(bits, c1, c2, c3, c2_there, c3_there, value, gram, low, high, keep, send, coef, sums):
     count, rank = c2.shape
     for bit in range(2):
 
@@ -291,19 +291,17 @@
     lhs = jnp.concatenate([c1[...], coef[...]], axis=1)
     for i in range(2):
         sums[i] = value[i] - dot(lhs, gram[i])
-    for keep, send, level in ((keep_a, send_a, 0), (keep_b, send_b, 1)):
-        for ref, parity in ((keep, bits[0]), (send, 1 - bits[0])):
-            for i in range(RING // 2):
-                place = 2 * i + parity
+    for ref, parity in ((keep, bits[0]), (send, 1 - bits[0])):
+        for i in range(RING // 2):
+            place = 2 * i + parity
+            here = pl.ds(pl.multiple_of(place * share, share), share)
+            for level in range(2):
                 for j in range(2):
-                    start = (2 * i + j) * share
-                    ref[start : start + share] = sums[
-                        level, pl.ds(pl.multiple_of(place * share, share), share), j * rank : (j + 1) * rank
-                    ]
-                if level == 0:
-                    start = rows + i * piece
-                    ref[start : start + piece] = high[pl.ds(pl.multiple_of(place * piece, piece), piece)]
-    send_a[rows + RING // 2 * piece :] = low[...]
+                    start = level * rows + (2 * i + j) * share
+                    ref[start : start + share] = sums[level, here, j * rank : (j + 1) * rank]
+            start = 2 * rows + i * piece
+            ref[start : start + piece] = high[pl.ds(pl.multiple_of(place * piece, piece), piece)]
+    send[keep.shape[0] :] = low[...]
 
 
 def fourth(bits, c1, c2, c3, c2_there, c3_there, value, gram, low, high):
@@ -315,8 +313,8 @@
         bits,
         [c1, c2, c3, c2_there, c3_there, value, gram, low, high],
         [
-            vmem(rows + extra, rank), vmem(rows + extra + low.shape[0], rank),
-            vmem(rows, rank), vmem(rows, rank), vmem(rows, wide, dtype=jnp.bfloat16),
+            vmem(2 * rows + extra, rank), vmem(2 * rows + extra + low.shape[0], rank),
+            vmem(rows, wide, dtype=jnp.bfloat16),
         ],
         12 * rows * rank * wide,
         16 * rows * wide,
@@ -324,83 +322,87 @@
     )
 
 
-def halve_body(steps, far, near, bits, keep, got, *refs):
-    low, (out, send, *lows) = refs[: len(refs) // 3], refs[len(refs) // 3 :]
-    rank = keep.shape[1]
-    extra = 3 * rank // 8 * steps if low else 0
-    rows = keep.shape[0] - extra
-    count, piece = rows // (2 * steps), extra // (2 * steps)
+def halve_body(steps, share, bits, keep, got, low, out, send, lows):
+    unit = keep.shape[0] // (2 * steps)
+    counts = (2 * share, 2 * share, unit - 4 * share)
     if steps == 2:
+        far, near = 1 + 2 * bits[1], 3 - 2 * bits[1]
         mine, theirs = [bits[6], bits[6] ^ near], [bits[6] ^ far, bits[6] ^ far ^ near]
     else:
         mine, theirs = [0], [1]
     for ref, slots in ((out, mine), (send, theirs)):
-        for i, slot in enumerate(slots):
-            here = pl.ds(slot * count, count)
-            ref[i * count : (i + 1) * count] = keep[here] + got[here]
-            if low:
-                there = pl.ds(rows + slot * piece, piece)
-                start = len(slots) * count + i * piece
-                ref[start : start + piece] = keep[there] + got[there]
-    if low:
-        done = low[0].shape[0]
-        lows[0][:done] = low[0][...]
-        lows[0][done:] = got[keep.shape[0] :]
-        send[out.shape[0] :] = lows[0][...]
-
-
-def halve(bits, steps, far, near, keep, got, *low):
-    rank, size = keep.shape[1], keep.shape[0] // 2
-    lows = [2 * v.shape[0] for v in low]
-    return local(
-        functools.partial(halve_body, steps, far, near),
-        bits,
-        [keep, got, *low],
-        [vmem(size, rank), vmem(size + sum(lows), rank)] + [vmem(v, rank) for v in lows],
+        base = 0
+        for count in counts:
+            for i, slot in enumerate(slots):
+                here = pl.ds(2 * steps * base + slot * count, count)
+                start = steps * base + i * count
+                ref[start : start + count] = keep[here] + got[here]
+            base += count
+    done = low.shape[0]
+    lows[:done] = low[...]
+    lows[done:] = got[keep.shape[0] :]
+    send[out.shape[0] :] = lows[...]
+
+
+def halve(bits, steps, share, keep, got, low):
+    rank, size, lows = keep.shape[1], keep.shape[0] // 2, 2 * low.shape[0]
+    return local(
+        functools.partial(halve_body, steps, share),
+        bits,
+        [keep, got, low],
+        [vmem(size, rank), vmem(size + lows, rank), vmem(lows, rank)],
         2 * keep.size,
         20 * keep.size,
     )
 
 
-def fourth_rows_body(bits, keep, got, low, own, other, gram, high):
+def turn(place):
+    return (place + 2 * (place & 1) - 1) & (RING - 1)
+
+
+def gather_body(bits, keep, got, low, own, other, fifth, gram, high):
     share, rank = own.shape
     rows = 2 * share
     total = keep[...] + got[: keep.shape[0]]
     choose(bits[2], total[:share], total[share:rows], own, other)
-    high[...] = total[rows:]
+    for j in range(2):
+        fifth[:, j * rank : (j + 1) * rank] = total[rows + j * share : rows + (j + 1) * share]
+    high[...] = total[2 * rows :]
     count = gram.shape[0] // RING
-    half_list = low.shape[0]
-    z0, z1, z2 = bits[0], bits[3], bits[5]
-    for i, mask in enumerate((0, 1, 2, 3, 6, 7, 4, 5)):
-        p0, p1, p2 = z0 ^ (mask & 1), z1 ^ (mask >> 1 & 1), z2 ^ (mask >> 2)
+    known = low.shape[0]
+    here = bits[0] + 2 * bits[6]
+    for i in range(RING):
+        second, third = (0, 2, 6, 4)[i // 2], (0, 6, 2, 4)[i // 2]
+        first = here ^ second
+        last = here ^ third
+        if i % 2:
+            first, last = first ^ 1, turn(last)
+        owner = jnp.where(bits[1] == 0, first, last)
+        p0, p1, p2 = owner & 1, owner >> 1 & 1, owner >> 2
         place = pl.multiple_of((p0 * 4 + (p1 ^ p2) * 2 + p2) * count, count)
         for j in range(2):
             start = 2 * i * count + j * count
-            if start < half_list:
+            if start < known:
                 part = low[start : start + count]
             else:
-                start += keep.shape[0] - half_list
+                start += keep.shape[0] - known
                 part = got[start : start + count]
             gram[pl.ds(place, count), j * rank : (j + 1) * rank] = part
 
 
-def fourth_rows(bits, keep, got, low, share):
+def gather_rows(bits, keep, got, low, share):
     rank = keep.shape[1]
     return local(
-        fourth_rows_body,
+        gather_body,
         bits,
         [keep, got, low],
-        [vmem(share, rank), vmem(share, rank), vmem(rank, 2 * rank), vmem(keep.shape[0] - 2 * share, rank)],
+        [
+            vmem(share, rank), vmem(share, rank), vmem(share, 2 * rank), vmem(rank, 2 * rank),
+            vmem(keep.shape[0] - 4 * share, rank),
+        ],
         2 * keep.size,
         20 * keep.size,
     )
-
-
-def fifth_rows_body(bits, keep, got, fifth):
-    share, rank = fifth.shape[0], keep.shape[1]
-    for j in range(2):
-        here = slice(j * share, (j + 1) * share)
-        fifth[:, j * rank : (j + 1) * rank] = keep[here] + got[here]
 
 
 def sixth_body(bits, c1, c23, packed, value, gram, keep, send, coef):
@@ -521,6 +523,13 @@
     bits = jnp.stack([z0, core, y0, z1, z1 ^ z2, z2, z1 + 2 * z2])
     over_x = functools.partial(swap, axis="gx", size=size_x)
     over_y = functools.partial(swap, axis="gy", size=size_y)
+
+    def by_core(value, *targets):
+        pairs = [
+            (x * size_y + y, targets[y & 1](x) * size_y + y) for x in range(size_x) for y in range(size_y)
+        ]
+        return lax.ppermute(value, ("gx", "gy"), pairs)
+
     ring = RING
     share = rows // ring
     by_y01, by_y1 = starts(y0 ^ y1, 3 * rank // 2), starts(y1, 3 * rank // 4)
@@ -561,20 +570,14 @@
     c2_there = over_x(c2, mask=1)
     c3_there = over_x(c3, mask=1)
 
-    keep_a, send_a, keep_b, send_b, c23 = fourth(bits, c1, c2, c3, c2_there, c3_there, value_45, gram_45, low, high)
-    turned = [(i & -RING) + ((i + 1 if i & 1 else i - 1) % RING) for i in range(size_x)]
-    got_a, got_b = over_x(send_a, mask=1), lax.ppermute(send_b, "gx", list(enumerate(turned)))
-    keep_a, send_a, low = halve(bits, 2, 1, 3, keep_a, got_a, low)
-    got_a = over_x(send_a, mask=2)
-    keep_b, send_b = halve(bits, 2, 3, 1, keep_b, got_b)
-    got_b = over_x(send_b, mask=6)
-    keep_a, send_a, low = halve(bits, 1, 0, 0, keep_a, got_a, low)
-    got_a = over_x(send_a, mask=6)
-    keep_b, send_b = halve(bits, 1, 0, 0, keep_b, got_b)
-    got_b = over_x(send_b, mask=2)
-    own, other, gram_45, high = fourth_rows(bits, keep_a, got_a, low, share)
+    keep, send, c23 = fourth(bits, c1, c2, c3, c2_there, c3_there, value_45, gram_45, low, high)
+    got = by_core(send, lambda i: i ^ 1, lambda i: (i & -RING) + turn(i & (RING - 1)))
+    keep, send, low = halve(bits, 2, share, keep, got, low)
+    got = by_core(send, lambda i: i ^ 2, lambda i: i ^ 6)
+    keep, send, low = halve(bits, 1, share, keep, got, low)
+    got = by_core(send, lambda i: i ^ 6, lambda i: i ^ 2)
+    own, other, left, gram_45, high = gather_rows(bits, keep, got, low, share)
     c4 = own + over_x(other, mask=8)
-    left = local(fifth_rows_body, bits, [keep_b, got_b], [vmem(share, wide)], keep_b.size, 12 * keep_b.size)[0]
     left = left - dot(c4, gram_45)
     received = over_x(jnp.concatenate([half(left, half_y1[1]), high]), mask=24)
     c5 = half(left, half_y1[0]) + received[:share]

time: 202 us -> 206 us (1.020)
  waiting for transfers between devices: 50.4 us -> 60.1 us
  blocking collectives: 66.2 us -> 64.1 us
  starting transfers between devices: 56.6 us -> 54.5 us
    ppermute x1 -> x3, waiting for transfers between devices: 0.01 us -> 20.1 us  [by_core(): return lax.ppermute(value, ('gx', 'gy'), pairs)]
    ppermute x24 -> x19, waiting for transfers between devices: 50.4 us -> 40 us  [swap(): lax.ppermute(value, axis, [(source, source ^ mask) for source in range(si...]
    ppermute x24 -> x19, starting transfers between devices: 52.8 us -> 45 us  [swap(): lax.ppermute(value, axis, [(source, source ^ mask) for source in range(si...]
    ppermute x1 -> x3, starting transfers between devices: 3.78 us -> 9.55 us  [by_core(): return lax.ppermute(value, ('gx', 'gy'), pairs)]
    all_to_all x3, blocking collectives: 66.2 us -> 64.1 us  [exchange(): lax.all_to_all(value, AXES, 0, 0, tiled=True, axis_index_groups=groups)]
    pallas_call x17 -> x14, Pallas kernels: 17.7 us -> 16.1 us  [local(): pl.pallas_call(body, out_shape=outs, in_specs=[pl.BlockSpec(memory_space=...]
  transfers between devices with their start and end apart: 25 -> 22, of which waited for: 19 -> 18; matrix products, arithmetic and copies ran while one was open for 0% -> 0% of each run, Pallas kernels for 7% -> 5%
where the time goes in v8:
time: 206 us; the launch traced here: 205 us
  blocking collectives  64.1 us (31%)
  waiting for transfers between devices  60.1 us (29%)
  starting transfers between devices  54.5 us (26%)
  Pallas kernels  24 us (12%)
    all_to_all x3, blocking collectives, exchange(): lax.all_to_all(value, AXES, 0, 0, tiled=True, axis_index_groups=groups)  64.1 us
    ppermute x19, starting transfers between devices, swap(): lax.ppermute(value, axis, [(source, source ^ mask) for source in range(si...  45 us
    ppermute x19, waiting for transfers between devices, swap(): lax.ppermute(value, axis, [(source, source ^ mask) for source in range(si...  40 us
    ppermute x3, waiting for transfers between devices, by_core(): return lax.ppermute(value, ('gx', 'gy'), pairs)  20.1 us
    pallas_call x14, Pallas kernels, local(): pl.pallas_call(body, out_shape=outs, in_specs=[pl.BlockSpec(memory_space=...  16.1 us
    ppermute x3, starting transfers between devices, by_core(): return lax.ppermute(value, ('gx', 'gy'), pairs)  9.55 us
    pallas_call x1, Pallas kernels, run(): pl.pallas_call(body, out_shape=out_shape, grid_spec=pltpu.PrefetchScalarG...  5.63 us
  transfers between devices with their start and end apart: 22, of which 18 were waited for; matrix products, arithmetic and copies ran while one was open for 0% of the time, Pallas kernels for 5%

profile of v8, /device:TPU:1, one launch (start us, length us, event | category | flops | bytes accessed | tf_op | source)
XLA Modules:
  0.0 205.3 jit_solution(5564414914140934570)
XLA Ops:
  0.1 5.6 %shard_map.46 = (bf16[512,1024]{1,0:T(8,128)(2,1)S(1)}, f32[512,128]{1,0:T(8,128)S(1)}, f32[512,128]{1,0:T(8,128)S(1)}) custom-call(s32[7]{0:T(128)S(1)} %stack.31.bits, bf16[512,1024]{1,0:T(8,128)(2,1)} %rhs, bf16[1,1024,1024]{2,1,0:T(8,128)(2,1)} %inverse.1, bf16[8,256,1024]{2,1,0:T(8,128)(2,1)} %proj.5, bf16[8,256,1024]{2,1,0:T(8,128)(2,1)} %proj.5), custom_call_target="tpu_custom_call" | custom-call | flops 1342177280 | bytes 4194304 | tf_op jit(solution)/shard_map/pallas_call | solution.py:70
  5.7 2.6 %collective-permute-start = (f32[512,128]{1,0:T(8,128)S(1)}, f32[512,128]{1,0:T(8,128)S(1)}, u32[]{:S(2)}, u32[]{:S(2)}) collective-permute-start(f32[512,128]{1,0:T(8,128)S(1)} %get-tuple-element.78), channel_id=1, source_target_pairs={{0,8},{8,0},{16,24},{24,16},{32,40},{40,32},{48,56},{56,48},{64,72... | collective-permute-start | bytes 786440 | tf_op jit(solution)/shard_map/ppermute | solution.py:29
  8.3 1.9 shard_map.48
  10.2 1.7 shard_map.47
  11.9 3.0 %shard_map.49 = (f32[3,512,256]{2,1,0:T(8,128)S(1)}, bf16[3,640,256]{2,1,0:T(8,128)(2,1)S(1)}, f32[3,128,256]{2,1,0:T(8,128)S(1)}) custom-call(s32[7]{0:T(128)S(1)} %stack.31.bits, bf16[512,1024]{1,0:T(8,128)(2,1)S(1)} %get-tuple-element.79.state, bf16[8,128,1024]{2,1,0:T(8,128)(2,1)S(1)} %copy-done.1, bf16[8,256,1024]{2,1,0:T(8,128)(2,1)S(1)} %copy-done), custom_call_target="tpu_custom_call" | custom-call | flops 2013265920 | bytes 3407872 | tf_op jit(solution)/shard_map/pallas_call | solution.py:101
  18.1 2.4 %collective-permute-done.4 = f32[192,256]{1,0:T(8,128)S(1)} collective-permute-done((f32[192,256]{1,0:T(8,128)S(1)}, f32[192,256]{1,0:T(8,128)S(1)}, u32[]{:S(2)}, u32[]{:S(2)}) %collective-permute-start.4) | collective-permute-done | bytes 196640 | tf_op jit(solution)/shard_map/ppermute | solution.py:29
  20.5 2.8 %collective-permute-start.5 = (f32[96,256]{1,0:T(8,128)S(1)}, f32[96,256]{1,0:T(8,128)S(1)}, u32[]{:S(2)}, u32[]{:S(2)}) collective-permute-start(f32[96,256]{1,0:T(8,128)S(1)} %constant_dynamic-slice_fusion.5), channel_id=1, source_target_pairs={{0,192},{8,200},{16,208},{24,216},{32,224},{40,232},{48,240},{56,2... | collective-permute-start | bytes 294920 | tf_op jit(solution)/shard_map/ppermute | solution.py:29
  23.4 2.0 collective-permute-done.5
  26.1 3.1 %collective-permute-start.2 = (f32[320,128]{1,0:T(8,128)S(1)}, f32[320,128]{1,0:T(8,128)S(1)}, u32[]{:S(2)}, u32[]{:S(2)}) collective-permute-start(f32[320,128]{1,0:T(8,128)S(1)} %get-tuple-element.92), channel_id=1, source_target_pairs={{0,16},{8,24},{16,0},{24,8},{32,48},{40,56},{48,32},{56,40},{64,80... | collective-permute-start | bytes 491528 | tf_op jit(solution)/shard_map/ppermute | solution.py:29
  29.2 8.5 %collective-permute-done.3.left = f32[384,256]{1,0:T(8,128)S(1)} collective-permute-done((f32[384,256]{1,0:T(8,128)S(1)}, f32[384,256]{1,0:T(8,128)S(1)}, u32[]{:S(2)}, u32[]{:S(2)}) %collective-permute-start.3) | collective-permute-done | bytes 393248 | tf_op jit(solution)/shard_map/ppermute | solution.py:29
  38.5 5.5 %collective-permute-start.6 = (f32[288,128]{1,0:T(8,128)S(1)}, f32[288,128]{1,0:T(8,128)S(1)}, u32[]{:S(2)}, u32[]{:S(2)}) collective-permute-start(f32[288,128]{1,0:T(8,128)S(1)} %get-tuple-element.104), channel_id=1, source_target_pairs={{0,48},{8,56},{16,32},{24,40},{32,16},{40,24},{48,0},{56,8},{64,11... | collective-permute-start | bytes 442376 | tf_op jit(solution)/shard_map/ppermute | solution.py:29
  44.0 5.7 %collective-permute-done.6 = f32[288,128]{1,0:T(8,128)S(1)} collective-permute-done((f32[288,128]{1,0:T(8,128)S(1)}, f32[288,128]{1,0:T(8,128)S(1)}, u32[]{:S(2)}, u32[]{:S(2)}) %collective-permute-start.6) | collective-permute-done | bytes 147488 | tf_op jit(solution)/shard_map/ppermute | solution.py:29
  52.2 2.5 %collective-permute-done.7 = f32[256,128]{1,0:T(8,128)S(1)} collective-permute-done((f32[256,128]{1,0:T(8,128)S(1)}, f32[256,128]{1,0:T(8,128)S(1)}, u32[]{:S(2)}, u32[]{:S(2)}) %collective-permute-start.7) | collective-permute-done | bytes 131104 | tf_op jit(solution)/shard_map/ppermute | solution.py:29
  54.7 2.3 %collective-permute-start.9 = (f32[256,128]{1,0:T(8,128)S(1)}, f32[256,128]{1,0:T(8,128)S(1)}, u32[]{:S(2)}, u32[]{:S(2)}) collective-permute-start(f32[256,128]{1,0:T(8,128)S(1)} %add.43.c3), channel_id=1, source_target_pairs={{0,8},{8,0},{16,24},{24,16},{32,40},{40,32},{48,56},{56,48},{64,72... | collective-permute-start | bytes 393224 | tf_op jit(solution)/shard_map/ppermute | solution.py:29
  57.0 3.2 %collective-permute-done.9.c3_there = f32[256,128]{1,0:T(8,128)S(1)} collective-permute-done((f32[256,128]{1,0:T(8,128)S(1)}, f32[256,128]{1,0:T(8,128)S(1)}, u32[]{:S(2)}, u32[]{:S(2)}) %collective-permute-start.9) | collective-permute-done | bytes 131104 | tf_op jit(solution)/shard_map/ppermute | solution.py:29
  61.3 3.1 %collective-permute-start.10 = (f32[1152,128]{1,0:T(8,128)S(1)}, f32[1152,128]{1,0:T(8,128)S(1)}, u32[]{:S(2)}, u32[]{:S(2)}) collective-permute-start(f32[1152,128]{1,0:T(8,128)S(1)} %get-tuple-element.111), channel_id=1, source_target_pairs={{0,8},{1,57},{2,10},{3,59},{4,12},{5,61},{6,14},{7,63},{8,0},{9,17... | collective-permute-start | bytes 1769480 | tf_op jit(solution)/shard_map/ppermute | solution.py:531
  64.4 7.3 %collective-permute-done.10.got = f32[1152,128]{1,0:T(8,128)S(1)} collective-permute-done((f32[1152,128]{1,0:T(8,128)S(1)}, f32[1152,128]{1,0:T(8,128)S(1)}, u32[]{:S(2)}, u32[]{:S(2)}) %collective-permute-start.10) | collective-permute-done | bytes 589856 | tf_op jit(solution)/shard_map/ppermute | solution.py:531
  72.3 3.2 %collective-permute-start.11 = (f32[624,128]{1,0:T(8,128)S(1)}, f32[624,128]{1,0:T(8,128)S(1)}, u32[]{:S(2)}, u32[]{:S(2)}) collective-permute-start(f32[624,128]{1,0:T(8,128)S(1)} %get-tuple-element.113), channel_id=1, source_target_pairs={{0,16},{1,49},{2,18},{3,51},{4,20},{5,53},{6,22},{7,55},{8,24},{9,... | collective-permute-start | bytes 958472 | tf_op jit(solution)/shard_map/ppermute | solution.py:531
  75.4 7.4 %collective-permute-done.11.got = f32[624,128]{1,0:T(8,128)S(1)} collective-permute-done((f32[624,128]{1,0:T(8,128)S(1)}, f32[624,128]{1,0:T(8,128)S(1)}, u32[]{:S(2)}, u32[]{:S(2)}) %collective-permute-start.11) | collective-permute-done | bytes 319520 | tf_op jit(solution)/shard_map/ppermute | solution.py:531
  83.4 3.3 %collective-permute-start.12 = (f32[408,128]{1,0:T(8,128)S(1)}, f32[408,128]{1,0:T(8,128)S(1)}, u32[]{:S(2)}, u32[]{:S(2)}) collective-permute-start(f32[408,128]{1,0:T(8,128)S(1)} %get-tuple-element.116), channel_id=1, source_target_pairs={{0,48},{1,17},{2,50},{3,19},{4,52},{5,21},{6,54},{7,23},{8,56},{9,... | collective-permute-start | bytes 626696 | tf_op jit(solution)/shard_map/ppermute | solution.py:531
  86.7 5.5 %collective-permute-done.12.got = f32[408,128]{1,0:T(8,128)S(1)} collective-permute-done((f32[408,128]{1,0:T(8,128)S(1)}, f32[408,128]{1,0:T(8,128)S(1)}, u32[]{:S(2)}, u32[]{:S(2)}) %collective-permute-start.12) | collective-permute-done | bytes 208928 | tf_op jit(solution)/shard_map/ppermute | solution.py:531
  92.9 3.0 %collective-permute-done.13 = f32[64,128]{1,0:T(8,128)S(1)} collective-permute-done((f32[64,128]{1,0:T(8,128)S(1)}, f32[64,128]{1,0:T(8,128)S(1)}, u32[]{:S(2)}, u32[]{:S(2)}) %collective-permute-start.13) | collective-permute-done | bytes 32800 | tf_op jit(solution)/shard_map/ppermute | solution.py:29
  97.4 3.0 %collective-permute-done.14 = f32[88,128]{1,0:T(8,128)S(1)} collective-permute-done((f32[88,128]{1,0:T(8,128)S(1)}, f32[88,128]{1,0:T(8,128)S(1)}, u32[]{:S(2)}, u32[]{:S(2)}) %collective-permute-start.14) | collective-permute-done | bytes 45088 | tf_op jit(solution)/shard_map/ppermute | solution.py:29
  100.6 3.0 %collective-permute-done.15 = f32[112,128]{1,0:T(8,128)S(1)} collective-permute-done((f32[112,128]{1,0:T(8,128)S(1)}, f32[112,128]{1,0:T(8,128)S(1)}, u32[]{:S(2)}, u32[]{:S(2)}) %collective-permute-start.15) | collective-permute-done | bytes 57376 | tf_op jit(solution)/shard_map/ppermute | solution.py:29
  103.7 20.7 %all_to_all.15.packed = f32[8,224,128]{2,1,0:T(8,128)S(1)} all-to-all(f32[8,224,128]{2,1,0:T(8,128)S(1)} %broadcast_in_dim.6), channel_id=1, replica_groups={{0,8,16,24,32,40,48,56},{64,72,80,88,96,104,112,120},{128,136,144,152,1..., dimensions={0} | all-to-all | bytes 1835008 | tf_op jit(solution)/shard_map/all_to_all | solution.py:33
  125.8 11.0 %collective-permute-start.16 = (f32[256,768]{1,0:T(8,128)S(1)}, f32[256,768]{1,0:T(8,128)S(1)}, u32[]{:S(2)}, u32[]{:S(2)}) collective-permute-start(f32[256,768]{1,0:T(8,128)S(1)} %get-tuple-element.130), channel_id=1, source_target_pairs={{0,1},{1,0},{2,3},{3,2},{4,5},{5,4},{6,7},{7,6},{8,9},{9,8},{10,11... | collective-permute-start | bytes 2359304 | tf_op jit(solution)/shard_map/ppermute | solution.py:29
  137.1 1.7 collective-permute-done.16.right
  139.4 23.5 %all_to_all.16.parts = f32[32,8,768]{2,1,0:T(8,128)S(1)} all-to-all(f32[32,8,768]{2,1,0:T(8,128)S(1)} %bitcast.25), channel_id=1, replica_groups={{0,8,16,24,32,40,48,56,64,72,80,88,96,104,112,120,128,136,144,152,160,1..., dimensions={0} | all-to-all | bytes 1572864 | tf_op jit(solution)/shard_map/all_to_all | solution.py:33
  167.2 2.5 %collective-permute-start.19 = (f32[8,128]{1,0:T(8,128)S(1)}, f32[8,128]{1,0:T(8,128)S(1)}, u32[]{:S(2)}, u32[]{:S(2)}) collective-permute-start(f32[8,128]{1,0:T(8,128)S(1)} %constant_dynamic-slice_fusion), channel_id=1, source_target_pairs={{0,6},{1,7},{2,4},{3,5},{4,2},{5,3},{6,0},{7,1},{8,14},{9,15},{10,... | collective-permute-start | bytes 12296 | tf_op jit(solution)/shard_map/ppermute | solution.py:29
  173.6 19.9 %all_to_all.17 = f32[32,8,512]{2,1,0:T(8,128)S(1)} all-to-all(f32[32,8,512]{2,1,0:T(8,128)S(1)} %broadcast_in_dim.7), channel_id=1, replica_groups={{0,8,16,24,32,40,48,56,64,72,80,88,96,104,112,120,128,136,144,152,160,1..., dimensions={0} | all-to-all | bytes 1048576 | tf_op jit(solution)/shard_map/all_to_all | solution.py:33
  193.5 8.0 %collective-permute-start.21 = (f32[256,384]{1,0:T(8,128)S(1)}, f32[256,384]{1,0:T(8,128)S(1)}, u32[]{:S(2)}, u32[]{:S(2)}) collective-permute-start(f32[256,384]{1,0:T(8,128)S(1)} %slice.94), channel_id=1, source_target_pairs={{0,1},{1,0},{2,3},{3,2},{4,5},{5,4},{6,7},{7,6},{8,9},{9,8},{10,11... | collective-permute-start | bytes 1179656 | tf_op jit(solution)/shard_map/ppermute | solution.py:29
  202.9 2.3 %shard_map.61 = f32[512,1024]{1,0:T(8,128)} custom-call(s32[7]{0:T(128)S(1)} %stack.31.bits, f32[512,1024]{1,0:T(8,128)S(1)} %shard_map.60.state, f32[256,512]{1,0:T(8,128)S(1)} %bitcast.24, f32[256,384]{1,0:T(8,128)S(1)} %collective-permute-done.21.received, bf16[8,128,1024]{2,1,0:T(8,128)(2,1)S(1)} %copy-done.1), custom_call_target="tpu_custom_call" | custom-call | flops 402653184 | bytes 3145728 | tf_op jit(solution)/shard_map/pallas_call | solution.py:498
  (78 shorter events, 23.8 us)
Async XLA Ops:
  0.1 8.2 %copy-start = (bf16[8,256,1024]{2,1,0:T(8,128)(2,1)S(1)}, bf16[8,256,1024]{2,1,0:T(8,128)(2,1)}, u32[]{:S(2)}) copy-start(bf16[8,256,1024]{2,1,0:T(8,128)(2,1)} %proj.5) | copy-start | bytes 12582916
  0.1 8.2 %copy-start.1 = (bf16[8,128,1024]{2,1,0:T(8,128)(2,1)S(1)}, bf16[8,128,1024]{2,1,0:T(8,128)(2,1)}, u32[]{:S(2)}) copy-start(bf16[8,128,1024]{2,1,0:T(8,128)(2,1)} %up.9) | copy-start | bytes 6291460
  5.7 9.2 %collective-permute-start = (f32[512,128]{1,0:T(8,128)S(1)}, f32[512,128]{1,0:T(8,128)S(1)}, u32[]{:S(2)}, u32[]{:S(2)}) collective-permute-start(f32[512,128]{1,0:T(8,128)S(1)} %get-tuple-element.78), channel_id=1, source_target_pairs={{0,8},{8,0},{16,24},{24,16},{32,40},{40,32},{48,56},{56,48},{64,72... | collective-permute-start | bytes 786440 | tf_op jit(solution)/shard_map/ppermute | solution.py:29
  14.9 5.5 %collective-permute-start.4 = (f32[192,256]{1,0:T(8,128)S(1)}, f32[192,256]{1,0:T(8,128)S(1)}, u32[]{:S(2)}, u32[]{:S(2)}) collective-permute-start(f32[192,256]{1,0:T(8,128)S(1)} %constant_dynamic-slice_fusion.6), channel_id=1, source_target_pairs={{0,64},{8,72},{16,80},{24,88},{32,96},{40,104},{48,112},{56,120},{... | collective-permute-start | bytes 589832 | tf_op jit(solution)/shard_map/ppermute | solution.py:29
  17.5 8.1 %collective-permute-start.1 = (f32[320,256]{1,0:T(8,128)S(1)}, f32[320,256]{1,0:T(8,128)S(1)}, u32[]{:S(2)}, u32[]{:S(2)}) collective-permute-start(f32[320,256]{1,0:T(8,128)S(1)} %get-tuple-element.90), channel_id=1, source_target_pairs={{0,8},{8,0},{16,24},{24,16},{32,40},{40,32},{48,56},{56,48},{64,72... | collective-permute-start | bytes 983048 | tf_op jit(solution)/shard_map/ppermute | solution.py:29
  20.5 4.8 %collective-permute-start.5 = (f32[96,256]{1,0:T(8,128)S(1)}, f32[96,256]{1,0:T(8,128)S(1)}, u32[]{:S(2)}, u32[]{:S(2)}) collective-permute-start(f32[96,256]{1,0:T(8,128)S(1)} %constant_dynamic-slice_fusion.5), channel_id=1, source_target_pairs={{0,192},{8,200},{16,208},{24,216},{32,224},{40,232},{48,240},{56,2... | collective-permute-start | bytes 294920 | tf_op jit(solution)/shard_map/ppermute | solution.py:29
  23.4 14.4 %collective-permute-start.3 = (f32[384,256]{1,0:T(8,128)S(1)}, f32[384,256]{1,0:T(8,128)S(1)}, u32[]{:S(2)}, u32[]{:S(2)}) collective-permute-start(f32[384,256]{1,0:T(8,128)S(1)} %get-tuple-element.95), channel_id=1, source_target_pairs={{0,8},{8,0},{16,24},{24,16},{32,40},{40,32},{48,56},{56,48},{64,72... | collective-permute-start | bytes 1179656 | tf_op jit(solution)/shard_map/ppermute | solution.py:29
  26.1 11.6 %collective-permute-start.2 = (f32[320,128]{1,0:T(8,128)S(1)}, f32[320,128]{1,0:T(8,128)S(1)}, u32[]{:S(2)}, u32[]{:S(2)}) collective-permute-start(f32[320,128]{1,0:T(8,128)S(1)} %get-tuple-element.92), channel_id=1, source_target_pairs={{0,16},{8,24},{16,0},{24,8},{32,48},{40,56},{48,32},{56,40},{64,80... | collective-permute-start | bytes 491528 | tf_op jit(solution)/shard_map/ppermute | solution.py:29
  38.5 11.3 %collective-permute-start.6 = (f32[288,128]{1,0:T(8,128)S(1)}, f32[288,128]{1,0:T(8,128)S(1)}, u32[]{:S(2)}, u32[]{:S(2)}) collective-permute-start(f32[288,128]{1,0:T(8,128)S(1)} %get-tuple-element.104), channel_id=1, source_target_pairs={{0,48},{8,56},{16,32},{24,40},{32,16},{40,24},{48,0},{56,8},{64,11... | collective-permute-start | bytes 442376 | tf_op jit(solution)/shard_map/ppermute | solution.py:29
  49.8 4.9 %collective-permute-start.7 = (f32[256,128]{1,0:T(8,128)S(1)}, f32[256,128]{1,0:T(8,128)S(1)}, u32[]{:S(2)}, u32[]{:S(2)}) collective-permute-start(f32[256,128]{1,0:T(8,128)S(1)} %slice_add_fusion), channel_id=1, source_target_pairs={{0,16},{8,24},{16,0},{24,8},{32,48},{40,56},{48,32},{56,40},{64,80... | collective-permute-start | bytes 393224 | tf_op jit(solution)/shard_map/ppermute | solution.py:29
  51.4 5.7 %collective-permute-start.8 = (f32[256,128]{1,0:T(8,128)S(1)}, f32[256,128]{1,0:T(8,128)S(1)}, u32[]{:S(2)}, u32[]{:S(2)}) collective-permute-start(f32[256,128]{1,0:T(8,128)S(1)} %get-tuple-element.102.c2), channel_id=1, source_target_pairs={{0,8},{8,0},{16,24},{24,16},{32,40},{40,32},{48,56},{56,48},{64,72... | collective-permute-start | bytes 393224 | tf_op jit(solution)/shard_map/ppermute | solution.py:29
  54.7 5.5 %collective-permute-start.9 = (f32[256,128]{1,0:T(8,128)S(1)}, f32[256,128]{1,0:T(8,128)S(1)}, u32[]{:S(2)}, u32[]{:S(2)}) collective-permute-start(f32[256,128]{1,0:T(8,128)S(1)} %add.43.c3), channel_id=1, source_target_pairs={{0,8},{8,0},{16,24},{24,16},{32,40},{40,32},{48,56},{56,48},{64,72... | collective-permute-start | bytes 393224 | tf_op jit(solution)/shard_map/ppermute | solution.py:29
  61.3 10.3 %collective-permute-start.10 = (f32[1152,128]{1,0:T(8,128)S(1)}, f32[1152,128]{1,0:T(8,128)S(1)}, u32[]{:S(2)}, u32[]{:S(2)}) collective-permute-start(f32[1152,128]{1,0:T(8,128)S(1)} %get-tuple-element.111), channel_id=1, source_target_pairs={{0,8},{1,57},{2,10},{3,59},{4,12},{5,61},{6,14},{7,63},{8,0},{9,17... | collective-permute-start | bytes 1769480 | tf_op jit(solution)/shard_map/ppermute | solution.py:531
  72.3 10.5 %collective-permute-start.11 = (f32[624,128]{1,0:T(8,128)S(1)}, f32[624,128]{1,0:T(8,128)S(1)}, u32[]{:S(2)}, u32[]{:S(2)}) collective-permute-start(f32[624,128]{1,0:T(8,128)S(1)} %get-tuple-element.113), channel_id=1, source_target_pairs={{0,16},{1,49},{2,18},{3,51},{4,20},{5,53},{6,22},{7,55},{8,24},{9,... | collective-permute-start | bytes 958472 | tf_op jit(solution)/shard_map/ppermute | solution.py:531
  83.4 8.8 %collective-permute-start.12 = (f32[408,128]{1,0:T(8,128)S(1)}, f32[408,128]{1,0:T(8,128)S(1)}, u32[]{:S(2)}, u32[]{:S(2)}) collective-permute-start(f32[408,128]{1,0:T(8,128)S(1)} %get-tuple-element.116), channel_id=1, source_target_pairs={{0,48},{1,17},{2,50},{3,19},{4,52},{5,21},{6,54},{7,23},{8,56},{9,... | collective-permute-start | bytes 626696 | tf_op jit(solution)/shard_map/ppermute | solution.py:531
  92.8 3.1 %collective-permute-start.13 = (f32[64,128]{1,0:T(8,128)S(1)}, f32[64,128]{1,0:T(8,128)S(1)}, u32[]{:S(2)}, u32[]{:S(2)}) collective-permute-start(f32[64,128]{1,0:T(8,128)S(1)} %get-tuple-element.119), channel_id=1, source_target_pairs={{0,64},{8,72},{16,80},{24,88},{32,96},{40,104},{48,112},{56,120},{... | collective-permute-start | bytes 98312 | tf_op jit(solution)/shard_map/ppermute | solution.py:29
  96.2 4.2 %collective-permute-start.14 = (f32[88,128]{1,0:T(8,128)S(1)}, f32[88,128]{1,0:T(8,128)S(1)}, u32[]{:S(2)}, u32[]{:S(2)}) collective-permute-start(f32[88,128]{1,0:T(8,128)S(1)} %pad_maximum_fusion.4), channel_id=1, source_target_pairs={{0,192},{8,200},{16,208},{24,216},{32,224},{40,232},{48,240},{56,2... | collective-permute-start | bytes 135176 | tf_op jit(solution)/shard_map/ppermute | solution.py:29
  100.5 3.1 %collective-permute-start.15 = (f32[112,128]{1,0:T(8,128)S(1)}, f32[112,128]{1,0:T(8,128)S(1)}, u32[]{:S(2)}, u32[]{:S(2)}) collective-permute-start(f32[112,128]{1,0:T(8,128)S(1)} %pad_maximum_fusion.3), channel_id=1, source_target_pairs={{0,64},{8,72},{16,80},{24,88},{32,96},{40,104},{48,112},{56,120},{... | collective-permute-start | bytes 172040 | tf_op jit(solution)/shard_map/ppermute | solution.py:29
  125.8 12.9 %collective-permute-start.16 = (f32[256,768]{1,0:T(8,128)S(1)}, f32[256,768]{1,0:T(8,128)S(1)}, u32[]{:S(2)}, u32[]{:S(2)}) collective-permute-start(f32[256,768]{1,0:T(8,128)S(1)} %get-tuple-element.130), channel_id=1, source_target_pairs={{0,1},{1,0},{2,3},{3,2},{4,5},{5,4},{6,7},{7,6},{8,9},{9,8},{10,11... | collective-permute-start | bytes 2359304 | tf_op jit(solution)/shard_map/ppermute | solution.py:29
  136.9 2.4 %collective-permute-start.17 = (f32[384,256]{1,0:T(8,128)S(1)}, f32[384,256]{1,0:T(8,128)S(1)}, u32[]{:S(2)}, u32[]{:S(2)}) collective-permute-start(f32[384,256]{1,0:T(8,128)S(1)} %pad_maximum_fusion), channel_id=1, source_target_pairs={{0,1},{1,0},{2,3},{3,2},{4,5},{5,4},{6,7},{7,6},{8,9},{9,8},{10,11... | collective-permute-start | bytes 1179656 | tf_op jit(solution)/shard_map/ppermute | solution.py:29
  164.1 2.8 %collective-permute-start.18 = (f32[8,128]{1,0:T(8,128)S(1)}, f32[8,128]{1,0:T(8,128)S(1)}, u32[]{:S(2)}, u32[]{:S(2)}) collective-permute-start(f32[8,128]{1,0:T(8,128)S(1)} %constant_dynamic-slice_fusion.1), channel_id=1, source_target_pairs={{0,2},{1,3},{2,0},{3,1},{4,6},{5,7},{6,4},{7,5},{8,10},{9,11},{10,... | collective-permute-start | bytes 12296 | tf_op jit(solution)/shard_map/ppermute | solution.py:29
  167.2 3.7 %collective-permute-start.19 = (f32[8,128]{1,0:T(8,128)S(1)}, f32[8,128]{1,0:T(8,128)S(1)}, u32[]{:S(2)}, u32[]{:S(2)}) collective-permute-start(f32[8,128]{1,0:T(8,128)S(1)} %constant_dynamic-slice_fusion), channel_id=1, source_target_pairs={{0,6},{1,7},{2,4},{3,5},{4,2},{5,3},{6,0},{7,1},{8,14},{9,15},{10,... | collective-permute-start | bytes 12296 | tf_op jit(solution)/shard_map/ppermute | solution.py:29
  171.0 2.5 %collective-permute-start.20 = (f32[8,128]{1,0:T(8,128)S(1)}, f32[8,128]{1,0:T(8,128)S(1)}, u32[]{:S(2)}, u32[]{:S(2)}) collective-permute-start(f32[8,128]{1,0:T(8,128)S(1)} %dynamic-slice_add_fusion.2), channel_id=1, source_target_pairs={{0,2},{1,3},{2,0},{3,1},{4,6},{5,7},{6,4},{7,5},{8,10},{9,11},{10,... | collective-permute-start | bytes 12296 | tf_op jit(solution)/shard_map/ppermute | solution.py:29
  193.5 9.3 %collective-permute-start.21 = (f32[256,384]{1,0:T(8,128)S(1)}, f32[256,384]{1,0:T(8,128)S(1)}, u32[]{:S(2)}, u32[]{:S(2)}) collective-permute-start(f32[256,384]{1,0:T(8,128)S(1)} %slice.94), channel_id=1, source_target_pairs={{0,1},{1,0},{2,3},{3,2},{4,5},{5,4},{6,7},{7,6},{8,9},{9,8},{10,11... | collective-permute-start | bytes 1179656 | tf_op jit(solution)/shard_map/ppermute | solution.py:29

commit v9 on v7

--- a/solution.py
+++ b/solution.py
@@ -54,42 +54,8 @@
     return pltpu.with_memory_space_constraint(value, pltpu.HBM)
 
 
-def whole(shape):
-    return pl.BlockSpec(shape, lambda j, bits: (0,) * len(shape))
-
-
-def block(shape, *index):
-    return pl.BlockSpec(shape, lambda j, bits: index)
-
-
-def columns(rows, width):
-    return pl.BlockSpec((rows, width), lambda j, bits: (0, j))
-
-
-def run(body, steps, bits, args, in_specs, out_shape, out_specs, scratch, flops, nbytes):
-    return pl.pallas_call(
-        body,
-        out_shape=out_shape,
-        grid_spec=pltpu.PrefetchScalarGridSpec(
-            num_scalar_prefetch=1,
-            grid=(steps,),
-            in_specs=in_specs,
-            out_specs=out_specs,
-            scratch_shapes=scratch,
-        ),
-        compiler_params=pltpu.CompilerParams(
-            dimension_semantics=("arbitrary",), vmem_limit_bytes=VMEM_BYTES
-        ),
-        cost_estimate=pl.CostEstimate(flops=flops, bytes_accessed=nbytes, transcendentals=0),
-    )(bits, *args)
-
-
 def f32(*shape):
     return jax.ShapeDtypeStruct(shape, jnp.float32)
-
-
-def bf16(*shape):
-    return jax.ShapeDtypeStruct(shape, jnp.bfloat16)
 
 
 def vmem(*shape, dtype=jnp.float32):
@@ -110,47 +76,48 @@
     )(bits, *args)
 
 
-def leaf_body(bits, rhs, inverse, own_rows, other_rows, state, own, other, sums):
-    rank = own.shape[1]
-    rounded = dot(rhs[...], inverse[...]).astype(jnp.bfloat16)
-    state[...] = rounded
-    part = dot_t(rounded, jnp.concatenate([own_rows[...], other_rows[...]], axis=0))
-
-    @pl.when(pl.program_id(0) == 0)
-    def _():
-        sums[...] = part
-
-    @pl.when(pl.program_id(0) > 0)
-    def _():
-        sums[...] += part
-
-    @pl.when(pl.program_id(0) == STEPS - 1)
-    def _():
-        own[...] = sums[:, :rank]
-        other[...] = sums[:, rank:]
+def leaf_body(bits, rhs, inverse, proj, state, own, other, left, right, rows, sums, done):
+    leaf, rank = state.shape[1], own.shape[1]
+    width = leaf // STEPS
+    copies = [pltpu.make_async_copy(rhs, left, done.at[0])]
+    for i in range(STEPS):
+        here = pl.ds(i * width, width)
+        copies.append(pltpu.make_async_copy(inverse.at[0, :, here], right.at[:, here], done.at[i + 1]))
+    copies.append(pltpu.make_async_copy(proj.at[0], rows, done.at[STEPS + 1]))
+    for copy in copies:
+        copy.start()
+    copies[0].wait()
+    for i in range(STEPS):
+        copies[i + 1].wait()
+        here = slice(i * width, (i + 1) * width)
+        state[:, here] = dot(left[...], right[:, here]).astype(jnp.bfloat16)
+    copies[-1].wait()
+    sums[...] = dot_t(state[...], rows[...])
+    choose(bits[0], sums[:, :rank], sums[:, rank:], own, other)
 
 
 def leaf_solve(bits, rhs, leaf_inverse, projection):
     rows, leaf = rhs.shape
-    rank = projection.shape[1] // 2
-    width = leaf // STEPS
-    return run(
+    wide = projection.shape[1]
+    rank = wide // 2
+    args = [hbm(rhs), hbm(leaf_inverse), hbm(projection)]
+    return pl.pallas_call(
         leaf_body,
-        STEPS,
-        bits,
-        [hbm(rhs), hbm(leaf_inverse), hbm(projection), hbm(projection)],
-        [
-            whole((rows, leaf)),
-            pl.BlockSpec((None, leaf, width), lambda j, bits: (0, 0, j)),
-            pl.BlockSpec((None, rank, width), lambda j, bits: (0, bits[0], j)),
-            pl.BlockSpec((None, rank, width), lambda j, bits: (0, 1 - bits[0], j)),
+        out_shape=[vmem(rows, leaf, dtype=jnp.bfloat16), vmem(rows, rank), vmem(rows, rank)],
+        in_specs=[pl.BlockSpec(memory_space=pltpu.SMEM)] + [pl.BlockSpec(memory_space=pltpu.HBM)] * 3,
+        out_specs=[pl.BlockSpec(memory_space=pltpu.VMEM)] * 3,
+        scratch_shapes=[
+            pltpu.VMEM((rows, leaf), jnp.bfloat16),
+            pltpu.VMEM((leaf, leaf), jnp.bfloat16),
+            pltpu.VMEM((wide, leaf), jnp.bfloat16),
+            pltpu.VMEM((rows, wide), jnp.float32),
+            pltpu.SemaphoreType.DMA((STEPS + 2,)),
         ],
-        [vmem(rows, leaf, dtype=jnp.bfloat16), vmem(rows, rank), vmem(rows, rank)],
-        [columns(rows, width), whole((rows, rank)), whole((rows, rank))],
-        [pltpu.VMEM((rows, 2 * rank), jnp.float32)],
-        2 * rows * leaf * (leaf + 2 * rank),
-        leaf * (4 * rows + 2 * leaf),
-    )
+        compiler_params=pltpu.CompilerParams(vmem_limit_bytes=VMEM_BYTES),
+        cost_estimate=pl.CostEstimate(
+            flops=2 * rows * leaf * (leaf + wide), bytes_accessed=leaf * (4 * rows + 2 * leaf), transcendentals=0
+        ),
+    )(bits, *args)
 
 
 def project_body(heights, depth, pairs, bits, state, up, proj, value, gram, *kept):

time: 202 us -> 202 us (level)
  no operation moved by 1% of the time
where the time goes in v9:
time: 202 us; the launch traced here: 201 us
  blocking collectives  66.2 us (33%)
  starting transfers between devices  55.4 us (27%)
  waiting for transfers between devices  51.5 us (25%)
  Pallas kernels  25.6 us (13%)
    all_to_all x3, blocking collectives, exchange(): lax.all_to_all(value, AXES, 0, 0, tiled=True, axis_index_groups=groups)  66.2 us
    ppermute x24, waiting for transfers between devices, swap(): lax.ppermute(value, axis, [(source, source ^ mask) for source in range(si...  51.5 us
    ppermute x24, starting transfers between devices, swap(): lax.ppermute(value, axis, [(source, source ^ mask) for source in range(si...  51.5 us
    pallas_call x17, Pallas kernels, local(): pl.pallas_call(body, out_shape=outs, in_specs=[pl.BlockSpec(memory_space=...  17.9 us
    pallas_call x1, Pallas kernels, leaf_solve(): pl.pallas_call(leaf_body, out_shape=[vmem(rows, leaf, dtype=jnp.bfloat16)...  5.49 us
  transfers between devices with their start and end apart: 25, of which 19 were waited for; matrix products, arithmetic and copies ran while one was open for 0% of the time, Pallas kernels for 7%

profile of v9, /device:TPU:1, one launch (start us, length us, event | category | flops | bytes accessed | tf_op | source)
XLA Modules:
  0.0 201.4 jit_solution(7618350052427956239)
XLA Ops:
  0.1 5.5 %shard_map.46 = (bf16[512,1024]{1,0:T(8,128)(2,1)S(1)}, f32[512,128]{1,0:T(8,128)S(1)}, f32[512,128]{1,0:T(8,128)S(1)}) custom-call(s32[7]{0:T(128)S(1)} %stack.31.bits, bf16[512,1024]{1,0:T(8,128)(2,1)} %rhs, bf16[1,1024,1024]{2,1,0:T(8,128)(2,1)} %inverse.1, bf16[8,256,1024]{2,1,0:T(8,128)(2,1)} %proj.7), custom_call_target="tpu_custom_call" | custom-call | flops 1342177280 | bytes 4194304 | tf_op jit(solution)/shard_map/pallas_call | solution.py:104
  5.6 2.6 %collective-permute-start = (f32[512,128]{1,0:T(8,128)S(1)}, f32[512,128]{1,0:T(8,128)S(1)}, u32[]{:S(2)}, u32[]{:S(2)}) collective-permute-start(f32[512,128]{1,0:T(8,128)S(1)} %get-tuple-element.83), channel_id=1, source_target_pairs={{0,8},{8,0},{16,24},{24,16},{32,40},{40,32},{48,56},{56,48},{64,72... | collective-permute-start | bytes 786440 | tf_op jit(solution)/shard_map/ppermute | solution.py:29
  8.2 1.9 shard_map.48
  10.0 1.7 shard_map.47
  11.8 3.0 %shard_map.49 = (f32[3,512,256]{2,1,0:T(8,128)S(1)}, bf16[3,640,256]{2,1,0:T(8,128)(2,1)S(1)}, f32[3,128,256]{2,1,0:T(8,128)S(1)}) custom-call(s32[7]{0:T(128)S(1)} %stack.31.bits, bf16[512,1024]{1,0:T(8,128)(2,1)S(1)} %get-tuple-element.84.state, bf16[8,128,1024]{2,1,0:T(8,128)(2,1)S(1)} %copy-done.1, bf16[8,256,1024]{2,1,0:T(8,128)(2,1)S(1)} %copy-done), custom_call_target="tpu_custom_call" | custom-call | flops 2013265920 | bytes 3407872 | tf_op jit(solution)/shard_map/pallas_call | solution.py:67
  18.0 2.4 %collective-permute-done.4 = f32[192,256]{1,0:T(8,128)S(1)} collective-permute-done((f32[192,256]{1,0:T(8,128)S(1)}, f32[192,256]{1,0:T(8,128)S(1)}, u32[]{:S(2)}, u32[]{:S(2)}) %collective-permute-start.4) | collective-permute-done | bytes 196640 | tf_op jit(solution)/shard_map/ppermute | solution.py:29
  20.4 2.8 %collective-permute-start.5 = (f32[96,256]{1,0:T(8,128)S(1)}, f32[96,256]{1,0:T(8,128)S(1)}, u32[]{:S(2)}, u32[]{:S(2)}) collective-permute-start(f32[96,256]{1,0:T(8,128)S(1)} %constant_dynamic-slice_fusion.5), channel_id=1, source_target_pairs={{0,192},{8,200},{16,208},{24,216},{32,224},{40,232},{48,240},{56,2... | collective-permute-start | bytes 294920 | tf_op jit(solution)/shard_map/ppermute | solution.py:29
  23.2 2.0 collective-permute-done.5
  26.0 3.1 %collective-permute-start.2 = (f32[320,128]{1,0:T(8,128)S(1)}, f32[320,128]{1,0:T(8,128)S(1)}, u32[]{:S(2)}, u32[]{:S(2)}) collective-permute-start(f32[320,128]{1,0:T(8,128)S(1)} %get-tuple-element.97), channel_id=1, source_target_pairs={{0,16},{8,24},{16,0},{24,8},{32,48},{40,56},{48,32},{56,40},{64,80... | collective-permute-start | bytes 491528 | tf_op jit(solution)/shard_map/ppermute | solution.py:29
  29.1 8.6 %collective-permute-done.3.left = f32[384,256]{1,0:T(8,128)S(1)} collective-permute-done((f32[384,256]{1,0:T(8,128)S(1)}, f32[384,256]{1,0:T(8,128)S(1)}, u32[]{:S(2)}, u32[]{:S(2)}) %collective-permute-start.3) | collective-permute-done | bytes 393248 | tf_op jit(solution)/shard_map/ppermute | solution.py:29
  38.4 5.5 %collective-permute-start.6 = (f32[288,128]{1,0:T(8,128)S(1)}, f32[288,128]{1,0:T(8,128)S(1)}, u32[]{:S(2)}, u32[]{:S(2)}) collective-permute-start(f32[288,128]{1,0:T(8,128)S(1)} %get-tuple-element.109), channel_id=1, source_target_pairs={{0,48},{8,56},{16,32},{24,40},{32,16},{40,24},{48,0},{56,8},{64,11... | collective-permute-start | bytes 442376 | tf_op jit(solution)/shard_map/ppermute | solution.py:29
  43.9 5.7 %collective-permute-done.6 = f32[288,128]{1,0:T(8,128)S(1)} collective-permute-done((f32[288,128]{1,0:T(8,128)S(1)}, f32[288,128]{1,0:T(8,128)S(1)}, u32[]{:S(2)}, u32[]{:S(2)}) %collective-permute-start.6) | collective-permute-done | bytes 147488 | tf_op jit(solution)/shard_map/ppermute | solution.py:29
  49.6 1.7 collective-permute-start.7
  52.1 2.4 %collective-permute-done.7 = f32[256,128]{1,0:T(8,128)S(1)} collective-permute-done((f32[256,128]{1,0:T(8,128)S(1)}, f32[256,128]{1,0:T(8,128)S(1)}, u32[]{:S(2)}, u32[]{:S(2)}) %collective-permute-start.7) | collective-permute-done | bytes 131104 | tf_op jit(solution)/shard_map/ppermute | solution.py:29
  54.5 2.4 %collective-permute-start.9 = (f32[256,128]{1,0:T(8,128)S(1)}, f32[256,128]{1,0:T(8,128)S(1)}, u32[]{:S(2)}, u32[]{:S(2)}) collective-permute-start(f32[256,128]{1,0:T(8,128)S(1)} %add.43.c3), channel_id=1, source_target_pairs={{0,8},{8,0},{16,24},{24,16},{32,40},{40,32},{48,56},{56,48},{64,72... | collective-permute-start | bytes 393224 | tf_op jit(solution)/shard_map/ppermute | solution.py:29
  56.9 3.1 %collective-permute-done.9.c3_there = f32[256,128]{1,0:T(8,128)S(1)} collective-permute-done((f32[256,128]{1,0:T(8,128)S(1)}, f32[256,128]{1,0:T(8,128)S(1)}, u32[]{:S(2)}, u32[]{:S(2)}) %collective-permute-start.9) | collective-permute-done | bytes 131104 | tf_op jit(solution)/shard_map/ppermute | solution.py:29
  62.1 3.9 %collective-permute-start.14 = (f32[512,128]{1,0:T(8,128)S(1)}, f32[512,128]{1,0:T(8,128)S(1)}, u32[]{:S(2)}, u32[]{:S(2)}) collective-permute-start(f32[512,128]{1,0:T(8,128)S(1)} %get-tuple-element.126), channel_id=1, source_target_pairs={{0,56},{8,16},{16,8},{24,32},{32,24},{40,48},{48,40},{56,0},{64,12... | collective-permute-start | bytes 786440 | tf_op jit(solution)/shard_map/ppermute | solution.py:533
  68.1 4.7 %collective-permute-start.11 = (f32[368,128]{1,0:T(8,128)S(1)}, f32[368,128]{1,0:T(8,128)S(1)}, u32[]{:S(2)}, u32[]{:S(2)}) collective-permute-start(f32[368,128]{1,0:T(8,128)S(1)} %get-tuple-element.118), channel_id=1, source_target_pairs={{0,16},{8,24},{16,0},{24,8},{32,48},{40,56},{48,32},{56,40},{64,80... | collective-permute-start | bytes 565256 | tf_op jit(solution)/shard_map/ppermute | solution.py:29
  73.4 4.7 %collective-permute-done.11.got = f32[368,128]{1,0:T(8,128)S(1)} collective-permute-done((f32[368,128]{1,0:T(8,128)S(1)}, f32[368,128]{1,0:T(8,128)S(1)}, u32[]{:S(2)}, u32[]{:S(2)}) %collective-permute-start.11) | collective-permute-done | bytes 188448 | tf_op jit(solution)/shard_map/ppermute | solution.py:29
  78.8 2.6 %collective-permute-done.15.got = f32[256,128]{1,0:T(8,128)S(1)} collective-permute-done((f32[256,128]{1,0:T(8,128)S(1)}, f32[256,128]{1,0:T(8,128)S(1)}, u32[]{:S(2)}, u32[]{:S(2)}) %collective-permute-start.15) | collective-permute-done | bytes 131104 | tf_op jit(solution)/shard_map/ppermute | solution.py:29
  82.3 3.3 %collective-permute-done.12.got = f32[280,128]{1,0:T(8,128)S(1)} collective-permute-done((f32[280,128]{1,0:T(8,128)S(1)}, f32[280,128]{1,0:T(8,128)S(1)}, u32[]{:S(2)}, u32[]{:S(2)}) %collective-permute-start.12) | collective-permute-done | bytes 143392 | tf_op jit(solution)/shard_map/ppermute | solution.py:29
  86.9 2.5 %collective-permute-done.13 = f32[64,128]{1,0:T(8,128)S(1)} collective-permute-done((f32[64,128]{1,0:T(8,128)S(1)}, f32[64,128]{1,0:T(8,128)S(1)}, u32[]{:S(2)}, u32[]{:S(2)}) %collective-permute-start.13) | collective-permute-done | bytes 32800 | tf_op jit(solution)/shard_map/ppermute | solution.py:29
  90.2 3.5 %collective-permute-done.17 = f32[88,128]{1,0:T(8,128)S(1)} collective-permute-done((f32[88,128]{1,0:T(8,128)S(1)}, f32[88,128]{1,0:T(8,128)S(1)}, u32[]{:S(2)}, u32[]{:S(2)}) %collective-permute-start.17) | collective-permute-done | bytes 45088 | tf_op jit(solution)/shard_map/ppermute | solution.py:29
  94.0 3.0 %collective-permute-done.18 = f32[112,128]{1,0:T(8,128)S(1)} collective-permute-done((f32[112,128]{1,0:T(8,128)S(1)}, f32[112,128]{1,0:T(8,128)S(1)}, u32[]{:S(2)}, u32[]{:S(2)}) %collective-permute-start.18) | collective-permute-done | bytes 57376 | tf_op jit(solution)/shard_map/ppermute | solution.py:29
  97.1 23.0 %all_to_all.15.packed = f32[8,224,128]{2,1,0:T(8,128)S(1)} all-to-all(f32[8,224,128]{2,1,0:T(8,128)S(1)} %broadcast_in_dim.6), channel_id=1, replica_groups={{0,8,16,24,32,40,48,56},{64,72,80,88,96,104,112,120},{128,136,144,152,1..., dimensions={0} | all-to-all | bytes 1835008 | tf_op jit(solution)/shard_map/all_to_all | solution.py:33
  121.6 11.6 %collective-permute-start.19 = (f32[256,768]{1,0:T(8,128)S(1)}, f32[256,768]{1,0:T(8,128)S(1)}, u32[]{:S(2)}, u32[]{:S(2)}) collective-permute-start(f32[256,768]{1,0:T(8,128)S(1)} %get-tuple-element.140), channel_id=1, source_target_pairs={{0,1},{1,0},{2,3},{3,2},{4,5},{5,4},{6,7},{7,6},{8,9},{9,8},{10,11... | collective-permute-start | bytes 2359304 | tf_op jit(solution)/shard_map/ppermute | solution.py:29
  133.4 1.7 collective-permute-done.19.right
  135.7 23.3 %all_to_all.16.parts = f32[32,8,768]{2,1,0:T(8,128)S(1)} all-to-all(f32[32,8,768]{2,1,0:T(8,128)S(1)} %bitcast.25), channel_id=1, replica_groups={{0,8,16,24,32,40,48,56,64,72,80,88,96,104,112,120,128,136,144,152,160,1..., dimensions={0} | all-to-all | bytes 1572864 | tf_op jit(solution)/shard_map/all_to_all | solution.py:33
  163.3 2.5 %collective-permute-start.22 = (f32[8,128]{1,0:T(8,128)S(1)}, f32[8,128]{1,0:T(8,128)S(1)}, u32[]{:S(2)}, u32[]{:S(2)}) collective-permute-start(f32[8,128]{1,0:T(8,128)S(1)} %constant_dynamic-slice_fusion), channel_id=1, source_target_pairs={{0,6},{1,7},{2,4},{3,5},{4,2},{5,3},{6,0},{7,1},{8,14},{9,15},{10,... | collective-permute-start | bytes 12296 | tf_op jit(solution)/shard_map/ppermute | solution.py:29
  169.7 19.9 %all_to_all.17 = f32[32,8,512]{2,1,0:T(8,128)S(1)} all-to-all(f32[32,8,512]{2,1,0:T(8,128)S(1)} %broadcast_in_dim.7), channel_id=1, replica_groups={{0,8,16,24,32,40,48,56,64,72,80,88,96,104,112,120,128,136,144,152,160,1..., dimensions={0} | all-to-all | bytes 1048576 | tf_op jit(solution)/shard_map/all_to_all | solution.py:33
  189.6 8.0 %collective-permute-start.24 = (f32[256,384]{1,0:T(8,128)S(1)}, f32[256,384]{1,0:T(8,128)S(1)}, u32[]{:S(2)}, u32[]{:S(2)}) collective-permute-start(f32[256,384]{1,0:T(8,128)S(1)} %slice.94), channel_id=1, source_target_pairs={{0,1},{1,0},{2,3},{3,2},{4,5},{5,4},{6,7},{7,6},{8,9},{9,8},{10,11... | collective-permute-start | bytes 1179656 | tf_op jit(solution)/shard_map/ppermute | solution.py:29
  199.0 2.3 %shard_map.64 = f32[512,1024]{1,0:T(8,128)} custom-call(s32[7]{0:T(128)S(1)} %stack.31.bits, f32[512,1024]{1,0:T(8,128)S(1)} %shard_map.63.state, f32[256,512]{1,0:T(8,128)S(1)} %bitcast.24, f32[256,384]{1,0:T(8,128)S(1)} %collective-permute-done.24.received, bf16[8,128,1024]{2,1,0:T(8,128)(2,1)S(1)} %copy-done.1), custom_call_target="tpu_custom_call" | custom-call | flops 402653184 | bytes 3145728 | tf_op jit(solution)/shard_map/pallas_call | solution.py:463
  (87 shorter events, 26.2 us)
Async XLA Ops:
  0.1 8.1 %copy-start = (bf16[8,256,1024]{2,1,0:T(8,128)(2,1)S(1)}, bf16[8,256,1024]{2,1,0:T(8,128)(2,1)}, u32[]{:S(2)}) copy-start(bf16[8,256,1024]{2,1,0:T(8,128)(2,1)} %proj.7) | copy-start | bytes 12582916
  0.1 8.1 %copy-start.1 = (bf16[8,128,1024]{2,1,0:T(8,128)(2,1)S(1)}, bf16[8,128,1024]{2,1,0:T(8,128)(2,1)}, u32[]{:S(2)}) copy-start(bf16[8,128,1024]{2,1,0:T(8,128)(2,1)} %up.9) | copy-start | bytes 6291460
  5.6 9.2 %collective-permute-start = (f32[512,128]{1,0:T(8,128)S(1)}, f32[512,128]{1,0:T(8,128)S(1)}, u32[]{:S(2)}, u32[]{:S(2)}) collective-permute-start(f32[512,128]{1,0:T(8,128)S(1)} %get-tuple-element.83), channel_id=1, source_target_pairs={{0,8},{8,0},{16,24},{24,16},{32,40},{40,32},{48,56},{56,48},{64,72... | collective-permute-start | bytes 786440 | tf_op jit(solution)/shard_map/ppermute | solution.py:29
  14.8 5.6 %collective-permute-start.4 = (f32[192,256]{1,0:T(8,128)S(1)}, f32[192,256]{1,0:T(8,128)S(1)}, u32[]{:S(2)}, u32[]{:S(2)}) collective-permute-start(f32[192,256]{1,0:T(8,128)S(1)} %constant_dynamic-slice_fusion.6), channel_id=1, source_target_pairs={{0,64},{8,72},{16,80},{24,88},{32,96},{40,104},{48,112},{56,120},{... | collective-permute-start | bytes 589832 | tf_op jit(solution)/shard_map/ppermute | solution.py:29
  17.3 8.1 %collective-permute-start.1 = (f32[320,256]{1,0:T(8,128)S(1)}, f32[320,256]{1,0:T(8,128)S(1)}, u32[]{:S(2)}, u32[]{:S(2)}) collective-permute-start(f32[320,256]{1,0:T(8,128)S(1)} %get-tuple-element.95), channel_id=1, source_target_pairs={{0,8},{8,0},{16,24},{24,16},{32,40},{40,32},{48,56},{56,48},{64,72... | collective-permute-start | bytes 983048 | tf_op jit(solution)/shard_map/ppermute | solution.py:29
  20.4 4.8 %collective-permute-start.5 = (f32[96,256]{1,0:T(8,128)S(1)}, f32[96,256]{1,0:T(8,128)S(1)}, u32[]{:S(2)}, u32[]{:S(2)}) collective-permute-start(f32[96,256]{1,0:T(8,128)S(1)} %constant_dynamic-slice_fusion.5), channel_id=1, source_target_pairs={{0,192},{8,200},{16,208},{24,216},{32,224},{40,232},{48,240},{56,2... | collective-permute-start | bytes 294920 | tf_op jit(solution)/shard_map/ppermute | solution.py:29
  23.2 14.4 %collective-permute-start.3 = (f32[384,256]{1,0:T(8,128)S(1)}, f32[384,256]{1,0:T(8,128)S(1)}, u32[]{:S(2)}, u32[]{:S(2)}) collective-permute-start(f32[384,256]{1,0:T(8,128)S(1)} %get-tuple-element.100), channel_id=1, source_target_pairs={{0,8},{8,0},{16,24},{24,16},{32,40},{40,32},{48,56},{56,48},{64,72... | collective-permute-start | bytes 1179656 | tf_op jit(solution)/shard_map/ppermute | solution.py:29
  26.0 11.6 %collective-permute-start.2 = (f32[320,128]{1,0:T(8,128)S(1)}, f32[320,128]{1,0:T(8,128)S(1)}, u32[]{:S(2)}, u32[]{:S(2)}) collective-permute-start(f32[320,128]{1,0:T(8,128)S(1)} %get-tuple-element.97), channel_id=1, source_target_pairs={{0,16},{8,24},{16,0},{24,8},{32,48},{40,56},{48,32},{56,40},{64,80... | collective-permute-start | bytes 491528 | tf_op jit(solution)/shard_map/ppermute | solution.py:29
  38.4 11.2 %collective-permute-start.6 = (f32[288,128]{1,0:T(8,128)S(1)}, f32[288,128]{1,0:T(8,128)S(1)}, u32[]{:S(2)}, u32[]{:S(2)}) collective-permute-start(f32[288,128]{1,0:T(8,128)S(1)} %get-tuple-element.109), channel_id=1, source_target_pairs={{0,48},{8,56},{16,32},{24,40},{32,16},{40,24},{48,0},{56,8},{64,11... | collective-permute-start | bytes 442376 | tf_op jit(solution)/shard_map/ppermute | solution.py:29
  49.6 4.9 %collective-permute-start.7 = (f32[256,128]{1,0:T(8,128)S(1)}, f32[256,128]{1,0:T(8,128)S(1)}, u32[]{:S(2)}, u32[]{:S(2)}) collective-permute-start(f32[256,128]{1,0:T(8,128)S(1)} %slice_add_fusion), channel_id=1, source_target_pairs={{0,16},{8,24},{16,0},{24,8},{32,48},{40,56},{48,32},{56,40},{64,80... | collective-permute-start | bytes 393224 | tf_op jit(solution)/shard_map/ppermute | solution.py:29
  51.3 5.6 %collective-permute-start.8 = (f32[256,128]{1,0:T(8,128)S(1)}, f32[256,128]{1,0:T(8,128)S(1)}, u32[]{:S(2)}, u32[]{:S(2)}) collective-permute-start(f32[256,128]{1,0:T(8,128)S(1)} %get-tuple-element.107.c2), channel_id=1, source_target_pairs={{0,8},{8,0},{16,24},{24,16},{32,40},{40,32},{48,56},{56,48},{64,72... | collective-permute-start | bytes 393224 | tf_op jit(solution)/shard_map/ppermute | solution.py:29
  54.5 5.5 %collective-permute-start.9 = (f32[256,128]{1,0:T(8,128)S(1)}, f32[256,128]{1,0:T(8,128)S(1)}, u32[]{:S(2)}, u32[]{:S(2)}) collective-permute-start(f32[256,128]{1,0:T(8,128)S(1)} %add.43.c3), channel_id=1, source_target_pairs={{0,8},{8,0},{16,24},{24,16},{32,40},{40,32},{48,56},{56,48},{64,72... | collective-permute-start | bytes 393224 | tf_op jit(solution)/shard_map/ppermute | solution.py:29
  61.3 6.2 %collective-permute-start.10 = (f32[640,128]{1,0:T(8,128)S(1)}, f32[640,128]{1,0:T(8,128)S(1)}, u32[]{:S(2)}, u32[]{:S(2)}) collective-permute-start(f32[640,128]{1,0:T(8,128)S(1)} %get-tuple-element.116), channel_id=1, source_target_pairs={{0,8},{8,0},{16,24},{24,16},{32,40},{40,32},{48,56},{56,48},{64,72... | collective-permute-start | bytes 983048 | tf_op jit(solution)/shard_map/ppermute | solution.py:29
  62.1 10.6 %collective-permute-start.14 = (f32[512,128]{1,0:T(8,128)S(1)}, f32[512,128]{1,0:T(8,128)S(1)}, u32[]{:S(2)}, u32[]{:S(2)}) collective-permute-start(f32[512,128]{1,0:T(8,128)S(1)} %get-tuple-element.126), channel_id=1, source_target_pairs={{0,56},{8,16},{16,8},{24,32},{32,24},{40,48},{48,40},{56,0},{64,12... | collective-permute-start | bytes 786440 | tf_op jit(solution)/shard_map/ppermute | solution.py:533
  68.1 10.1 %collective-permute-start.11 = (f32[368,128]{1,0:T(8,128)S(1)}, f32[368,128]{1,0:T(8,128)S(1)}, u32[]{:S(2)}, u32[]{:S(2)}) collective-permute-start(f32[368,128]{1,0:T(8,128)S(1)} %get-tuple-element.118), channel_id=1, source_target_pairs={{0,16},{8,24},{16,0},{24,8},{32,48},{40,56},{48,32},{56,40},{64,80... | collective-permute-start | bytes 565256 | tf_op jit(solution)/shard_map/ppermute | solution.py:29
  73.3 8.1 %collective-permute-start.15 = (f32[256,128]{1,0:T(8,128)S(1)}, f32[256,128]{1,0:T(8,128)S(1)}, u32[]{:S(2)}, u32[]{:S(2)}) collective-permute-start(f32[256,128]{1,0:T(8,128)S(1)} %get-tuple-element.128), channel_id=1, source_target_pairs={{0,48},{8,56},{16,32},{24,40},{32,16},{40,24},{48,0},{56,8},{64,11... | collective-permute-start | bytes 393224 | tf_op jit(solution)/shard_map/ppermute | solution.py:29
  78.7 6.9 %collective-permute-start.12 = (f32[280,128]{1,0:T(8,128)S(1)}, f32[280,128]{1,0:T(8,128)S(1)}, u32[]{:S(2)}, u32[]{:S(2)}) collective-permute-start(f32[280,128]{1,0:T(8,128)S(1)} %get-tuple-element.121), channel_id=1, source_target_pairs={{0,48},{8,56},{16,32},{24,40},{32,16},{40,24},{48,0},{56,8},{64,11... | collective-permute-start | bytes 430088 | tf_op jit(solution)/shard_map/ppermute | solution.py:29
  82.0 4.3 %collective-permute-start.16 = (f32[128,128]{1,0:T(8,128)S(1)}, f32[128,128]{1,0:T(8,128)S(1)}, u32[]{:S(2)}, u32[]{:S(2)}) collective-permute-start(f32[128,128]{1,0:T(8,128)S(1)} %get-tuple-element.130), channel_id=1, source_target_pairs={{0,16},{8,24},{16,0},{24,8},{32,48},{40,56},{48,32},{56,40},{64,80... | collective-permute-start | bytes 196616 | tf_op jit(solution)/shard_map/ppermute | solution.py:29
  86.2 3.1 %collective-permute-start.13 = (f32[64,128]{1,0:T(8,128)S(1)}, f32[64,128]{1,0:T(8,128)S(1)}, u32[]{:S(2)}, u32[]{:S(2)}) collective-permute-start(f32[64,128]{1,0:T(8,128)S(1)} %get-tuple-element.124), channel_id=1, source_target_pairs={{0,64},{8,72},{16,80},{24,88},{32,96},{40,104},{48,112},{56,120},{... | collective-permute-start | bytes 98312 | tf_op jit(solution)/shard_map/ppermute | solution.py:29
  89.6 4.2 %collective-permute-start.17 = (f32[88,128]{1,0:T(8,128)S(1)}, f32[88,128]{1,0:T(8,128)S(1)}, u32[]{:S(2)}, u32[]{:S(2)}) collective-permute-start(f32[88,128]{1,0:T(8,128)S(1)} %pad_maximum_fusion.4), channel_id=1, source_target_pairs={{0,192},{8,200},{16,208},{24,216},{32,224},{40,232},{48,240},{56,2... | collective-permute-start | bytes 135176 | tf_op jit(solution)/shard_map/ppermute | solution.py:29
  93.9 3.1 %collective-permute-start.18 = (f32[112,128]{1,0:T(8,128)S(1)}, f32[112,128]{1,0:T(8,128)S(1)}, u32[]{:S(2)}, u32[]{:S(2)}) collective-permute-start(f32[112,128]{1,0:T(8,128)S(1)} %pad_maximum_fusion.3), channel_id=1, source_target_pairs={{0,64},{8,72},{16,80},{24,88},{32,96},{40,104},{48,112},{56,120},{... | collective-permute-start | bytes 172040 | tf_op jit(solution)/shard_map/ppermute | solution.py:29
  121.6 13.5 %collective-permute-start.19 = (f32[256,768]{1,0:T(8,128)S(1)}, f32[256,768]{1,0:T(8,128)S(1)}, u32[]{:S(2)}, u32[]{:S(2)}) collective-permute-start(f32[256,768]{1,0:T(8,128)S(1)} %get-tuple-element.140), channel_id=1, source_target_pairs={{0,1},{1,0},{2,3},{3,2},{4,5},{5,4},{6,7},{7,6},{8,9},{9,8},{10,11... | collective-permute-start | bytes 2359304 | tf_op jit(solution)/shard_map/ppermute | solution.py:29
  133.3 2.4 %collective-permute-start.20 = (f32[384,256]{1,0:T(8,128)S(1)}, f32[384,256]{1,0:T(8,128)S(1)}, u32[]{:S(2)}, u32[]{:S(2)}) collective-permute-start(f32[384,256]{1,0:T(8,128)S(1)} %pad_maximum_fusion), channel_id=1, source_target_pairs={{0,1},{1,0},{2,3},{3,2},{4,5},{5,4},{6,7},{7,6},{8,9},{9,8},{10,11... | collective-permute-start | bytes 1179656 | tf_op jit(solution)/shard_map/ppermute | solution.py:29
  160.2 2.8 %collective-permute-start.21 = (f32[8,128]{1,0:T(8,128)S(1)}, f32[8,128]{1,0:T(8,128)S(1)}, u32[]{:S(2)}, u32[]{:S(2)}) collective-permute-start(f32[8,128]{1,0:T(8,128)S(1)} %constant_dynamic-slice_fusion.1), channel_id=1, source_target_pairs={{0,2},{1,3},{2,0},{3,1},{4,6},{5,7},{6,4},{7,5},{8,10},{9,11},{10,... | collective-permute-start | bytes 12296 | tf_op jit(solution)/shard_map/ppermute | solution.py:29
  163.3 3.7 %collective-permute-start.22 = (f32[8,128]{1,0:T(8,128)S(1)}, f32[8,128]{1,0:T(8,128)S(1)}, u32[]{:S(2)}, u32[]{:S(2)}) collective-permute-start(f32[8,128]{1,0:T(8,128)S(1)} %constant_dynamic-slice_fusion), channel_id=1, source_target_pairs={{0,6},{1,7},{2,4},{3,5},{4,2},{5,3},{6,0},{7,1},{8,14},{9,15},{10,... | collective-permute-start | bytes 12296 | tf_op jit(solution)/shard_map/ppermute | solution.py:29
  167.1 2.5 %collective-permute-start.23 = (f32[8,128]{1,0:T(8,128)S(1)}, f32[8,128]{1,0:T(8,128)S(1)}, u32[]{:S(2)}, u32[]{:S(2)}) collective-permute-start(f32[8,128]{1,0:T(8,128)S(1)} %dynamic-slice_add_fusion.2), channel_id=1, source_target_pairs={{0,2},{1,3},{2,0},{3,1},{4,6},{5,7},{6,4},{7,5},{8,10},{9,11},{10,... | collective-permute-start | bytes 12296 | tf_op jit(solution)/shard_map/ppermute | solution.py:29
  189.6 9.3 %collective-permute-start.24 = (f32[256,384]{1,0:T(8,128)S(1)}, f32[256,384]{1,0:T(8,128)S(1)}, u32[]{:S(2)}, u32[]{:S(2)}) collective-permute-start(f32[256,384]{1,0:T(8,128)S(1)} %slice.94), channel_id=1, source_target_pairs={{0,1},{1,0},{2,3},{3,2},{4,5},{5,4},{6,7},{7,6},{8,9},{9,8},{10,11... | collective-permute-start | bytes 1179656 | tf_op jit(solution)/shard_map/ppermute | solution.py:29

commit v10 on v9

--- a/solution.py
+++ b/solution.py
@@ -514,13 +514,13 @@
     keep, send, keep_3, send_3, c1 = second(bits, own, received, value, gram, kept, kept_45)
     received = over_x(send, mask=1)
     left = over_x(send_3, mask=1)
+    own, send, low = third(bits, keep, received)
+    send, kept_678 = lax.optimization_barrier((send, kept_678))
     high, high_send = split(kept_678.reshape(3 * rank, wide), by_y01)
     high, high_send = split(high + over_x(high_send, mask=8), by_y1)
     high = high + over_x(high_send, mask=24)
     high = jnp.concatenate([high[:, :rank], high[:, rank:]])
 
-    own, send, low = third(bits, keep, received)
-    left, high = lax.optimization_barrier((left, high))
     c2, own, send, low = correct(bits, own, over_x(send, mask=2), low, keep_3, left)
     received = over_x(send, mask=6)
     c3, low = own + received[: rows // 2], low + received[rows // 2 :]

time: 202 us -> 203 us (level)
  starting transfers between devices: 55.4 us -> 58.1 us
    ppermute x24, starting transfers between devices: 51.5 us -> 55.4 us  [swap(): lax.ppermute(value, axis, [(source, source ^ mask) for source in range(si...]
  transfers between devices with their start and end apart: 25 -> 25, of which waited for: 19 -> 17; matrix products, arithmetic and copies ran while one was open for 0% -> 0% of each run, Pallas kernels for 7% -> 6%
where the time goes in v10:
time: 203 us
  blocking collectives  65.3 us (32%)
  starting transfers between devices  58.1 us (29%)
  waiting for transfers between devices  51 us (25%)
  Pallas kernels  25.6 us (13%)
    all_to_all x3, blocking collectives, exchange(): lax.all_to_all(value, AXES, 0, 0, tiled=True, axis_index_groups=groups)  65.3 us
    ppermute x24, starting transfers between devices, swap(): lax.ppermute(value, axis, [(source, source ^ mask) for source in range(si...  55.4 us
    ppermute x24, waiting for transfers between devices, swap(): lax.ppermute(value, axis, [(source, source ^ mask) for source in range(si...  51 us
    pallas_call x17, Pallas kernels, local(): pl.pallas_call(body, out_shape=outs, in_specs=[pl.BlockSpec(memory_space=...  17.9 us
    pallas_call x1, Pallas kernels, leaf_solve(): pl.pallas_call(leaf_body, out_shape=[vmem(rows, leaf, dtype=jnp.bfloat16)...  5.49 us
  transfers between devices with their start and end apart: 25, of which 17 were waited for; matrix products, arithmetic and copies ran while one was open for 0% of the time, Pallas kernels for 6%

profile of v10, /device:TPU:1, one launch (start us, length us, event | category | flops | bytes accessed | tf_op | source)
XLA Modules:
  0.0 202.7 jit_solution(518203491164270967)
XLA Ops:
  0.1 5.5 %shard_map.46 = (bf16[512,1024]{1,0:T(8,128)(2,1)S(1)}, f32[512,128]{1,0:T(8,128)S(1)}, f32[512,128]{1,0:T(8,128)S(1)}) custom-call(s32[7]{0:T(128)S(1)} %stack.31.bits, bf16[512,1024]{1,0:T(8,128)(2,1)} %rhs, bf16[1,1024,1024]{2,1,0:T(8,128)(2,1)} %inverse.1, bf16[8,256,1024]{2,1,0:T(8,128)(2,1)} %proj.7), custom_call_target="tpu_custom_call" | custom-call | flops 1342177280 | bytes 4194304 | tf_op jit(solution)/shard_map/pallas_call | solution.py:104
  5.6 2.6 %collective-permute-start = (f32[512,128]{1,0:T(8,128)S(1)}, f32[512,128]{1,0:T(8,128)S(1)}, u32[]{:S(2)}, u32[]{:S(2)}) collective-permute-start(f32[512,128]{1,0:T(8,128)S(1)} %get-tuple-element.83), channel_id=1, source_target_pairs={{0,8},{8,0},{16,24},{24,16},{32,40},{40,32},{48,56},{56,48},{64,72... | collective-permute-start | bytes 786440 | tf_op jit(solution)/shard_map/ppermute | solution.py:29
  8.2 1.9 shard_map.48
  10.0 1.7 shard_map.47
  11.8 3.0 %shard_map.49 = (f32[3,512,256]{2,1,0:T(8,128)S(1)}, bf16[3,640,256]{2,1,0:T(8,128)(2,1)S(1)}, f32[3,128,256]{2,1,0:T(8,128)S(1)}) custom-call(s32[7]{0:T(128)S(1)} %stack.31.bits, bf16[512,1024]{1,0:T(8,128)(2,1)S(1)} %get-tuple-element.84.state, bf16[8,128,1024]{2,1,0:T(8,128)(2,1)S(1)} %copy-done.1, bf16[8,256,1024]{2,1,0:T(8,128)(2,1)S(1)} %copy-done), custom_call_target="tpu_custom_call" | custom-call | flops 2013265920 | bytes 3407872 | tf_op jit(solution)/shard_map/pallas_call | solution.py:67
  16.6 7.7 %collective-permute-done.1.received = f32[320,256]{1,0:T(8,128)S(1)} collective-permute-done((f32[320,256]{1,0:T(8,128)S(1)}, f32[320,256]{1,0:T(8,128)S(1)}, u32[]{:S(2)}, u32[]{:S(2)}) %collective-permute-start.1) | collective-permute-done | bytes 327712 | tf_op jit(solution)/shard_map/ppermute | solution.py:29
  26.3 3.0 %collective-permute-start.2 = (f32[320,128]{1,0:T(8,128)S(1)}, f32[320,128]{1,0:T(8,128)S(1)}, u32[]{:S(2)}, u32[]{:S(2)}) collective-permute-start(f32[320,128]{1,0:T(8,128)S(1)} %get-tuple-element.99), channel_id=1, source_target_pairs={{0,16},{8,24},{16,0},{24,8},{32,48},{40,56},{48,32},{56,40},{64,80... | collective-permute-start | bytes 491528 | tf_op jit(solution)/shard_map/ppermute | solution.py:29
  29.6 2.8 %collective-permute-start.9 = (f32[96,256]{1,0:T(8,128)S(1)}, f32[96,256]{1,0:T(8,128)S(1)}, u32[]{:S(2)}, u32[]{:S(2)}) collective-permute-start(f32[96,256]{1,0:T(8,128)S(1)} %constant_dynamic-slice_fusion.5), channel_id=1, source_target_pairs={{0,192},{8,200},{16,208},{24,216},{32,224},{40,232},{48,240},{56,2... | collective-permute-start | bytes 294920 | tf_op jit(solution)/shard_map/ppermute | solution.py:29
  32.4 6.8 %collective-permute-done.3.left = f32[384,256]{1,0:T(8,128)S(1)} collective-permute-done((f32[384,256]{1,0:T(8,128)S(1)}, f32[384,256]{1,0:T(8,128)S(1)}, u32[]{:S(2)}, u32[]{:S(2)}) %collective-permute-start.3) | collective-permute-done | bytes 393248 | tf_op jit(solution)/shard_map/ppermute | solution.py:29
  40.0 1.8 collective-permute-start.6
  41.8 3.5 %collective-permute-start.4 = (f32[288,128]{1,0:T(8,128)S(1)}, f32[288,128]{1,0:T(8,128)S(1)}, u32[]{:S(2)}, u32[]{:S(2)}) collective-permute-start(f32[288,128]{1,0:T(8,128)S(1)} %get-tuple-element.105), channel_id=1, source_target_pairs={{0,48},{8,56},{16,32},{24,40},{32,16},{40,24},{48,0},{56,8},{64,11... | collective-permute-start | bytes 442376 | tf_op jit(solution)/shard_map/ppermute | solution.py:29
  45.3 4.1 %collective-permute-done.4 = f32[288,128]{1,0:T(8,128)S(1)} collective-permute-done((f32[288,128]{1,0:T(8,128)S(1)}, f32[288,128]{1,0:T(8,128)S(1)}, u32[]{:S(2)}, u32[]{:S(2)}) %collective-permute-start.4) | collective-permute-done | bytes 147488 | tf_op jit(solution)/shard_map/ppermute | solution.py:29
  49.5 5.8 %collective-permute-done.5 = f32[256,128]{1,0:T(8,128)S(1)} collective-permute-done((f32[256,128]{1,0:T(8,128)S(1)}, f32[256,128]{1,0:T(8,128)S(1)}, u32[]{:S(2)}, u32[]{:S(2)}) %collective-permute-start.5) | collective-permute-done | bytes 131104 | tf_op jit(solution)/shard_map/ppermute | solution.py:29
  55.4 4.4 %collective-permute-done.7.c3_there = f32[256,128]{1,0:T(8,128)S(1)} collective-permute-done((f32[256,128]{1,0:T(8,128)S(1)}, f32[256,128]{1,0:T(8,128)S(1)}, u32[]{:S(2)}, u32[]{:S(2)}) %collective-permute-start.7) | collective-permute-done | bytes 131104 | tf_op jit(solution)/shard_map/ppermute | solution.py:29
  62.2 2.7 %collective-permute-start.14 = (f32[512,128]{1,0:T(8,128)S(1)}, f32[512,128]{1,0:T(8,128)S(1)}, u32[]{:S(2)}, u32[]{:S(2)}) collective-permute-start(f32[512,128]{1,0:T(8,128)S(1)} %get-tuple-element.126), channel_id=1, source_target_pairs={{0,56},{8,16},{16,8},{24,32},{32,24},{40,48},{48,40},{56,0},{64,12... | collective-permute-start | bytes 786440 | tf_op jit(solution)/shard_map/ppermute | solution.py:533
  64.8 2.8 %collective-permute-done.10.got = f32[640,128]{1,0:T(8,128)S(1)} collective-permute-done((f32[640,128]{1,0:T(8,128)S(1)}, f32[640,128]{1,0:T(8,128)S(1)}, u32[]{:S(2)}, u32[]{:S(2)}) %collective-permute-start.10) | collective-permute-done | bytes 327712 | tf_op jit(solution)/shard_map/ppermute | solution.py:29
  68.3 1.9 collective-permute-start.11
  70.8 2.8 %collective-permute-start.15 = (f32[256,128]{1,0:T(8,128)S(1)}, f32[256,128]{1,0:T(8,128)S(1)}, u32[]{:S(2)}, u32[]{:S(2)}) collective-permute-start(f32[256,128]{1,0:T(8,128)S(1)} %get-tuple-element.128), channel_id=1, source_target_pairs={{0,48},{8,56},{16,32},{24,40},{32,16},{40,24},{48,0},{56,8},{64,11... | collective-permute-start | bytes 393224 | tf_op jit(solution)/shard_map/ppermute | solution.py:29
  73.5 3.8 %collective-permute-done.11.got = f32[368,128]{1,0:T(8,128)S(1)} collective-permute-done((f32[368,128]{1,0:T(8,128)S(1)}, f32[368,128]{1,0:T(8,128)S(1)}, u32[]{:S(2)}, u32[]{:S(2)}) %collective-permute-start.11) | collective-permute-done | bytes 188448 | tf_op jit(solution)/shard_map/ppermute | solution.py:29
  77.9 2.6 %collective-permute-start.12 = (f32[280,128]{1,0:T(8,128)S(1)}, f32[280,128]{1,0:T(8,128)S(1)}, u32[]{:S(2)}, u32[]{:S(2)}) collective-permute-start(f32[280,128]{1,0:T(8,128)S(1)} %get-tuple-element.121), channel_id=1, source_target_pairs={{0,48},{8,56},{16,32},{24,40},{32,16},{40,24},{48,0},{56,8},{64,11... | collective-permute-start | bytes 430088 | tf_op jit(solution)/shard_map/ppermute | solution.py:29
  81.1 2.5 %collective-permute-start.16 = (f32[128,128]{1,0:T(8,128)S(1)}, f32[128,128]{1,0:T(8,128)S(1)}, u32[]{:S(2)}, u32[]{:S(2)}) collective-permute-start(f32[128,128]{1,0:T(8,128)S(1)} %get-tuple-element.130), channel_id=1, source_target_pairs={{0,16},{8,24},{16,0},{24,8},{32,48},{40,56},{48,32},{56,40},{64,80... | collective-permute-start | bytes 196616 | tf_op jit(solution)/shard_map/ppermute | solution.py:29
  84.9 2.9 %collective-permute-done.16.got = f32[128,128]{1,0:T(8,128)S(1)} collective-permute-done((f32[128,128]{1,0:T(8,128)S(1)}, f32[128,128]{1,0:T(8,128)S(1)}, u32[]{:S(2)}, u32[]{:S(2)}) %collective-permute-start.16) | collective-permute-done | bytes 65568 | tf_op jit(solution)/shard_map/ppermute | solution.py:29
  90.2 2.6 %collective-permute-done.17 = f32[88,128]{1,0:T(8,128)S(1)} collective-permute-done((f32[88,128]{1,0:T(8,128)S(1)}, f32[88,128]{1,0:T(8,128)S(1)}, u32[]{:S(2)}, u32[]{:S(2)}) %collective-permute-start.17) | collective-permute-done | bytes 45088 | tf_op jit(solution)/shard_map/ppermute | solution.py:29
  93.0 3.3 %collective-permute-done.18 = f32[112,128]{1,0:T(8,128)S(1)} collective-permute-done((f32[112,128]{1,0:T(8,128)S(1)}, f32[112,128]{1,0:T(8,128)S(1)}, u32[]{:S(2)}, u32[]{:S(2)}) %collective-permute-start.18) | collective-permute-done | bytes 57376 | tf_op jit(solution)/shard_map/ppermute | solution.py:29
  96.5 23.1 %all_to_all.15.packed = f32[8,224,128]{2,1,0:T(8,128)S(1)} all-to-all(f32[8,224,128]{2,1,0:T(8,128)S(1)} %broadcast_in_dim.6), channel_id=1, replica_groups={{0,8,16,24,32,40,48,56},{64,72,80,88,96,104,112,120},{128,136,144,152,1..., dimensions={0} | all-to-all | bytes 1835008 | tf_op jit(solution)/shard_map/all_to_all | solution.py:33
  121.0 15.3 %collective-permute-start.19 = (f32[256,768]{1,0:T(8,128)S(1)}, f32[256,768]{1,0:T(8,128)S(1)}, u32[]{:S(2)}, u32[]{:S(2)}) collective-permute-start(f32[256,768]{1,0:T(8,128)S(1)} %get-tuple-element.140), channel_id=1, source_target_pairs={{0,1},{1,0},{2,3},{3,2},{4,5},{5,4},{6,7},{7,6},{8,9},{9,8},{10,11... | collective-permute-start | bytes 2359304 | tf_op jit(solution)/shard_map/ppermute | solution.py:29
  136.6 1.7 collective-permute-done.19.right
  138.9 22.2 %all_to_all.16.parts = f32[32,8,768]{2,1,0:T(8,128)S(1)} all-to-all(f32[32,8,768]{2,1,0:T(8,128)S(1)} %bitcast.25), channel_id=1, replica_groups={{0,8,16,24,32,40,48,56,64,72,80,88,96,104,112,120,128,136,144,152,160,1..., dimensions={0} | all-to-all | bytes 1572864 | tf_op jit(solution)/shard_map/all_to_all | solution.py:33
  165.6 2.8 %collective-permute-start.22 = (f32[8,128]{1,0:T(8,128)S(1)}, f32[8,128]{1,0:T(8,128)S(1)}, u32[]{:S(2)}, u32[]{:S(2)}) collective-permute-start(f32[8,128]{1,0:T(8,128)S(1)} %constant_dynamic-slice_fusion), channel_id=1, source_target_pairs={{0,6},{1,7},{2,4},{3,5},{4,2},{5,3},{6,0},{7,1},{8,14},{9,15},{10,... | collective-permute-start | bytes 12296 | tf_op jit(solution)/shard_map/ppermute | solution.py:29
  172.0 19.9 %all_to_all.17 = f32[32,8,512]{2,1,0:T(8,128)S(1)} all-to-all(f32[32,8,512]{2,1,0:T(8,128)S(1)} %broadcast_in_dim.7), channel_id=1, replica_groups={{0,8,16,24,32,40,48,56,64,72,80,88,96,104,112,120,128,136,144,152,160,1..., dimensions={0} | all-to-all | bytes 1048576 | tf_op jit(solution)/shard_map/all_to_all | solution.py:33
  191.9 7.0 %collective-permute-start.24 = (f32[256,384]{1,0:T(8,128)S(1)}, f32[256,384]{1,0:T(8,128)S(1)}, u32[]{:S(2)}, u32[]{:S(2)}) collective-permute-start(f32[256,384]{1,0:T(8,128)S(1)} %slice.94), channel_id=1, source_target_pairs={{0,1},{1,0},{2,3},{3,2},{4,5},{5,4},{6,7},{7,6},{8,9},{9,8},{10,11... | collective-permute-start | bytes 1179656 | tf_op jit(solution)/shard_map/ppermute | solution.py:29
  200.2 2.3 %shard_map.64 = f32[512,1024]{1,0:T(8,128)} custom-call(s32[7]{0:T(128)S(1)} %stack.31.bits, f32[512,1024]{1,0:T(8,128)S(1)} %shard_map.63.state, f32[256,512]{1,0:T(8,128)S(1)} %bitcast.24, f32[256,384]{1,0:T(8,128)S(1)} %collective-permute-done.24.received, bf16[8,128,1024]{2,1,0:T(8,128)(2,1)S(1)} %copy-done.1), custom_call_target="tpu_custom_call" | custom-call | flops 402653184 | bytes 3145728 | tf_op jit(solution)/shard_map/pallas_call | solution.py:463
  (87 shorter events, 25.5 us)
Async XLA Ops:
  0.1 8.1 %copy-start = (bf16[8,256,1024]{2,1,0:T(8,128)(2,1)S(1)}, bf16[8,256,1024]{2,1,0:T(8,128)(2,1)}, u32[]{:S(2)}) copy-start(bf16[8,256,1024]{2,1,0:T(8,128)(2,1)} %proj.7) | copy-start | bytes 12582916
  0.1 8.1 %copy-start.1 = (bf16[8,128,1024]{2,1,0:T(8,128)(2,1)S(1)}, bf16[8,128,1024]{2,1,0:T(8,128)(2,1)}, u32[]{:S(2)}) copy-start(bf16[8,128,1024]{2,1,0:T(8,128)(2,1)} %up.9) | copy-start | bytes 6291460
  5.6 9.2 %collective-permute-start = (f32[512,128]{1,0:T(8,128)S(1)}, f32[512,128]{1,0:T(8,128)S(1)}, u32[]{:S(2)}, u32[]{:S(2)}) collective-permute-start(f32[512,128]{1,0:T(8,128)S(1)} %get-tuple-element.83), channel_id=1, source_target_pairs={{0,8},{8,0},{16,24},{24,16},{32,40},{40,32},{48,56},{56,48},{64,72... | collective-permute-start | bytes 786440 | tf_op jit(solution)/shard_map/ppermute | solution.py:29
  15.9 8.4 %collective-permute-start.1 = (f32[320,256]{1,0:T(8,128)S(1)}, f32[320,256]{1,0:T(8,128)S(1)}, u32[]{:S(2)}, u32[]{:S(2)}) collective-permute-start(f32[320,256]{1,0:T(8,128)S(1)} %get-tuple-element.95), channel_id=1, source_target_pairs={{0,8},{8,0},{16,24},{24,16},{32,40},{40,32},{48,56},{56,48},{64,72... | collective-permute-start | bytes 983048 | tf_op jit(solution)/shard_map/ppermute | solution.py:29
  24.9 4.6 %collective-permute-start.8 = (f32[192,256]{1,0:T(8,128)S(1)}, f32[192,256]{1,0:T(8,128)S(1)}, u32[]{:S(2)}, u32[]{:S(2)}) collective-permute-start(f32[192,256]{1,0:T(8,128)S(1)} %constant_dynamic-slice_fusion.6), channel_id=1, source_target_pairs={{0,64},{8,72},{16,80},{24,88},{32,96},{40,104},{48,112},{56,120},{... | collective-permute-start | bytes 589832 | tf_op jit(solution)/shard_map/ppermute | solution.py:29
  26.3 13.0 %collective-permute-start.3 = (f32[384,256]{1,0:T(8,128)S(1)}, f32[384,256]{1,0:T(8,128)S(1)}, u32[]{:S(2)}, u32[]{:S(2)}) collective-permute-start(f32[384,256]{1,0:T(8,128)S(1)} %get-tuple-element.102), channel_id=1, source_target_pairs={{0,8},{8,0},{16,24},{24,16},{32,40},{40,32},{48,56},{56,48},{64,72... | collective-permute-start | bytes 1179656 | tf_op jit(solution)/shard_map/ppermute | solution.py:29
  26.3 13.0 %collective-permute-start.2 = (f32[320,128]{1,0:T(8,128)S(1)}, f32[320,128]{1,0:T(8,128)S(1)}, u32[]{:S(2)}, u32[]{:S(2)}) collective-permute-start(f32[320,128]{1,0:T(8,128)S(1)} %get-tuple-element.99), channel_id=1, source_target_pairs={{0,16},{8,24},{16,0},{24,8},{32,48},{40,56},{48,32},{56,40},{64,80... | collective-permute-start | bytes 491528 | tf_op jit(solution)/shard_map/ppermute | solution.py:29
  29.6 15.7 %collective-permute-start.9 = (f32[96,256]{1,0:T(8,128)S(1)}, f32[96,256]{1,0:T(8,128)S(1)}, u32[]{:S(2)}, u32[]{:S(2)}) collective-permute-start(f32[96,256]{1,0:T(8,128)S(1)} %constant_dynamic-slice_fusion.5), channel_id=1, source_target_pairs={{0,192},{8,200},{16,208},{24,216},{32,224},{40,232},{48,240},{56,2... | collective-permute-start | bytes 294920 | tf_op jit(solution)/shard_map/ppermute | solution.py:29
  40.0 15.4 %collective-permute-start.6 = (f32[256,128]{1,0:T(8,128)S(1)}, f32[256,128]{1,0:T(8,128)S(1)}, u32[]{:S(2)}, u32[]{:S(2)}) collective-permute-start(f32[256,128]{1,0:T(8,128)S(1)} %get-tuple-element.103.c2), channel_id=1, source_target_pairs={{0,8},{8,0},{16,24},{24,16},{32,40},{40,32},{48,56},{56,48},{64,72... | collective-permute-start | bytes 393224 | tf_op jit(solution)/shard_map/ppermute | solution.py:29
  41.8 7.6 %collective-permute-start.4 = (f32[288,128]{1,0:T(8,128)S(1)}, f32[288,128]{1,0:T(8,128)S(1)}, u32[]{:S(2)}, u32[]{:S(2)}) collective-permute-start(f32[288,128]{1,0:T(8,128)S(1)} %get-tuple-element.105), channel_id=1, source_target_pairs={{0,48},{8,56},{16,32},{24,40},{32,16},{40,24},{48,0},{56,8},{64,11... | collective-permute-start | bytes 442376 | tf_op jit(solution)/shard_map/ppermute | solution.py:29
  49.4 5.9 %collective-permute-start.5 = (f32[256,128]{1,0:T(8,128)S(1)}, f32[256,128]{1,0:T(8,128)S(1)}, u32[]{:S(2)}, u32[]{:S(2)}) collective-permute-start(f32[256,128]{1,0:T(8,128)S(1)} %slice_add_fusion), channel_id=1, source_target_pairs={{0,16},{8,24},{16,0},{24,8},{32,48},{40,56},{48,32},{56,40},{64,80... | collective-permute-start | bytes 393224 | tf_op jit(solution)/shard_map/ppermute | solution.py:29
  55.3 4.5 %collective-permute-start.7 = (f32[256,128]{1,0:T(8,128)S(1)}, f32[256,128]{1,0:T(8,128)S(1)}, u32[]{:S(2)}, u32[]{:S(2)}) collective-permute-start(f32[256,128]{1,0:T(8,128)S(1)} %add.41.c3), channel_id=1, source_target_pairs={{0,8},{8,0},{16,24},{24,16},{32,40},{40,32},{48,56},{56,48},{64,72... | collective-permute-start | bytes 393224 | tf_op jit(solution)/shard_map/ppermute | solution.py:29
  61.1 6.6 %collective-permute-start.10 = (f32[640,128]{1,0:T(8,128)S(1)}, f32[640,128]{1,0:T(8,128)S(1)}, u32[]{:S(2)}, u32[]{:S(2)}) collective-permute-start(f32[640,128]{1,0:T(8,128)S(1)} %get-tuple-element.116), channel_id=1, source_target_pairs={{0,8},{8,0},{16,24},{24,16},{32,40},{40,32},{48,56},{56,48},{64,72... | collective-permute-start | bytes 983048 | tf_op jit(solution)/shard_map/ppermute | solution.py:29
  62.2 8.0 %collective-permute-start.14 = (f32[512,128]{1,0:T(8,128)S(1)}, f32[512,128]{1,0:T(8,128)S(1)}, u32[]{:S(2)}, u32[]{:S(2)}) collective-permute-start(f32[512,128]{1,0:T(8,128)S(1)} %get-tuple-element.126), channel_id=1, source_target_pairs={{0,56},{8,16},{16,8},{24,32},{32,24},{40,48},{48,40},{56,0},{64,12... | collective-permute-start | bytes 786440 | tf_op jit(solution)/shard_map/ppermute | solution.py:533
  68.3 9.1 %collective-permute-start.11 = (f32[368,128]{1,0:T(8,128)S(1)}, f32[368,128]{1,0:T(8,128)S(1)}, u32[]{:S(2)}, u32[]{:S(2)}) collective-permute-start(f32[368,128]{1,0:T(8,128)S(1)} %get-tuple-element.118), channel_id=1, source_target_pairs={{0,16},{8,24},{16,0},{24,8},{32,48},{40,56},{48,32},{56,40},{64,80... | collective-permute-start | bytes 565256 | tf_op jit(solution)/shard_map/ppermute | solution.py:29
  70.8 9.7 %collective-permute-start.15 = (f32[256,128]{1,0:T(8,128)S(1)}, f32[256,128]{1,0:T(8,128)S(1)}, u32[]{:S(2)}, u32[]{:S(2)}) collective-permute-start(f32[256,128]{1,0:T(8,128)S(1)} %get-tuple-element.128), channel_id=1, source_target_pairs={{0,48},{8,56},{16,32},{24,40},{32,16},{40,24},{48,0},{56,8},{64,11... | collective-permute-start | bytes 393224 | tf_op jit(solution)/shard_map/ppermute | solution.py:29
  77.9 6.2 %collective-permute-start.12 = (f32[280,128]{1,0:T(8,128)S(1)}, f32[280,128]{1,0:T(8,128)S(1)}, u32[]{:S(2)}, u32[]{:S(2)}) collective-permute-start(f32[280,128]{1,0:T(8,128)S(1)} %get-tuple-element.121), channel_id=1, source_target_pairs={{0,48},{8,56},{16,32},{24,40},{32,16},{40,24},{48,0},{56,8},{64,11... | collective-permute-start | bytes 430088 | tf_op jit(solution)/shard_map/ppermute | solution.py:29
  81.1 6.7 %collective-permute-start.16 = (f32[128,128]{1,0:T(8,128)S(1)}, f32[128,128]{1,0:T(8,128)S(1)}, u32[]{:S(2)}, u32[]{:S(2)}) collective-permute-start(f32[128,128]{1,0:T(8,128)S(1)} %get-tuple-element.130), channel_id=1, source_target_pairs={{0,16},{8,24},{16,0},{24,8},{32,48},{40,56},{48,32},{56,40},{64,80... | collective-permute-start | bytes 196616 | tf_op jit(solution)/shard_map/ppermute | solution.py:29
  84.7 3.6 %collective-permute-start.13 = (f32[64,128]{1,0:T(8,128)S(1)}, f32[64,128]{1,0:T(8,128)S(1)}, u32[]{:S(2)}, u32[]{:S(2)}) collective-permute-start(f32[64,128]{1,0:T(8,128)S(1)} %get-tuple-element.124), channel_id=1, source_target_pairs={{0,64},{8,72},{16,80},{24,88},{32,96},{40,104},{48,112},{56,120},{... | collective-permute-start | bytes 98312 | tf_op jit(solution)/shard_map/ppermute | solution.py:29
  88.6 4.2 %collective-permute-start.17 = (f32[88,128]{1,0:T(8,128)S(1)}, f32[88,128]{1,0:T(8,128)S(1)}, u32[]{:S(2)}, u32[]{:S(2)}) collective-permute-start(f32[88,128]{1,0:T(8,128)S(1)} %pad_maximum_fusion.4), channel_id=1, source_target_pairs={{0,192},{8,200},{16,208},{24,216},{32,224},{40,232},{48,240},{56,2... | collective-permute-start | bytes 135176 | tf_op jit(solution)/shard_map/ppermute | solution.py:29
  92.9 3.4 %collective-permute-start.18 = (f32[112,128]{1,0:T(8,128)S(1)}, f32[112,128]{1,0:T(8,128)S(1)}, u32[]{:S(2)}, u32[]{:S(2)}) collective-permute-start(f32[112,128]{1,0:T(8,128)S(1)} %pad_maximum_fusion.3), channel_id=1, source_target_pairs={{0,64},{8,72},{16,80},{24,88},{32,96},{40,104},{48,112},{56,120},{... | collective-permute-start | bytes 172040 | tf_op jit(solution)/shard_map/ppermute | solution.py:29
  121.0 17.2 %collective-permute-start.19 = (f32[256,768]{1,0:T(8,128)S(1)}, f32[256,768]{1,0:T(8,128)S(1)}, u32[]{:S(2)}, u32[]{:S(2)}) collective-permute-start(f32[256,768]{1,0:T(8,128)S(1)} %get-tuple-element.140), channel_id=1, source_target_pairs={{0,1},{1,0},{2,3},{3,2},{4,5},{5,4},{6,7},{7,6},{8,9},{9,8},{10,11... | collective-permute-start | bytes 2359304 | tf_op jit(solution)/shard_map/ppermute | solution.py:29
  136.5 2.4 %collective-permute-start.20 = (f32[384,256]{1,0:T(8,128)S(1)}, f32[384,256]{1,0:T(8,128)S(1)}, u32[]{:S(2)}, u32[]{:S(2)}) collective-permute-start(f32[384,256]{1,0:T(8,128)S(1)} %pad_maximum_fusion), channel_id=1, source_target_pairs={{0,1},{1,0},{2,3},{3,2},{4,5},{5,4},{6,7},{7,6},{8,9},{9,8},{10,11... | collective-permute-start | bytes 1179656 | tf_op jit(solution)/shard_map/ppermute | solution.py:29
  162.4 2.8 %collective-permute-start.21 = (f32[8,128]{1,0:T(8,128)S(1)}, f32[8,128]{1,0:T(8,128)S(1)}, u32[]{:S(2)}, u32[]{:S(2)}) collective-permute-start(f32[8,128]{1,0:T(8,128)S(1)} %constant_dynamic-slice_fusion.1), channel_id=1, source_target_pairs={{0,2},{1,3},{2,0},{3,1},{4,6},{5,7},{6,4},{7,5},{8,10},{9,11},{10,... | collective-permute-start | bytes 12296 | tf_op jit(solution)/shard_map/ppermute | solution.py:29
  165.6 3.8 %collective-permute-start.22 = (f32[8,128]{1,0:T(8,128)S(1)}, f32[8,128]{1,0:T(8,128)S(1)}, u32[]{:S(2)}, u32[]{:S(2)}) collective-permute-start(f32[8,128]{1,0:T(8,128)S(1)} %constant_dynamic-slice_fusion), channel_id=1, source_target_pairs={{0,6},{1,7},{2,4},{3,5},{4,2},{5,3},{6,0},{7,1},{8,14},{9,15},{10,... | collective-permute-start | bytes 12296 | tf_op jit(solution)/shard_map/ppermute | solution.py:29
  169.4 2.5 %collective-permute-start.23 = (f32[8,128]{1,0:T(8,128)S(1)}, f32[8,128]{1,0:T(8,128)S(1)}, u32[]{:S(2)}, u32[]{:S(2)}) collective-permute-start(f32[8,128]{1,0:T(8,128)S(1)} %dynamic-slice_add_fusion.2), channel_id=1, source_target_pairs={{0,2},{1,3},{2,0},{3,1},{4,6},{5,7},{6,4},{7,5},{8,10},{9,11},{10,... | collective-permute-start | bytes 12296 | tf_op jit(solution)/shard_map/ppermute | solution.py:29
  191.9 8.3 %collective-permute-start.24 = (f32[256,384]{1,0:T(8,128)S(1)}, f32[256,384]{1,0:T(8,128)S(1)}, u32[]{:S(2)}, u32[]{:S(2)}) collective-permute-start(f32[256,384]{1,0:T(8,128)S(1)} %slice.94), channel_id=1, source_target_pairs={{0,1},{1,0},{2,3},{3,2},{4,5},{5,4},{6,7},{7,6},{8,9},{9,8},{10,11... | collective-permute-start | bytes 1179656 | tf_op jit(solution)/shard_map/ppermute | solution.py:29
